TPU v7x, 32 devices: a whole 2x2x4 slice. The times are simulated.
32 devices in a mesh: grp: 2 (over x), limb: 16 (over z, y, core).
Axes of the slice: x: 2, y: 2, z: 4, core: 2. Of those that a mesh axis runs over, the one named last changes fastest.
Arguments:
- digits: float32 [8, 3, 16, 65536], P('grp', None, None, 'limb'), may hold values from 0 to 2047, as said below
- keys: float32 [8, 3, 2, 16, 65536], P('grp', None, None, None, 'limb'), may hold values from 0 to 2047, as said below
- requests: int32 [8, 8], P('grp'), may hold values from 0 to 1, as said below
- rotations: int32 [8], replicated, may hold values from 1 to 256, as said below
- moduli: int32 [16], replicated, may hold values from 2048 to 4095
Outputs:
- switched: float32 [8, 2, 16, 65536], P('grp', None, None, 'limb')
Inputs may be any that keep to these rules, and one draw needn't show every extreme that they name: `digits`: every entry is an integer. `keys`: every entry is an integer. `requests`: for each block of ciphertexts k * 4 to (k + 1) * 4 - 1 and each owner group's keys g * 4 to (g + 1) * 4 - 1, between 1 and 2 of those ciphertexts request one or more of those keys; in every draw some owner group is requested by exactly 2 ciphertexts of every block. `rotations`: the largest amount is exactly 256.
All inputs are finite; a program needn't handle non-finite values.
Results may differ from a plain program's by a relative error of at most 0.0003.
Values sent between devices are 32-bit elements; how exact they have to be, the bound alone decides.
No kernel may reach another device: no remote copies, remote signals or barrier semaphores. Data moves between devices by JAX's collectives and lax.ppermute only.
A program may use at most 64 MiB of HBM per device.

v0:
```python
import jax
import jax.numpy as jnp
from jax import lax
from jax.sharding import PartitionSpec as P

RMAX = 256
CAP = 2


exact_mode = lax.Precision.HIGHEST


def from_behind(value, axis, steps):
    count = lax.axis_size(axis)
    pairs = [(source, (source + steps) % count) for source in range(count)]
    return lax.ppermute(value, axis, pairs)


def reduce_mod(amount, modulus):
    quotient = jnp.floor(amount * (1.0 / modulus))
    remainder = amount - quotient * modulus
    remainder = jnp.where(remainder < 0, remainder + modulus, remainder)
    return jnp.where(remainder >= modulus, remainder - modulus, remainder)


def per_device(digits, keys, requests, rotations, moduli):
    groups = lax.axis_size("grp")
    key_count = keys.shape[0]
    cipher_count = digits.shape[0]
    columns = digits.shape[-1]
    capacity = CAP
    widest = 2 * RMAX
    modulus = moduli.astype(jnp.float32)[:, None]
    wanted = requests.astype(jnp.float32).reshape(cipher_count, groups, key_count)
    needed = (jnp.sum(wanted, axis=2) > 0).astype(jnp.float32)
    rank_in = jnp.cumsum(needed, axis=0) - 1.0
    slot_index = jnp.arange(capacity, dtype=jnp.float32)
    chooser = needed.T[:, None, :] * (rank_in.T[:, None, :] == slot_index[None, :, None]).astype(
        jnp.float32
    )
    outgoing = jnp.einsum("hsc,cjlx->hsjlx", chooser, digits, precision=exact_mode)
    key_marks = jnp.einsum("hsc,chi->hsi", chooser, wanted, precision=exact_mode)
    amounts = 2 * lax.dynamic_slice_in_dim(rotations, lax.axis_index("grp") * key_count, key_count)
    position = jnp.arange(columns)
    incoming = lax.all_to_all(outgoing, "grp", split_axis=0, concat_axis=0, tiled=True)
    marks = lax.all_to_all(key_marks, "grp", split_axis=0, concat_axis=0, tiled=True)
    resident = jnp.zeros(incoming.shape[:2] + (2,) + incoming.shape[3:], jnp.float32)
    rim_parts = []
    for key_index in range(key_count):
        combined = incoming[:, :, 0, None] * keys[key_index, 0]
        for digit_index in range(1, incoming.shape[2]):
            combined = combined + incoming[:, :, digit_index, None] * keys[key_index, digit_index]
        product = reduce_mod(combined, modulus) * marks[:, :, key_index, None, None, None]
        rotated = jnp.roll(product, -amounts[key_index], axis=4)
        inside = position < columns - amounts[key_index]
        resident = resident + jnp.where(inside, rotated, 0.0)
        rim_parts.append(jnp.where(inside, 0.0, rotated))
    rim_sum = rim_parts[0]
    for extra in rim_parts[1:]:
        rim_sum = rim_sum + extra
    rim_tail = rim_sum[..., columns - widest :]
    returned = (
        lax.all_to_all(resident, "grp", split_axis=0, concat_axis=0, tiled=True),
        lax.all_to_all(rim_tail, "grp", split_axis=0, concat_axis=0, tiled=True),
    )
    resident_back, tail_back = returned
    gathered = jnp.einsum("hsc,hsplx->cplx", chooser, resident_back, precision=exact_mode)
    tail_sum = jnp.einsum("hsc,hsplx->cplx", chooser, tail_back, precision=exact_mode)
    arrived = from_behind(tail_sum, "limb", -1)
    gathered = gathered + jnp.pad(arrived, ((0, 0),) * 3 + ((columns - widest, 0),))
    return reduce_mod(gathered, modulus) / modulus


def solution(mesh):
    in_specs = (
        P("grp", None, None, "limb"),
        P("grp", None, None, None, "limb"),
        P("grp", None),
        P(),
        P(),
    )
    out_specs = P("grp", None, None, "limb")
    return jax.shard_map(
        per_device, mesh=mesh, in_specs=in_specs, out_specs=out_specs, check_vma=False
    )
```

profile of v0, /device:TPU:0, one launch (start us, length us, event | category | flops | bytes accessed | tf_op | source)
XLA Modules:
  0.0 146.2 jit_solution(5528420706276619517)
XLA Ops:
  0.0 0.7 convert_element_type.18
  0.7 0.1 reshape.28
  0.8 0.1 reduce_sum.9
  0.9 0.1 copy.25
  1.0 0.1 copy.26
  1.1 0.7 fusion.15
  1.8 4.2 %all-to-all-start.1 = ((f32[2,2,4]{2,1,0:T(2,128)}), f32[2,2,4]{2,1,0:T(2,128)S(1)}, u32[]{:S(2)}, u32[]{:S(2)}) async-start(f32[2,2,4]{2,1,0:T(2,128)} %fusion.15), calls=%async_computation.1 | async-start | bytes 4096 | tf_op jit(solution)/shard_map/all_to_all | solution.py:46
  6.1 0.0 copy-start.12
  6.1 13.1 %fusion = f32[2,2,3,16,4096]{4,1,3,2,0:T(2,128)} fusion(f32[4,3,16,4096]{3,2,1,0:T(8,128)} %param.7, f32[2,4]{1,0:T(2,128)S(1)} %copy.26, f32[2,4]{1,0:T(2,128)S(1)} %copy.25), kind=kOutput, calls=%fused_computation.19 | convolution fusion | flops 37748768 | bytes 6291520 | tf_op jit(solution)/shard_map/hsc,cjlx->hsjlx/dot_general | solution.py:41
  19.1 0.0 copy-done.12
  19.1 0.1 dynamic-slice_multiply_fusion
  19.2 0.6 fusion.41
  21.0 0.0 copy-start.13
  21.0 0.0 all-to-all-done.1
  21.0 4.1 %all-to-all-start = ((f32[2,2,3,16,4096]{4,1,3,2,0:T(2,128)}), f32[2,2,3,16,4096]{4,1,3,2,0:T(2,128)S(1)}, u32[]{:S(2)}, u32[]{:S(2)}) async-start(f32[2,2,3,16,4096]{4,1,3,2,0:T(2,128)} %fusion), calls=%async_computation | async-start | bytes 6291456 | tf_op jit(solution)/shard_map/all_to_all | solution.py:45
  28.9 0.0 copy-done.13
  29.1 5.5 %slice_bitcast_fusion.5 = (f32[2,16,4096]{2,1,0:T(8,128)}, f32[2,16,4096]{2,1,0:T(8,128)}, f32[2,16,4096]{2,1,0:T(8,128)}, f32[2,16,4096]{2,1,0:T(8,128)}, f32[2...) fusion(f32[4,3,2,16,4096]{4,3,2,1,0:T(8,128)} %param.8), kind=kLoop, calls=%fused_computation.39 | loop fusion | bytes 12582912 | tf_op jit(solution)/shard_map/mul | solution.py:50
  34.6 0.1 slice_reduce_fusion.3
  34.7 27.0 %all-to-all-done = f32[2,2,3,16,4096]{4,1,3,2,0:T(2,128)S(1)} async-done(((f32[2,2,3,16,4096]{4,1,3,2,0:T(2,128)}), f32[2,2,3,16,4096]{4,1,3,2,0:T(2,128)S(1)}, u32[]{:S(2)}, u32[]{:S(2)}) %all-to-all-start) | async-done | bytes 3145760 | tf_op jit(solution)/shard_map/all_to_all | solution.py:45
  61.7 0.0 copy-start
  61.7 0.0 copy-start.1
  61.7 0.0 copy-start.2
  61.7 0.2 slice_bitcast_fusion.2
  62.0 0.8 copy-done
  62.8 0.2 copy-done.1
  62.9 0.2 copy-done.2
  63.1 0.0 copy-start.3
  63.1 0.0 copy-start.4
  63.1 0.0 copy-start.5
  63.1 0.0 copy-start.6
  63.1 0.0 copy-start.7
  63.1 0.0 copy-start.8
  63.1 0.0 copy-start.9
  63.1 0.0 copy-start.10
  63.1 0.0 copy-start.11
  63.2 4.6 %fusion.8 = f32[2,2,2,16,4096]{4,1,3,2,0:T(2,128)S(1)} fusion(f32[16]{0:T(128)S(1)} %broadcast_divide_fusion, f32[2,2]{1,0:T(2,128)S(1)} %get-tuple-element.6, f32[2,16,4096]{2,1,0:T(8,128)S(1)} %copy-done, f32[2,2,16,4096]{3,1,2,0:T(2,128)S(1)} %get-tuple-element.31, f32[2,16,4096]{2,1,0:T(8,128)S(1)} %copy-done.1, ...), kind=kLoop, calls=%fused_computation.27 | loop fusion | flops 8388608 | bytes 6815888 | tf_op jit(solution)/shard_map/mul | solution.py:53
  67.7 0.0 copy-done.3
  67.7 0.0 copy-done.4
  67.7 0.0 copy-done.5
  67.8 0.0 copy-done.6
  67.8 0.0 copy-done.7
  67.8 0.0 copy-done.8
  67.8 0.0 copy-done.9
  67.8 0.0 copy-done.10
  67.8 0.0 copy-done.11
  67.8 13.4 %fusion.11 = (f32[2,2,2,16,4096]{4,1,3,2,0:T(2,128)S(1)}, f32[2,2,2,16,4096]{4,1,3,2,0:T(2,128)S(1)}, f32[2,2,2,16,4096]{4,1,3,2,0:T(2,128)S(1)}) fusion(f32[16]{0:T(128)S(1)} %broadcast_divide_fusion, f32[2,2]{1,0:T(2,128)S(1)} %get-tuple-element.7, f32[2,16,4096]{2,1,0:T(8,128)S(1)} %copy-done.10, f32[2,16,4096]{2,1,0:T(8,128)S(1)} %copy-done.11, ...), kind=kLoop, calls=%fused_computation.30 | loop fusion | flops 25165824 | bytes 14155952 | tf_op jit(solution)/shard_map/mul | solution.py:53
  81.2 18.7 %select_add_fusion = (f32[2,2,2,16,4096]{4,1,3,2,0:T(2,128)}, f32[2,2,2,16,4096]{4,1,3,2,0:T(2,128)S(1)}, f32[2,2,2,16,4096]{4,1,3,2,0:T(2,128)S(1)}, f32[2,2,2,...) fusion(pred[4096]{0:T(1024)(128)(4,1)S(1)} %get-tuple-element.39, pred[4096]{0:T(1024)(128)(4,1)S(1)} %get-tuple-element.40, ...), kind=kLoop, calls=%fused_computation.32 | loop fusion | flops 5767168 | bytes 18890768 | tf_op jit(solution)/shard_map/add | solution.py:56
  99.9 0.5 fusion.12
  100.5 7.6 %all_to_all.20 = f32[2,2,2,16,512]{4,1,3,2,0:T(2,128)S(1)} all-to-all(f32[2,2,2,16,512]{4,1,3,2,0:T(2,128)S(1)} %fusion.12), channel_id=1, replica_groups=mesh['grp'=2,'limb'=16] {'grp'}, dimensions={0} | all-to-all | bytes 524288 | tf_op jit(solution)/shard_map/all_to_all | solution.py:64
  108.0 4.8 %all-to-all-start.2 = ((f32[2,2,2,16,4096]{4,1,3,2,0:T(2,128)}), f32[2,2,2,16,4096]{4,1,3,2,0:T(2,128)}, u32[]{:S(2)}, u32[]{:S(2)}) async-start(f32[2,2,2,16,4096]{4,1,3,2,0:T(2,128)} %get-tuple-element.10), calls=%async_computation.2 | async-start | bytes 4194304 | tf_op jit(solution)/shard_map/all_to_all | solution.py:63
  112.9 0.8 convolution_bitcast_fusion.1
  113.6 0.1 copy.31
  113.7 2.5 %collective-permute-start = (f32[4,2,16,512]{3,2,1,0:T(8,128)S(1)}, f32[4,2,16,512]{3,2,1,0:T(8,128)S(1)}, u32[]{:S(2)}, u32[]{:S(2)}) collective-permute-start(f32[4,2,16,512]{3,2,1,0:T(8,128)S(1)} %copy.31), channel_id=1, source_target_pairs={{0,15},{1,0},{2,1},{3,2},{4,3},{5,4},{6,5},{7,6},{8,7},{9,8},{10,9... | collective-permute-start | bytes 786440 | tf_op jit(solution)/shard_map/ppermute | solution.py:16
  116.2 20.0 %all-to-all-done.2 = f32[2,2,2,16,4096]{4,1,3,2,0:T(2,128)} async-done(((f32[2,2,2,16,4096]{4,1,3,2,0:T(2,128)}), f32[2,2,2,16,4096]{4,1,3,2,0:T(2,128)}, u32[]{:S(2)}, u32[]{:S(2)}) %all-to-all-start.2) | async-done | bytes 2097184 | tf_op jit(solution)/shard_map/all_to_all | solution.py:63
  136.3 7.3 %convolution_bitcast_fusion = f32[4,2,16,4096]{3,0,2,1:T(4,128)S(1)} fusion(f32[2,2,2,16,4096]{4,1,3,2,0:T(2,128)} %all-to-all-done.2, f32[2,4]{1,0:T(2,128)S(1)} %copy.26, f32[2,4]{1,0:T(2,128)S(1)} %copy.25), kind=kOutput, calls=%fused_computation.10 | convolution fusion | flops 25165856 | bytes 4194368 | tf_op jit(solution)/shard_map/hsc,hsplx->cplx/dot_general | solution.py:67
  143.6 0.0 collective-permute-done
  143.6 2.6 %fusion.7 = f32[4,2,16,4096]{3,2,1,0:T(8,128)} fusion(f32[4,2,16,4096]{3,0,2,1:T(4,128)S(1)} %convolution_bitcast_fusion, f32[4,2,16,512]{3,2,1,0:T(8,128)S(1)} %collective-permute-done, f32[16]{0:T(128)S(1)} %convert_element_type.22, f32[16]{0:T(128)S(1)} %broadcast_divide_fusion), kind=kLoop, calls=%fused_computation.26 | loop fusion | flops 6291456 | bytes 4456576 | tf_op jit(solution)/shard_map/div | solution.py:71
  (11 shorter events, 0.1 us)
Async XLA Ops:
  1.8 19.2 %all-to-all-start.1 = ((f32[2,2,4]{2,1,0:T(2,128)}), f32[2,2,4]{2,1,0:T(2,128)S(1)}, u32[]{:S(2)}, u32[]{:S(2)}) async-start(f32[2,2,4]{2,1,0:T(2,128)} %fusion.15), calls=%async_computation.1 | async-start | bytes 4096 | tf_op jit(solution)/shard_map/all_to_all | solution.py:46
  6.1 13.1 %copy-start.12 = (s32[8]{0:T(128)S(1)}, s32[8]{0:T(128)}, u32[]{:S(2)}) copy-start(s32[8]{0:T(128)} %param.10) | copy-start | bytes 100
  21.0 7.9 %copy-start.13 = (s32[16]{0:T(128)S(1)}, s32[16]{0:T(128)}, u32[]{:S(2)}) copy-start(s32[16]{0:T(128)} %param.11) | copy-start | bytes 196
  21.0 40.7 %all-to-all-start = ((f32[2,2,3,16,4096]{4,1,3,2,0:T(2,128)}), f32[2,2,3,16,4096]{4,1,3,2,0:T(2,128)S(1)}, u32[]{:S(2)}, u32[]{:S(2)}) async-start(f32[2,2,3,16,4096]{4,1,3,2,0:T(2,128)} %fusion), calls=%async_computation | async-start | bytes 6291456 | tf_op jit(solution)/shard_map/all_to_all | solution.py:45
  61.7 1.0 copy-start
  61.7 1.2 copy-start.1
  61.7 1.4 copy-start.2
  63.1 4.6 %copy-start.3 = (f32[2,16,4096]{2,1,0:T(8,128)S(1)}, f32[2,16,4096]{2,1,0:T(8,128)}, u32[]{:S(2)}) copy-start(f32[2,16,4096]{2,1,0:T(8,128)} %get-tuple-element.15) | copy-start | bytes 1572868
  63.1 4.6 %copy-start.4 = (f32[2,16,4096]{2,1,0:T(8,128)S(1)}, f32[2,16,4096]{2,1,0:T(8,128)}, u32[]{:S(2)}) copy-start(f32[2,16,4096]{2,1,0:T(8,128)} %get-tuple-element.16) | copy-start | bytes 1572868
  63.1 4.7 %copy-start.5 = (f32[2,16,4096]{2,1,0:T(8,128)S(1)}, f32[2,16,4096]{2,1,0:T(8,128)}, u32[]{:S(2)}) copy-start(f32[2,16,4096]{2,1,0:T(8,128)} %get-tuple-element.17) | copy-start | bytes 1572868
  63.1 4.7 %copy-start.6 = (f32[2,16,4096]{2,1,0:T(8,128)S(1)}, f32[2,16,4096]{2,1,0:T(8,128)}, u32[]{:S(2)}) copy-start(f32[2,16,4096]{2,1,0:T(8,128)} %get-tuple-element.18) | copy-start | bytes 1572868
  63.1 4.7 %copy-start.7 = (f32[2,16,4096]{2,1,0:T(8,128)S(1)}, f32[2,16,4096]{2,1,0:T(8,128)}, u32[]{:S(2)}) copy-start(f32[2,16,4096]{2,1,0:T(8,128)} %get-tuple-element.19) | copy-start | bytes 1572868
  63.1 4.7 %copy-start.8 = (f32[2,16,4096]{2,1,0:T(8,128)S(1)}, f32[2,16,4096]{2,1,0:T(8,128)}, u32[]{:S(2)}) copy-start(f32[2,16,4096]{2,1,0:T(8,128)} %get-tuple-element.20) | copy-start | bytes 1572868
  63.1 4.7 %copy-start.9 = (f32[2,16,4096]{2,1,0:T(8,128)S(1)}, f32[2,16,4096]{2,1,0:T(8,128)}, u32[]{:S(2)}) copy-start(f32[2,16,4096]{2,1,0:T(8,128)} %get-tuple-element.21) | copy-start | bytes 1572868
  63.1 4.7 %copy-start.10 = (f32[2,16,4096]{2,1,0:T(8,128)S(1)}, f32[2,16,4096]{2,1,0:T(8,128)}, u32[]{:S(2)}) copy-start(f32[2,16,4096]{2,1,0:T(8,128)} %get-tuple-element.25) | copy-start | bytes 1572868
  63.1 4.7 %copy-start.11 = (f32[2,16,4096]{2,1,0:T(8,128)S(1)}, f32[2,16,4096]{2,1,0:T(8,128)}, u32[]{:S(2)}) copy-start(f32[2,16,4096]{2,1,0:T(8,128)} %get-tuple-element.26) | copy-start | bytes 1572868
  108.0 28.2 %all-to-all-start.2 = ((f32[2,2,2,16,4096]{4,1,3,2,0:T(2,128)}), f32[2,2,2,16,4096]{4,1,3,2,0:T(2,128)}, u32[]{:S(2)}, u32[]{:S(2)}) async-start(f32[2,2,2,16,4096]{4,1,3,2,0:T(2,128)} %get-tuple-element.10), calls=%async_computation.2 | async-start | bytes 4194304 | tf_op jit(solution)/shard_map/all_to_all | solution.py:63
  113.7 29.9 %collective-permute-start = (f32[4,2,16,512]{3,2,1,0:T(8,128)S(1)}, f32[4,2,16,512]{3,2,1,0:T(8,128)S(1)}, u32[]{:S(2)}, u32[]{:S(2)}) collective-permute-start(f32[4,2,16,512]{3,2,1,0:T(8,128)S(1)} %copy.31), channel_id=1, source_target_pairs={{0,15},{1,0},{2,1},{3,2},{4,3},{5,4},{6,5},{7,6},{8,7},{9,8},{10,9... | collective-permute-start | bytes 786440 | tf_op jit(solution)/shard_map/ppermute | solution.py:16
where the time goes:
time: 147 us; the launch traced here: 146 us
  waiting for transfers between devices  47 us (32%)
  other arithmetic  40.8 us (28%)
  matrix products  21.9 us (15%)
  starting transfers between devices  15.7 us (11%)
  local copies, waits for them, and re-layouts  8.03 us (5%)
  blocking collectives  7.56 us (5%)
  between operations  5.25 us (4%)
    all_to_all x1, waiting for transfers between devices, per_device(): lax.all_to_all(outgoing, 'grp', split_axis=0, concat_axis=0, tiled=True)  27 us
    all_to_all x1, waiting for transfers between devices, per_device(): lax.all_to_all(resident, 'grp', split_axis=0, concat_axis=0, tiled=True)  20 us
    add x1, other arithmetic, per_device(): resident = resident + jnp.where(inside, rotated, 0.0)  18.7 us
    mul x2, other arithmetic, per_device(): reduce_mod(combined, modulus) * marks[:, :, key_index, None, None, None]  18 us
    dot_general x1, matrix products, per_device(): jnp.einsum('hsc,cjlx->hsjlx', chooser, digits, precision=exact_mode)  13.1 us
    all_to_all x1, blocking collectives, per_device(): lax.all_to_all(rim_tail, 'grp', split_axis=0, concat_axis=0, tiled=True)  7.56 us
    dot_general x1, matrix products, per_device(): jnp.einsum('hsc,hsplx->cplx', chooser, resident_back, precision=exact_mode)  7.33 us
    mul x2, local copies, waits for them, and re-layouts, per_device(): combined = incoming[:, :, 0, None] * keys[key_index, 0]  5.71 us
  transfers between devices with their start and end apart: 4, of which 2 were waited for; matrix products, arithmetic and copies ran while one was open for 19% of the time, Pallas kernels for 0%

commit v1 on v0

v1 whole, which is shorter than its diff:
```python
import functools

import jax
import jax.numpy as jnp
from jax import lax
from jax.experimental import pallas as pl
from jax.experimental.pallas import tpu as pltpu
from jax.sharding import PartitionSpec as P

RMAX = 256
CAP = 2
WIDEST = 2 * RMAX
LANES = 128
ROWS = 8


def shifted(value, axis, steps):
    count = lax.axis_size(axis)
    pairs = [(source, (source + steps) % count) for source in range(count)]
    return lax.ppermute(value, axis, pairs)


def slot_ciphers(requests, ciphers, key_count, owner):
    needed = []
    for cipher in range(ciphers):
        flag = requests[cipher, owner * key_count]
        for key in range(1, key_count):
            flag = flag | requests[cipher, owner * key_count + key]
        needed.append(flag)
    slots = [jnp.int32(0)] * CAP
    rank = jnp.int32(0)
    for want in (1, 0):
        for cipher in range(ciphers):
            here = needed[cipher] == want
            for slot in range(CAP):
                slots[slot] = jnp.where(here & (rank == slot), cipher, slots[slot])
            rank = rank + here.astype(jnp.int32)
    return slots


def gather_kernel(slot, ciphers, key_count, requests, owner, digits, out, held, in_sems, out_sems):
    cipher = slot_ciphers(requests, ciphers, key_count, owner[0])[slot]
    parts = held.shape[0]
    loads = [pltpu.make_async_copy(digits.at[cipher, j], held.at[j], in_sems.at[j]) for j in range(parts)]
    stores = [pltpu.make_async_copy(held.at[j], out.at[j], out_sems.at[j]) for j in range(parts)]
    for load in loads:
        load.start()
    for load, store in zip(loads, stores):
        load.wait()
        store.start()
    for store in stores:
        store.wait()


def gather_slot(digits, requests, owner, slot):
    ciphers, parts, limbs, columns = digits.shape
    key_count = requests.shape[1] // lax.axis_size("grp")
    return pl.pallas_call(
        functools.partial(gather_kernel, slot, ciphers, key_count),
        out_shape=jax.ShapeDtypeStruct((parts, limbs, columns), jnp.float32),
        in_specs=[
            pl.BlockSpec(memory_space=pltpu.SMEM),
            pl.BlockSpec(memory_space=pltpu.SMEM),
            pl.BlockSpec(memory_space=pl.ANY),
        ],
        out_specs=pl.BlockSpec(memory_space=pl.ANY),
        scratch_shapes=[
            pltpu.VMEM((parts, limbs, columns), jnp.float32),
            pltpu.SemaphoreType.DMA((parts,)),
            pltpu.SemaphoreType.DMA((parts,)),
        ],
        cost_estimate=pl.CostEstimate(flops=0, transcendentals=0, bytes_accessed=8 * parts * limbs * columns),
        name="gather_digits",
    )(requests, owner, digits)


def products_kernel(slots, digit_parts, ciphers, key_count, local, requests, owner, rotations, *refs):
    digit_refs = refs[: len(slots)]
    keys, modulus_ref = refs[len(slots) : len(slots) + 2]
    tail, resident, rolled = refs[len(slots) + 2 :]
    key = pl.program_id(1)
    columns = resident.shape[-1]
    pad = WIDEST // LANES
    tiles = columns // LANES

    @pl.when(key == 0)
    def _():
        tail[...] = jnp.zeros_like(tail)
        resident[...] = jnp.zeros_like(resident)
        rolled[...] = jnp.zeros_like(rolled)

    amount = 2 * rotations[owner[0] * key_count + key]
    skipped = amount // LANES
    within = amount - skipped * LANES
    turn = lax.rem(LANES - within, LANES)
    modulus = modulus_ref[...]
    inverse = 1.0 / modulus
    lane = lax.broadcasted_iota(jnp.int32, (ROWS, LANES), 1)
    from_this = lane < LANES - within
    chosen = slot_ciphers(requests, ciphers, key_count, owner[0])

    for place, slot in enumerate(slots):
        mark = requests[chosen[slot], owner[0] * key_count + key]

        @pl.when(mark > 0)
        def _():
            for poly in range(2):
                for tile in range(tiles):
                    at = pl.ds(tile * LANES, LANES)
                    combined = digit_refs[place][0, :, at] * keys[0, poly, :, at]
                    for part in range(1, digit_parts):
                        combined = combined + digit_refs[place][part, :, at] * keys[part, poly, :, at]
                    quotient = jnp.floor(combined * inverse)
                    remainder = combined - quotient * modulus
                    rolled[:, pl.ds((pad + tile) * LANES, LANES)] = pltpu.roll(remainder, turn, 1)
                for tile in range(pad + tiles):
                    start = pl.multiple_of((skipped + tile) * LANES, LANES)
                    after = pl.multiple_of((skipped + tile + 1) * LANES, LANES)
                    moved = jnp.where(from_this, rolled[:, pl.ds(start, LANES)], rolled[:, pl.ds(after, LANES)])
                    if tile < pad:
                        at = pl.ds(tile * LANES, LANES)
                        tail[place, poly, :, at] = tail[place, poly, :, at] + moved
                    else:
                        at = pl.ds((tile - pad) * LANES, LANES)
                        resident[place, poly, :, at] = resident[place, poly, :, at] + moved


def products(digits, keys, requests, owner, rotations, modulus, slots, local):
    key_count, parts, polys, limbs, columns = keys.shape
    ciphers = requests.shape[0]
    count = len(slots)
    pad = WIDEST // LANES

    if local:
        def digit_spec(slot):
            def index(block, key, requests, owner, rotations):
                return (slot_ciphers(requests, ciphers, key_count, owner[0])[slot], 0, block, 0)
            return pl.BlockSpec((pl.Squeezed(), parts, ROWS, columns), index)
        digit_specs = [digit_spec(slot) for slot in slots]
        digit_args = [digits] * count
    else:
        digit_specs = [pl.BlockSpec((parts, ROWS, columns), lambda block, key, *_: (0, block, 0))] * count
        digit_args = list(digits)
    tail_shape = (count, polys, limbs, WIDEST)
    resident_shape = (count, polys, limbs, columns)
    work = count * key_count * polys * limbs * columns
    return pl.pallas_call(
        functools.partial(products_kernel, slots, parts, ciphers, key_count, local),
        out_shape=[
            jax.ShapeDtypeStruct(tail_shape, jnp.float32),
            jax.ShapeDtypeStruct(resident_shape, jnp.float32),
        ],
        grid_spec=pltpu.PrefetchScalarGridSpec(
            num_scalar_prefetch=3,
            grid=(limbs // ROWS, key_count),
            in_specs=digit_specs
            + [
                pl.BlockSpec(
                    (pl.Squeezed(), parts, polys, ROWS, columns), lambda block, key, *_: (key, 0, 0, block, 0)
                ),
                pl.BlockSpec((ROWS, LANES), lambda block, key, *_: (block, 0)),
            ],
            out_specs=[
                pl.BlockSpec((count, polys, ROWS, WIDEST), lambda block, key, *_: (0, 0, block, 0)),
                pl.BlockSpec((count, polys, ROWS, columns), lambda block, key, *_: (0, 0, block, 0)),
            ],
            scratch_shapes=[pltpu.VMEM((ROWS, columns + 2 * pad * LANES + LANES), jnp.float32)],
        ),
        compiler_params=pltpu.CompilerParams(dimension_semantics=("arbitrary", "arbitrary")),
        cost_estimate=pl.CostEstimate(
            flops=20 * work, transcendentals=0, bytes_accessed=4 * (keys.size + count * limbs * columns * (parts + polys))
        ),
        name="products",
    )(requests, owner, rotations, *digit_args, keys, modulus)


def add_tail_kernel(arrived, held, out):
    out[...] = held[...] + arrived[...]


def add_tail(resident, arrived):
    count, polys, limbs, columns = resident.shape
    last = columns // WIDEST - 1
    here = pl.BlockSpec((count, polys, limbs, WIDEST), lambda i: (0, 0, 0, last))
    return pl.pallas_call(
        add_tail_kernel,
        out_shape=jax.ShapeDtypeStruct(resident.shape, jnp.float32),
        grid=(1,),
        in_specs=[pl.BlockSpec((count, polys, limbs, WIDEST), lambda i: (0, 0, 0, 0)), here],
        out_specs=here,
        input_output_aliases={1: 0},
        name="add_tail",
    )(arrived, resident)


def reduce_mod(amount, modulus):
    quotient = jnp.floor(amount * (1.0 / modulus))
    remainder = amount - quotient * modulus
    remainder = jnp.where(remainder < 0, remainder + modulus, remainder)
    return jnp.where(remainder >= modulus, remainder - modulus, remainder)


def gather_sums_kernel(owners, groups, ciphers, key_count, requests, me, modulus, *refs):
    parts = refs[: len(owners)]
    out, held = refs[len(owners) :]
    cipher = pl.program_id(1)
    out[...] = jnp.zeros_like(out)
    for part, (steps, slots) in zip(parts, owners):
        owner = lax.rem(me[0] + steps, groups)
        chosen = slot_ciphers(requests, ciphers, key_count, owner)
        for place, slot in enumerate(slots):

            @pl.when(chosen[slot] == cipher)
            def _():
                out[...] = out[...] + part[place]

    last = slot_ciphers(requests, ciphers, key_count, lax.rem(me[0] + groups - 1, groups))[CAP - 1]

    @pl.when(cipher == last)
    def _():
        held[...] = out[...]

    wide = modulus[:, :1]
    out[...] = reduce_mod(out[...], wide) / wide


def gather_sums(parts, owners, requests, me, modulus, ciphers):
    polys, limbs, columns = parts[0].shape[1:]
    groups = lax.axis_size("grp")
    key_count = requests.shape[1] // groups
    return pl.pallas_call(
        functools.partial(gather_sums_kernel, owners, groups, ciphers, key_count),
        out_shape=[
            jax.ShapeDtypeStruct((ciphers, polys, limbs, columns), jnp.float32),
            jax.ShapeDtypeStruct((polys, limbs, columns), jnp.float32),
        ],
        grid_spec=pltpu.PrefetchScalarGridSpec(
            num_scalar_prefetch=2,
            grid=(limbs // ROWS, ciphers),
            in_specs=[pl.BlockSpec((ROWS, LANES), lambda block, cipher, *_: (block, 0))]
            + [
                pl.BlockSpec((part.shape[0], polys, ROWS, columns), lambda block, cipher, *_: (0, 0, block, 0))
                for part in parts
            ],
            out_specs=[
                pl.BlockSpec((pl.Squeezed(), polys, ROWS, columns), lambda block, cipher, *_: (cipher, 0, block, 0)),
                pl.BlockSpec((polys, ROWS, columns), lambda block, cipher, *_: (0, block, 0)),
            ],
        ),
        compiler_params=pltpu.CompilerParams(dimension_semantics=("arbitrary", "arbitrary")),
        cost_estimate=pl.CostEstimate(
            flops=20 * ciphers * polys * limbs * columns,
            transcendentals=0,
            bytes_accessed=4 * (ciphers + 2 + 2 * len(parts)) * polys * limbs * columns,
        ),
        name="gather_sums",
    )(requests, me, modulus, *parts)


def last_slot_kernel(requests, me, modulus, part, held, before, out):
    wide = modulus[:, :1]
    out[...] = reduce_mod(held[...] + part[...], wide) / wide


def last_slot(part, held, result, requests, me, modulus):
    ciphers, polys, limbs, columns = result.shape
    groups = lax.axis_size("grp")
    key_count = requests.shape[1] // groups

    def place(poly, block, requests, me):
        owner = lax.rem(me[0] + groups - 1, groups)
        return (slot_ciphers(requests, ciphers, key_count, owner)[CAP - 1], poly, block, 0)

    return pl.pallas_call(
        last_slot_kernel,
        out_shape=jax.ShapeDtypeStruct(result.shape, jnp.float32),
        grid_spec=pltpu.PrefetchScalarGridSpec(
            num_scalar_prefetch=2,
            grid=(polys, limbs // ROWS),
            in_specs=[
                pl.BlockSpec((ROWS, LANES), lambda poly, block, *_: (block, 0)),
                pl.BlockSpec((pl.Squeezed(), pl.Squeezed(), ROWS, columns), lambda poly, block, *_: (0, poly, block, 0)),
                pl.BlockSpec((pl.Squeezed(), ROWS, columns), lambda poly, block, *_: (poly, block, 0)),
                pl.BlockSpec(memory_space=pl.ANY),
            ],
            out_specs=pl.BlockSpec((pl.Squeezed(), pl.Squeezed(), ROWS, columns), place),
        ),
        input_output_aliases={5: 0},
        compiler_params=pltpu.CompilerParams(dimension_semantics=("arbitrary", "arbitrary")),
        name="last_slot",
    )(requests, me, modulus, part, held, result)


def per_device(digits, keys, requests, rotations, moduli):
    groups = lax.axis_size("grp")
    ciphers = digits.shape[0]
    limbs = digits.shape[2]
    me = lax.axis_index("grp").astype(jnp.int32).reshape(1)
    modulus = jnp.broadcast_to(moduli.astype(jnp.float32)[:, None], (limbs, LANES))

    sent = {}
    asked = {}
    for steps in range(1, groups):
        owner = lax.rem(me + steps, groups)
        for slot in range(CAP):
            sent[steps, slot] = shifted(gather_slot(digits, requests, owner, slot), "grp", steps)
        asked[steps] = shifted(requests, "grp", steps)

    tail, resident = products(digits, keys, requests, me, rotations, modulus, tuple(range(CAP)), True)
    parts = [add_tail(resident, shifted(tail, "limb", -1))]
    owners = [(0, tuple(range(CAP)))]
    for steps in range(1, groups):
        for slot in range(CAP):
            tail, resident = products(
                [sent[steps, slot]], keys, asked[steps], me, rotations, modulus, (slot,), False
            )
            whole = add_tail(resident, shifted(tail, "limb", -1))
            parts.append(shifted(whole, "grp", -steps))
            owners.append((steps, (slot,)))
    result, held = gather_sums(parts[:-1], tuple(owners[:-1]), requests, me, modulus, ciphers)
    return last_slot(parts[-1], held, result, requests, me, modulus)


def solution(mesh):
    in_specs = (
        P("grp", None, None, "limb"),
        P("grp", None, None, None, "limb"),
        P("grp", None),
        P(),
        P(),
    )
    out_specs = P("grp", None, None, "limb")
    return jax.shard_map(
        per_device, mesh=mesh, in_specs=in_specs, out_specs=out_specs, check_vma=False
    )
```

time: 147 us -> 100 us (0.68)
  Pallas kernels: 0 us -> 44.5 us
  other arithmetic: 40.8 us -> 0.01 us
  matrix products: 21.9 us -> 0 us
  waiting for transfers between devices: 47 us -> 32.8 us
  blocking collectives: 7.56 us -> 0 us
  between operations: 5.25 us -> 0.05 us
  local copies, waits for them, and re-layouts: 8.03 us -> 5.29 us
    all_to_all x3 -> x0, waiting for transfers between devices: 47 us -> none  [the longest x1 27 us: per_device(): lax.all_to_all(outgoing, 'grp', split_axis=0, concat_axis=0, tiled=True)]
    pallas_call x0 -> x10, Pallas kernels: none -> 44.5 us  [the longest x3 22.9 us: products(): pl.pallas_call(functools.partial(products_kernel, slots, parts, ciphers,...]
    ppermute x1 -> x8, waiting for transfers between devices: 0.01 us -> 32.8 us  [shifted(): return lax.ppermute(value, axis, pairs)]
    dot_general x4 -> x0, matrix products: 21.9 us -> none  [the longest x1 13.1 us: per_device(): jnp.einsum('hsc,cjlx->hsjlx', chooser, digits, precision=exact_mode)]
    add x2 -> x0, other arithmetic: 19.2 us -> none  [the longest x1 18.7 us: per_device(): resident = resident + jnp.where(inside, rotated, 0.0)]
    mul x3 -> x0, other arithmetic: 18.1 us -> none  [the longest x2 18 us: per_device(): reduce_mod(combined, modulus) * marks[:, :, key_index, None, None, None]]
    ppermute x1 -> x8, starting transfers between devices: 2.49 us -> 16.8 us  [shifted(): return lax.ppermute(value, axis, pairs)]
    all_to_all x3 -> x0, starting transfers between devices: 13.2 us -> none  [the longest x1 4.81 us: per_device(): lax.all_to_all(resident, 'grp', split_axis=0, concat_axis=0, tiled=True)]
  transfers between devices with their start and end apart: 4 -> 8, of which waited for: 2 -> 2; matrix products, arithmetic and copies ran while one was open for 19% -> 1% of each run, Pallas kernels for 0% -> 38%
where the time goes in v1:
time: 100 us; the launch traced here: 99.4 us
  Pallas kernels  44.5 us (44%)
  waiting for transfers between devices  32.8 us (33%)
  starting transfers between devices  16.8 us (17%)
  local copies, waits for them, and re-layouts  5.29 us (5%)
    ppermute x8, waiting for transfers between devices, shifted(): return lax.ppermute(value, axis, pairs)  32.8 us
    pallas_call x3, Pallas kernels, products(): pl.pallas_call(functools.partial(products_kernel, slots, parts, ciphers,...  22.9 us
    ppermute x8, starting transfers between devices, shifted(): return lax.ppermute(value, axis, pairs)  16.8 us
    pallas_call x1, Pallas kernels, gather_sums(): pl.pallas_call(functools.partial(gather_sums_kernel, owners, groups, ciph...  7.3 us
    pallas_call x2, Pallas kernels, gather_slot(): pl.pallas_call(functools.partial(gather_kernel, slot, ciphers, key_count)...  5.33 us
    pallas_call x3, Pallas kernels, add_tail(): pl.pallas_call(add_tail_kernel, out_shape=jax.ShapeDtypeStruct(resident.s...  4.68 us
    unnamed x20, local copies, waits for them, and re-layouts  4.53 us
    pallas_call x1, Pallas kernels, last_slot(): pl.pallas_call(last_slot_kernel, out_shape=jax.ShapeDtypeStruct(result.sh...  4.31 us
  transfers between devices with their start and end apart: 8, of which 2 were waited for; matrix products, arithmetic and copies ran while one was open for 1% of the time, Pallas kernels for 38%

profile of v1, /device:TPU:0, one launch (start us, length us, event | category | flops | bytes accessed | tf_op | source)
XLA Modules:
  0.0 99.4 jit_solution(15006144247865914911)
XLA Ops:
  0.0 0.0 copy-start.7
  0.0 0.0 copy-start.9
  0.0 2.7 %gather_digits.3 = f32[3,16,4096]{2,1,0:T(8,128)} custom-call(s32[4,8]{1,0:T(4,128)} %requests.9, s32[1]{0:T(128)S(6)} %rem.18.owner, f32[4,3,16,4096]{3,2,1,0:T(8,128)} %digits.3), custom_call_target="tpu_custom_call" | custom-call | bytes 1572864 | tf_op jit(solution)/shard_map/gather_digits/pallas_call | solution.py:58
  2.7 3.0 %collective-permute-start.5 = (f32[3,16,4096]{2,1,0:T(8,128)}, f32[3,16,4096]{2,1,0:T(8,128)S(1)}, u32[]{:S(2)}, u32[]{:S(2)}) collective-permute-start(f32[3,16,4096]{2,1,0:T(8,128)} %gather_digits.3), channel_id=1, source_target_pairs={{0,16},{16,0},{1,17},{17,1},{2,18},{18,2},{3,19},{19,3},{4,20},{20... | collective-permute-start | bytes 2359304 | tf_op jit(solution)/shard_map/ppermute | solution.py:20
  5.8 2.6 %gather_digits.2 = f32[3,16,4096]{2,1,0:T(8,128)} custom-call(s32[4,8]{1,0:T(4,128)} %requests.9, s32[1]{0:T(128)S(6)} %rem.18.owner, f32[4,3,16,4096]{3,2,1,0:T(8,128)} %digits.3), custom_call_target="tpu_custom_call" | custom-call | bytes 1572864 | tf_op jit(solution)/shard_map/gather_digits/pallas_call | solution.py:58
  8.4 0.1 collective-permute-start.1
  8.5 0.0 copy-done.7
  8.5 2.0 %collective-permute-start = (s32[4,8]{1,0:T(4,128)S(1)}, s32[4,8]{1,0:T(4,128)S(1)}, u32[]{:S(2)}, u32[]{:S(2)}) collective-permute-start(s32[4,8]{1,0:T(4,128)S(1)} %copy-done.7), channel_id=1, source_target_pairs={{0,16},{16,0},{1,17},{17,1},{2,18},{18,2},{3,19},{19,3},{4,20},{20... | collective-permute-start | bytes 392 | tf_op jit(solution)/shard_map/ppermute | solution.py:20
  10.5 0.0 copy-done.9
  10.5 29.9 %collective-permute-done.requests = s32[4,8]{1,0:T(4,128)S(1)} collective-permute-done((s32[4,8]{1,0:T(4,128)S(1)}, s32[4,8]{1,0:T(4,128)S(1)}, u32[]{:S(2)}, u32[]{:S(2)}) %collective-permute-start) | collective-permute-done | bytes 160 | tf_op jit(solution)/shard_map/ppermute | solution.py:20
  40.4 0.0 copy-start.8
  40.4 0.0 collective-permute-done.5.refs_0_
  40.4 0.0 copy-start.1
  40.4 0.8 broadcast_in_dim.2.refs_2_.refs_3_.modulus
  41.2 0.0 copy-done.8
  41.2 0.1 copy-done.1
  41.3 7.1 %products.5 = (f32[1,2,16,512]{3,2,1,0:T(8,128)}, f32[1,2,16,4096]{3,2,1,0:T(8,128)}) custom-call(s32[4,8]{1,0:T(4,128)} %copy-done.8, s32[1]{0:T(128)} %bitcast.owner.me, s32[8]{0:T(128)} %rotations.5, f32[3,16,4096]{2,1,0:T(8,128)} %copy-done.1, f32[4,3,2,16,4096]{4,3,2,1,0:T(8,128)} %refs_1_.5, f32[16,128]{1,0:T(8,128)} %broadcast_in_dim.2.refs_2_.refs_3_.modulus), custom_call_target="tpu_custom_call" | custom-call | flops 10485760 | bytes 7602176 | tf_op jit(solution)/shard_map/products/pallas_call | solution.py:147
  48.5 3.4 %collective-permute-start.6 = (f32[1,2,16,512]{3,2,1,0:T(8,128)}, f32[1,2,16,512]{3,2,1,0:T(8,128)S(1)}, u32[]{:S(2)}, u32[]{:S(2)}) collective-permute-start(f32[1,2,16,512]{3,2,1,0:T(8,128)} %get-tuple-element.17), channel_id=1, source_target_pairs={{0,15},{1,0},{2,1},{3,2},{4,3},{5,4},{6,5},{7,6},{8,7},{9,8},{10,9... | collective-permute-start | bytes 196616 | tf_op jit(solution)/shard_map/ppermute | solution.py:20
  51.9 0.0 collective-permute-done.1.refs_0_
  51.9 0.0 copy-start
  51.9 0.9 copy-done
  52.7 6.9 %products.3 = (f32[1,2,16,512]{3,2,1,0:T(8,128)}, f32[1,2,16,4096]{3,2,1,0:T(8,128)}) custom-call(s32[4,8]{1,0:T(4,128)} %copy-done.8, s32[1]{0:T(128)} %bitcast.owner.me, s32[8]{0:T(128)} %rotations.5, f32[3,16,4096]{2,1,0:T(8,128)} %copy-done, f32[4,3,2,16,4096]{4,3,2,1,0:T(8,128)} %refs_1_.5, f32[16,128]{1,0:T(8,128)} %broadcast_in_dim.2.refs_2_.refs_3_.modulus), custom_call_target="tpu_custom_call" | custom-call | flops 10485760 | bytes 7602176 | tf_op jit(solution)/shard_map/products/pallas_call | solution.py:147
  59.6 1.5 %collective-permute-start.2 = (f32[1,2,16,512]{3,2,1,0:T(8,128)}, f32[1,2,16,512]{3,2,1,0:T(8,128)S(1)}, u32[]{:S(2)}, u32[]{:S(2)}) collective-permute-start(f32[1,2,16,512]{3,2,1,0:T(8,128)} %get-tuple-element.13), channel_id=1, source_target_pairs={{0,15},{1,0},{2,1},{3,2},{4,3},{5,4},{6,5},{7,6},{8,7},{9,8},{10,9... | collective-permute-start | bytes 196616 | tf_op jit(solution)/shard_map/ppermute | solution.py:20
  61.1 0.0 collective-permute-done.6.arrived
  61.1 0.0 copy-start.5
  61.1 0.6 copy-done.5
  61.8 1.5 %add_tail.5 = f32[1,2,16,4096]{3,2,1,0:T(8,128)} custom-call(f32[1,2,16,512]{3,2,1,0:T(8,128)} %copy-done.5, f32[1,2,16,4096]{3,2,1,0:T(8,128)} %get-tuple-element.18.held), custom_call_target="tpu_custom_call", output_to_operand_aliasing={{}: (1, {})} | custom-call | tf_op jit(solution)/shard_map/add_tail/pallas_call | solution.py:185
  63.3 2.6 %collective-permute-start.7 = (f32[1,2,16,4096]{3,2,1,0:T(8,128)}, f32[1,2,16,4096]{3,2,1,0:T(8,128)S(1)}, u32[]{:S(2)}, u32[]{:S(2)}) collective-permute-start(f32[1,2,16,4096]{3,2,1,0:T(8,128)} %add_tail.5), channel_id=1, source_target_pairs={{0,16},{16,0},{1,17},{17,1},{2,18},{18,2},{3,19},{19,3},{4,20},{20... | collective-permute-start | bytes 1572872 | tf_op jit(solution)/shard_map/ppermute | solution.py:20
  65.8 0.0 collective-permute-done.2.arrived
  65.8 0.0 copy-start.6
  65.9 0.6 copy-done.6
  66.5 1.5 %add_tail.3 = f32[1,2,16,4096]{3,2,1,0:T(8,128)} custom-call(f32[1,2,16,512]{3,2,1,0:T(8,128)} %copy-done.6, f32[1,2,16,4096]{3,2,1,0:T(8,128)} %get-tuple-element.14.held), custom_call_target="tpu_custom_call", output_to_operand_aliasing={{}: (1, {})} | custom-call | tf_op jit(solution)/shard_map/add_tail/pallas_call | solution.py:185
  68.0 0.1 collective-permute-start.3
  68.1 8.9 %products.4 = (f32[2,2,16,512]{3,2,1,0:T(8,128)}, f32[2,2,16,4096]{3,2,1,0:T(8,128)}) custom-call(s32[4,8]{1,0:T(4,128)} %requests.9, s32[1]{0:T(128)} %bitcast.owner.me, s32[8]{0:T(128)} %rotations.5, f32[4,3,16,4096]{3,2,1,0:T(8,128)} %digits.3, f32[4,3,16,4096]{3,2,1,0:T(8,128)} %digits.3, f32[4,3,2,16,4096]{4,3,2,1,0:T(8,128)} %refs_1_.5, ...), custom_call_target="tpu_custom_call" | custom-call | flops 20971520 | bytes 8912896 | tf_op jit(solution)/shard_map/products/pallas_call | solution.py:147
  77.0 4.1 %collective-permute-start.4 = (f32[2,2,16,512]{3,2,1,0:T(8,128)}, f32[2,2,16,512]{3,2,1,0:T(8,128)S(1)}, u32[]{:S(2)}, u32[]{:S(2)}) collective-permute-start(f32[2,2,16,512]{3,2,1,0:T(8,128)} %get-tuple-element.15), channel_id=1, source_target_pairs={{0,15},{1,0},{2,1},{3,2},{4,3},{5,4},{6,5},{7,6},{8,7},{9,8},{10,9... | collective-permute-start | bytes 393224 | tf_op jit(solution)/shard_map/ppermute | solution.py:20
  81.1 2.8 %collective-permute-done.4.arrived = f32[2,2,16,512]{3,2,1,0:T(8,128)S(1)} collective-permute-done((f32[2,2,16,512]{3,2,1,0:T(8,128)}, f32[2,2,16,512]{3,2,1,0:T(8,128)S(1)}, u32[]{:S(2)}, u32[]{:S(2)}) %collective-permute-start.4) | collective-permute-done | bytes 131104 | tf_op jit(solution)/shard_map/ppermute | solution.py:20
  83.9 0.0 copy-start.4
  83.9 0.7 copy-done.4
  84.5 1.7 %add_tail.4.refs_0_ = f32[2,2,16,4096]{3,2,1,0:T(8,128)} custom-call(f32[2,2,16,512]{3,2,1,0:T(8,128)} %copy-done.4, f32[2,2,16,4096]{3,2,1,0:T(8,128)} %get-tuple-element.16.held), custom_call_target="tpu_custom_call", output_to_operand_aliasing={{}: (1, {})} | custom-call | tf_op jit(solution)/shard_map/add_tail/pallas_call | solution.py:185
  86.2 0.0 collective-permute-done.7.refs_1_
  86.2 0.0 copy-start.2
  86.2 0.8 copy-done.2
  87.0 7.3 %gather_sums.1 = (f32[4,2,16,4096]{3,2,1,0:T(8,128)}, f32[2,16,4096]{2,1,0:T(8,128)}) custom-call(s32[4,8]{1,0:T(4,128)} %requests.9, s32[1]{0:T(128)} %bitcast.owner.me, f32[16,128]{1,0:T(8,128)} %broadcast_in_dim.2.refs_2_.refs_3_.modulus, f32[2,2,16,4096]{3,2,1,0:T(8,128)} %add_tail.4.refs_0_, f32[1,2,16,4096]{3,2,1,0:T(8,128)} %copy-done.2), custom_call_target="tpu_custom_call" | custom-call | flops 10485760 | bytes 5242880 | tf_op jit(solution)/shard_map/gather_sums/pallas_call | solution.py:231
  94.3 0.0 collective-permute-done.3.part
  94.3 0.0 copy-start.3
  94.3 0.8 copy-done.3
  95.1 4.3 %last_slot.1 = f32[4,2,16,4096]{3,2,1,0:T(8,128)} custom-call(s32[4,8]{1,0:T(4,128)} %requests.9, s32[1]{0:T(128)} %bitcast.owner.me, f32[16,128]{1,0:T(8,128)} %broadcast_in_dim.2.refs_2_.refs_3_.modulus, f32[1,2,16,4096]{3,2,1,0:T(8,128)} %copy-done.3, f32[2,16,4096]{2,1,0:T(8,128)} %get-tuple-element.19.held, ...), custom_call_target="tpu_custom_call", output_to_operand_aliasing={{}: (5, {})} | custom-call | tf_op jit(solution)/shard_map/last_slot/pallas_call | solution.py:274
  (1 shorter events, 0.0 us)
Async XLA Ops:
  0.0 8.5 %copy-start.7 = (s32[4,8]{1,0:T(4,128)S(1)}, s32[4,8]{1,0:T(4,128)}, u32[]{:S(2)}) copy-start(s32[4,8]{1,0:T(4,128)} %requests.9) | copy-start | bytes 388
  0.0 10.5 %copy-start.9 = (s32[16]{0:T(128)S(1)}, s32[16]{0:T(128)}, u32[]{:S(2)}) copy-start(s32[16]{0:T(128)} %param.9) | copy-start | bytes 196
  2.7 37.7 %collective-permute-start.5 = (f32[3,16,4096]{2,1,0:T(8,128)}, f32[3,16,4096]{2,1,0:T(8,128)S(1)}, u32[]{:S(2)}, u32[]{:S(2)}) collective-permute-start(f32[3,16,4096]{2,1,0:T(8,128)} %gather_digits.3), channel_id=1, source_target_pairs={{0,16},{16,0},{1,17},{17,1},{2,18},{18,2},{3,19},{19,3},{4,20},{20... | collective-permute-start | bytes 2359304 | tf_op jit(solution)/shard_map/ppermute | solution.py:20
  8.4 43.5 %collective-permute-start.1 = (f32[3,16,4096]{2,1,0:T(8,128)}, f32[3,16,4096]{2,1,0:T(8,128)S(1)}, u32[]{:S(2)}, u32[]{:S(2)}) collective-permute-start(f32[3,16,4096]{2,1,0:T(8,128)} %gather_digits.2), channel_id=1, source_target_pairs={{0,16},{16,0},{1,17},{17,1},{2,18},{18,2},{3,19},{19,3},{4,20},{20... | collective-permute-start | bytes 2359304 | tf_op jit(solution)/shard_map/ppermute | solution.py:20
  8.5 32.0 %collective-permute-start = (s32[4,8]{1,0:T(4,128)S(1)}, s32[4,8]{1,0:T(4,128)S(1)}, u32[]{:S(2)}, u32[]{:S(2)}) collective-permute-start(s32[4,8]{1,0:T(4,128)S(1)} %copy-done.7), channel_id=1, source_target_pairs={{0,16},{16,0},{1,17},{17,1},{2,18},{18,2},{3,19},{19,3},{4,20},{20... | collective-permute-start | bytes 392 | tf_op jit(solution)/shard_map/ppermute | solution.py:20
  40.4 0.8 copy-start.8
  40.4 0.9 copy-start.1
  48.5 12.7 %collective-permute-start.6 = (f32[1,2,16,512]{3,2,1,0:T(8,128)}, f32[1,2,16,512]{3,2,1,0:T(8,128)S(1)}, u32[]{:S(2)}, u32[]{:S(2)}) collective-permute-start(f32[1,2,16,512]{3,2,1,0:T(8,128)} %get-tuple-element.17), channel_id=1, source_target_pairs={{0,15},{1,0},{2,1},{3,2},{4,3},{5,4},{6,5},{7,6},{8,7},{9,8},{10,9... | collective-permute-start | bytes 196616 | tf_op jit(solution)/shard_map/ppermute | solution.py:20
  51.9 0.9 copy-start
  59.6 6.2 %collective-permute-start.2 = (f32[1,2,16,512]{3,2,1,0:T(8,128)}, f32[1,2,16,512]{3,2,1,0:T(8,128)S(1)}, u32[]{:S(2)}, u32[]{:S(2)}) collective-permute-start(f32[1,2,16,512]{3,2,1,0:T(8,128)} %get-tuple-element.13), channel_id=1, source_target_pairs={{0,15},{1,0},{2,1},{3,2},{4,3},{5,4},{6,5},{7,6},{8,7},{9,8},{10,9... | collective-permute-start | bytes 196616 | tf_op jit(solution)/shard_map/ppermute | solution.py:20
  61.1 0.6 copy-start.5
  63.3 23.0 %collective-permute-start.7 = (f32[1,2,16,4096]{3,2,1,0:T(8,128)}, f32[1,2,16,4096]{3,2,1,0:T(8,128)S(1)}, u32[]{:S(2)}, u32[]{:S(2)}) collective-permute-start(f32[1,2,16,4096]{3,2,1,0:T(8,128)} %add_tail.5), channel_id=1, source_target_pairs={{0,16},{16,0},{1,17},{17,1},{2,18},{18,2},{3,19},{19,3},{4,20},{20... | collective-permute-start | bytes 1572872 | tf_op jit(solution)/shard_map/ppermute | solution.py:20
  65.8 0.6 copy-start.6
  68.0 26.3 %collective-permute-start.3 = (f32[1,2,16,4096]{3,2,1,0:T(8,128)}, f32[1,2,16,4096]{3,2,1,0:T(8,128)S(1)}, u32[]{:S(2)}, u32[]{:S(2)}) collective-permute-start(f32[1,2,16,4096]{3,2,1,0:T(8,128)} %add_tail.3), channel_id=1, source_target_pairs={{0,16},{16,0},{1,17},{17,1},{2,18},{18,2},{3,19},{19,3},{4,20},{20... | collective-permute-start | bytes 1572872 | tf_op jit(solution)/shard_map/ppermute | solution.py:20
  77.0 6.9 %collective-permute-start.4 = (f32[2,2,16,512]{3,2,1,0:T(8,128)}, f32[2,2,16,512]{3,2,1,0:T(8,128)S(1)}, u32[]{:S(2)}, u32[]{:S(2)}) collective-permute-start(f32[2,2,16,512]{3,2,1,0:T(8,128)} %get-tuple-element.15), channel_id=1, source_target_pairs={{0,15},{1,0},{2,1},{3,2},{4,3},{5,4},{6,5},{7,6},{8,7},{9,8},{10,9... | collective-permute-start | bytes 393224 | tf_op jit(solution)/shard_map/ppermute | solution.py:20
  83.9 0.7 copy-start.4
  86.2 0.8 copy-start.2
  94.3 0.8 copy-start.3

commit v2 on v1

v2 whole, which is shorter than its diff:
```python
import functools

import jax
import jax.numpy as jnp
from jax import lax
from jax.experimental import pallas as pl
from jax.experimental.pallas import tpu as pltpu
from jax.sharding import PartitionSpec as P

RMAX = 256
CAP = 2
WIDEST = 2 * RMAX
LANES = 128
ROWS = 8
SMEM = pl.BlockSpec(memory_space=pltpu.SMEM)
VMEM = pl.BlockSpec(memory_space=pltpu.VMEM)


def shifted(value, axis, steps):
    count = lax.axis_size(axis)
    pairs = [(source, (source + steps) % count) for source in range(count)]
    return lax.ppermute(value, axis, pairs)


def slot_ciphers(requests, ciphers, key_count, owner):
    needed = []
    for cipher in range(ciphers):
        flag = requests[cipher, owner * key_count]
        for key in range(1, key_count):
            flag = flag | requests[cipher, owner * key_count + key]
        needed.append(flag)
    slots = [jnp.int32(0)] * CAP
    rank = jnp.int32(0)
    for want in (1, 0):
        for cipher in range(ciphers):
            here = needed[cipher] == want
            for slot in range(CAP):
                slots[slot] = jnp.where(here & (rank == slot), cipher, slots[slot])
            rank = rank + here.astype(jnp.int32)
    return slots


def gather_kernel(slot, ciphers, key_count, requests, owner, digits, out, sems):
    cipher = slot_ciphers(requests, ciphers, key_count, owner[0])[slot]
    loads = [pltpu.make_async_copy(digits.at[cipher, j], out.at[j], sems.at[j]) for j in range(out.shape[0])]
    for load in loads:
        load.start()
    for load in loads:
        load.wait()


def gather_slot(digits, requests, owner, slot):
    ciphers, parts, limbs, columns = digits.shape
    key_count = requests.shape[1] // lax.axis_size("grp")
    return pl.pallas_call(
        functools.partial(gather_kernel, slot, ciphers, key_count),
        out_shape=jax.ShapeDtypeStruct((parts, limbs, columns), jnp.float32),
        in_specs=[SMEM, SMEM, pl.BlockSpec(memory_space=pltpu.HBM)],
        out_specs=VMEM,
        scratch_shapes=[pltpu.SemaphoreType.DMA((parts,))],
        compiler_params=pltpu.CompilerParams(vmem_limit_bytes=4 << 20),
        cost_estimate=pl.CostEstimate(flops=0, transcendentals=0, bytes_accessed=8 * parts * limbs * columns),
        name="gather_digits",
    )(requests, owner, pltpu.with_memory_space_constraint(digits, pltpu.HBM))


def products_kernel(slots, local, requests, owner, rotations, digits, keys, modulus_ref, tail, resident, rolled):
    key_count, parts, polys, limbs, columns = keys.shape
    ciphers = requests.shape[0]
    pad = WIDEST // LANES
    tiles = columns // LANES
    tail[...] = jnp.zeros_like(tail)
    resident[...] = jnp.zeros_like(resident)
    rolled[...] = jnp.zeros_like(rolled)
    lane = lax.broadcasted_iota(jnp.int32, (ROWS, LANES), 1)
    chosen = slot_ciphers(requests, ciphers, key_count, owner[0])

    def add_key(step, carry):
        block = step // key_count
        key = step - block * key_count
        rows = pl.ds(pl.multiple_of(block * ROWS, ROWS), ROWS)
        amount = 2 * rotations[owner[0] * key_count + key]
        skipped = amount // LANES
        within = amount - skipped * LANES
        turn = lax.rem(LANES - within, LANES)
        from_this = lane < LANES - within
        modulus = modulus_ref[rows, :]
        inverse = 1.0 / modulus
        for place, slot in enumerate(slots):
            source = chosen[slot] if local else place

            @pl.when(requests[chosen[slot], owner[0] * key_count + key] > 0)
            def _():
                for poly in range(polys):
                    for tile in range(tiles):
                        at = pl.ds(tile * LANES, LANES)
                        combined = digits[source, 0, rows, at] * keys[key, 0, poly, rows, at]
                        for part in range(1, parts):
                            combined = combined + digits[source, part, rows, at] * keys[key, part, poly, rows, at]
                        quotient = jnp.floor(combined * inverse)
                        remainder = combined - quotient * modulus
                        rolled[:, pl.ds((pad + tile) * LANES, LANES)] = pltpu.roll(remainder, turn, 1)
                    for tile in range(pad + tiles):
                        start = pl.multiple_of((skipped + tile) * LANES, LANES)
                        after = pl.multiple_of((skipped + tile + 1) * LANES, LANES)
                        moved = jnp.where(from_this, rolled[:, pl.ds(start, LANES)], rolled[:, pl.ds(after, LANES)])
                        if tile < pad:
                            at = pl.ds(tile * LANES, LANES)
                            tail[place, poly, rows, at] = tail[place, poly, rows, at] + moved
                        else:
                            at = pl.ds((tile - pad) * LANES, LANES)
                            resident[place, poly, rows, at] = resident[place, poly, rows, at] + moved
        return carry

    lax.fori_loop(0, (limbs // ROWS) * key_count, add_key, 0)


def products(digits, keys, requests, owner, rotations, modulus, slots, local):
    key_count, parts, polys, limbs, columns = keys.shape
    count = len(slots)
    pad = WIDEST // LANES
    work = count * key_count * polys * limbs * columns
    return pl.pallas_call(
        functools.partial(products_kernel, slots, local),
        out_shape=[
            jax.ShapeDtypeStruct((count, polys, limbs, WIDEST), jnp.float32),
            jax.ShapeDtypeStruct((count, polys, limbs, columns), jnp.float32),
        ],
        in_specs=[SMEM, SMEM, SMEM, VMEM, VMEM, VMEM],
        out_specs=[VMEM, VMEM],
        scratch_shapes=[pltpu.VMEM((ROWS, columns + 2 * pad * LANES + LANES), jnp.float32)],
        compiler_params=pltpu.CompilerParams(vmem_limit_bytes=20 << 20),
        cost_estimate=pl.CostEstimate(
            flops=20 * work, transcendentals=0, bytes_accessed=4 * (keys.size + count * limbs * columns * (parts + polys))
        ),
        name="products",
    )(requests, owner, rotations, digits, keys, modulus)


def add_tail_kernel(arrived, held, out):
    columns = held.shape[-1]
    at = pl.ds(columns - WIDEST, WIDEST)
    out[:, :, :, at] = held[:, :, :, at] + arrived[...]


def add_tail(resident, arrived):
    return pl.pallas_call(
        add_tail_kernel,
        out_shape=jax.ShapeDtypeStruct(resident.shape, jnp.float32),
        in_specs=[VMEM, VMEM],
        out_specs=VMEM,
        input_output_aliases={1: 0},
        compiler_params=pltpu.CompilerParams(vmem_limit_bytes=8 << 20),
        name="add_tail",
    )(arrived, resident)


def reduce_mod(amount, modulus):
    quotient = jnp.floor(amount * (1.0 / modulus))
    remainder = amount - quotient * modulus
    remainder = jnp.where(remainder < 0, remainder + modulus, remainder)
    return jnp.where(remainder >= modulus, remainder - modulus, remainder)


def gather_sums_kernel(owners, groups, ciphers, key_count, requests, me, modulus, *refs):
    parts = refs[: len(owners)]
    out, held = refs[len(owners) :]
    cipher = pl.program_id(1)
    out[...] = jnp.zeros_like(out)
    for part, (steps, slots) in zip(parts, owners):
        owner = lax.rem(me[0] + steps, groups)
        chosen = slot_ciphers(requests, ciphers, key_count, owner)
        for place, slot in enumerate(slots):

            @pl.when(chosen[slot] == cipher)
            def _():
                out[...] = out[...] + part[place]

    last = slot_ciphers(requests, ciphers, key_count, lax.rem(me[0] + groups - 1, groups))[CAP - 1]

    @pl.when(cipher == last)
    def _():
        held[...] = out[...]

    wide = modulus[:, :1]
    out[...] = reduce_mod(out[...], wide) / wide


def gather_sums(parts, owners, requests, me, modulus, ciphers):
    polys, limbs, columns = parts[0].shape[1:]
    groups = lax.axis_size("grp")
    key_count = requests.shape[1] // groups
    return pl.pallas_call(
        functools.partial(gather_sums_kernel, owners, groups, ciphers, key_count),
        out_shape=[
            jax.ShapeDtypeStruct((ciphers, polys, limbs, columns), jnp.float32),
            jax.ShapeDtypeStruct((polys, limbs, columns), jnp.float32),
        ],
        grid_spec=pltpu.PrefetchScalarGridSpec(
            num_scalar_prefetch=2,
            grid=(limbs // ROWS, ciphers),
            in_specs=[pl.BlockSpec((ROWS, LANES), lambda block, cipher, *_: (block, 0))]
            + [
                pl.BlockSpec((part.shape[0], polys, ROWS, columns), lambda block, cipher, *_: (0, 0, block, 0))
                for part in parts
            ],
            out_specs=[
                pl.BlockSpec((pl.Squeezed(), polys, ROWS, columns), lambda block, cipher, *_: (cipher, 0, block, 0)),
                pl.BlockSpec((polys, ROWS, columns), lambda block, cipher, *_: (0, block, 0)),
            ],
        ),
        compiler_params=pltpu.CompilerParams(dimension_semantics=("arbitrary", "arbitrary"), vmem_limit_bytes=12 << 20),
        cost_estimate=pl.CostEstimate(
            flops=20 * ciphers * polys * limbs * columns,
            transcendentals=0,
            bytes_accessed=4 * (ciphers + 2 + 2 * len(parts)) * polys * limbs * columns,
        ),
        name="gather_sums",
    )(requests, me, modulus, *parts)


def last_slot_kernel(groups, key_count, requests, me, modulus, part, held, before, out, done, sems):
    ciphers, polys, limbs, _ = out.shape
    cipher = slot_ciphers(requests, ciphers, key_count, lax.rem(me[0] + groups - 1, groups))[CAP - 1]
    stores = []
    for poly in range(polys):
        for block in range(limbs // ROWS):
            rows = pl.ds(block * ROWS, ROWS)
            wide = modulus[rows, :1]
            done[poly, rows, :] = reduce_mod(held[poly, rows, :] + part[0, poly, rows, :], wide) / wide
            store = pltpu.make_async_copy(
                done.at[poly, rows], out.at[cipher, poly, rows], sems.at[poly * (limbs // ROWS) + block]
            )
            store.start()
            stores.append(store)
    for store in stores:
        store.wait()


def last_slot(part, held, result, requests, me, modulus):
    _, polys, limbs, columns = result.shape
    groups = lax.axis_size("grp")
    key_count = requests.shape[1] // groups
    hbm = pl.BlockSpec(memory_space=pltpu.HBM)
    return pl.pallas_call(
        functools.partial(last_slot_kernel, groups, key_count),
        out_shape=jax.ShapeDtypeStruct(result.shape, jnp.float32),
        in_specs=[SMEM, SMEM, VMEM, VMEM, VMEM, hbm],
        out_specs=hbm,
        scratch_shapes=[
            pltpu.VMEM((polys, limbs, columns), jnp.float32),
            pltpu.SemaphoreType.DMA((polys * (limbs // ROWS),)),
        ],
        input_output_aliases={5: 0},
        compiler_params=pltpu.CompilerParams(vmem_limit_bytes=8 << 20),
        name="last_slot",
    )(requests, me, modulus, part, held, result)


def key_switch(digits, keys, requests, rotations, moduli):
    groups = lax.axis_size("grp")
    ciphers = digits.shape[0]
    limbs = digits.shape[2]
    me = lax.axis_index("grp").astype(jnp.int32).reshape(1)
    modulus = jnp.broadcast_to(moduli.astype(jnp.float32)[:, None], (limbs, LANES))
    turns = [(steps, slot) for steps in range(1, groups) for slot in range(CAP)]

    sent = {}
    asked = {}
    for steps, slot in turns:
        owner = lax.rem(me + steps, groups)
        picked = gather_slot(digits, requests, owner, slot)
        sent[steps, slot] = shifted(picked, "grp", steps)
        if slot == 0:
            asked[steps] = shifted(requests, "grp", steps)

    tail, resident = products(digits, keys, requests, me, rotations, modulus, tuple(range(CAP)), True)
    arrived = shifted(tail, "limb", -1)
    parts = [add_tail(resident, arrived)]
    owners = [(0, tuple(range(CAP)))]
    for steps, slot in turns:
        tail, resident = products(sent[steps, slot][None], keys, asked[steps], me, rotations, modulus, (slot,), False)
        arrived = shifted(tail, "limb", -1)
        whole = add_tail(resident, arrived)
        parts.append(shifted(whole, "grp", -steps))
        owners.append((steps, (slot,)))
    result, held = gather_sums(parts[:-1], tuple(owners[:-1]), requests, me, modulus, ciphers)
    return last_slot(parts[-1], held, result, requests, me, modulus)


def solution(mesh):
    in_specs = (
        P("grp", None, None, "limb"),
        P("grp", None, None, None, "limb"),
        P("grp", None),
        P(),
        P(),
    )
    out_specs = P("grp", None, None, "limb")
    return jax.shard_map(key_switch, mesh=mesh, in_specs=in_specs, out_specs=out_specs, check_vma=False)
```

time: 100 us -> 75.3 us (0.75)
  Pallas kernels: 44.5 us -> 18.3 us
  waiting for transfers between devices: 32.8 us -> 41.6 us
  local copies, waits for them, and re-layouts: 5.29 us -> 0.08 us
  starting transfers between devices: 16.8 us -> 15.1 us
    pallas_call x4, Pallas kernels: 27.2 us -> 8.39 us  [the longest x3 6.72 us: products(): pl.pallas_call(functools.partial(products_kernel, slots, local), out_shap...]
    ppermute x8, waiting for transfers between devices: 32.8 us -> 41.6 us  [shifted(): return lax.ppermute(value, axis, pairs)]
    pallas_call x3, Pallas kernels: 4.68 us -> 0.05 us  [add_tail(): pl.pallas_call(add_tail_kernel, out_shape=jax.ShapeDtypeStruct(resident.s...]
    unnamed x20 -> x8, local copies, waits for them, and re-layouts: 4.53 us -> 0.01 us
    ppermute x8, starting transfers between devices: 16.8 us -> 15.1 us  [shifted(): return lax.ppermute(value, axis, pairs)]
    pallas_call x1, Pallas kernels: 7.3 us -> 5.59 us  [gather_sums(): pl.pallas_call(functools.partial(gather_sums_kernel, owners, groups, ciph...]
    pallas_call x2, Pallas kernels: 5.33 us -> 4.22 us  [gather_slot(): pl.pallas_call(functools.partial(gather_kernel, slot, ciphers, key_count)...]
  transfers between devices with their start and end apart: 8 -> 8, of which waited for: 2 -> 5; matrix products, arithmetic and copies ran while one was open for 1% -> 0% of each run, Pallas kernels for 38% -> 19%
where the time goes in v2:
time: 75.3 us; the launch traced here: 75.1 us
  waiting for transfers between devices  41.6 us (55%)
  Pallas kernels  18.3 us (24%)
  starting transfers between devices  15.1 us (20%)
    ppermute x8, waiting for transfers between devices, shifted(): return lax.ppermute(value, axis, pairs)  41.6 us
    ppermute x8, starting transfers between devices, shifted(): return lax.ppermute(value, axis, pairs)  15.1 us
    pallas_call x3, Pallas kernels, products(): pl.pallas_call(functools.partial(products_kernel, slots, local), out_shap...  6.72 us
    pallas_call x1, Pallas kernels, gather_sums(): pl.pallas_call(functools.partial(gather_sums_kernel, owners, groups, ciph...  5.59 us
    pallas_call x2, Pallas kernels, gather_slot(): pl.pallas_call(functools.partial(gather_kernel, slot, ciphers, key_count)...  4.22 us
    pallas_call x1, Pallas kernels, last_slot(): pl.pallas_call(functools.partial(last_slot_kernel, groups, key_count), ou...  1.68 us
  transfers between devices with their start and end apart: 8, of which 5 were waited for; matrix products, arithmetic and copies ran while one was open for 0% of the time, Pallas kernels for 19%

profile of v2, /device:TPU:0, one launch (start us, length us, event | category | flops | bytes accessed | tf_op | source)
XLA Modules:
  0.0 75.1 jit_solution(5303520414676592248)
XLA Ops:
  0.0 0.0 copy-start.3
  0.0 0.0 copy-start
  0.0 0.0 copy-start.2
  0.0 2.4 %gather_digits.3 = f32[3,16,4096]{2,1,0:T(8,128)S(1)} custom-call(s32[4,8]{1,0:T(4,128)} %requests.9, s32[1]{0:T(128)S(6)} %rem.19.owner, f32[4,3,16,4096]{3,2,1,0:T(8,128)} %digits.5), custom_call_target="tpu_custom_call" | custom-call | bytes 1572864 | tf_op jit(solution)/shard_map/gather_digits/pallas_call | solution.py:55
  2.4 3.0 %collective-permute-start.5 = (f32[3,16,4096]{2,1,0:T(8,128)S(1)}, f32[3,16,4096]{2,1,0:T(8,128)S(1)}, u32[]{:S(2)}, u32[]{:S(2)}) collective-permute-start(f32[3,16,4096]{2,1,0:T(8,128)S(1)} %gather_digits.3), channel_id=1, source_target_pairs={{0,16},{16,0},{1,17},{17,1},{2,18},{18,2},{3,19},{19,3},{4,20},{20... | collective-permute-start | bytes 2359304 | tf_op jit(solution)/shard_map/ppermute | solution.py:22
  5.4 1.9 %gather_digits.2 = f32[3,16,4096]{2,1,0:T(8,128)S(1)} custom-call(s32[4,8]{1,0:T(4,128)} %requests.9, s32[1]{0:T(128)S(6)} %rem.19.owner, f32[4,3,16,4096]{3,2,1,0:T(8,128)} %digits.5), custom_call_target="tpu_custom_call" | custom-call | bytes 1572864 | tf_op jit(solution)/shard_map/gather_digits/pallas_call | solution.py:55
  7.3 0.1 collective-permute-start.1
  7.4 2.0 %collective-permute-start = (s32[4,8]{1,0:T(4,128)}, s32[4,8]{1,0:T(4,128)S(1)}, u32[]{:S(2)}, u32[]{:S(2)}) collective-permute-start(s32[4,8]{1,0:T(4,128)} %requests.9), channel_id=1, source_target_pairs={{0,16},{16,0},{1,17},{17,1},{2,18},{18,2},{3,19},{19,3},{4,20},{20... | collective-permute-start | bytes 392 | tf_op jit(solution)/shard_map/ppermute | solution.py:22
  9.4 0.0 copy-done.3
  9.4 30.5 %collective-permute-done.requests = s32[4,8]{1,0:T(4,128)S(1)} collective-permute-done((s32[4,8]{1,0:T(4,128)}, s32[4,8]{1,0:T(4,128)S(1)}, u32[]{:S(2)}, u32[]{:S(2)}) %collective-permute-start) | collective-permute-done | bytes 160 | tf_op jit(solution)/shard_map/ppermute | solution.py:22
  39.9 0.0 collective-permute-done.5
  39.9 0.1 broadcast_in_dim.12.modulus_ref.modulus
  39.9 0.0 copy-done
  39.9 0.0 copy-done.2
  39.9 2.6 %products.5 = (f32[1,2,16,512]{3,2,1,0:T(8,128)S(1)}, f32[1,2,16,4096]{3,2,1,0:T(8,128)S(1)}) custom-call(s32[4,8]{1,0:T(4,128)S(1)} %collective-permute-done.requests, s32[1]{0:T(128)} %bitcast.owner.me, s32[8]{0:T(128)S(1)} %copy-done.2, f32[1,3,16,4096]{3,2,1,0:T(8,128)S(1)} %bitcast.4, f32[4,3,2,16,4096]{4,3,2,1,0:T(8,128)S(1)} %copy-done, ...), custom_call_target="tpu_custom_call" | custom-call | flops 10485760 | bytes 7602176 | tf_op jit(solution)/shard_map/products/pallas_call | solution.py:123
  42.5 3.4 %collective-permute-start.6 = (f32[1,2,16,512]{3,2,1,0:T(8,128)S(1)}, f32[1,2,16,512]{3,2,1,0:T(8,128)S(1)}, u32[]{:S(2)}, u32[]{:S(2)}) collective-permute-start(f32[1,2,16,512]{3,2,1,0:T(8,128)S(1)} %get-tuple-element.17), channel_id=1, source_target_pairs={{0,15},{1,0},{2,1},{3,2},{4,3},{5,4},{6,5},{7,6},{8,7},{9,8},{10,9... | collective-permute-start | bytes 196616 | tf_op jit(solution)/shard_map/ppermute | solution.py:22
  46.0 0.0 collective-permute-done.1
  46.0 0.0 copy-start.1
  46.0 1.7 %products.3 = (f32[1,2,16,512]{3,2,1,0:T(8,128)S(1)}, f32[1,2,16,4096]{3,2,1,0:T(8,128)S(1)}) custom-call(s32[4,8]{1,0:T(4,128)S(1)} %collective-permute-done.requests, s32[1]{0:T(128)} %bitcast.owner.me, s32[8]{0:T(128)S(1)} %copy-done.2, f32[1,3,16,4096]{3,2,1,0:T(8,128)S(1)} %bitcast.3, f32[4,3,2,16,4096]{4,3,2,1,0:T(8,128)S(1)} %copy-done, ...), custom_call_target="tpu_custom_call" | custom-call | flops 10485760 | bytes 7602176 | tf_op jit(solution)/shard_map/products/pallas_call | solution.py:123
  47.7 1.6 %collective-permute-start.2 = (f32[1,2,16,512]{3,2,1,0:T(8,128)S(1)}, f32[1,2,16,512]{3,2,1,0:T(8,128)S(1)}, u32[]{:S(2)}, u32[]{:S(2)}) collective-permute-start(f32[1,2,16,512]{3,2,1,0:T(8,128)S(1)} %get-tuple-element.13), channel_id=1, source_target_pairs={{0,15},{1,0},{2,1},{3,2},{4,3},{5,4},{6,5},{7,6},{8,7},{9,8},{10,9... | collective-permute-start | bytes 196616 | tf_op jit(solution)/shard_map/ppermute | solution.py:22
  49.3 0.0 collective-permute-done.6.arrived
  49.3 0.3 collective-permute-start.7
  49.6 1.6 %collective-permute-done.2.arrived = f32[1,2,16,512]{3,2,1,0:T(8,128)S(1)} collective-permute-done((f32[1,2,16,512]{3,2,1,0:T(8,128)S(1)}, f32[1,2,16,512]{3,2,1,0:T(8,128)S(1)}, u32[]{:S(2)}, u32[]{:S(2)}) %collective-permute-start.2) | collective-permute-done | bytes 65568 | tf_op jit(solution)/shard_map/ppermute | solution.py:22
  51.2 0.3 collective-permute-start.3
  51.5 0.0 copy-done.1
  51.5 2.4 %products.4 = (f32[2,2,16,512]{3,2,1,0:T(8,128)S(1)}, f32[2,2,16,4096]{3,2,1,0:T(8,128)S(1)}) custom-call(s32[4,8]{1,0:T(4,128)} %requests.9, s32[1]{0:T(128)} %bitcast.owner.me, s32[8]{0:T(128)S(1)} %copy-done.2, f32[4,3,16,4096]{3,2,1,0:T(8,128)S(1)} %copy-done.1, f32[4,3,2,16,4096]{4,3,2,1,0:T(8,128)S(1)} %copy-done, ...), custom_call_target="tpu_custom_call" | custom-call | flops 20971520 | bytes 8912896 | tf_op jit(solution)/shard_map/products/pallas_call | solution.py:123
  53.9 4.4 %collective-permute-start.4 = (f32[2,2,16,512]{3,2,1,0:T(8,128)S(1)}, f32[2,2,16,512]{3,2,1,0:T(8,128)S(1)}, u32[]{:S(2)}, u32[]{:S(2)}) collective-permute-start(f32[2,2,16,512]{3,2,1,0:T(8,128)S(1)} %get-tuple-element.15), channel_id=1, source_target_pairs={{0,15},{1,0},{2,1},{3,2},{4,3},{5,4},{6,5},{7,6},{8,7},{9,8},{10,9... | collective-permute-start | bytes 393224 | tf_op jit(solution)/shard_map/ppermute | solution.py:22
  58.3 2.5 %collective-permute-done.4.arrived = f32[2,2,16,512]{3,2,1,0:T(8,128)S(1)} collective-permute-done((f32[2,2,16,512]{3,2,1,0:T(8,128)S(1)}, f32[2,2,16,512]{3,2,1,0:T(8,128)S(1)}, u32[]{:S(2)}, u32[]{:S(2)}) %collective-permute-start.4) | collective-permute-done | bytes 131104 | tf_op jit(solution)/shard_map/ppermute | solution.py:22
  60.8 3.4 %collective-permute-done.7.refs_1_ = f32[1,2,16,4096]{3,2,1,0:T(8,128)S(1)} collective-permute-done((f32[1,2,16,4096]{3,2,1,0:T(8,128)S(1)}, f32[1,2,16,4096]{3,2,1,0:T(8,128)S(1)}, u32[]{:S(2)}, u32[]{:S(2)}) %collective-permute-start.7) | collective-permute-done | bytes 524320 | tf_op jit(solution)/shard_map/ppermute | solution.py:22
  64.2 5.6 %gather_sums.1 = (f32[4,2,16,4096]{3,2,1,0:T(8,128)}, f32[2,16,4096]{2,1,0:T(8,128)S(1)}) custom-call(s32[4,8]{1,0:T(4,128)} %requests.9, s32[1]{0:T(128)} %bitcast.owner.me, f32[16,128]{1,0:T(8,128)S(1)} %broadcast_in_dim.12.modulus_ref.modulus, f32[2,2,16,4096]{3,2,1,0:T(8,128)S(1)} %add_tail.4.refs_0_, f32[1,2,16,4096]{3,2,1,0:T(8,128)S(1)} %collective-permute-done.7.refs_1_), custom_call_target="tpu_custom_call" | custom-call | flops 10485760 | bytes 5242880 | tf_op jit(solution)/shard_map/gather_sums/pallas_call | solution.py:193
  69.8 3.7 %collective-permute-done.3.part = f32[1,2,16,4096]{3,2,1,0:T(8,128)S(1)} collective-permute-done((f32[1,2,16,4096]{3,2,1,0:T(8,128)S(1)}, f32[1,2,16,4096]{3,2,1,0:T(8,128)S(1)}, u32[]{:S(2)}, u32[]{:S(2)}) %collective-permute-start.3) | collective-permute-done | bytes 524320 | tf_op jit(solution)/shard_map/ppermute | solution.py:22
  73.4 1.7 %last_slot.1 = f32[4,2,16,4096]{3,2,1,0:T(8,128)} custom-call(s32[4,8]{1,0:T(4,128)} %requests.9, s32[1]{0:T(128)} %bitcast.owner.me, f32[16,128]{1,0:T(8,128)S(1)} %broadcast_in_dim.12.modulus_ref.modulus, f32[1,2,16,4096]{3,2,1,0:T(8,128)S(1)} %collective-permute-done.3.part, ...), custom_call_target="tpu_custom_call", output_to_operand_aliasing={{}: (5, {})} | custom-call | tf_op jit(solution)/shard_map/last_slot/pallas_call | solution.py:245
  (4 shorter events, 0.1 us)
Async XLA Ops:
  0.0 9.4 %copy-start.3 = (s32[16]{0:T(128)S(1)}, s32[16]{0:T(128)}, u32[]{:S(2)}) copy-start(s32[16]{0:T(128)} %param.9) | copy-start | bytes 196
  0.0 39.9 %copy-start = (f32[4,3,2,16,4096]{4,3,2,1,0:T(8,128)S(1)}, f32[4,3,2,16,4096]{4,3,2,1,0:T(8,128)}, u32[]{:S(2)}) copy-start(f32[4,3,2,16,4096]{4,3,2,1,0:T(8,128)} %keys.5) | copy-start | bytes 18874372
  0.0 39.9 %copy-start.2 = (s32[8]{0:T(128)S(1)}, s32[8]{0:T(128)}, u32[]{:S(2)}) copy-start(s32[8]{0:T(128)} %rotations.5) | copy-start | bytes 100
  2.4 37.5 %collective-permute-start.5 = (f32[3,16,4096]{2,1,0:T(8,128)S(1)}, f32[3,16,4096]{2,1,0:T(8,128)S(1)}, u32[]{:S(2)}, u32[]{:S(2)}) collective-permute-start(f32[3,16,4096]{2,1,0:T(8,128)S(1)} %gather_digits.3), channel_id=1, source_target_pairs={{0,16},{16,0},{1,17},{17,1},{2,18},{18,2},{3,19},{19,3},{4,20},{20... | collective-permute-start | bytes 2359304 | tf_op jit(solution)/shard_map/ppermute | solution.py:22
  7.3 38.7 %collective-permute-start.1 = (f32[3,16,4096]{2,1,0:T(8,128)S(1)}, f32[3,16,4096]{2,1,0:T(8,128)S(1)}, u32[]{:S(2)}, u32[]{:S(2)}) collective-permute-start(f32[3,16,4096]{2,1,0:T(8,128)S(1)} %gather_digits.2), channel_id=1, source_target_pairs={{0,16},{16,0},{1,17},{17,1},{2,18},{18,2},{3,19},{19,3},{4,20},{20... | collective-permute-start | bytes 2359304 | tf_op jit(solution)/shard_map/ppermute | solution.py:22
  7.4 32.5 %collective-permute-start = (s32[4,8]{1,0:T(4,128)}, s32[4,8]{1,0:T(4,128)S(1)}, u32[]{:S(2)}, u32[]{:S(2)}) collective-permute-start(s32[4,8]{1,0:T(4,128)} %requests.9), channel_id=1, source_target_pairs={{0,16},{16,0},{1,17},{17,1},{2,18},{18,2},{3,19},{19,3},{4,20},{20... | collective-permute-start | bytes 392 | tf_op jit(solution)/shard_map/ppermute | solution.py:22
  42.5 6.8 %collective-permute-start.6 = (f32[1,2,16,512]{3,2,1,0:T(8,128)S(1)}, f32[1,2,16,512]{3,2,1,0:T(8,128)S(1)}, u32[]{:S(2)}, u32[]{:S(2)}) collective-permute-start(f32[1,2,16,512]{3,2,1,0:T(8,128)S(1)} %get-tuple-element.17), channel_id=1, source_target_pairs={{0,15},{1,0},{2,1},{3,2},{4,3},{5,4},{6,5},{7,6},{8,7},{9,8},{10,9... | collective-permute-start | bytes 196616 | tf_op jit(solution)/shard_map/ppermute | solution.py:22
  46.0 5.5 %copy-start.1 = (f32[4,3,16,4096]{3,2,1,0:T(8,128)S(1)}, f32[4,3,16,4096]{3,2,1,0:T(8,128)}, u32[]{:S(2)}) copy-start(f32[4,3,16,4096]{3,2,1,0:T(8,128)} %digits.5) | copy-start | bytes 9437188
  47.7 3.5 %collective-permute-start.2 = (f32[1,2,16,512]{3,2,1,0:T(8,128)S(1)}, f32[1,2,16,512]{3,2,1,0:T(8,128)S(1)}, u32[]{:S(2)}, u32[]{:S(2)}) collective-permute-start(f32[1,2,16,512]{3,2,1,0:T(8,128)S(1)} %get-tuple-element.13), channel_id=1, source_target_pairs={{0,15},{1,0},{2,1},{3,2},{4,3},{5,4},{6,5},{7,6},{8,7},{9,8},{10,9... | collective-permute-start | bytes 196616 | tf_op jit(solution)/shard_map/ppermute | solution.py:22
  49.3 14.9 %collective-permute-start.7 = (f32[1,2,16,4096]{3,2,1,0:T(8,128)S(1)}, f32[1,2,16,4096]{3,2,1,0:T(8,128)S(1)}, u32[]{:S(2)}, u32[]{:S(2)}) collective-permute-start(f32[1,2,16,4096]{3,2,1,0:T(8,128)S(1)} %add_tail.5), channel_id=1, source_target_pairs={{0,16},{16,0},{1,17},{17,1},{2,18},{18,2},{3,19},{19,3},{4,20},{20... | collective-permute-start | bytes 1572872 | tf_op jit(solution)/shard_map/ppermute | solution.py:22
  51.2 22.2 %collective-permute-start.3 = (f32[1,2,16,4096]{3,2,1,0:T(8,128)S(1)}, f32[1,2,16,4096]{3,2,1,0:T(8,128)S(1)}, u32[]{:S(2)}, u32[]{:S(2)}) collective-permute-start(f32[1,2,16,4096]{3,2,1,0:T(8,128)S(1)} %add_tail.3), channel_id=1, source_target_pairs={{0,16},{16,0},{1,17},{17,1},{2,18},{18,2},{3,19},{19,3},{4,20},{20... | collective-permute-start | bytes 1572872 | tf_op jit(solution)/shard_map/ppermute | solution.py:22
  53.9 6.9 %collective-permute-start.4 = (f32[2,2,16,512]{3,2,1,0:T(8,128)S(1)}, f32[2,2,16,512]{3,2,1,0:T(8,128)S(1)}, u32[]{:S(2)}, u32[]{:S(2)}) collective-permute-start(f32[2,2,16,512]{3,2,1,0:T(8,128)S(1)} %get-tuple-element.15), channel_id=1, source_target_pairs={{0,15},{1,0},{2,1},{3,2},{4,3},{5,4},{6,5},{7,6},{8,7},{9,8},{10,9... | collective-permute-start | bytes 393224 | tf_op jit(solution)/shard_map/ppermute | solution.py:22

commit v3 on v2

v3 whole, which is shorter than its diff:
```python
import functools

import jax
import jax.numpy as jnp
from jax import lax
from jax.experimental import pallas as pl
from jax.experimental.pallas import tpu as pltpu
from jax.sharding import PartitionSpec as P

RMAX = 256
CAP = 2
WIDEST = 2 * RMAX
LANES = 128
ROWS = 8
SMEM = pl.BlockSpec(memory_space=pltpu.SMEM)
VMEM = pl.BlockSpec(memory_space=pltpu.VMEM)


def shifted(value, axis, steps):
    count = lax.axis_size(axis)
    pairs = [(source, (source + steps) % count) for source in range(count)]
    return lax.ppermute(value, axis, pairs)


def slot_ciphers(requests, ciphers, key_count, owner):
    needed = []
    for cipher in range(ciphers):
        flag = requests[cipher, owner * key_count]
        for key in range(1, key_count):
            flag = flag | requests[cipher, owner * key_count + key]
        needed.append(flag)
    slots = [jnp.int32(0)] * CAP
    rank = jnp.int32(0)
    for want in (1, 0):
        for cipher in range(ciphers):
            here = needed[cipher] == want
            for slot in range(CAP):
                slots[slot] = jnp.where(here & (rank == slot), cipher, slots[slot])
            rank = rank + here.astype(jnp.int32)
    return slots


def gather_kernel(wanted, ciphers, key_count, requests, owner, digits, *refs):
    outs, sems = refs[: len(wanted)], refs[len(wanted)]
    chosen = slot_ciphers(requests, ciphers, key_count, owner[0])
    loads = []
    for out, (slot, block) in zip(outs, wanted):
        for part in range(out.shape[0]):
            source = digits.at[chosen[slot], part, pl.ds(block * ROWS, ROWS)]
            loads.append(pltpu.make_async_copy(source, out.at[part], sems.at[len(loads)]))
    for load in loads:
        load.start()
    for load in loads:
        load.wait()


def gather(digits, requests, owner, wanted):
    ciphers, parts, _, columns = digits.shape
    key_count = requests.shape[1] // lax.axis_size("grp")
    return pl.pallas_call(
        functools.partial(gather_kernel, wanted, ciphers, key_count),
        out_shape=[jax.ShapeDtypeStruct((parts, ROWS, columns), jnp.float32)] * len(wanted),
        in_specs=[SMEM, SMEM, pl.BlockSpec(memory_space=pltpu.HBM)],
        out_specs=[VMEM] * len(wanted),
        scratch_shapes=[pltpu.SemaphoreType.DMA((parts * len(wanted),))],
        compiler_params=pltpu.CompilerParams(vmem_limit_bytes=4 << 20),
        cost_estimate=pl.CostEstimate(
            flops=0, transcendentals=0, bytes_accessed=8 * len(wanted) * parts * ROWS * columns
        ),
        name="gather_digits",
    )(requests, owner, pltpu.with_memory_space_constraint(digits, pltpu.HBM))


def products_kernel(slots, blocks, local, requests, owner, rotations, digits, keys, modulus_ref, tail, resident, rolled):
    key_count, parts, polys, _, columns = keys.shape
    ciphers = requests.shape[0]
    pad = WIDEST // LANES
    tiles = columns // LANES
    tail[...] = jnp.zeros_like(tail)
    resident[...] = jnp.zeros_like(resident)
    rolled[...] = jnp.zeros_like(rolled)
    lane = lax.broadcasted_iota(jnp.int32, (ROWS, LANES), 1)
    chosen = slot_ciphers(requests, ciphers, key_count, owner[0])

    def add_key(step, carry):
        block = step // key_count
        key = step - block * key_count
        rows = pl.ds(pl.multiple_of(block * ROWS, ROWS), ROWS)
        limbs = pl.ds(pl.multiple_of((blocks[0] + block) * ROWS, ROWS), ROWS)
        amount = 2 * rotations[owner[0] * key_count + key]
        skipped = amount // LANES
        within = amount - skipped * LANES
        turn = lax.rem(LANES - within, LANES)
        from_this = lane < LANES - within
        modulus = modulus_ref[limbs, :]
        inverse = 1.0 / modulus
        for place, slot in enumerate(slots):
            source = chosen[slot] if local else place

            @pl.when(requests[chosen[slot], owner[0] * key_count + key] > 0)
            def _():
                for poly in range(polys):
                    for tile in range(tiles):
                        at = pl.ds(tile * LANES, LANES)
                        combined = digits[source, 0, rows, at] * keys[key, 0, poly, limbs, at]
                        for part in range(1, parts):
                            combined = combined + digits[source, part, rows, at] * keys[key, part, poly, limbs, at]
                        quotient = jnp.floor(combined * inverse)
                        remainder = combined - quotient * modulus
                        rolled[:, pl.ds((pad + tile) * LANES, LANES)] = pltpu.roll(remainder, turn, 1)
                    for tile in range(pad + tiles):
                        start = pl.multiple_of((skipped + tile) * LANES, LANES)
                        after = pl.multiple_of((skipped + tile + 1) * LANES, LANES)
                        moved = jnp.where(from_this, rolled[:, pl.ds(start, LANES)], rolled[:, pl.ds(after, LANES)])
                        if tile < pad:
                            at = pl.ds(tile * LANES, LANES)
                            tail[place, poly, rows, at] = tail[place, poly, rows, at] + moved
                        else:
                            at = pl.ds((tile - pad) * LANES, LANES)
                            resident[place, poly, rows, at] = resident[place, poly, rows, at] + moved
        return carry

    lax.fori_loop(0, len(blocks) * key_count, add_key, 0)


def products(digits, keys, requests, owner, rotations, modulus, slots, blocks, local):
    key_count, parts, polys, _, columns = keys.shape
    count = len(slots)
    limbs = len(blocks) * ROWS
    pad = WIDEST // LANES
    work = count * key_count * polys * limbs * columns
    return pl.pallas_call(
        functools.partial(products_kernel, slots, blocks, local),
        out_shape=[
            jax.ShapeDtypeStruct((count, polys, limbs, WIDEST), jnp.float32),
            jax.ShapeDtypeStruct((count, polys, limbs, columns), jnp.float32),
        ],
        in_specs=[SMEM, SMEM, SMEM, VMEM, VMEM, VMEM],
        out_specs=[VMEM, VMEM],
        scratch_shapes=[pltpu.VMEM((ROWS, columns + 2 * pad * LANES + LANES), jnp.float32)],
        compiler_params=pltpu.CompilerParams(vmem_limit_bytes=20 << 20),
        cost_estimate=pl.CostEstimate(
            flops=20 * work, transcendentals=0, bytes_accessed=4 * (key_count * parts * polys * limbs * columns + count * limbs * columns * (parts + polys))
        ),
        name="products",
    )(requests, owner, rotations, digits, keys, modulus)


def add_tail_kernel(arrived, held, out):
    columns = held.shape[-1]
    at = pl.ds(columns - WIDEST, WIDEST)
    out[:, :, :, at] = held[:, :, :, at] + arrived[...]


def add_tail(resident, arrived):
    return pl.pallas_call(
        add_tail_kernel,
        out_shape=jax.ShapeDtypeStruct(resident.shape, jnp.float32),
        in_specs=[VMEM, VMEM],
        out_specs=VMEM,
        input_output_aliases={1: 0},
        compiler_params=pltpu.CompilerParams(vmem_limit_bytes=8 << 20),
        name="add_tail",
    )(arrived, resident)


def reduce_mod(amount, modulus):
    quotient = jnp.floor(amount * (1.0 / modulus))
    remainder = amount - quotient * modulus
    remainder = jnp.where(remainder < 0, remainder + modulus, remainder)
    return jnp.where(remainder >= modulus, remainder - modulus, remainder)


def sums_kernel(owners, groups, ciphers, key_count, keep, requests, me, modulus, *refs):
    parts = refs[: len(owners)]
    out = refs[len(owners)]
    cipher = pl.program_id(1)
    out[...] = jnp.zeros_like(out)
    for part, (steps, slots) in zip(parts, owners):
        chosen = slot_ciphers(requests, ciphers, key_count, lax.rem(me[0] + steps, groups))
        for place, slot in enumerate(slots):

            @pl.when(chosen[slot] == cipher)
            def _():
                out[...] = out[...] + part[place]

    if keep:
        held = refs[len(owners) + 1]
        chosen = slot_ciphers(requests, ciphers, key_count, lax.rem(me[0] + groups - 1, groups))
        for slot in range(CAP):

            @pl.when(chosen[slot] == cipher)
            def _():
                held[slot] = out[...]

    wide = modulus[:, :1]
    out[...] = reduce_mod(out[...], wide) / wide


def sums(parts, owners, requests, me, modulus, ciphers, keep):
    polys, limbs, columns = parts[0].shape[1:]
    groups = lax.axis_size("grp")
    key_count = requests.shape[1] // groups
    shapes = [jax.ShapeDtypeStruct((ciphers, polys, limbs, columns), jnp.float32)]
    specs = [pl.BlockSpec((pl.Squeezed(), polys, ROWS, columns), lambda block, cipher, *_: (cipher, 0, block, 0))]
    if keep:
        shapes.append(jax.ShapeDtypeStruct((CAP, polys, limbs, columns), jnp.float32))
        specs.append(pl.BlockSpec((CAP, polys, ROWS, columns), lambda block, cipher, *_: (0, 0, block, 0)))
    return pl.pallas_call(
        functools.partial(sums_kernel, owners, groups, ciphers, key_count, keep),
        out_shape=shapes,
        grid_spec=pltpu.PrefetchScalarGridSpec(
            num_scalar_prefetch=2,
            grid=(limbs // ROWS, ciphers),
            in_specs=[pl.BlockSpec((ROWS, LANES), lambda block, cipher, *_: (block, 0))]
            + [
                pl.BlockSpec((part.shape[0], polys, ROWS, columns), lambda block, cipher, *_: (0, 0, block, 0))
                for part in parts
            ],
            out_specs=specs,
        ),
        compiler_params=pltpu.CompilerParams(
            dimension_semantics=("arbitrary", "arbitrary"), vmem_limit_bytes=24 << 20
        ),
        cost_estimate=pl.CostEstimate(
            flops=20 * ciphers * polys * limbs * columns,
            transcendentals=0,
            bytes_accessed=4 * (ciphers + 2 + 2 * len(parts)) * polys * limbs * columns,
        ),
        name="sums",
    )(requests, me, modulus, *parts)


def finish_kernel(slot, block, groups, key_count, requests, me, modulus, part, held, before, out, done, sems):
    ciphers, polys, _, _ = out.shape
    cipher = slot_ciphers(requests, ciphers, key_count, lax.rem(me[0] + groups - 1, groups))[slot]
    rows = pl.ds(block * ROWS, ROWS)
    wide = modulus[rows, :1]
    stores = []
    for poly in range(polys):
        done[poly] = reduce_mod(held[slot, poly, rows, :] + part[0, poly], wide) / wide
        stores.append(pltpu.make_async_copy(done.at[poly], out.at[cipher, poly, rows], sems.at[poly]))
        stores[-1].start()
    for store in stores:
        store.wait()


def finish(part, held, result, requests, me, modulus, slot, block):
    _, polys, _, columns = result.shape
    groups = lax.axis_size("grp")
    key_count = requests.shape[1] // groups
    hbm = pl.BlockSpec(memory_space=pltpu.HBM)
    return pl.pallas_call(
        functools.partial(finish_kernel, slot, block, groups, key_count),
        out_shape=jax.ShapeDtypeStruct(result.shape, jnp.float32),
        in_specs=[SMEM, SMEM, VMEM, VMEM, VMEM, hbm],
        out_specs=hbm,
        scratch_shapes=[pltpu.VMEM((polys, ROWS, columns), jnp.float32), pltpu.SemaphoreType.DMA((polys,))],
        input_output_aliases={5: 0},
        compiler_params=pltpu.CompilerParams(vmem_limit_bytes=8 << 20),
        cost_estimate=pl.CostEstimate(
            flops=20 * polys * ROWS * columns, transcendentals=0, bytes_accessed=12 * polys * ROWS * columns
        ),
        name="finish",
    )(requests, me, modulus, part, held, result)


def per_device(digits, keys, requests, rotations, moduli):
    me = lax.axis_index("grp").astype(jnp.int32).reshape(1)
    modulus = jnp.broadcast_to(moduli.astype(jnp.float32)[:, None], (digits.shape[2], LANES))
    way = key_switch_pair if lax.axis_size("grp") == 2 else key_switch_any
    return way(digits, keys, requests, rotations, modulus, me)


def key_switch_any(digits, keys, requests, rotations, modulus, me):
    groups = lax.axis_size("grp")
    blocks = tuple(range(digits.shape[2] // ROWS))
    slots = tuple(range(CAP))
    tail, resident = products(digits, keys, requests, me, rotations, modulus, slots, blocks, True)
    parts = [add_tail(resident, shifted(tail, "limb", -1))]
    owners = [(0, slots)]
    for steps in range(1, groups):
        asked = shifted(requests, "grp", steps)
        owner = lax.rem(me + steps, groups)
        for slot in slots:
            picked = gather(digits, requests, owner, tuple((slot, block) for block in blocks))
            back = []
            for block in blocks:
                arrived = shifted(picked[block], "grp", steps)
                tail, resident = products(
                    arrived[None], keys, asked, me, rotations, modulus, (slot,), (block,), False
                )
                back.append(shifted(add_tail(resident, shifted(tail, "limb", -1)), "grp", -steps))
            parts.append(jnp.concatenate(back, axis=2))
            owners.append((steps, (slot,)))
    return sums(parts, tuple(owners), requests, me, modulus, digits.shape[0], False)[0]


def key_switch_pair(digits, keys, requests, rotations, modulus, me):
    key_count = keys.shape[0]
    other = 1 - me
    asked = shifted(requests, "grp", 1)
    first = gather(digits, requests, other, ((0, 0),))[0]
    ours = jnp.where(me == 0, requests, asked)[:, key_count:]
    theirs = jnp.where(me == 0, asked, requests)[:, :key_count]
    two_right = jnp.sum(jnp.max(ours, axis=1)) > 1
    two_left = jnp.sum(jnp.max(theirs, axis=1)) > 1
    case = jnp.where(two_right == two_left, 0, jnp.where(two_right, 1, 2))

    def branch(pairs):
        def run(first, digits, keys, requests, asked, rotations, modulus, me):
            return exchange(pairs, first, digits, keys, requests, asked, rotations, modulus, me)

        return run

    ways = ([(0, 1), (1, 0)], [(0, 1)], [(1, 0)])
    branches = [branch((ways[0], pairs)) for pairs in ways]
    return lax.switch(case, branches, first, digits, keys, requests, asked, rotations, modulus, me)


def exchange(pairs, first, digits, keys, requests, asked, rotations, modulus, me):
    blocks = tuple(range(digits.shape[2] // ROWS))
    slots = tuple(range(CAP))
    turns = [(slot, block) for slot in slots for block in blocks]
    other = 1 - me
    picked = dict(zip(turns[1:], gather(digits, requests, other, tuple(turns[1:]))))
    picked[turns[0]] = first
    sent = {}
    for slot, block in turns:
        sent[slot, block] = lax.ppermute(picked[slot, block], "grp", pairs[slot])
    tail, resident = products(digits, keys, requests, me, rotations, modulus, slots, blocks, True)
    arrived = shifted(tail, "limb", -1)
    local = add_tail(resident, arrived)
    result, held = sums([local], ((0, slots),), requests, me, modulus, digits.shape[0], True)
    back = {}
    for slot, block in turns:
        tail, resident = products(
            sent[slot, block][None], keys, asked, me, rotations, modulus, (slot,), (block,), False
        )
        arrived = shifted(tail, "limb", -1)
        whole = add_tail(resident, arrived)
        back[slot, block] = lax.ppermute(whole, "grp", [(target, source) for source, target in pairs[slot]])
    for slot, block in turns:
        result = finish(back[slot, block], held, result, requests, me, modulus, slot, block)
    return result


def solution(mesh):
    in_specs = (
        P("grp", None, None, "limb"),
        P("grp", None, None, None, "limb"),
        P("grp", None),
        P(),
        P(),
    )
    out_specs = P("grp", None, None, "limb")
    return jax.shard_map(
        per_device, mesh=mesh, in_specs=in_specs, out_specs=out_specs, check_vma=False
    )
```

time: 75.3 us -> 71.6 us (0.951)
  waiting for transfers between devices: 41.6 us -> 18.5 us
  starting transfers between devices: 15.1 us -> 24.4 us
  Pallas kernels: 18.3 us -> 24.8 us
  other arithmetic: 0.01 us -> 2.11 us
  between operations: 0.07 us -> 1.27 us
    ppermute x8 -> x6, waiting for transfers between devices: 41.6 us -> 2.53 us  [shifted(): return lax.ppermute(value, axis, pairs)]
    ppermute x0 -> x8, waiting for transfers between devices: none -> 15.9 us  [the longest x4 15.9 us: exchange(): sent[slot, block] = lax.ppermute(picked[slot, block], 'grp', pairs[slot])]
    ppermute x0 -> x8, starting transfers between devices: none -> 12.1 us  [the longest x4 6.69 us: exchange(): sent[slot, block] = lax.ppermute(picked[slot, block], 'grp', pairs[slot])]
    pallas_call x7 -> x12, Pallas kernels: 18.2 us -> 24.8 us  [the longest x5 10.1 us: products(): pl.pallas_call(functools.partial(products_kernel, slots, blocks, local),...]
    ppermute x8 -> x6, starting transfers between devices: 15.1 us -> 12.3 us  [shifted(): return lax.ppermute(value, axis, pairs)]
    reduce_sum x0 -> x2, other arithmetic: none -> 1.27 us  [the longest x1 0.64 us: key_switch_pair(): two_right = jnp.sum(jnp.max(ours, axis=1)) > 1]
  transfers between devices with their start and end apart: 8 -> 14, of which waited for: 5 -> 5; matrix products, arithmetic and copies ran while one was open for 0% -> 1% of each run, Pallas kernels for 19% -> 33%
where the time goes in v3:
time: 71.6 us; the launch traced here: 71.4 us
  Pallas kernels  24.8 us (35%)
  starting transfers between devices  24.4 us (34%)
  waiting for transfers between devices  18.5 us (26%)
  other arithmetic  2.11 us (3%)
  between operations  1.27 us (2%)
    ppermute x4, waiting for transfers between devices, exchange(): sent[slot, block] = lax.ppermute(picked[slot, block], 'grp', pairs[slot])  15.9 us
    ppermute x6, starting transfers between devices, shifted(): return lax.ppermute(value, axis, pairs)  12.3 us
    pallas_call x5, Pallas kernels, products(): pl.pallas_call(functools.partial(products_kernel, slots, blocks, local),...  10.1 us
    ppermute x4, starting transfers between devices, exchange(): sent[slot, block] = lax.ppermute(picked[slot, block], 'grp', pairs[slot])  6.69 us
    pallas_call x4, Pallas kernels, finish(): pl.pallas_call(functools.partial(finish_kernel, slot, block, groups, key_...  5.66 us
    ppermute x4, starting transfers between devices, exchange(): lax.ppermute(whole, 'grp', [(target, source) for source, target in pairs[...  5.39 us
    pallas_call x1, Pallas kernels, sums(): pl.pallas_call(functools.partial(sums_kernel, owners, groups, ciphers, ke...  5.23 us
    pallas_call x2, Pallas kernels, gather(): pl.pallas_call(functools.partial(gather_kernel, wanted, ciphers, key_coun...  3.78 us
  transfers between devices with their start and end apart: 14, of which 5 were waited for; matrix products, arithmetic and copies ran while one was open for 1% of the time, Pallas kernels for 33%

profile of v3, /device:TPU:0, one launch (start us, length us, event | category | flops | bytes accessed | tf_op | source)
XLA Modules:
  0.0 71.4 jit_solution(11655300644758252860)
XLA Ops:
  0.0 0.0 copy-start.6
  0.0 0.0 copy-start.7
  0.0 3.0 %collective-permute-start.39 = (s32[4,8]{1,0:T(4,128)}, s32[4,8]{1,0:T(4,128)S(1)}, u32[]{:S(2)}, u32[]{:S(2)}) collective-permute-start(s32[4,8]{1,0:T(4,128)} %requests.1), channel_id=1, source_target_pairs={{0,16},{16,0},{1,17},{17,1},{2,18},{18,2},{3,19},{19,3},{4,20},{20... | collective-permute-start | bytes 392 | tf_op jit(solution)/shard_map/ppermute | solution.py:22
  3.0 0.7 convert_element_type.3
  3.6 1.8 %gather_digits.7 = f32[3,8,4096]{2,1,0:T(8,128)S(1)} custom-call(s32[4,8]{1,0:T(4,128)} %requests.1, s32[1]{0:T(128)S(6)} %sub.12.owner, f32[4,3,16,4096]{3,2,1,0:T(8,128)} %digits.1), custom_call_target="tpu_custom_call" | custom-call | bytes 786432 | tf_op jit(solution)/shard_map/gather_digits/pallas_call | solution.py:60
  5.4 0.0 collective-permute-done.39
  5.4 0.0 copy-done.6
  5.5 0.2 slice_reduce_fusion
  5.6 0.6 reduce_sum.18
  6.3 0.6 reduce_sum.19
  8.1 0.0 copy-done.7
  8.1 63.2 %conditional.1 = (f32[4,2,16,4096]{3,2,1,0:T(8,128)}) conditional(s32[]{:T(128)} %clamp.3, (s32[1]{0:T(128)}, s32[4,8]{1,0:T(4,128)S(1)}, f32[4,3,16,4096]{3,2,1,0:T(8,128)}, s32[4,8]{1,0:T(4,128)S(1)}, s32[8]{0:T(128)S(1)}, /*index=5*/f32[4,3,2,16,4096]{4,3,2,1,0:T(8,128)}, f32[16]{0:T(128)S(1)}, ...), branch_computations={%region_4.5_spmd, %region_5.6_spmd, %region_6.7_spmd} | conditional | flops 57671680 | bytes 83108496 | solution.py:318
  8.2 1.4 %collective-permute-start.36 = (f32[3,8,4096]{2,1,0:T(8,128)S(1)}, f32[3,8,4096]{2,1,0:T(8,128)S(1)}, u32[]{:S(2)}, u32[]{:S(2)}) collective-permute-start(f32[3,8,4096]{2,1,0:T(8,128)S(1)} %get-tuple-element.122), channel_id=1, source_target_pairs={{0,16},{16,0},{1,17},{17,1},{2,18},{18,2},{3,19},{19,3},{4,20},{20... | collective-permute-start | bytes 1179656 | tf_op jit(solution)/shard_map/cond/branch_2_fun/ppermute | solution.py:330
  9.6 2.0 %gather_digits.6 = (f32[3,8,4096]{2,1,0:T(8,128)S(1)}, f32[3,8,4096]{2,1,0:T(8,128)S(1)}, f32[3,8,4096]{2,1,0:T(8,128)S(1)}) custom-call(s32[4,8]{1,0:T(4,128)S(1)} %get-tuple-element.103.requests, s32[1]{0:T(128)S(6)} %sub.10.owner, f32[4,3,16,4096]{3,2,1,0:T(8,128)} %get-tuple-element.108.digits), custom_call_target="tpu_custom_call" | custom-call | bytes 2359296 | tf_op jit(solution)/shard_map/cond/branch_2_fun/gather_digits/pallas_call | solution.py:60
  11.6 1.3 %collective-permute-start.30 = (f32[3,8,4096]{2,1,0:T(8,128)S(1)}, f32[3,8,4096]{2,1,0:T(8,128)S(1)}, u32[]{:S(2)}, u32[]{:S(2)}) collective-permute-start(f32[3,8,4096]{2,1,0:T(8,128)S(1)} %get-tuple-element.116), channel_id=1, source_target_pairs={{16,0},{17,1},{18,2},{19,3},{20,4},{21,5},{22,6},{23,7},{24,8},{25... | collective-permute-start | bytes 1179656 | tf_op jit(solution)/shard_map/cond/branch_2_fun/ppermute | solution.py:330
  12.9 2.7 %collective-permute-start.33 = (f32[3,8,4096]{2,1,0:T(8,128)S(1)}, f32[3,8,4096]{2,1,0:T(8,128)S(1)}, u32[]{:S(2)}, u32[]{:S(2)}) collective-permute-start(f32[3,8,4096]{2,1,0:T(8,128)S(1)} %get-tuple-element.119), channel_id=1, source_target_pairs={{0,16},{16,0},{1,17},{17,1},{2,18},{18,2},{3,19},{19,3},{4,20},{20... | collective-permute-start | bytes 1179656 | tf_op jit(solution)/shard_map/cond/branch_2_fun/ppermute | solution.py:330
  15.6 1.3 %collective-permute-start.26 = (f32[3,8,4096]{2,1,0:T(8,128)S(1)}, f32[3,8,4096]{2,1,0:T(8,128)S(1)}, u32[]{:S(2)}, u32[]{:S(2)}) collective-permute-start(f32[3,8,4096]{2,1,0:T(8,128)S(1)} %get-tuple-element.109), channel_id=1, source_target_pairs={{16,0},{17,1},{18,2},{19,3},{20,4},{21,5},{22,6},{23,7},{24,8},{25... | collective-permute-start | bytes 1179656 | tf_op jit(solution)/shard_map/cond/branch_2_fun/ppermute | solution.py:330
  16.9 3.3 %collective-permute-done.36 = f32[3,8,4096]{2,1,0:T(8,128)S(1)} collective-permute-done((f32[3,8,4096]{2,1,0:T(8,128)S(1)}, f32[3,8,4096]{2,1,0:T(8,128)S(1)}, u32[]{:S(2)}, u32[]{:S(2)}) %collective-permute-start.36) | collective-permute-done | bytes 393248 | tf_op jit(solution)/shard_map/cond/branch_2_fun/ppermute | solution.py:330
  20.2 0.1 broadcast_in_dim.57.modulus_ref.modulus
  20.3 0.0 copy-start.2
  20.3 3.9 %products.29 = (f32[1,2,8,512]{3,2,1,0:T(8,128)S(1)}, f32[1,2,8,4096]{3,2,1,0:T(8,128)S(1)}) custom-call(s32[4,8]{1,0:T(4,128)S(1)} %get-tuple-element.106.requests, s32[1]{0:T(128)} %get-tuple-element.104.owner.me, s32[8]{0:T(128)S(1)} %get-tuple-element.138.rotations, f32[1,3,8,4096]{3,2,1,0:T(8,128)S(1)} %bitcast.25, ...), custom_call_target="tpu_custom_call" | custom-call | flops 5242880 | bytes 3801088 | tf_op jit(solution)/shard_map/cond/branch_2_fun/products/pallas_call | solution.py:132
  24.2 1.5 %collective-permute-start.37 = (f32[1,2,8,512]{3,2,1,0:T(8,128)S(1)}, f32[1,2,8,512]{3,2,1,0:T(8,128)S(1)}, u32[]{:S(2)}, u32[]{:S(2)}) collective-permute-start(f32[1,2,8,512]{3,2,1,0:T(8,128)S(1)} %get-tuple-element.123), channel_id=1, source_target_pairs={{0,15},{1,0},{2,1},{3,2},{4,3},{5,4},{6,5},{7,6},{8,7},{9,8},{10,9... | collective-permute-start | bytes 98312 | tf_op jit(solution)/shard_map/cond/branch_2_fun/ppermute | solution.py:22
  25.7 2.9 %collective-permute-done.30 = f32[3,8,4096]{2,1,0:T(8,128)S(1)} collective-permute-done((f32[3,8,4096]{2,1,0:T(8,128)S(1)}, f32[3,8,4096]{2,1,0:T(8,128)S(1)}, u32[]{:S(2)}, u32[]{:S(2)}) %collective-permute-start.30) | collective-permute-done | bytes 393248 | tf_op jit(solution)/shard_map/cond/branch_2_fun/ppermute | solution.py:330
  28.6 0.0 copy-done.2
  28.6 1.2 %products.27 = (f32[1,2,8,512]{3,2,1,0:T(8,128)S(1)}, f32[1,2,8,4096]{3,2,1,0:T(8,128)S(1)}) custom-call(s32[4,8]{1,0:T(4,128)S(1)} %get-tuple-element.106.requests, s32[1]{0:T(128)} %get-tuple-element.104.owner.me, s32[8]{0:T(128)S(1)} %get-tuple-element.138.rotations, f32[1,3,8,4096]{3,2,1,0:T(8,128)S(1)} %bitcast.22, ...), custom_call_target="tpu_custom_call" | custom-call | flops 5242880 | bytes 3801088 | tf_op jit(solution)/shard_map/cond/branch_2_fun/products/pallas_call | solution.py:132
  29.8 1.5 %collective-permute-start.31 = (f32[1,2,8,512]{3,2,1,0:T(8,128)S(1)}, f32[1,2,8,512]{3,2,1,0:T(8,128)S(1)}, u32[]{:S(2)}, u32[]{:S(2)}) collective-permute-start(f32[1,2,8,512]{3,2,1,0:T(8,128)S(1)} %get-tuple-element.117), channel_id=1, source_target_pairs={{0,15},{1,0},{2,1},{3,2},{4,3},{5,4},{6,5},{7,6},{8,7},{9,8},{10,9... | collective-permute-start | bytes 98312 | tf_op jit(solution)/shard_map/cond/branch_2_fun/ppermute | solution.py:22
  31.3 5.8 %collective-permute-done.33 = f32[3,8,4096]{2,1,0:T(8,128)S(1)} collective-permute-done((f32[3,8,4096]{2,1,0:T(8,128)S(1)}, f32[3,8,4096]{2,1,0:T(8,128)S(1)}, u32[]{:S(2)}, u32[]{:S(2)}) %collective-permute-start.33) | collective-permute-done | bytes 393248 | tf_op jit(solution)/shard_map/cond/branch_2_fun/ppermute | solution.py:330
  37.1 1.6 %products.28 = (f32[1,2,8,512]{3,2,1,0:T(8,128)S(1)}, f32[1,2,8,4096]{3,2,1,0:T(8,128)S(1)}) custom-call(s32[4,8]{1,0:T(4,128)S(1)} %get-tuple-element.106.requests, s32[1]{0:T(128)} %get-tuple-element.104.owner.me, s32[8]{0:T(128)S(1)} %get-tuple-element.138.rotations, f32[1,3,8,4096]{3,2,1,0:T(8,128)S(1)} %bitcast.19, ...), custom_call_target="tpu_custom_call" | custom-call | flops 5242880 | bytes 3801088 | tf_op jit(solution)/shard_map/cond/branch_2_fun/products/pallas_call | solution.py:132
  38.6 1.5 %collective-permute-start.34 = (f32[1,2,8,512]{3,2,1,0:T(8,128)S(1)}, f32[1,2,8,512]{3,2,1,0:T(8,128)S(1)}, u32[]{:S(2)}, u32[]{:S(2)}) collective-permute-start(f32[1,2,8,512]{3,2,1,0:T(8,128)S(1)} %get-tuple-element.120), channel_id=1, source_target_pairs={{0,15},{1,0},{2,1},{3,2},{4,3},{5,4},{6,5},{7,6},{8,7},{9,8},{10,9... | collective-permute-start | bytes 98312 | tf_op jit(solution)/shard_map/cond/branch_2_fun/ppermute | solution.py:22
  40.1 3.9 %collective-permute-done.26 = f32[3,8,4096]{2,1,0:T(8,128)S(1)} collective-permute-done((f32[3,8,4096]{2,1,0:T(8,128)S(1)}, f32[3,8,4096]{2,1,0:T(8,128)S(1)}, u32[]{:S(2)}, u32[]{:S(2)}) %collective-permute-start.26) | collective-permute-done | bytes 393248 | tf_op jit(solution)/shard_map/cond/branch_2_fun/ppermute | solution.py:330
  44.1 0.0 copy-start.5
  44.1 1.1 %products.25 = (f32[1,2,8,512]{3,2,1,0:T(8,128)S(1)}, f32[1,2,8,4096]{3,2,1,0:T(8,128)S(1)}) custom-call(s32[4,8]{1,0:T(4,128)S(1)} %get-tuple-element.106.requests, s32[1]{0:T(128)} %get-tuple-element.104.owner.me, s32[8]{0:T(128)S(1)} %get-tuple-element.138.rotations, f32[1,3,8,4096]{3,2,1,0:T(8,128)S(1)} %bitcast.16, ...), custom_call_target="tpu_custom_call" | custom-call | flops 5242880 | bytes 3801088 | tf_op jit(solution)/shard_map/cond/branch_2_fun/products/pallas_call | solution.py:132
  45.2 2.9 %collective-permute-start.27 = (f32[1,2,8,512]{3,2,1,0:T(8,128)S(1)}, f32[1,2,8,512]{3,2,1,0:T(8,128)S(1)}, u32[]{:S(2)}, u32[]{:S(2)}) collective-permute-start(f32[1,2,8,512]{3,2,1,0:T(8,128)S(1)} %get-tuple-element.111), channel_id=1, source_target_pairs={{0,15},{1,0},{2,1},{3,2},{4,3},{5,4},{6,5},{7,6},{8,7},{9,8},{10,9... | collective-permute-start | bytes 98312 | tf_op jit(solution)/shard_map/cond/branch_2_fun/ppermute | solution.py:22
  48.2 0.0 collective-permute-done.37.arrived
  48.2 0.1 collective-permute-start.38
  48.2 0.0 collective-permute-done.34.arrived
  48.3 2.1 %collective-permute-start.35 = (f32[1,2,8,4096]{3,2,1,0:T(8,128)S(1)}, f32[1,2,8,4096]{3,2,1,0:T(8,128)S(1)}, u32[]{:S(2)}, u32[]{:S(2)}) collective-permute-start(f32[1,2,8,4096]{3,2,1,0:T(8,128)S(1)} %add_tail.28), channel_id=1, source_target_pairs={{16,0},{0,16},{17,1},{1,17},{18,2},{2,18},{19,3},{3,19},{20,4},{4,... | collective-permute-start | bytes 786440 | tf_op jit(solution)/shard_map/cond/branch_2_fun/ppermute | solution.py:342
  50.3 0.0 collective-permute-done.31.arrived
  50.4 1.9 %collective-permute-start.32 = (f32[1,2,8,4096]{3,2,1,0:T(8,128)S(1)}, f32[1,2,8,4096]{3,2,1,0:T(8,128)S(1)}, u32[]{:S(2)}, u32[]{:S(2)}) collective-permute-start(f32[1,2,8,4096]{3,2,1,0:T(8,128)S(1)} %add_tail.27), channel_id=1, source_target_pairs={{0,16},{1,17},{2,18},{3,19},{4,20},{5,21},{6,22},{7,23},{8,24},{9,... | collective-permute-start | bytes 786440 | tf_op jit(solution)/shard_map/cond/branch_2_fun/ppermute | solution.py:342
  52.3 0.0 collective-permute-done.27.arrived
  52.3 1.3 %collective-permute-start.28 = (f32[1,2,8,4096]{3,2,1,0:T(8,128)S(1)}, f32[1,2,8,4096]{3,2,1,0:T(8,128)S(1)}, u32[]{:S(2)}, u32[]{:S(2)}) collective-permute-start(f32[1,2,8,4096]{3,2,1,0:T(8,128)S(1)} %add_tail.25), channel_id=1, source_target_pairs={{0,16},{1,17},{2,18},{3,19},{4,20},{5,21},{6,22},{7,23},{8,24},{9,... | collective-permute-start | bytes 786440 | tf_op jit(solution)/shard_map/cond/branch_2_fun/ppermute | solution.py:342
  53.6 0.0 copy-done.5
  53.7 2.3 %products.26 = (f32[2,2,16,512]{3,2,1,0:T(8,128)S(1)}, f32[2,2,16,4096]{3,2,1,0:T(8,128)S(1)}) custom-call(s32[4,8]{1,0:T(4,128)S(1)} %get-tuple-element.103.requests, s32[1]{0:T(128)} %get-tuple-element.104.owner.me, s32[8]{0:T(128)S(1)} %get-tuple-element.138.rotations, f32[4,3,16,4096]{3,2,1,0:T(8,128)S(1)} %copy-done.5, ...), custom_call_target="tpu_custom_call" | custom-call | flops 20971520 | bytes 8912896 | tf_op jit(solution)/shard_map/cond/branch_2_fun/products/pallas_call | solution.py:132
  56.0 1.9 %collective-permute-start.29 = (f32[2,2,16,512]{3,2,1,0:T(8,128)S(1)}, f32[2,2,16,512]{3,2,1,0:T(8,128)S(1)}, u32[]{:S(2)}, u32[]{:S(2)}) collective-permute-start(f32[2,2,16,512]{3,2,1,0:T(8,128)S(1)} %get-tuple-element.113), channel_id=1, source_target_pairs={{0,15},{1,0},{2,1},{3,2},{4,3},{5,4},{6,5},{7,6},{8,7},{9,8},{10,9... | collective-permute-start | bytes 393224 | tf_op jit(solution)/shard_map/cond/branch_2_fun/ppermute | solution.py:22
  57.9 2.5 %collective-permute-done.29.arrived = f32[2,2,16,512]{3,2,1,0:T(8,128)S(1)} collective-permute-done((f32[2,2,16,512]{3,2,1,0:T(8,128)S(1)}, f32[2,2,16,512]{3,2,1,0:T(8,128)S(1)}, u32[]{:S(2)}, u32[]{:S(2)}) %collective-permute-start.29) | collective-permute-done | bytes 131104 | tf_op jit(solution)/shard_map/cond/branch_2_fun/ppermute | solution.py:22
  60.4 5.2 %sums.5 = (f32[4,2,16,4096]{3,2,1,0:T(8,128)}, f32[2,2,16,4096]{3,2,1,0:T(8,128)S(1)}) custom-call(s32[4,8]{1,0:T(4,128)S(1)} %get-tuple-element.103.requests, s32[1]{0:T(128)} %get-tuple-element.104.owner.me, f32[16,128]{1,0:T(8,128)S(1)} %broadcast_in_dim.57.modulus_ref.modulus, f32[2,2,16,4096]{3,2,1,0:T(8,128)S(1)} %add_tail.26.refs_0_), custom_call_target="tpu_custom_call" | custom-call | flops 10485760 | bytes 4194304 | tf_op jit(solution)/shard_map/cond/branch_2_fun/sums/pallas_call | solution.py:209
  65.7 0.0 collective-permute-done.38.part
  65.7 1.4 %finish.20.before = f32[4,2,16,4096]{3,2,1,0:T(8,128)} custom-call(s32[4,8]{1,0:T(4,128)S(1)} %get-tuple-element.103.requests, s32[1]{0:T(128)} %get-tuple-element.104.owner.me, f32[16,128]{1,0:T(8,128)S(1)} %broadcast_in_dim.57.modulus_ref.modulus, f32[1,2,8,4096]{3,2,1,0:T(8,128)S(1)} %collective-permute-done.38.part, ...), custom_call_target="tpu_custom_call", output_to_operand_aliasing={{}: (5, {})} | custom-call | flops 1310720 | bytes 786432 | tf_op jit(solution)/shard_map/cond/branch_2_fun/finish/pallas_call | solution.py:253
  67.1 0.0 collective-permute-done.35.part
  67.1 1.4 %finish.21.before = f32[4,2,16,4096]{3,2,1,0:T(8,128)} custom-call(s32[4,8]{1,0:T(4,128)S(1)} %get-tuple-element.103.requests, s32[1]{0:T(128)} %get-tuple-element.104.owner.me, f32[16,128]{1,0:T(8,128)S(1)} %broadcast_in_dim.57.modulus_ref.modulus, f32[1,2,8,4096]{3,2,1,0:T(8,128)S(1)} %collective-permute-done.35.part, ...), custom_call_target="tpu_custom_call", output_to_operand_aliasing={{}: (5, {})} | custom-call | flops 1310720 | bytes 786432 | tf_op jit(solution)/shard_map/cond/branch_2_fun/finish/pallas_call | solution.py:253
  68.5 0.0 collective-permute-done.32.part
  68.5 1.4 %finish.22.before = f32[4,2,16,4096]{3,2,1,0:T(8,128)} custom-call(s32[4,8]{1,0:T(4,128)S(1)} %get-tuple-element.103.requests, s32[1]{0:T(128)} %get-tuple-element.104.owner.me, f32[16,128]{1,0:T(8,128)S(1)} %broadcast_in_dim.57.modulus_ref.modulus, f32[1,2,8,4096]{3,2,1,0:T(8,128)S(1)} %collective-permute-done.32.part, ...), custom_call_target="tpu_custom_call", output_to_operand_aliasing={{}: (5, {})} | custom-call | flops 1310720 | bytes 786432 | tf_op jit(solution)/shard_map/cond/branch_2_fun/finish/pallas_call | solution.py:253
  69.9 0.0 collective-permute-done.28.part
  70.0 1.4 %finish.23 = f32[4,2,16,4096]{3,2,1,0:T(8,128)} custom-call(s32[4,8]{1,0:T(4,128)S(1)} %get-tuple-element.103.requests, s32[1]{0:T(128)} %get-tuple-element.104.owner.me, f32[16,128]{1,0:T(8,128)S(1)} %broadcast_in_dim.57.modulus_ref.modulus, f32[1,2,8,4096]{3,2,1,0:T(8,128)S(1)} %collective-permute-done.28.part, ...), custom_call_target="tpu_custom_call", output_to_operand_aliasing={{}: (5, {})} | custom-call | flops 1310720 | bytes 786432 | tf_op jit(solution)/shard_map/cond/branch_2_fun/finish/pallas_call | solution.py:253
  (6 shorter events, 0.1 us)
Async XLA Ops:
  0.0 5.4 %copy-start.6 = (s32[4,8]{1,0:T(4,128)S(1)}, s32[4,8]{1,0:T(4,128)}, u32[]{:S(2)}) copy-start(s32[4,8]{1,0:T(4,128)} %requests.1) | copy-start | bytes 388
  0.0 8.1 %copy-start.7 = (s32[8]{0:T(128)S(1)}, s32[8]{0:T(128)}, u32[]{:S(2)}) copy-start(s32[8]{0:T(128)} %param.11) | copy-start | bytes 100
  0.0 5.4 %collective-permute-start.39 = (s32[4,8]{1,0:T(4,128)}, s32[4,8]{1,0:T(4,128)S(1)}, u32[]{:S(2)}, u32[]{:S(2)}) collective-permute-start(s32[4,8]{1,0:T(4,128)} %requests.1), channel_id=1, source_target_pairs={{0,16},{16,0},{1,17},{17,1},{2,18},{18,2},{3,19},{19,3},{4,20},{20... | collective-permute-start | bytes 392 | tf_op jit(solution)/shard_map/ppermute | solution.py:22
  8.2 12.1 %collective-permute-start.36 = (f32[3,8,4096]{2,1,0:T(8,128)S(1)}, f32[3,8,4096]{2,1,0:T(8,128)S(1)}, u32[]{:S(2)}, u32[]{:S(2)}) collective-permute-start(f32[3,8,4096]{2,1,0:T(8,128)S(1)} %get-tuple-element.122), channel_id=1, source_target_pairs={{0,16},{16,0},{1,17},{17,1},{2,18},{18,2},{3,19},{19,3},{4,20},{20... | collective-permute-start | bytes 1179656 | tf_op jit(solution)/shard_map/cond/branch_2_fun/ppermute | solution.py:330
  11.6 17.1 %collective-permute-start.30 = (f32[3,8,4096]{2,1,0:T(8,128)S(1)}, f32[3,8,4096]{2,1,0:T(8,128)S(1)}, u32[]{:S(2)}, u32[]{:S(2)}) collective-permute-start(f32[3,8,4096]{2,1,0:T(8,128)S(1)} %get-tuple-element.116), channel_id=1, source_target_pairs={{16,0},{17,1},{18,2},{19,3},{20,4},{21,5},{22,6},{23,7},{24,8},{25... | collective-permute-start | bytes 1179656 | tf_op jit(solution)/shard_map/cond/branch_2_fun/ppermute | solution.py:330
  12.9 24.2 %collective-permute-start.33 = (f32[3,8,4096]{2,1,0:T(8,128)S(1)}, f32[3,8,4096]{2,1,0:T(8,128)S(1)}, u32[]{:S(2)}, u32[]{:S(2)}) collective-permute-start(f32[3,8,4096]{2,1,0:T(8,128)S(1)} %get-tuple-element.119), channel_id=1, source_target_pairs={{0,16},{16,0},{1,17},{17,1},{2,18},{18,2},{3,19},{19,3},{4,20},{20... | collective-permute-start | bytes 1179656 | tf_op jit(solution)/shard_map/cond/branch_2_fun/ppermute | solution.py:330
  15.6 28.5 %collective-permute-start.26 = (f32[3,8,4096]{2,1,0:T(8,128)S(1)}, f32[3,8,4096]{2,1,0:T(8,128)S(1)}, u32[]{:S(2)}, u32[]{:S(2)}) collective-permute-start(f32[3,8,4096]{2,1,0:T(8,128)S(1)} %get-tuple-element.109), channel_id=1, source_target_pairs={{16,0},{17,1},{18,2},{19,3},{20,4},{21,5},{22,6},{23,7},{24,8},{25... | collective-permute-start | bytes 1179656 | tf_op jit(solution)/shard_map/cond/branch_2_fun/ppermute | solution.py:330
  20.3 8.4 %copy-start.2 = (f32[4,3,2,16,4096]{4,3,2,1,0:T(8,128)S(1)}, f32[4,3,2,16,4096]{4,3,2,1,0:T(8,128)}, u32[]{:S(2)}) copy-start(f32[4,3,2,16,4096]{4,3,2,1,0:T(8,128)} %get-tuple-element.141.keys) | copy-start | bytes 18874372 | tf_op jit(solution)/shard_map/cond
  24.2 23.9 %collective-permute-start.37 = (f32[1,2,8,512]{3,2,1,0:T(8,128)S(1)}, f32[1,2,8,512]{3,2,1,0:T(8,128)S(1)}, u32[]{:S(2)}, u32[]{:S(2)}) collective-permute-start(f32[1,2,8,512]{3,2,1,0:T(8,128)S(1)} %get-tuple-element.123), channel_id=1, source_target_pairs={{0,15},{1,0},{2,1},{3,2},{4,3},{5,4},{6,5},{7,6},{8,7},{9,8},{10,9... | collective-permute-start | bytes 98312 | tf_op jit(solution)/shard_map/cond/branch_2_fun/ppermute | solution.py:22
  29.8 20.5 %collective-permute-start.31 = (f32[1,2,8,512]{3,2,1,0:T(8,128)S(1)}, f32[1,2,8,512]{3,2,1,0:T(8,128)S(1)}, u32[]{:S(2)}, u32[]{:S(2)}) collective-permute-start(f32[1,2,8,512]{3,2,1,0:T(8,128)S(1)} %get-tuple-element.117), channel_id=1, source_target_pairs={{0,15},{1,0},{2,1},{3,2},{4,3},{5,4},{6,5},{7,6},{8,7},{9,8},{10,9... | collective-permute-start | bytes 98312 | tf_op jit(solution)/shard_map/cond/branch_2_fun/ppermute | solution.py:22
  38.6 9.6 %collective-permute-start.34 = (f32[1,2,8,512]{3,2,1,0:T(8,128)S(1)}, f32[1,2,8,512]{3,2,1,0:T(8,128)S(1)}, u32[]{:S(2)}, u32[]{:S(2)}) collective-permute-start(f32[1,2,8,512]{3,2,1,0:T(8,128)S(1)} %get-tuple-element.120), channel_id=1, source_target_pairs={{0,15},{1,0},{2,1},{3,2},{4,3},{5,4},{6,5},{7,6},{8,7},{9,8},{10,9... | collective-permute-start | bytes 98312 | tf_op jit(solution)/shard_map/cond/branch_2_fun/ppermute | solution.py:22
  44.1 9.6 %copy-start.5 = (f32[4,3,16,4096]{3,2,1,0:T(8,128)S(1)}, f32[4,3,16,4096]{3,2,1,0:T(8,128)}, u32[]{:S(2)}) copy-start(f32[4,3,16,4096]{3,2,1,0:T(8,128)} %get-tuple-element.108.digits) | copy-start | bytes 9437188 | tf_op jit(solution)/shard_map/cond
  45.2 7.1 %collective-permute-start.27 = (f32[1,2,8,512]{3,2,1,0:T(8,128)S(1)}, f32[1,2,8,512]{3,2,1,0:T(8,128)S(1)}, u32[]{:S(2)}, u32[]{:S(2)}) collective-permute-start(f32[1,2,8,512]{3,2,1,0:T(8,128)S(1)} %get-tuple-element.111), channel_id=1, source_target_pairs={{0,15},{1,0},{2,1},{3,2},{4,3},{5,4},{6,5},{7,6},{8,7},{9,8},{10,9... | collective-permute-start | bytes 98312 | tf_op jit(solution)/shard_map/cond/branch_2_fun/ppermute | solution.py:22
  48.2 17.5 %collective-permute-start.38 = (f32[1,2,8,4096]{3,2,1,0:T(8,128)S(1)}, f32[1,2,8,4096]{3,2,1,0:T(8,128)S(1)}, u32[]{:S(2)}, u32[]{:S(2)}) collective-permute-start(f32[1,2,8,4096]{3,2,1,0:T(8,128)S(1)} %add_tail.29), channel_id=1, source_target_pairs={{16,0},{0,16},{17,1},{1,17},{18,2},{2,18},{19,3},{3,19},{20,4},{4,... | collective-permute-start | bytes 786440 | tf_op jit(solution)/shard_map/cond/branch_2_fun/ppermute | solution.py:342
  48.3 18.8 %collective-permute-start.35 = (f32[1,2,8,4096]{3,2,1,0:T(8,128)S(1)}, f32[1,2,8,4096]{3,2,1,0:T(8,128)S(1)}, u32[]{:S(2)}, u32[]{:S(2)}) collective-permute-start(f32[1,2,8,4096]{3,2,1,0:T(8,128)S(1)} %add_tail.28), channel_id=1, source_target_pairs={{16,0},{0,16},{17,1},{1,17},{18,2},{2,18},{19,3},{3,19},{20,4},{4,... | collective-permute-start | bytes 786440 | tf_op jit(solution)/shard_map/cond/branch_2_fun/ppermute | solution.py:342
  50.4 18.2 %collective-permute-start.32 = (f32[1,2,8,4096]{3,2,1,0:T(8,128)S(1)}, f32[1,2,8,4096]{3,2,1,0:T(8,128)S(1)}, u32[]{:S(2)}, u32[]{:S(2)}) collective-permute-start(f32[1,2,8,4096]{3,2,1,0:T(8,128)S(1)} %add_tail.27), channel_id=1, source_target_pairs={{0,16},{1,17},{2,18},{3,19},{4,20},{5,21},{6,22},{7,23},{8,24},{9,... | collective-permute-start | bytes 786440 | tf_op jit(solution)/shard_map/cond/branch_2_fun/ppermute | solution.py:342
  52.3 17.6 %collective-permute-start.28 = (f32[1,2,8,4096]{3,2,1,0:T(8,128)S(1)}, f32[1,2,8,4096]{3,2,1,0:T(8,128)S(1)}, u32[]{:S(2)}, u32[]{:S(2)}) collective-permute-start(f32[1,2,8,4096]{3,2,1,0:T(8,128)S(1)} %add_tail.25), channel_id=1, source_target_pairs={{0,16},{1,17},{2,18},{3,19},{4,20},{5,21},{6,22},{7,23},{8,24},{9,... | collective-permute-start | bytes 786440 | tf_op jit(solution)/shard_map/cond/branch_2_fun/ppermute | solution.py:342
  56.0 4.4 %collective-permute-start.29 = (f32[2,2,16,512]{3,2,1,0:T(8,128)S(1)}, f32[2,2,16,512]{3,2,1,0:T(8,128)S(1)}, u32[]{:S(2)}, u32[]{:S(2)}) collective-permute-start(f32[2,2,16,512]{3,2,1,0:T(8,128)S(1)} %get-tuple-element.113), channel_id=1, source_target_pairs={{0,15},{1,0},{2,1},{3,2},{4,3},{5,4},{6,5},{7,6},{8,7},{9,8},{10,9... | collective-permute-start | bytes 393224 | tf_op jit(solution)/shard_map/cond/branch_2_fun/ppermute | solution.py:22

commit v4 on v3

v4 whole, which is shorter than its diff:
```python
import functools

import jax
import jax.numpy as jnp
from jax import lax
from jax.experimental import pallas as pl
from jax.experimental.pallas import tpu as pltpu
from jax.sharding import PartitionSpec as P

RMAX = 256
CAP = 2
WIDEST = 2 * RMAX
LANES = 128
ROWS = 8
SMEM = pl.BlockSpec(memory_space=pltpu.SMEM)
VMEM = pl.BlockSpec(memory_space=pltpu.VMEM)


def shifted(value, axis, steps):
    count = lax.axis_size(axis)
    pairs = [(source, (source + steps) % count) for source in range(count)]
    return lax.ppermute(value, axis, pairs)


def slot_ciphers(requests, ciphers, key_count, owner):
    needed = []
    for cipher in range(ciphers):
        flag = requests[cipher, owner * key_count]
        for key in range(1, key_count):
            flag = flag | requests[cipher, owner * key_count + key]
        needed.append(flag)
    return ranked(needed)


def ranked(needed):
    slots = [jnp.int32(0)] * CAP
    rank = jnp.int32(0)
    for want in (1, 0):
        for cipher in range(len(needed)):
            here = needed[cipher] == want
            for slot in range(CAP):
                slots[slot] = jnp.where(here & (rank == slot), cipher, slots[slot])
            rank = rank + here.astype(jnp.int32)
    return slots


def group_after(steps, groups):
    return lax.rem(lax.axis_index("grp") + steps, groups)


def gather_kernel(wanted, cuts, steps, groups, requests, digits, *refs):
    outs, sems = refs[: len(wanted)], refs[len(wanted)]
    ciphers, parts, _, columns = digits.shape
    chosen = slot_ciphers(requests, ciphers, requests.shape[1] // groups, group_after(steps, groups))
    width = columns // cuts
    loads = []
    for out, (slot, block) in zip(outs, wanted):
        for part in range(parts):
            for cut in range(cuts):
                at = pl.ds(cut * width, width)
                source = digits.at[chosen[slot], part, pl.ds(block * ROWS, ROWS), at]
                loads.append(pltpu.make_async_copy(source, out.at[part, :, at], sems.at[len(loads)]))
    for load in loads:
        load.start()
    for load in loads:
        load.wait()


def gather(digits, requests, steps, wanted, cuts=1):
    parts, _, columns = digits.shape[1:]
    return pl.pallas_call(
        functools.partial(gather_kernel, wanted, cuts, steps, lax.axis_size("grp")),
        out_shape=[jax.ShapeDtypeStruct((parts, ROWS, columns), jnp.float32)] * len(wanted),
        in_specs=[SMEM, pl.BlockSpec(memory_space=pltpu.HBM)],
        out_specs=[VMEM] * len(wanted),
        scratch_shapes=[pltpu.SemaphoreType.DMA((cuts * parts * len(wanted),))],
        compiler_params=pltpu.CompilerParams(vmem_limit_bytes=4 << 20),
        cost_estimate=pl.CostEstimate(
            flops=0, transcendentals=0, bytes_accessed=8 * len(wanted) * parts * ROWS * columns
        ),
        name="gather_digits",
    )(requests, pltpu.with_memory_space_constraint(digits, pltpu.HBM))


def products_kernel(slots, blocks, local, requests, rotations, digits, keys, modulus_ref, tail, resident, rolled):
    key_count, parts, polys, _, columns = keys.shape
    ciphers = requests.shape[0]
    pad = WIDEST // LANES
    tiles = columns // LANES
    tail[...] = jnp.zeros_like(tail)
    resident[...] = jnp.zeros_like(resident)
    rolled[...] = jnp.zeros_like(rolled)
    lane = lax.broadcasted_iota(jnp.int32, (ROWS, LANES), 1)
    me = lax.axis_index("grp")
    chosen = slot_ciphers(requests, ciphers, key_count, me)

    def add_key(step, carry):
        block = step // key_count
        key = step - block * key_count
        rows = pl.ds(pl.multiple_of(block * ROWS, ROWS), ROWS)
        limbs = pl.ds(pl.multiple_of((blocks[0] + block) * ROWS, ROWS), ROWS)
        amount = 2 * rotations[me * key_count + key]
        skipped = amount // LANES
        within = amount - skipped * LANES
        turn = lax.rem(LANES - within, LANES)
        from_this = lane < LANES - within
        modulus = modulus_ref[limbs, :]
        inverse = 1.0 / modulus
        for place, slot in enumerate(slots):
            source = chosen[slot] if local else place

            @pl.when(requests[chosen[slot], me * key_count + key] > 0)
            def _():
                for poly in range(polys):
                    for tile in range(tiles):
                        at = pl.ds(tile * LANES, LANES)
                        combined = digits[source, 0, rows, at] * keys[key, 0, poly, limbs, at]
                        for part in range(1, parts):
                            combined = combined + digits[source, part, rows, at] * keys[key, part, poly, limbs, at]
                        quotient = jnp.floor(combined * inverse)
                        remainder = combined - quotient * modulus
                        rolled[:, pl.ds((pad + tile) * LANES, LANES)] = pltpu.roll(remainder, turn, 1)
                    for tile in range(pad + tiles):
                        start = pl.multiple_of((skipped + tile) * LANES, LANES)
                        after = pl.multiple_of((skipped + tile + 1) * LANES, LANES)
                        moved = jnp.where(from_this, rolled[:, pl.ds(start, LANES)], rolled[:, pl.ds(after, LANES)])
                        if tile < pad:
                            at = pl.ds(tile * LANES, LANES)
                            tail[place, poly, rows, at] = tail[place, poly, rows, at] + moved
                        else:
                            at = pl.ds((tile - pad) * LANES, LANES)
                            resident[place, poly, rows, at] = resident[place, poly, rows, at] + moved
        return carry

    lax.fori_loop(0, len(blocks) * key_count, add_key, 0)


def products(digits, keys, requests, rotations, modulus, slots, blocks, local):
    key_count, parts, polys, _, columns = keys.shape
    count = len(slots)
    limbs = len(blocks) * ROWS
    pad = WIDEST // LANES
    work = count * key_count * polys * limbs * columns
    return pl.pallas_call(
        functools.partial(products_kernel, slots, blocks, local),
        out_shape=[
            jax.ShapeDtypeStruct((count, polys, limbs, WIDEST), jnp.float32),
            jax.ShapeDtypeStruct((count, polys, limbs, columns), jnp.float32),
        ],
        in_specs=[SMEM, SMEM, VMEM, VMEM, VMEM],
        out_specs=[VMEM, VMEM],
        scratch_shapes=[pltpu.VMEM((ROWS, columns + 2 * pad * LANES + LANES), jnp.float32)],
        compiler_params=pltpu.CompilerParams(vmem_limit_bytes=20 << 20),
        cost_estimate=pl.CostEstimate(
            flops=20 * work, transcendentals=0, bytes_accessed=4 * (key_count * parts * polys * limbs * columns + count * limbs * columns * (parts + polys))
        ),
        name="products",
    )(requests, rotations, digits, keys, modulus)


def add_tail_kernel(arrived, held, out):
    columns = held.shape[-1]
    at = pl.ds(columns - WIDEST, WIDEST)
    out[:, :, :, at] = held[:, :, :, at] + arrived[...]


def add_tail(resident, arrived):
    return pl.pallas_call(
        add_tail_kernel,
        out_shape=jax.ShapeDtypeStruct(resident.shape, jnp.float32),
        in_specs=[VMEM, VMEM],
        out_specs=VMEM,
        input_output_aliases={1: 0},
        compiler_params=pltpu.CompilerParams(vmem_limit_bytes=8 << 20),
        name="add_tail",
    )(arrived, resident)


def reduce_mod(amount, modulus):
    quotient = jnp.floor(amount * (1.0 / modulus))
    remainder = amount - quotient * modulus
    remainder = jnp.where(remainder < 0, remainder + modulus, remainder)
    return jnp.where(remainder >= modulus, remainder - modulus, remainder)


def sums_kernel(owners, groups, ciphers, key_count, keep, requests, modulus, *refs):
    parts = refs[: len(owners)]
    out = refs[len(owners)]
    cipher = pl.program_id(1)
    out[...] = jnp.zeros_like(out)
    for part, (steps, slots) in zip(parts, owners):
        chosen = slot_ciphers(requests, ciphers, key_count, group_after(steps, groups))
        for place, slot in enumerate(slots):

            @pl.when(chosen[slot] == cipher)
            def _():
                out[...] = out[...] + part[place]

    if keep:
        held = refs[len(owners) + 1]
        chosen = slot_ciphers(requests, ciphers, key_count, group_after(groups - 1, groups))
        for slot in range(CAP):

            @pl.when(chosen[slot] == cipher)
            def _():
                held[slot] = out[...]

    wide = modulus[:, :1]
    out[...] = reduce_mod(out[...], wide) / wide


def sums(parts, owners, requests, modulus, ciphers, keep):
    polys, limbs, columns = parts[0].shape[1:]
    groups = lax.axis_size("grp")
    key_count = requests.shape[1] // groups
    shapes = [jax.ShapeDtypeStruct((ciphers, polys, limbs, columns), jnp.float32)]
    specs = [pl.BlockSpec((pl.Squeezed(), polys, ROWS, columns), lambda block, cipher, *_: (cipher, 0, block, 0))]
    if keep:
        shapes.append(jax.ShapeDtypeStruct((CAP, polys, limbs, columns), jnp.float32))
        specs.append(pl.BlockSpec((CAP, polys, ROWS, columns), lambda block, cipher, *_: (0, 0, block, 0)))
    return pl.pallas_call(
        functools.partial(sums_kernel, owners, groups, ciphers, key_count, keep),
        out_shape=shapes,
        grid_spec=pltpu.PrefetchScalarGridSpec(
            num_scalar_prefetch=1,
            grid=(limbs // ROWS, ciphers),
            in_specs=[pl.BlockSpec((ROWS, LANES), lambda block, cipher, *_: (block, 0))]
            + [
                pl.BlockSpec((part.shape[0], polys, ROWS, columns), lambda block, cipher, *_: (0, 0, block, 0))
                for part in parts
            ],
            out_specs=specs,
        ),
        compiler_params=pltpu.CompilerParams(
            dimension_semantics=("arbitrary", "arbitrary"), vmem_limit_bytes=24 << 20
        ),
        cost_estimate=pl.CostEstimate(
            flops=20 * ciphers * polys * limbs * columns,
            transcendentals=0,
            bytes_accessed=4 * (ciphers + 2 + 2 * len(parts)) * polys * limbs * columns,
        ),
        name="sums",
    )(requests, modulus, *parts)


def finish_kernel(slot, block, groups, requests, modulus, part, held, before, out, done, sems):
    ciphers, polys, _, _ = out.shape
    key_count = requests.shape[1] // groups
    rows = pl.ds(block * ROWS, ROWS)
    wide = modulus[rows, :1]
    for poly in range(polys):
        done[poly] = reduce_mod(held[slot, poly, rows, :] + part[0, poly], wide) / wide
    asks = requests[...]
    column = lax.broadcasted_iota(jnp.int32, asks.shape, 1) // key_count
    row = lax.broadcasted_iota(jnp.int32, asks.shape, 0)
    asks = jnp.where(column == group_after(groups - 1, groups), asks, 0)
    needed = [jnp.max(jnp.where(row == cipher, asks, 0)) for cipher in range(ciphers)]
    cipher = ranked(needed)[slot]
    stores = [
        pltpu.make_async_copy(done.at[poly], out.at[cipher, poly, rows], sems.at[poly]) for poly in range(polys)
    ]
    for store in stores:
        store.start()
    for store in stores:
        store.wait()


def finish(part, held, result, requests, modulus, slot, block):
    _, polys, _, columns = result.shape
    groups = lax.axis_size("grp")
    hbm = pl.BlockSpec(memory_space=pltpu.HBM)
    return pl.pallas_call(
        functools.partial(finish_kernel, slot, block, groups),
        out_shape=jax.ShapeDtypeStruct(result.shape, jnp.float32),
        in_specs=[VMEM, VMEM, VMEM, VMEM, hbm],
        out_specs=hbm,
        scratch_shapes=[pltpu.VMEM((polys, ROWS, columns), jnp.float32), pltpu.SemaphoreType.DMA((polys,))],
        input_output_aliases={4: 0},
        compiler_params=pltpu.CompilerParams(vmem_limit_bytes=8 << 20),
        cost_estimate=pl.CostEstimate(
            flops=20 * polys * ROWS * columns, transcendentals=0, bytes_accessed=12 * polys * ROWS * columns
        ),
        name="finish",
    )(requests, modulus, part, held, result)


def per_device(digits, keys, requests, rotations, moduli):
    modulus = jnp.broadcast_to(moduli.astype(jnp.float32)[:, None], (digits.shape[2], LANES))
    way = key_switch_pair if lax.axis_size("grp") == 2 else key_switch_any
    return way(digits, keys, requests, rotations, modulus)


def key_switch_any(digits, keys, requests, rotations, modulus):
    groups = lax.axis_size("grp")
    blocks = tuple(range(digits.shape[2] // ROWS))
    slots = tuple(range(CAP))
    tail, resident = products(digits, keys, requests, rotations, modulus, slots, blocks, True)
    parts = [add_tail(resident, shifted(tail, "limb", -1))]
    owners = [(0, slots)]
    for steps in range(1, groups):
        asked = shifted(requests, "grp", steps)
        for slot in slots:
            picked = gather(digits, requests, steps, tuple((slot, block) for block in blocks))
            back = []
            for block in blocks:
                arrived = shifted(picked[block], "grp", steps)
                tail, resident = products(
                    arrived[None], keys, asked, rotations, modulus, (slot,), (block,), False
                )
                back.append(shifted(add_tail(resident, shifted(tail, "limb", -1)), "grp", -steps))
            parts.append(jnp.concatenate(back, axis=2))
            owners.append((steps, (slot,)))
    return sums(parts, tuple(owners), requests, modulus, digits.shape[0], False)[0]


def key_switch_pair(digits, keys, requests, rotations, modulus):
    blocks = tuple(range(digits.shape[2] // ROWS))
    slots = tuple(range(CAP))
    key_count = keys.shape[0]
    both = [(0, 1), (1, 0)]
    turns = [(slot, block) for slot in slots for block in blocks]
    picked = {turns[0]: gather(digits, requests, 1, (turns[0],), 4)[0]}
    picked.update(zip(turns[1:], gather(digits, requests, 1, tuple(turns[1:]))))
    sent = {}
    for block in blocks:
        sent[0, block] = lax.ppermute(picked[0, block], "grp", both)
    asked = shifted(requests, "grp", 1)
    tail, resident = products(digits, keys, requests, rotations, modulus, slots, blocks, True)
    arrived = shifted(tail, "limb", -1)
    local = add_tail(resident, arrived)
    me = lax.axis_index("grp")
    rightward = jnp.where(me == 0, requests, asked)[:, key_count:]
    leftward = jnp.where(me == 0, asked, requests)[:, :key_count]
    two_right = jnp.sum(jnp.max(rightward, axis=1)) > 1
    two_left = jnp.sum(jnp.max(leftward, axis=1)) > 1
    case = jnp.where(two_right == two_left, 0, jnp.where(two_right, 1, 2))
    ahead = remote(sent[0, 0], keys, asked, rotations, modulus, 0, 0)

    def branch(pairs):
        def run(*operands):
            return exchange((both, pairs), *operands)

        return run

    branches = [branch(pairs) for pairs in (both, [(0, 1)], [(1, 0)])]
    operands = (ahead, [picked[turn] for turn in turns[len(blocks) :]], [sent[0, block] for block in blocks[1:]], local)
    return lax.switch(case, branches, *operands, keys, requests, asked, rotations, modulus)


def remote(arrived, keys, asked, rotations, modulus, slot, block):
    tail, resident = products(arrived[None], keys, asked, rotations, modulus, (slot,), (block,), False)
    wrapped = shifted(tail, "limb", -1)
    return add_tail(resident, wrapped)


def exchange(pairs, ahead, picked, arrived, local, keys, requests, asked, rotations, modulus):
    ciphers = requests.shape[0]
    blocks = local.shape[2] // ROWS
    turns = [(slot, block) for slot in range(CAP) for block in range(blocks)]
    sent = dict(zip(turns[1:blocks], arrived))
    for (slot, block), piece in zip(turns[blocks:], picked):
        sent[slot, block] = lax.ppermute(piece, "grp", pairs[slot])
    result, held = sums([local], ((0, tuple(range(CAP))),), requests, modulus, ciphers, True)
    back = {}
    for turn in turns:
        slot, block = turn
        whole = ahead if turn == turns[0] else remote(sent[turn], keys, asked, rotations, modulus, slot, block)
        back[turn] = lax.ppermute(whole, "grp", [(target, source) for source, target in pairs[slot]])
    for slot, block in turns:
        result = finish(back[slot, block], held, result, requests, modulus, slot, block)
    return result


def solution(mesh):
    in_specs = (
        P("grp", None, None, "limb"),
        P("grp", None, None, None, "limb"),
        P("grp", None),
        P(),
        P(),
    )
    out_specs = P("grp", None, None, "limb")
    return jax.shard_map(
        per_device, mesh=mesh, in_specs=in_specs, out_specs=out_specs, check_vma=False
    )
```

time: 71.6 us -> 77.3 us (1.080)
  starting transfers between devices: 24.4 us -> 30 us
  Pallas kernels: 24.8 us -> 28.5 us
  waiting for transfers between devices: 18.5 us -> 15.2 us
    ppermute x4, waiting for transfers between devices: 15.9 us -> 5.21 us  [the longest x2 5.21 us: exchange(): sent[slot, block] = lax.ppermute(piece, 'grp', pairs[slot])]
    ppermute x6, starting transfers between devices: 12.3 us -> 18.7 us  [shifted(): return lax.ppermute(value, axis, pairs)]
    ppermute x4, waiting for transfers between devices: 0.01 us -> 5.09 us  [exchange(): lax.ppermute(whole, 'grp', [(target, source) for source, target in pairs[...]
    pallas_call x5, Pallas kernels: 10.1 us -> 14.5 us  [products(): pl.pallas_call(functools.partial(products_kernel, slots, blocks, local),...]
    ppermute x6, waiting for transfers between devices: 2.53 us -> 4.93 us  [shifted(): return lax.ppermute(value, axis, pairs)]
  transfers between devices with their start and end apart: 14 -> 14, of which waited for: 5 -> 6; matrix products, arithmetic and copies ran while one was open for 1% -> 2% of each run, Pallas kernels for 33% -> 33%
where the time goes in v4:
time: 77.3 us; the launch traced here: 76.9 us
  starting transfers between devices  30 us (39%)
  Pallas kernels  28.5 us (37%)
  waiting for transfers between devices  15.2 us (20%)
  other arithmetic  1.47 us (2%)
  between operations  1.39 us (2%)
    ppermute x6, starting transfers between devices, shifted(): return lax.ppermute(value, axis, pairs)  18.7 us
    pallas_call x5, Pallas kernels, products(): pl.pallas_call(functools.partial(products_kernel, slots, blocks, local),...  14.5 us
    ppermute x4, starting transfers between devices, exchange(): lax.ppermute(whole, 'grp', [(target, source) for source, target in pairs[...  5.34 us
    pallas_call x1, Pallas kernels, sums(): pl.pallas_call(functools.partial(sums_kernel, owners, groups, ciphers, ke...  5.26 us
    ppermute x2, waiting for transfers between devices, exchange(): sent[slot, block] = lax.ppermute(piece, 'grp', pairs[slot])  5.21 us
    ppermute x4, waiting for transfers between devices, exchange(): lax.ppermute(whole, 'grp', [(target, source) for source, target in pairs[...  5.09 us
    ppermute x6, waiting for transfers between devices, shifted(): return lax.ppermute(value, axis, pairs)  4.93 us
    pallas_call x2, Pallas kernels, gather(): pl.pallas_call(functools.partial(gather_kernel, wanted, cuts, steps, lax....  4.66 us
  transfers between devices with their start and end apart: 14, of which 6 were waited for; matrix products, arithmetic and copies ran while one was open for 2% of the time, Pallas kernels for 33%

profile of v4, /device:TPU:0, one launch (start us, length us, event | category | flops | bytes accessed | tf_op | source)
XLA Modules:
  0.0 76.9 jit_solution(15507869034606452852)
XLA Ops:
  0.0 0.0 copy-start.4
  0.0 1.9 %gather_digits.3 = f32[3,8,4096]{2,1,0:T(8,128)S(1)} custom-call(s32[4,8]{1,0:T(4,128)} %requests.5, f32[4,3,16,4096]{3,2,1,0:T(8,128)} %digits.5), custom_call_target="tpu_custom_call" | custom-call | bytes 786432 | tf_op jit(solution)/shard_map/gather_digits/pallas_call | solution.py:71
  1.9 0.0 copy-start.6
  1.9 0.0 copy-start
  1.9 0.0 copy-start.5
  2.0 3.0 %collective-permute-start.30 = (f32[3,8,4096]{2,1,0:T(8,128)S(1)}, f32[3,8,4096]{2,1,0:T(8,128)S(1)}, u32[]{:S(2)}, u32[]{:S(2)}) collective-permute-start(f32[3,8,4096]{2,1,0:T(8,128)S(1)} %gather_digits.3), channel_id=1, source_target_pairs={{0,16},{16,0},{1,17},{17,1},{2,18},{18,2},{3,19},{19,3},{4,20},{20... | collective-permute-start | bytes 1179656 | tf_op jit(solution)/shard_map/ppermute | solution.py:326
  5.0 0.0 copy-done.4
  5.0 2.8 %gather_digits.2 = (f32[3,8,4096]{2,1,0:T(8,128)S(1)}, f32[3,8,4096]{2,1,0:T(8,128)S(1)}, f32[3,8,4096]{2,1,0:T(8,128)}) custom-call(s32[4,8]{1,0:T(4,128)S(1)} %copy-done.4, f32[4,3,16,4096]{3,2,1,0:T(8,128)} %digits.5), custom_call_target="tpu_custom_call" | custom-call | bytes 2359296 | tf_op jit(solution)/shard_map/gather_digits/pallas_call | solution.py:71
  7.8 0.3 collective-permute-start.29
  8.1 1.8 %collective-permute-start.27 = (s32[4,8]{1,0:T(4,128)S(1)}, s32[4,8]{1,0:T(4,128)S(1)}, u32[]{:S(2)}, u32[]{:S(2)}) collective-permute-start(s32[4,8]{1,0:T(4,128)S(1)} %copy-done.4), channel_id=1, source_target_pairs={{0,16},{16,0},{1,17},{17,1},{2,18},{18,2},{3,19},{19,3},{4,20},{20... | collective-permute-start | bytes 392 | tf_op jit(solution)/shard_map/ppermute | solution.py:22
  9.8 0.0 copy-done.6
  9.9 0.1 broadcast_in_dim.36.modulus_ref
  9.9 0.0 copy-done
  9.9 0.0 copy-done.5
  9.9 4.5 %products.20 = (f32[2,2,16,512]{3,2,1,0:T(8,128)S(1)}, f32[2,2,16,4096]{3,2,1,0:T(8,128)S(1)}) custom-call(s32[4,8]{1,0:T(4,128)S(1)} %copy-done.4, s32[8]{0:T(128)S(1)} %copy-done.5, f32[4,3,16,4096]{3,2,1,0:T(8,128)S(1)} %copy-done, f32[4,3,2,16,4096]{4,3,2,1,0:T(8,128)} %keys.3, f32[16,128]{1,0:T(8,128)S(1)} %broadcast_in_dim.36.modulus_ref), custom_call_target="tpu_custom_call" | custom-call | flops 20971520 | bytes 8912896 | tf_op jit(solution)/shard_map/products/pallas_call | solution.py:144
  14.4 3.2 %collective-permute-start.28 = (f32[2,2,16,512]{3,2,1,0:T(8,128)S(1)}, f32[2,2,16,512]{3,2,1,0:T(8,128)S(1)}, u32[]{:S(2)}, u32[]{:S(2)}) collective-permute-start(f32[2,2,16,512]{3,2,1,0:T(8,128)S(1)} %get-tuple-element.131), channel_id=1, source_target_pairs={{0,15},{1,0},{2,1},{3,2},{4,3},{5,4},{6,5},{7,6},{8,7},{9,8},{10,9... | collective-permute-start | bytes 393224 | tf_op jit(solution)/shard_map/ppermute | solution.py:22
  17.7 4.9 %collective-permute-done.27.requests = s32[4,8]{1,0:T(4,128)S(1)} collective-permute-done((s32[4,8]{1,0:T(4,128)S(1)}, s32[4,8]{1,0:T(4,128)S(1)}, u32[]{:S(2)}, u32[]{:S(2)}) %collective-permute-start.27) | collective-permute-done | bytes 160 | tf_op jit(solution)/shard_map/ppermute | solution.py:22
  22.6 0.0 collective-permute-done.30
  22.6 3.8 %products.21 = (f32[1,2,8,512]{3,2,1,0:T(8,128)S(1)}, f32[1,2,8,4096]{3,2,1,0:T(8,128)S(1)}) custom-call(s32[4,8]{1,0:T(4,128)S(1)} %collective-permute-done.27.requests, s32[8]{0:T(128)S(1)} %copy-done.5, f32[1,3,8,4096]{3,2,1,0:T(8,128)S(1)} %bitcast.10, f32[4,3,2,16,4096]{4,3,2,1,0:T(8,128)} %keys.3, f32[16,128]{1,0:T(8,128)S(1)} %broadcast_in_dim.36.modulus_ref), custom_call_target="tpu_custom_call" | custom-call | flops 5242880 | bytes 3801088 | tf_op jit(solution)/shard_map/products/pallas_call | solution.py:144
  26.4 3.4 %collective-permute-start.31 = (f32[1,2,8,512]{3,2,1,0:T(8,128)S(1)}, f32[1,2,8,512]{3,2,1,0:T(8,128)S(1)}, u32[]{:S(2)}, u32[]{:S(2)}) collective-permute-start(f32[1,2,8,512]{3,2,1,0:T(8,128)S(1)} %get-tuple-element.135), channel_id=1, source_target_pairs={{0,15},{1,0},{2,1},{3,2},{4,3},{5,4},{6,5},{7,6},{8,7},{9,8},{10,9... | collective-permute-start | bytes 98312 | tf_op jit(solution)/shard_map/ppermute | solution.py:22
  29.8 0.2 slice_reduce_fusion
  30.0 0.6 reduce_sum.18
  30.6 0.6 reduce_sum.19
  32.6 0.0 collective-permute-done.28.arrived
  32.6 0.0 collective-permute-done.31.arrived
  32.6 0.0 collective-permute-done.29
  32.7 44.2 %conditional.1 = (f32[4,2,16,4096]{3,2,1,0:T(8,128)}) conditional(s32[]{:T(128)} %clamp.3, (f32[3,8,4096]{2,1,0:T(8,128)}, s32[4,8]{1,0:T(4,128)S(1)}, s32[8]{0:T(128)S(1)}, f32[4,3,2,16,4096]{4,3,2,1,0:T(8,128)}, f32[16,128]{1,0:T(8,128)S(1)}, /*index=5*/s32[4,8]{1,0:T(4,128)S(1)}, f32[2,2,16,4096]{3,2,1,0:T(8,128)S(1)}, ...), branch_computations={%region_4.5_spmd, %region_5.6_spmd, %region_6.7_spmd} | conditional | flops 31457280 | bytes 51642764 | solution.py:347
  32.7 1.3 %collective-permute-start.21 = (f32[3,8,4096]{2,1,0:T(8,128)S(1)}, f32[3,8,4096]{2,1,0:T(8,128)S(1)}, u32[]{:S(2)}, u32[]{:S(2)}) collective-permute-start(f32[3,8,4096]{2,1,0:T(8,128)S(1)} %get-tuple-element.115), channel_id=1, source_target_pairs={{16,0},{17,1},{18,2},{19,3},{20,4},{21,5},{22,6},{23,7},{24,8},{25... | collective-permute-start | bytes 1179656 | tf_op jit(solution)/shard_map/cond/branch_2_fun/ppermute | solution.py:362
  34.0 1.3 %collective-permute-start.18 = (f32[3,8,4096]{2,1,0:T(8,128)}, f32[3,8,4096]{2,1,0:T(8,128)S(1)}, u32[]{:S(2)}, u32[]{:S(2)}) collective-permute-start(f32[3,8,4096]{2,1,0:T(8,128)} %get-tuple-element.109), channel_id=1, source_target_pairs={{16,0},{17,1},{18,2},{19,3},{20,4},{21,5},{22,6},{23,7},{24,8},{25... | collective-permute-start | bytes 1179656 | tf_op jit(solution)/shard_map/cond/branch_2_fun/ppermute | solution.py:362
  35.3 0.0 copy-start.3
  35.3 4.0 %products.19 = (f32[1,2,8,512]{3,2,1,0:T(8,128)S(1)}, f32[1,2,8,4096]{3,2,1,0:T(8,128)S(1)}) custom-call(s32[4,8]{1,0:T(4,128)S(1)} %get-tuple-element.107.requests, s32[8]{0:T(128)S(1)} %get-tuple-element.108.rotations, f32[1,3,8,4096]{3,2,1,0:T(8,128)S(1)} %bitcast.19, f32[4,3,2,16,4096]{4,3,2,1,0:T(8,128)} %get-tuple-element.110.keys, ...), custom_call_target="tpu_custom_call" | custom-call | flops 5242880 | bytes 3801088 | tf_op jit(solution)/shard_map/cond/branch_2_fun/products/pallas_call | solution.py:144
  39.3 3.3 %collective-permute-start.24 = (f32[1,2,8,512]{3,2,1,0:T(8,128)S(1)}, f32[1,2,8,512]{3,2,1,0:T(8,128)S(1)}, u32[]{:S(2)}, u32[]{:S(2)}) collective-permute-start(f32[1,2,8,512]{3,2,1,0:T(8,128)S(1)} %get-tuple-element.119), channel_id=1, source_target_pairs={{0,15},{1,0},{2,1},{3,2},{4,3},{5,4},{6,5},{7,6},{8,7},{9,8},{10,9... | collective-permute-start | bytes 98312 | tf_op jit(solution)/shard_map/cond/branch_2_fun/ppermute | solution.py:22
  42.6 4.0 %collective-permute-done.21 = f32[3,8,4096]{2,1,0:T(8,128)S(1)} collective-permute-done((f32[3,8,4096]{2,1,0:T(8,128)S(1)}, f32[3,8,4096]{2,1,0:T(8,128)S(1)}, u32[]{:S(2)}, u32[]{:S(2)}) %collective-permute-start.21) | collective-permute-done | bytes 393248 | tf_op jit(solution)/shard_map/cond/branch_2_fun/ppermute | solution.py:362
  46.6 0.0 copy-done.3
  46.6 1.1 %products.18 = (f32[1,2,8,512]{3,2,1,0:T(8,128)S(1)}, f32[1,2,8,4096]{3,2,1,0:T(8,128)S(1)}) custom-call(s32[4,8]{1,0:T(4,128)S(1)} %get-tuple-element.107.requests, s32[8]{0:T(128)S(1)} %get-tuple-element.108.rotations, f32[1,3,8,4096]{3,2,1,0:T(8,128)S(1)} %bitcast.16, f32[4,3,2,16,4096]{4,3,2,1,0:T(8,128)S(1)} %copy-done.3, ...), custom_call_target="tpu_custom_call" | custom-call | flops 5242880 | bytes 3801088 | tf_op jit(solution)/shard_map/cond/branch_2_fun/products/pallas_call | solution.py:144
  47.7 2.4 %collective-permute-start.22 = (f32[1,2,8,512]{3,2,1,0:T(8,128)S(1)}, f32[1,2,8,512]{3,2,1,0:T(8,128)S(1)}, u32[]{:S(2)}, u32[]{:S(2)}) collective-permute-start(f32[1,2,8,512]{3,2,1,0:T(8,128)S(1)} %get-tuple-element.116), channel_id=1, source_target_pairs={{0,15},{1,0},{2,1},{3,2},{4,3},{5,4},{6,5},{7,6},{8,7},{9,8},{10,9... | collective-permute-start | bytes 98312 | tf_op jit(solution)/shard_map/cond/branch_2_fun/ppermute | solution.py:22
  50.1 1.2 %collective-permute-done.18 = f32[3,8,4096]{2,1,0:T(8,128)S(1)} collective-permute-done((f32[3,8,4096]{2,1,0:T(8,128)}, f32[3,8,4096]{2,1,0:T(8,128)S(1)}, u32[]{:S(2)}, u32[]{:S(2)}) %collective-permute-start.18) | collective-permute-done | bytes 393248 | tf_op jit(solution)/shard_map/cond/branch_2_fun/ppermute | solution.py:362
  51.3 1.1 %products.17 = (f32[1,2,8,512]{3,2,1,0:T(8,128)S(1)}, f32[1,2,8,4096]{3,2,1,0:T(8,128)S(1)}) custom-call(s32[4,8]{1,0:T(4,128)S(1)} %get-tuple-element.107.requests, s32[8]{0:T(128)S(1)} %get-tuple-element.108.rotations, f32[1,3,8,4096]{3,2,1,0:T(8,128)S(1)} %bitcast.13, f32[4,3,2,16,4096]{4,3,2,1,0:T(8,128)S(1)} %copy-done.3, ...), custom_call_target="tpu_custom_call" | custom-call | flops 5242880 | bytes 3801088 | tf_op jit(solution)/shard_map/cond/branch_2_fun/products/pallas_call | solution.py:144
  52.4 4.6 %collective-permute-start.19 = (f32[1,2,8,512]{3,2,1,0:T(8,128)S(1)}, f32[1,2,8,512]{3,2,1,0:T(8,128)S(1)}, u32[]{:S(2)}, u32[]{:S(2)}) collective-permute-start(f32[1,2,8,512]{3,2,1,0:T(8,128)S(1)} %get-tuple-element.111), channel_id=1, source_target_pairs={{0,15},{1,0},{2,1},{3,2},{4,3},{5,4},{6,5},{7,6},{8,7},{9,8},{10,9... | collective-permute-start | bytes 98312 | tf_op jit(solution)/shard_map/cond/branch_2_fun/ppermute | solution.py:22
  57.0 0.0 collective-permute-start.26
  57.0 0.0 collective-permute-done.24.arrived
  57.1 2.1 %collective-permute-start.25 = (f32[1,2,8,4096]{3,2,1,0:T(8,128)S(1)}, f32[1,2,8,4096]{3,2,1,0:T(8,128)S(1)}, u32[]{:S(2)}, u32[]{:S(2)}) collective-permute-start(f32[1,2,8,4096]{3,2,1,0:T(8,128)S(1)} %add_tail.19), channel_id=1, source_target_pairs={{16,0},{0,16},{17,1},{1,17},{18,2},{2,18},{19,3},{3,19},{20,4},{4,... | collective-permute-start | bytes 786440 | tf_op jit(solution)/shard_map/cond/branch_2_fun/ppermute | solution.py:368
  59.1 0.0 collective-permute-done.22.arrived
  59.2 1.9 %collective-permute-start.23 = (f32[1,2,8,4096]{3,2,1,0:T(8,128)S(1)}, f32[1,2,8,4096]{3,2,1,0:T(8,128)S(1)}, u32[]{:S(2)}, u32[]{:S(2)}) collective-permute-start(f32[1,2,8,4096]{3,2,1,0:T(8,128)S(1)} %add_tail.18), channel_id=1, source_target_pairs={{0,16},{1,17},{2,18},{3,19},{4,20},{5,21},{6,22},{7,23},{8,24},{9,... | collective-permute-start | bytes 786440 | tf_op jit(solution)/shard_map/cond/branch_2_fun/ppermute | solution.py:368
  61.1 0.0 collective-permute-done.19.arrived
  61.1 1.3 %collective-permute-start.20 = (f32[1,2,8,4096]{3,2,1,0:T(8,128)S(1)}, f32[1,2,8,4096]{3,2,1,0:T(8,128)S(1)}, u32[]{:S(2)}, u32[]{:S(2)}) collective-permute-start(f32[1,2,8,4096]{3,2,1,0:T(8,128)S(1)} %add_tail.17), channel_id=1, source_target_pairs={{0,16},{1,17},{2,18},{3,19},{4,20},{5,21},{6,22},{7,23},{8,24},{9,... | collective-permute-start | bytes 786440 | tf_op jit(solution)/shard_map/cond/branch_2_fun/ppermute | solution.py:368
  62.4 5.3 %sums.5 = (f32[4,2,16,4096]{3,2,1,0:T(8,128)}, f32[2,2,16,4096]{3,2,1,0:T(8,128)S(1)}) custom-call(s32[4,8]{1,0:T(4,128)S(1)} %get-tuple-element.105.requests, f32[16,128]{1,0:T(8,128)S(1)} %get-tuple-element.106.modulus_ref.modulus, f32[2,2,16,4096]{3,2,1,0:T(8,128)S(1)} %get-tuple-element.113.refs_0_), custom_call_target="tpu_custom_call" | custom-call | flops 10485760 | bytes 4194304 | tf_op jit(solution)/shard_map/cond/branch_2_fun/sums/pallas_call | solution.py:221
  67.7 0.0 collective-permute-done.26.part
  67.7 1.0 %finish.20.before = f32[4,2,16,4096]{3,2,1,0:T(8,128)} custom-call(s32[4,8]{1,0:T(4,128)S(1)} %get-tuple-element.105.requests, f32[16,128]{1,0:T(8,128)S(1)} %get-tuple-element.106.modulus_ref.modulus, f32[1,2,8,4096]{3,2,1,0:T(8,128)S(1)} %collective-permute-done.26.part, ...), custom_call_target="tpu_custom_call", output_to_operand_aliasing={{}: (4, {})} | custom-call | flops 1310720 | bytes 786432 | tf_op jit(solution)/shard_map/cond/branch_2_fun/finish/pallas_call | solution.py:272
  68.7 0.6 collective-permute-done.25.part
  69.4 1.0 %finish.21.before = f32[4,2,16,4096]{3,2,1,0:T(8,128)} custom-call(s32[4,8]{1,0:T(4,128)S(1)} %get-tuple-element.105.requests, f32[16,128]{1,0:T(8,128)S(1)} %get-tuple-element.106.modulus_ref.modulus, f32[1,2,8,4096]{3,2,1,0:T(8,128)S(1)} %collective-permute-done.25.part, ...), custom_call_target="tpu_custom_call", output_to_operand_aliasing={{}: (4, {})} | custom-call | flops 1310720 | bytes 786432 | tf_op jit(solution)/shard_map/cond/branch_2_fun/finish/pallas_call | solution.py:272
  70.4 2.7 %collective-permute-done.23.part = f32[1,2,8,4096]{3,2,1,0:T(8,128)S(1)} collective-permute-done((f32[1,2,8,4096]{3,2,1,0:T(8,128)S(1)}, f32[1,2,8,4096]{3,2,1,0:T(8,128)S(1)}, u32[]{:S(2)}, u32[]{:S(2)}) %collective-permute-start.23) | collective-permute-done | bytes 262176 | tf_op jit(solution)/shard_map/cond/branch_2_fun/ppermute | solution.py:368
  73.0 1.0 %finish.22.before = f32[4,2,16,4096]{3,2,1,0:T(8,128)} custom-call(s32[4,8]{1,0:T(4,128)S(1)} %get-tuple-element.105.requests, f32[16,128]{1,0:T(8,128)S(1)} %get-tuple-element.106.modulus_ref.modulus, f32[1,2,8,4096]{3,2,1,0:T(8,128)S(1)} %collective-permute-done.23.part, ...), custom_call_target="tpu_custom_call", output_to_operand_aliasing={{}: (4, {})} | custom-call | flops 1310720 | bytes 786432 | tf_op jit(solution)/shard_map/cond/branch_2_fun/finish/pallas_call | solution.py:272
  74.1 1.8 %collective-permute-done.20.part = f32[1,2,8,4096]{3,2,1,0:T(8,128)S(1)} collective-permute-done((f32[1,2,8,4096]{3,2,1,0:T(8,128)S(1)}, f32[1,2,8,4096]{3,2,1,0:T(8,128)S(1)}, u32[]{:S(2)}, u32[]{:S(2)}) %collective-permute-start.20) | collective-permute-done | bytes 262176 | tf_op jit(solution)/shard_map/cond/branch_2_fun/ppermute | solution.py:368
  75.9 1.0 %finish.23 = f32[4,2,16,4096]{3,2,1,0:T(8,128)} custom-call(s32[4,8]{1,0:T(4,128)S(1)} %get-tuple-element.105.requests, f32[16,128]{1,0:T(8,128)S(1)} %get-tuple-element.106.modulus_ref.modulus, f32[1,2,8,4096]{3,2,1,0:T(8,128)S(1)} %collective-permute-done.20.part, f32[2,2,16,4096]{3,2,1,0:T(8,128)S(1)} %get-tuple-element.114.held, ...), custom_call_target="tpu_custom_call", output_to_operand_aliasing={{}: (4, {})} | custom-call | flops 1310720 | bytes 786432 | tf_op jit(solution)/shard_map/cond/branch_2_fun/finish/pallas_call | solution.py:272
  (7 shorter events, 0.1 us)
Async XLA Ops:
  0.0 5.0 %copy-start.4 = (s32[4,8]{1,0:T(4,128)S(1)}, s32[4,8]{1,0:T(4,128)}, u32[]{:S(2)}) copy-start(s32[4,8]{1,0:T(4,128)} %requests.5) | copy-start | bytes 388
  1.9 7.9 %copy-start.6 = (s32[16]{0:T(128)S(1)}, s32[16]{0:T(128)}, u32[]{:S(2)}) copy-start(s32[16]{0:T(128)} %param.12) | copy-start | bytes 196
  1.9 8.0 %copy-start = (f32[4,3,16,4096]{3,2,1,0:T(8,128)S(1)}, f32[4,3,16,4096]{3,2,1,0:T(8,128)}, u32[]{:S(2)}) copy-start(f32[4,3,16,4096]{3,2,1,0:T(8,128)} %digits.5) | copy-start | bytes 9437188
  1.9 8.0 %copy-start.5 = (s32[8]{0:T(128)S(1)}, s32[8]{0:T(128)}, u32[]{:S(2)}) copy-start(s32[8]{0:T(128)} %rotations.3) | copy-start | bytes 100
  2.0 20.6 %collective-permute-start.30 = (f32[3,8,4096]{2,1,0:T(8,128)S(1)}, f32[3,8,4096]{2,1,0:T(8,128)S(1)}, u32[]{:S(2)}, u32[]{:S(2)}) collective-permute-start(f32[3,8,4096]{2,1,0:T(8,128)S(1)} %gather_digits.3), channel_id=1, source_target_pairs={{0,16},{16,0},{1,17},{17,1},{2,18},{18,2},{3,19},{19,3},{4,20},{20... | collective-permute-start | bytes 1179656 | tf_op jit(solution)/shard_map/ppermute | solution.py:326
  7.8 24.9 %collective-permute-start.29 = (f32[3,8,4096]{2,1,0:T(8,128)S(1)}, f32[3,8,4096]{2,1,0:T(8,128)S(1)}, u32[]{:S(2)}, u32[]{:S(2)}) collective-permute-start(f32[3,8,4096]{2,1,0:T(8,128)S(1)} %get-tuple-element.134), channel_id=1, source_target_pairs={{0,16},{16,0},{1,17},{17,1},{2,18},{18,2},{3,19},{19,3},{4,20},{20... | collective-permute-start | bytes 1179656 | tf_op jit(solution)/shard_map/ppermute | solution.py:326
  8.1 14.5 %collective-permute-start.27 = (s32[4,8]{1,0:T(4,128)S(1)}, s32[4,8]{1,0:T(4,128)S(1)}, u32[]{:S(2)}, u32[]{:S(2)}) collective-permute-start(s32[4,8]{1,0:T(4,128)S(1)} %copy-done.4), channel_id=1, source_target_pairs={{0,16},{16,0},{1,17},{17,1},{2,18},{18,2},{3,19},{19,3},{4,20},{20... | collective-permute-start | bytes 392 | tf_op jit(solution)/shard_map/ppermute | solution.py:22
  14.4 18.1 %collective-permute-start.28 = (f32[2,2,16,512]{3,2,1,0:T(8,128)S(1)}, f32[2,2,16,512]{3,2,1,0:T(8,128)S(1)}, u32[]{:S(2)}, u32[]{:S(2)}) collective-permute-start(f32[2,2,16,512]{3,2,1,0:T(8,128)S(1)} %get-tuple-element.131), channel_id=1, source_target_pairs={{0,15},{1,0},{2,1},{3,2},{4,3},{5,4},{6,5},{7,6},{8,7},{9,8},{10,9... | collective-permute-start | bytes 393224 | tf_op jit(solution)/shard_map/ppermute | solution.py:22
  26.4 6.2 %collective-permute-start.31 = (f32[1,2,8,512]{3,2,1,0:T(8,128)S(1)}, f32[1,2,8,512]{3,2,1,0:T(8,128)S(1)}, u32[]{:S(2)}, u32[]{:S(2)}) collective-permute-start(f32[1,2,8,512]{3,2,1,0:T(8,128)S(1)} %get-tuple-element.135), channel_id=1, source_target_pairs={{0,15},{1,0},{2,1},{3,2},{4,3},{5,4},{6,5},{7,6},{8,7},{9,8},{10,9... | collective-permute-start | bytes 98312 | tf_op jit(solution)/shard_map/ppermute | solution.py:22
  32.7 13.9 %collective-permute-start.21 = (f32[3,8,4096]{2,1,0:T(8,128)S(1)}, f32[3,8,4096]{2,1,0:T(8,128)S(1)}, u32[]{:S(2)}, u32[]{:S(2)}) collective-permute-start(f32[3,8,4096]{2,1,0:T(8,128)S(1)} %get-tuple-element.115), channel_id=1, source_target_pairs={{16,0},{17,1},{18,2},{19,3},{20,4},{21,5},{22,6},{23,7},{24,8},{25... | collective-permute-start | bytes 1179656 | tf_op jit(solution)/shard_map/cond/branch_2_fun/ppermute | solution.py:362
  34.0 17.3 %collective-permute-start.18 = (f32[3,8,4096]{2,1,0:T(8,128)}, f32[3,8,4096]{2,1,0:T(8,128)S(1)}, u32[]{:S(2)}, u32[]{:S(2)}) collective-permute-start(f32[3,8,4096]{2,1,0:T(8,128)} %get-tuple-element.109), channel_id=1, source_target_pairs={{16,0},{17,1},{18,2},{19,3},{20,4},{21,5},{22,6},{23,7},{24,8},{25... | collective-permute-start | bytes 1179656 | tf_op jit(solution)/shard_map/cond/branch_2_fun/ppermute | solution.py:362
  35.3 11.3 %copy-start.3 = (f32[4,3,2,16,4096]{4,3,2,1,0:T(8,128)S(1)}, f32[4,3,2,16,4096]{4,3,2,1,0:T(8,128)}, u32[]{:S(2)}) copy-start(f32[4,3,2,16,4096]{4,3,2,1,0:T(8,128)} %get-tuple-element.110.keys) | copy-start | bytes 18874372 | tf_op jit(solution)/shard_map/cond
  39.3 17.8 %collective-permute-start.24 = (f32[1,2,8,512]{3,2,1,0:T(8,128)S(1)}, f32[1,2,8,512]{3,2,1,0:T(8,128)S(1)}, u32[]{:S(2)}, u32[]{:S(2)}) collective-permute-start(f32[1,2,8,512]{3,2,1,0:T(8,128)S(1)} %get-tuple-element.119), channel_id=1, source_target_pairs={{0,15},{1,0},{2,1},{3,2},{4,3},{5,4},{6,5},{7,6},{8,7},{9,8},{10,9... | collective-permute-start | bytes 98312 | tf_op jit(solution)/shard_map/cond/branch_2_fun/ppermute | solution.py:22
  47.7 11.4 %collective-permute-start.22 = (f32[1,2,8,512]{3,2,1,0:T(8,128)S(1)}, f32[1,2,8,512]{3,2,1,0:T(8,128)S(1)}, u32[]{:S(2)}, u32[]{:S(2)}) collective-permute-start(f32[1,2,8,512]{3,2,1,0:T(8,128)S(1)} %get-tuple-element.116), channel_id=1, source_target_pairs={{0,15},{1,0},{2,1},{3,2},{4,3},{5,4},{6,5},{7,6},{8,7},{9,8},{10,9... | collective-permute-start | bytes 98312 | tf_op jit(solution)/shard_map/cond/branch_2_fun/ppermute | solution.py:22
  52.4 8.7 %collective-permute-start.19 = (f32[1,2,8,512]{3,2,1,0:T(8,128)S(1)}, f32[1,2,8,512]{3,2,1,0:T(8,128)S(1)}, u32[]{:S(2)}, u32[]{:S(2)}) collective-permute-start(f32[1,2,8,512]{3,2,1,0:T(8,128)S(1)} %get-tuple-element.111), channel_id=1, source_target_pairs={{0,15},{1,0},{2,1},{3,2},{4,3},{5,4},{6,5},{7,6},{8,7},{9,8},{10,9... | collective-permute-start | bytes 98312 | tf_op jit(solution)/shard_map/cond/branch_2_fun/ppermute | solution.py:22
  57.0 10.7 %collective-permute-start.26 = (f32[1,2,8,4096]{3,2,1,0:T(8,128)S(1)}, f32[1,2,8,4096]{3,2,1,0:T(8,128)S(1)}, u32[]{:S(2)}, u32[]{:S(2)}) collective-permute-start(f32[1,2,8,4096]{3,2,1,0:T(8,128)S(1)} %get-tuple-element.121), channel_id=1, source_target_pairs={{16,0},{0,16},{17,1},{1,17},{18,2},{2,18},{19,3},{3,19},{20,4},{4,... | collective-permute-start | bytes 786440 | tf_op jit(solution)/shard_map/cond/branch_2_fun/ppermute | solution.py:368
  57.1 12.3 %collective-permute-start.25 = (f32[1,2,8,4096]{3,2,1,0:T(8,128)S(1)}, f32[1,2,8,4096]{3,2,1,0:T(8,128)S(1)}, u32[]{:S(2)}, u32[]{:S(2)}) collective-permute-start(f32[1,2,8,4096]{3,2,1,0:T(8,128)S(1)} %add_tail.19), channel_id=1, source_target_pairs={{16,0},{0,16},{17,1},{1,17},{18,2},{2,18},{19,3},{3,19},{20,4},{4,... | collective-permute-start | bytes 786440 | tf_op jit(solution)/shard_map/cond/branch_2_fun/ppermute | solution.py:368
  59.2 13.9 %collective-permute-start.23 = (f32[1,2,8,4096]{3,2,1,0:T(8,128)S(1)}, f32[1,2,8,4096]{3,2,1,0:T(8,128)S(1)}, u32[]{:S(2)}, u32[]{:S(2)}) collective-permute-start(f32[1,2,8,4096]{3,2,1,0:T(8,128)S(1)} %add_tail.18), channel_id=1, source_target_pairs={{0,16},{1,17},{2,18},{3,19},{4,20},{5,21},{6,22},{7,23},{8,24},{9,... | collective-permute-start | bytes 786440 | tf_op jit(solution)/shard_map/cond/branch_2_fun/ppermute | solution.py:368
  61.1 14.7 %collective-permute-start.20 = (f32[1,2,8,4096]{3,2,1,0:T(8,128)S(1)}, f32[1,2,8,4096]{3,2,1,0:T(8,128)S(1)}, u32[]{:S(2)}, u32[]{:S(2)}) collective-permute-start(f32[1,2,8,4096]{3,2,1,0:T(8,128)S(1)} %add_tail.17), channel_id=1, source_target_pairs={{0,16},{1,17},{2,18},{3,19},{4,20},{5,21},{6,22},{7,23},{8,24},{9,... | collective-permute-start | bytes 786440 | tf_op jit(solution)/shard_map/cond/branch_2_fun/ppermute | solution.py:368

commit v5 on v4

--- a/solution.py
+++ b/solution.py
@@ -33,12 +33,12 @@
 
 
 def ranked(needed):
-    slots = [jnp.int32(0)] * CAP
+    slots = [jnp.int32(0)] * len(needed)
     rank = jnp.int32(0)
     for want in (1, 0):
         for cipher in range(len(needed)):
             here = needed[cipher] == want
-            for slot in range(CAP):
+            for slot in range(len(needed)):
                 slots[slot] = jnp.where(here & (rank == slot), cipher, slots[slot])
             rank = rank + here.astype(jnp.int32)
     return slots
@@ -82,29 +82,47 @@
     )(requests, pltpu.with_memory_space_constraint(digits, pltpu.HBM))
 
 
-def products_kernel(slots, blocks, local, requests, rotations, digits, keys, modulus_ref, tail, resident, rolled):
+def products_kernel(slots, blocks, local, load, requests, rotations, digits, keys, modulus_ref, tail, resident, *refs):
     key_count, parts, polys, _, columns = keys.shape
     ciphers = requests.shape[0]
     pad = WIDEST // LANES
     tiles = columns // LANES
+    rolled = refs[0]
+    me = lax.axis_index("grp")
+    chosen = slot_ciphers(requests, ciphers, key_count, me)
+    first = blocks[0]
+
+    def wanted(key):
+        flag = requests[chosen[slots[0]], me * key_count + key]
+        for slot in slots[1:]:
+            flag = flag | requests[chosen[slot], me * key_count + key]
+        return flag > 0
+
+    if load:
+        whole, (keys, sems) = keys, refs[1:]
+        here = pl.ds(blocks[0] * ROWS, len(blocks) * ROWS)
+        first = 0
+
+        def copy(key):
+            return pltpu.make_async_copy(whole.at[key, :, :, here], keys.at[key], sems.at[key])
+
+        for key in range(key_count):
+            pl.when(wanted(key))(copy(key).start)
+
     tail[...] = jnp.zeros_like(tail)
     resident[...] = jnp.zeros_like(resident)
     rolled[...] = jnp.zeros_like(rolled)
     lane = lax.broadcasted_iota(jnp.int32, (ROWS, LANES), 1)
-    me = lax.axis_index("grp")
-    chosen = slot_ciphers(requests, ciphers, key_count, me)
-
-    def add_key(step, carry):
-        block = step // key_count
-        key = step - block * key_count
+
+    def add_key(key, block):
         rows = pl.ds(pl.multiple_of(block * ROWS, ROWS), ROWS)
-        limbs = pl.ds(pl.multiple_of((blocks[0] + block) * ROWS, ROWS), ROWS)
+        limbs = pl.ds(pl.multiple_of((first + block) * ROWS, ROWS), ROWS)
         amount = 2 * rotations[me * key_count + key]
         skipped = amount // LANES
         within = amount - skipped * LANES
         turn = lax.rem(LANES - within, LANES)
         from_this = lane < LANES - within
-        modulus = modulus_ref[limbs, :]
+        modulus = modulus_ref[pl.ds(pl.multiple_of((blocks[0] + block) * ROWS, ROWS), ROWS), :]
         inverse = 1.0 / modulus
         for place, slot in enumerate(slots):
             source = chosen[slot] if local else place
@@ -130,29 +148,44 @@
                         else:
                             at = pl.ds((tile - pad) * LANES, LANES)
                             resident[place, poly, rows, at] = resident[place, poly, rows, at] + moved
+
+    def add_step(step, carry):
+        key = step // len(blocks)
+        block = step - key * len(blocks)
+        if load:
+            pl.when((block == 0) & wanted(key))(lambda: copy(key).wait())
+
+        add_key(key, block)
         return carry
 
-    lax.fori_loop(0, len(blocks) * key_count, add_key, 0)
-
-
-def products(digits, keys, requests, rotations, modulus, slots, blocks, local):
+    lax.fori_loop(0, len(blocks) * key_count, add_step, 0)
+
+
+def products(digits, keys, requests, rotations, modulus, slots, blocks, local, load):
     key_count, parts, polys, _, columns = keys.shape
     count = len(slots)
     limbs = len(blocks) * ROWS
     pad = WIDEST // LANES
     work = count * key_count * polys * limbs * columns
+    scratch = [pltpu.VMEM((ROWS, columns + 2 * pad * LANES + LANES), jnp.float32)]
+    if load:
+        scratch.append(pltpu.VMEM((key_count, parts, polys, limbs, columns), jnp.float32))
+        scratch.append(pltpu.SemaphoreType.DMA((key_count,)))
+        keys = pltpu.with_memory_space_constraint(keys, pltpu.HBM)
     return pl.pallas_call(
-        functools.partial(products_kernel, slots, blocks, local),
+        functools.partial(products_kernel, slots, blocks, local, load),
         out_shape=[
             jax.ShapeDtypeStruct((count, polys, limbs, WIDEST), jnp.float32),
             jax.ShapeDtypeStruct((count, polys, limbs, columns), jnp.float32),
         ],
-        in_specs=[SMEM, SMEM, VMEM, VMEM, VMEM],
+        in_specs=[SMEM, SMEM, VMEM, pl.BlockSpec(memory_space=pltpu.HBM) if load else VMEM, VMEM],
         out_specs=[VMEM, VMEM],
-        scratch_shapes=[pltpu.VMEM((ROWS, columns + 2 * pad * LANES + LANES), jnp.float32)],
+        scratch_shapes=scratch,
         compiler_params=pltpu.CompilerParams(vmem_limit_bytes=20 << 20),
         cost_estimate=pl.CostEstimate(
-            flops=20 * work, transcendentals=0, bytes_accessed=4 * (key_count * parts * polys * limbs * columns + count * limbs * columns * (parts + polys))
+            flops=20 * work,
+            transcendentals=0,
+            bytes_accessed=4 * (key_count * parts * polys * limbs * columns + count * limbs * columns * (parts + polys)),
         ),
         name="products",
     )(requests, rotations, digits, keys, modulus)
@@ -183,9 +216,8 @@
     return jnp.where(remainder >= modulus, remainder - modulus, remainder)
 
 
-def sums_kernel(owners, groups, ciphers, key_count, keep, requests, modulus, *refs):
-    parts = refs[: len(owners)]
-    out = refs[len(owners)]
+def sums_kernel(owners, groups, ciphers, key_count, requests, modulus, *refs):
+    parts, out = refs[: len(owners)], refs[len(owners)]
     cipher = pl.program_id(1)
     out[...] = jnp.zeros_like(out)
     for part, (steps, slots) in zip(parts, owners):
@@ -196,31 +228,17 @@
             def _():
                 out[...] = out[...] + part[place]
 
-    if keep:
-        held = refs[len(owners) + 1]
-        chosen = slot_ciphers(requests, ciphers, key_count, group_after(groups - 1, groups))
-        for slot in range(CAP):
-
-            @pl.when(chosen[slot] == cipher)
-            def _():
-                held[slot] = out[...]
-
     wide = modulus[:, :1]
     out[...] = reduce_mod(out[...], wide) / wide
 
 
-def sums(parts, owners, requests, modulus, ciphers, keep):
+def sums(parts, owners, requests, modulus, ciphers):
     polys, limbs, columns = parts[0].shape[1:]
     groups = lax.axis_size("grp")
     key_count = requests.shape[1] // groups
-    shapes = [jax.ShapeDtypeStruct((ciphers, polys, limbs, columns), jnp.float32)]
-    specs = [pl.BlockSpec((pl.Squeezed(), polys, ROWS, columns), lambda block, cipher, *_: (cipher, 0, block, 0))]
-    if keep:
-        shapes.append(jax.ShapeDtypeStruct((CAP, polys, limbs, columns), jnp.float32))
-        specs.append(pl.BlockSpec((CAP, polys, ROWS, columns), lambda block, cipher, *_: (0, 0, block, 0)))
     return pl.pallas_call(
-        functools.partial(sums_kernel, owners, groups, ciphers, key_count, keep),
-        out_shape=shapes,
+        functools.partial(sums_kernel, owners, groups, ciphers, key_count),
+        out_shape=jax.ShapeDtypeStruct((ciphers, polys, limbs, columns), jnp.float32),
         grid_spec=pltpu.PrefetchScalarGridSpec(
             num_scalar_prefetch=1,
             grid=(limbs // ROWS, ciphers),
@@ -229,59 +247,85 @@
                 pl.BlockSpec((part.shape[0], polys, ROWS, columns), lambda block, cipher, *_: (0, 0, block, 0))
                 for part in parts
             ],
-            out_specs=specs,
+            out_specs=pl.BlockSpec(
+                (pl.Squeezed(), polys, ROWS, columns), lambda block, cipher, *_: (cipher, 0, block, 0)
+            ),
         ),
         compiler_params=pltpu.CompilerParams(
             dimension_semantics=("arbitrary", "arbitrary"), vmem_limit_bytes=24 << 20
         ),
-        cost_estimate=pl.CostEstimate(
-            flops=20 * ciphers * polys * limbs * columns,
-            transcendentals=0,
-            bytes_accessed=4 * (ciphers + 2 + 2 * len(parts)) * polys * limbs * columns,
-        ),
         name="sums",
     )(requests, modulus, *parts)
 
 
-def finish_kernel(slot, block, groups, requests, modulus, part, held, before, out, done, sems):
-    ciphers, polys, _, _ = out.shape
-    key_count = requests.shape[1] // groups
-    rows = pl.ds(block * ROWS, ROWS)
-    wide = modulus[rows, :1]
-    for poly in range(polys):
-        done[poly] = reduce_mod(held[slot, poly, rows, :] + part[0, poly], wide) / wide
+def orders_of(requests, groups):
+    ciphers, columns = requests.shape
+    key_count = columns // groups
+    bits = key_count.bit_length()
     asks = requests[...]
-    column = lax.broadcasted_iota(jnp.int32, asks.shape, 1) // key_count
     row = lax.broadcasted_iota(jnp.int32, asks.shape, 0)
-    asks = jnp.where(column == group_after(groups - 1, groups), asks, 0)
-    needed = [jnp.max(jnp.where(row == cipher, asks, 0)) for cipher in range(ciphers)]
-    cipher = ranked(needed)[slot]
-    stores = [
-        pltpu.make_async_copy(done.at[poly], out.at[cipher, poly, rows], sems.at[poly]) for poly in range(polys)
+    owner = lax.broadcasted_iota(jnp.int32, asks.shape, 1) // key_count
+    me = group_after(0, groups)
+    after = group_after(1, groups)
+    place = jnp.where(owner == me, 0, ciphers) + row
+    code = jnp.sum(jnp.where((owner == me) | (owner == after), asks << (place * bits), 0))
+    flags = [
+        ((code >> (place * bits)) & ((1 << bits) - 1) > 0).astype(jnp.int32) for place in range(2 * ciphers)
     ]
-    for store in stores:
-        store.start()
+    return ranked(flags[:ciphers]), ranked(flags[ciphers:]), flags[:ciphers]
+
+
+def finish_kernel(ranks, blocks, groups, requests, modulus, local, *refs):
+    part = None
+    if len(refs) == 5:
+        part, _, out, done, sems = refs
+    else:
+        out, done, sems = refs
+    polys = out.shape[1]
+    ours, theirs, _ = orders_of(requests, groups)
+    stores = []
+    for at, rank in enumerate(ranks):
+        cipher = theirs[rank]
+        weights = [jnp.where(ours[slot] == cipher, 1.0, 0.0) for slot in range(CAP)]
+        for which, block in enumerate(blocks):
+            rows = pl.ds(block * ROWS, ROWS)
+            here = pl.ds(which * ROWS, ROWS)
+            wide = modulus[rows, :1]
+            for poly in range(polys):
+                total = local[0, poly, rows, :] * weights[0]
+                for slot in range(1, CAP):
+                    total = total + local[slot, poly, rows, :] * weights[slot]
+                if part is not None:
+                    total = total + part[0, poly]
+                done[at, poly, here, :] = reduce_mod(total, wide) / wide
+                stores.append(
+                    pltpu.make_async_copy(done.at[at, poly, here], out.at[cipher, poly, rows], sems.at[len(stores)])
+                )
+                stores[-1].start()
     for store in stores:
         store.wait()
 
 
-def finish(part, held, result, requests, modulus, slot, block):
-    _, polys, _, columns = result.shape
-    groups = lax.axis_size("grp")
+def finish(local, requests, modulus, ciphers, ranks, blocks, part=None, before=None):
+    _, polys, _, columns = local.shape
     hbm = pl.BlockSpec(memory_space=pltpu.HBM)
+    limbs = modulus.shape[0]
+    work = len(ranks) * polys * len(blocks) * ROWS * columns
+    more = [] if part is None else [part, before]
     return pl.pallas_call(
-        functools.partial(finish_kernel, slot, block, groups),
-        out_shape=jax.ShapeDtypeStruct(result.shape, jnp.float32),
-        in_specs=[VMEM, VMEM, VMEM, VMEM, hbm],
+        functools.partial(finish_kernel, ranks, blocks, lax.axis_size("grp")),
+        out_shape=jax.ShapeDtypeStruct((ciphers, polys, limbs, columns), jnp.float32),
+        in_specs=[VMEM, VMEM, VMEM] + ([] if part is None else [VMEM, hbm]),
         out_specs=hbm,
-        scratch_shapes=[pltpu.VMEM((polys, ROWS, columns), jnp.float32), pltpu.SemaphoreType.DMA((polys,))],
-        input_output_aliases={4: 0},
+        scratch_shapes=[
+            pltpu.VMEM((len(ranks), polys, len(blocks) * ROWS, columns), jnp.float32),
+            pltpu.SemaphoreType.DMA((len(ranks) * polys * len(blocks),)),
+        ],
+        input_output_aliases={} if part is None else {4: 0},
         compiler_params=pltpu.CompilerParams(vmem_limit_bytes=8 << 20),
-        cost_estimate=pl.CostEstimate(
-            flops=20 * polys * ROWS * columns, transcendentals=0, bytes_accessed=12 * polys * ROWS * columns
-        ),
+        cost_estimate=pl.CostEstimate(flops=20 * work, transcendentals=0, bytes_accessed=12 * work),
         name="finish",
-    )(requests, modulus, part, held, result)
+    )(requests, modulus, local, *more)
 
 
 def per_device(digits, keys, requests, rotations, moduli):
@@ -294,7 +338,7 @@
     groups = lax.axis_size("grp")
     blocks = tuple(range(digits.shape[2] // ROWS))
     slots = tuple(range(CAP))
-    tail, resident = products(digits, keys, requests, rotations, modulus, slots, blocks, True)
+    tail, resident = products(digits, keys, requests, rotations, modulus, slots, blocks, True, True)
     parts = [add_tail(resident, shifted(tail, "limb", -1))]
     owners = [(0, slots)]
     for steps in range(1, groups):
@@ -305,12 +349,12 @@
             for block in blocks:
                 arrived = shifted(picked[block], "grp", steps)
                 tail, resident = products(
-                    arrived[None], keys, asked, rotations, modulus, (slot,), (block,), False
+                    arrived[None], keys, asked, rotations, modulus, (slot,), (block,), False, True
                 )
                 back.append(shifted(add_tail(resident, shifted(tail, "limb", -1)), "grp", -steps))
             parts.append(jnp.concatenate(back, axis=2))
             owners.append((steps, (slot,)))
-    return sums(parts, tuple(owners), requests, modulus, digits.shape[0], False)[0]
+    return sums(parts, tuple(owners), requests, modulus, digits.shape[0])
 
 
 def key_switch_pair(digits, keys, requests, rotations, modulus):
@@ -325,7 +369,7 @@
     for block in blocks:
         sent[0, block] = lax.ppermute(picked[0, block], "grp", both)
     asked = shifted(requests, "grp", 1)
-    tail, resident = products(digits, keys, requests, rotations, modulus, slots, blocks, True)
+    tail, resident = products(digits, keys, requests, rotations, modulus, slots, blocks, True, True)
     arrived = shifted(tail, "limb", -1)
     local = add_tail(resident, arrived)
     me = lax.axis_index("grp")
@@ -348,7 +392,7 @@
 
 
 def remote(arrived, keys, asked, rotations, modulus, slot, block):
-    tail, resident = products(arrived[None], keys, asked, rotations, modulus, (slot,), (block,), False)
+    tail, resident = products(arrived[None], keys, asked, rotations, modulus, (slot,), (block,), False, slot == 0)
     wrapped = shifted(tail, "limb", -1)
     return add_tail(resident, wrapped)
 
@@ -360,14 +404,14 @@
     sent = dict(zip(turns[1:blocks], arrived))
     for (slot, block), piece in zip(turns[blocks:], picked):
         sent[slot, block] = lax.ppermute(piece, "grp", pairs[slot])
-    result, held = sums([local], ((0, tuple(range(CAP))),), requests, modulus, ciphers, True)
+    result = finish(local, requests, modulus, ciphers, tuple(range(CAP, ciphers)), tuple(range(blocks)))
     back = {}
     for turn in turns:
         slot, block = turn
         whole = ahead if turn == turns[0] else remote(sent[turn], keys, asked, rotations, modulus, slot, block)
         back[turn] = lax.ppermute(whole, "grp", [(target, source) for source, target in pairs[slot]])
     for slot, block in turns:
-        result = finish(back[slot, block], held, result, requests, modulus, slot, block)
+        result = finish(local, requests, modulus, ciphers, (slot,), (block,), back[slot, block], result)
     return result
 
 

time: 77.3 us -> 76.2 us (0.986)
  Pallas kernels: 28.5 us -> 21.8 us
  waiting for transfers between devices: 15.2 us -> 20.9 us
    pallas_call x10, Pallas kernels: 23.8 us -> 17.1 us  [the longest x5 11.7 us: products(): pl.pallas_call(functools.partial(products_kernel, slots, blocks, local, l...]
    ppermute x4, waiting for transfers between devices: 5.09 us -> 8.95 us  [exchange(): lax.ppermute(whole, 'grp', [(target, source) for source, target in pairs[...]
    ppermute x2, waiting for transfers between devices: 5.21 us -> 6.2 us  [exchange(): sent[slot, block] = lax.ppermute(piece, 'grp', pairs[slot])]
    ppermute x6, waiting for transfers between devices: 4.93 us -> 5.71 us  [shifted(): return lax.ppermute(value, axis, pairs)]
  transfers between devices with their start and end apart: 14 -> 14, of which waited for: 6 -> 7; matrix products, arithmetic and copies ran while one was open for 2% -> 2% of each run, Pallas kernels for 33% -> 25%
where the time goes in v5:
time: 76.2 us; the launch traced here: 75.8 us
  starting transfers between devices  29.9 us (39%)
  Pallas kernels  21.8 us (29%)
  waiting for transfers between devices  20.9 us (27%)
  other arithmetic  1.52 us (2%)
  between operations  1.39 us (2%)
    ppermute x6, starting transfers between devices, shifted(): return lax.ppermute(value, axis, pairs)  18.7 us
    pallas_call x5, Pallas kernels, products(): pl.pallas_call(functools.partial(products_kernel, slots, blocks, local, l...  11.7 us
    ppermute x4, waiting for transfers between devices, exchange(): lax.ppermute(whole, 'grp', [(target, source) for source, target in pairs[...  8.95 us
    ppermute x2, waiting for transfers between devices, exchange(): sent[slot, block] = lax.ppermute(piece, 'grp', pairs[slot])  6.2 us
    ppermute x6, waiting for transfers between devices, shifted(): return lax.ppermute(value, axis, pairs)  5.71 us
    pallas_call x5, Pallas kernels, finish(): pl.pallas_call(functools.partial(finish_kernel, ranks, blocks, lax.axis_s...  5.37 us
    ppermute x4, starting transfers between devices, exchange(): lax.ppermute(whole, 'grp', [(target, source) for source, target in pairs[...  5.34 us
    pallas_call x2, Pallas kernels, gather(): pl.pallas_call(functools.partial(gather_kernel, wanted, cuts, steps, lax....  4.67 us
  transfers between devices with their start and end apart: 14, of which 7 were waited for; matrix products, arithmetic and copies ran while one was open for 2% of the time, Pallas kernels for 25%

profile of v5, /device:TPU:0, one launch (start us, length us, event | category | flops | bytes accessed | tf_op | source)
XLA Modules:
  0.0 75.8 jit_solution(9595779283599197663)
XLA Ops:
  0.0 0.0 copy-start.4
  0.0 1.9 %gather_digits.3 = f32[3,8,4096]{2,1,0:T(8,128)S(1)} custom-call(s32[4,8]{1,0:T(4,128)} %requests.5, f32[4,3,16,4096]{3,2,1,0:T(8,128)} %digits.5), custom_call_target="tpu_custom_call" | custom-call | bytes 786432 | tf_op jit(solution)/shard_map/gather_digits/pallas_call | solution.py:71
  1.9 0.0 copy-start.6
  1.9 0.0 copy-start
  1.9 0.0 copy-start.5
  2.0 3.0 %collective-permute-start.29 = (f32[3,8,4096]{2,1,0:T(8,128)S(1)}, f32[3,8,4096]{2,1,0:T(8,128)S(1)}, u32[]{:S(2)}, u32[]{:S(2)}) collective-permute-start(f32[3,8,4096]{2,1,0:T(8,128)S(1)} %gather_digits.3), channel_id=1, source_target_pairs={{0,16},{16,0},{1,17},{17,1},{2,18},{18,2},{3,19},{19,3},{4,20},{20... | collective-permute-start | bytes 1179656 | tf_op jit(solution)/shard_map/ppermute | solution.py:370
  5.0 0.0 copy-done.4
  5.0 2.8 %gather_digits.2 = (f32[3,8,4096]{2,1,0:T(8,128)S(1)}, f32[3,8,4096]{2,1,0:T(8,128)S(1)}, f32[3,8,4096]{2,1,0:T(8,128)}) custom-call(s32[4,8]{1,0:T(4,128)S(1)} %copy-done.4, f32[4,3,16,4096]{3,2,1,0:T(8,128)} %digits.5), custom_call_target="tpu_custom_call" | custom-call | bytes 2359296 | tf_op jit(solution)/shard_map/gather_digits/pallas_call | solution.py:71
  7.8 0.3 collective-permute-start.28
  8.1 1.8 %collective-permute-start.27 = (s32[4,8]{1,0:T(4,128)S(1)}, s32[4,8]{1,0:T(4,128)S(1)}, u32[]{:S(2)}, u32[]{:S(2)}) collective-permute-start(s32[4,8]{1,0:T(4,128)S(1)} %copy-done.4), channel_id=1, source_target_pairs={{0,16},{16,0},{1,17},{17,1},{2,18},{18,2},{3,19},{19,3},{4,20},{20... | collective-permute-start | bytes 392 | tf_op jit(solution)/shard_map/ppermute | solution.py:22
  9.8 0.0 copy-done.6
  9.9 0.1 broadcast_in_dim.36.modulus_ref
  9.9 0.0 copy-done
  9.9 0.0 copy-done.5
  9.9 3.7 %products.21 = (f32[2,2,16,512]{3,2,1,0:T(8,128)S(1)}, f32[2,2,16,4096]{3,2,1,0:T(8,128)S(1)}) custom-call(s32[4,8]{1,0:T(4,128)S(1)} %copy-done.4, s32[8]{0:T(128)S(1)} %copy-done.5, f32[4,3,16,4096]{3,2,1,0:T(8,128)S(1)} %copy-done, f32[4,3,2,16,4096]{4,3,2,1,0:T(8,128)} %keys.3, f32[16,128]{1,0:T(8,128)S(1)} %broadcast_in_dim.36.modulus_ref), custom_call_target="tpu_custom_call" | custom-call | flops 20971520 | bytes 8912896 | tf_op jit(solution)/shard_map/products/pallas_call | solution.py:175
  13.7 3.2 %collective-permute-start.31 = (f32[2,2,16,512]{3,2,1,0:T(8,128)S(1)}, f32[2,2,16,512]{3,2,1,0:T(8,128)S(1)}, u32[]{:S(2)}, u32[]{:S(2)}) collective-permute-start(f32[2,2,16,512]{3,2,1,0:T(8,128)S(1)} %get-tuple-element.129), channel_id=1, source_target_pairs={{0,15},{1,0},{2,1},{3,2},{4,3},{5,4},{6,5},{7,6},{8,7},{9,8},{10,9... | collective-permute-start | bytes 393224 | tf_op jit(solution)/shard_map/ppermute | solution.py:22
  16.9 5.7 %collective-permute-done.27.requests = s32[4,8]{1,0:T(4,128)S(1)} collective-permute-done((s32[4,8]{1,0:T(4,128)S(1)}, s32[4,8]{1,0:T(4,128)S(1)}, u32[]{:S(2)}, u32[]{:S(2)}) %collective-permute-start.27) | collective-permute-done | bytes 160 | tf_op jit(solution)/shard_map/ppermute | solution.py:22
  22.6 0.0 collective-permute-done.29
  22.6 2.8 %products.20 = (f32[1,2,8,512]{3,2,1,0:T(8,128)S(1)}, f32[1,2,8,4096]{3,2,1,0:T(8,128)S(1)}) custom-call(s32[4,8]{1,0:T(4,128)S(1)} %collective-permute-done.27.requests, s32[8]{0:T(128)S(1)} %copy-done.5, f32[1,3,8,4096]{3,2,1,0:T(8,128)S(1)} %bitcast.10, f32[4,3,2,16,4096]{4,3,2,1,0:T(8,128)} %keys.3, f32[16,128]{1,0:T(8,128)S(1)} %broadcast_in_dim.36.modulus_ref), custom_call_target="tpu_custom_call" | custom-call | flops 5242880 | bytes 3801088 | tf_op jit(solution)/shard_map/products/pallas_call | solution.py:175
  25.4 3.4 %collective-permute-start.30 = (f32[1,2,8,512]{3,2,1,0:T(8,128)S(1)}, f32[1,2,8,512]{3,2,1,0:T(8,128)S(1)}, u32[]{:S(2)}, u32[]{:S(2)}) collective-permute-start(f32[1,2,8,512]{3,2,1,0:T(8,128)S(1)} %get-tuple-element.127), channel_id=1, source_target_pairs={{0,15},{1,0},{2,1},{3,2},{4,3},{5,4},{6,5},{7,6},{8,7},{9,8},{10,9... | collective-permute-start | bytes 98312 | tf_op jit(solution)/shard_map/ppermute | solution.py:22
  28.8 0.2 slice_reduce_fusion
  29.0 0.6 reduce_sum.18
  29.6 0.7 reduce_sum.19
  31.6 0.0 collective-permute-done.31.arrived
  31.6 0.0 collective-permute-done.30.arrived
  31.7 0.0 collective-permute-done.28
  31.7 44.1 %conditional.1 = (f32[4,2,16,4096]{3,2,1,0:T(8,128)}) conditional(s32[]{:T(128)} %clamp.3, (f32[3,8,4096]{2,1,0:T(8,128)}, s32[4,8]{1,0:T(4,128)S(1)}, s32[8]{0:T(128)S(1)}, f32[4,3,2,16,4096]{4,3,2,1,0:T(8,128)}, f32[16,128]{1,0:T(8,128)S(1)}, /*index=5*/f32[3,8,4096]{2,1,0:T(8,128)S(1)}, f32[3,8,4096]{2,1,0:T(8,128)S(1)}, ...), branch_computations={%region_4.5_spmd, %region_5.6_spmd, %region_6.7_spmd} | conditional | flops 26214400 | bytes 50594188 | solution.py:391
  31.7 1.3 %collective-permute-start.21 = (f32[3,8,4096]{2,1,0:T(8,128)S(1)}, f32[3,8,4096]{2,1,0:T(8,128)S(1)}, u32[]{:S(2)}, u32[]{:S(2)}) collective-permute-start(f32[3,8,4096]{2,1,0:T(8,128)S(1)} %get-tuple-element.110), channel_id=1, source_target_pairs={{16,0},{17,1},{18,2},{19,3},{20,4},{21,5},{22,6},{23,7},{24,8},{25... | collective-permute-start | bytes 1179656 | tf_op jit(solution)/shard_map/cond/branch_2_fun/ppermute | solution.py:406
  33.0 1.3 %collective-permute-start.18 = (f32[3,8,4096]{2,1,0:T(8,128)}, f32[3,8,4096]{2,1,0:T(8,128)S(1)}, u32[]{:S(2)}, u32[]{:S(2)}) collective-permute-start(f32[3,8,4096]{2,1,0:T(8,128)} %get-tuple-element.106), channel_id=1, source_target_pairs={{16,0},{17,1},{18,2},{19,3},{20,4},{21,5},{22,6},{23,7},{24,8},{25... | collective-permute-start | bytes 1179656 | tf_op jit(solution)/shard_map/cond/branch_2_fun/ppermute | solution.py:406
  34.3 0.0 copy-start.3
  34.3 3.0 %products.19 = (f32[1,2,8,512]{3,2,1,0:T(8,128)S(1)}, f32[1,2,8,4096]{3,2,1,0:T(8,128)S(1)}) custom-call(s32[4,8]{1,0:T(4,128)S(1)} %get-tuple-element.104.requests, s32[8]{0:T(128)S(1)} %get-tuple-element.105.rotations, f32[1,3,8,4096]{3,2,1,0:T(8,128)S(1)} %bitcast.19, f32[4,3,2,16,4096]{4,3,2,1,0:T(8,128)} %get-tuple-element.107.keys, ...), custom_call_target="tpu_custom_call" | custom-call | flops 5242880 | bytes 3801088 | tf_op jit(solution)/shard_map/cond/branch_2_fun/products/pallas_call | solution.py:175
  37.4 3.2 %collective-permute-start.24 = (f32[1,2,8,512]{3,2,1,0:T(8,128)S(1)}, f32[1,2,8,512]{3,2,1,0:T(8,128)S(1)}, u32[]{:S(2)}, u32[]{:S(2)}) collective-permute-start(f32[1,2,8,512]{3,2,1,0:T(8,128)S(1)} %get-tuple-element.114), channel_id=1, source_target_pairs={{0,15},{1,0},{2,1},{3,2},{4,3},{5,4},{6,5},{7,6},{8,7},{9,8},{10,9... | collective-permute-start | bytes 98312 | tf_op jit(solution)/shard_map/cond/branch_2_fun/ppermute | solution.py:22
  40.6 5.0 %collective-permute-done.21 = f32[3,8,4096]{2,1,0:T(8,128)S(1)} collective-permute-done((f32[3,8,4096]{2,1,0:T(8,128)S(1)}, f32[3,8,4096]{2,1,0:T(8,128)S(1)}, u32[]{:S(2)}, u32[]{:S(2)}) %collective-permute-start.21) | collective-permute-done | bytes 393248 | tf_op jit(solution)/shard_map/cond/branch_2_fun/ppermute | solution.py:406
  45.6 0.0 copy-done.3
  45.6 1.1 %products.18 = (f32[1,2,8,512]{3,2,1,0:T(8,128)S(1)}, f32[1,2,8,4096]{3,2,1,0:T(8,128)S(1)}) custom-call(s32[4,8]{1,0:T(4,128)S(1)} %get-tuple-element.104.requests, s32[8]{0:T(128)S(1)} %get-tuple-element.105.rotations, f32[1,3,8,4096]{3,2,1,0:T(8,128)S(1)} %bitcast.16, f32[4,3,2,16,4096]{4,3,2,1,0:T(8,128)S(1)} %copy-done.3, ...), custom_call_target="tpu_custom_call" | custom-call | flops 5242880 | bytes 3801088 | tf_op jit(solution)/shard_map/cond/branch_2_fun/products/pallas_call | solution.py:175
  46.7 2.4 %collective-permute-start.22 = (f32[1,2,8,512]{3,2,1,0:T(8,128)S(1)}, f32[1,2,8,512]{3,2,1,0:T(8,128)S(1)}, u32[]{:S(2)}, u32[]{:S(2)}) collective-permute-start(f32[1,2,8,512]{3,2,1,0:T(8,128)S(1)} %get-tuple-element.111), channel_id=1, source_target_pairs={{0,15},{1,0},{2,1},{3,2},{4,3},{5,4},{6,5},{7,6},{8,7},{9,8},{10,9... | collective-permute-start | bytes 98312 | tf_op jit(solution)/shard_map/cond/branch_2_fun/ppermute | solution.py:22
  49.1 1.2 %collective-permute-done.18 = f32[3,8,4096]{2,1,0:T(8,128)S(1)} collective-permute-done((f32[3,8,4096]{2,1,0:T(8,128)}, f32[3,8,4096]{2,1,0:T(8,128)S(1)}, u32[]{:S(2)}, u32[]{:S(2)}) %collective-permute-start.18) | collective-permute-done | bytes 393248 | tf_op jit(solution)/shard_map/cond/branch_2_fun/ppermute | solution.py:406
  50.3 1.1 %products.17 = (f32[1,2,8,512]{3,2,1,0:T(8,128)S(1)}, f32[1,2,8,4096]{3,2,1,0:T(8,128)S(1)}) custom-call(s32[4,8]{1,0:T(4,128)S(1)} %get-tuple-element.104.requests, s32[8]{0:T(128)S(1)} %get-tuple-element.105.rotations, f32[1,3,8,4096]{3,2,1,0:T(8,128)S(1)} %bitcast.13, f32[4,3,2,16,4096]{4,3,2,1,0:T(8,128)S(1)} %copy-done.3, ...), custom_call_target="tpu_custom_call" | custom-call | flops 5242880 | bytes 3801088 | tf_op jit(solution)/shard_map/cond/branch_2_fun/products/pallas_call | solution.py:175
  51.4 4.7 %collective-permute-start.19 = (f32[1,2,8,512]{3,2,1,0:T(8,128)S(1)}, f32[1,2,8,512]{3,2,1,0:T(8,128)S(1)}, u32[]{:S(2)}, u32[]{:S(2)}) collective-permute-start(f32[1,2,8,512]{3,2,1,0:T(8,128)S(1)} %get-tuple-element.108), channel_id=1, source_target_pairs={{0,15},{1,0},{2,1},{3,2},{4,3},{5,4},{6,5},{7,6},{8,7},{9,8},{10,9... | collective-permute-start | bytes 98312 | tf_op jit(solution)/shard_map/cond/branch_2_fun/ppermute | solution.py:22
  56.0 0.0 collective-permute-start.26
  56.0 0.0 collective-permute-done.24.arrived
  56.1 2.1 %collective-permute-start.25 = (f32[1,2,8,4096]{3,2,1,0:T(8,128)S(1)}, f32[1,2,8,4096]{3,2,1,0:T(8,128)S(1)}, u32[]{:S(2)}, u32[]{:S(2)}) collective-permute-start(f32[1,2,8,4096]{3,2,1,0:T(8,128)S(1)} %add_tail.19), channel_id=1, source_target_pairs={{16,0},{0,16},{17,1},{1,17},{18,2},{2,18},{19,3},{3,19},{20,4},{4,... | collective-permute-start | bytes 786440 | tf_op jit(solution)/shard_map/cond/branch_2_fun/ppermute | solution.py:412
  58.1 0.0 collective-permute-done.22.arrived
  58.2 1.9 %collective-permute-start.23 = (f32[1,2,8,4096]{3,2,1,0:T(8,128)S(1)}, f32[1,2,8,4096]{3,2,1,0:T(8,128)S(1)}, u32[]{:S(2)}, u32[]{:S(2)}) collective-permute-start(f32[1,2,8,4096]{3,2,1,0:T(8,128)S(1)} %add_tail.18), channel_id=1, source_target_pairs={{0,16},{1,17},{2,18},{3,19},{4,20},{5,21},{6,22},{7,23},{8,24},{9,... | collective-permute-start | bytes 786440 | tf_op jit(solution)/shard_map/cond/branch_2_fun/ppermute | solution.py:412
  60.1 0.0 collective-permute-done.19.arrived
  60.1 1.3 %collective-permute-start.20 = (f32[1,2,8,4096]{3,2,1,0:T(8,128)S(1)}, f32[1,2,8,4096]{3,2,1,0:T(8,128)S(1)}, u32[]{:S(2)}, u32[]{:S(2)}) collective-permute-start(f32[1,2,8,4096]{3,2,1,0:T(8,128)S(1)} %add_tail.17), channel_id=1, source_target_pairs={{0,16},{1,17},{2,18},{3,19},{4,20},{5,21},{6,22},{7,23},{8,24},{9,... | collective-permute-start | bytes 786440 | tf_op jit(solution)/shard_map/cond/branch_2_fun/ppermute | solution.py:412
  61.5 1.4 %finish.25.refs_1_ = f32[4,2,16,4096]{3,2,1,0:T(8,128)} custom-call(s32[4,8]{1,0:T(4,128)S(1)} %get-tuple-element.101.requests, f32[16,128]{1,0:T(8,128)S(1)} %get-tuple-element.102.modulus_ref.modulus, f32[2,2,16,4096]{3,2,1,0:T(8,128)S(1)} %get-tuple-element.103.local), custom_call_target="tpu_custom_call" | custom-call | flops 5242880 | bytes 3145728 | tf_op jit(solution)/shard_map/cond/branch_2_fun/finish/pallas_call | solution.py:315
  62.9 0.1 collective-permute-done.26.refs_0_
  63.0 1.0 %finish.26.refs_1_ = f32[4,2,16,4096]{3,2,1,0:T(8,128)} custom-call(s32[4,8]{1,0:T(4,128)S(1)} %get-tuple-element.101.requests, f32[16,128]{1,0:T(8,128)S(1)} %get-tuple-element.102.modulus_ref.modulus, f32[2,2,16,4096]{3,2,1,0:T(8,128)S(1)} %get-tuple-element.103.local, ...), custom_call_target="tpu_custom_call", output_to_operand_aliasing={{}: (4, {})} | custom-call | flops 1310720 | bytes 786432 | tf_op jit(solution)/shard_map/cond/branch_2_fun/finish/pallas_call | solution.py:315
  64.0 4.4 %collective-permute-done.25.refs_0_ = f32[1,2,8,4096]{3,2,1,0:T(8,128)S(1)} collective-permute-done((f32[1,2,8,4096]{3,2,1,0:T(8,128)S(1)}, f32[1,2,8,4096]{3,2,1,0:T(8,128)S(1)}, u32[]{:S(2)}, u32[]{:S(2)}) %collective-permute-start.25) | collective-permute-done | bytes 262176 | tf_op jit(solution)/shard_map/cond/branch_2_fun/ppermute | solution.py:412
  68.4 1.0 %finish.27.refs_1_ = f32[4,2,16,4096]{3,2,1,0:T(8,128)} custom-call(s32[4,8]{1,0:T(4,128)S(1)} %get-tuple-element.101.requests, f32[16,128]{1,0:T(8,128)S(1)} %get-tuple-element.102.modulus_ref.modulus, f32[2,2,16,4096]{3,2,1,0:T(8,128)S(1)} %get-tuple-element.103.local, ...), custom_call_target="tpu_custom_call", output_to_operand_aliasing={{}: (4, {})} | custom-call | flops 1310720 | bytes 786432 | tf_op jit(solution)/shard_map/cond/branch_2_fun/finish/pallas_call | solution.py:315
  69.4 2.7 %collective-permute-done.23.refs_0_ = f32[1,2,8,4096]{3,2,1,0:T(8,128)S(1)} collective-permute-done((f32[1,2,8,4096]{3,2,1,0:T(8,128)S(1)}, f32[1,2,8,4096]{3,2,1,0:T(8,128)S(1)}, u32[]{:S(2)}, u32[]{:S(2)}) %collective-permute-start.23) | collective-permute-done | bytes 262176 | tf_op jit(solution)/shard_map/cond/branch_2_fun/ppermute | solution.py:412
  72.0 1.0 %finish.28.refs_1_ = f32[4,2,16,4096]{3,2,1,0:T(8,128)} custom-call(s32[4,8]{1,0:T(4,128)S(1)} %get-tuple-element.101.requests, f32[16,128]{1,0:T(8,128)S(1)} %get-tuple-element.102.modulus_ref.modulus, f32[2,2,16,4096]{3,2,1,0:T(8,128)S(1)} %get-tuple-element.103.local, ...), custom_call_target="tpu_custom_call", output_to_operand_aliasing={{}: (4, {})} | custom-call | flops 1310720 | bytes 786432 | tf_op jit(solution)/shard_map/cond/branch_2_fun/finish/pallas_call | solution.py:315
  73.0 1.8 %collective-permute-done.20.refs_0_ = f32[1,2,8,4096]{3,2,1,0:T(8,128)S(1)} collective-permute-done((f32[1,2,8,4096]{3,2,1,0:T(8,128)S(1)}, f32[1,2,8,4096]{3,2,1,0:T(8,128)S(1)}, u32[]{:S(2)}, u32[]{:S(2)}) %collective-permute-start.20) | collective-permute-done | bytes 262176 | tf_op jit(solution)/shard_map/cond/branch_2_fun/ppermute | solution.py:412
  74.8 1.0 %finish.29 = f32[4,2,16,4096]{3,2,1,0:T(8,128)} custom-call(s32[4,8]{1,0:T(4,128)S(1)} %get-tuple-element.101.requests, f32[16,128]{1,0:T(8,128)S(1)} %get-tuple-element.102.modulus_ref.modulus, f32[2,2,16,4096]{3,2,1,0:T(8,128)S(1)} %get-tuple-element.103.local, ...), custom_call_target="tpu_custom_call", output_to_operand_aliasing={{}: (4, {})} | custom-call | flops 1310720 | bytes 786432 | tf_op jit(solution)/shard_map/cond/branch_2_fun/finish/pallas_call | solution.py:315
  (7 shorter events, 0.1 us)
Async XLA Ops:
  0.0 5.0 %copy-start.4 = (s32[4,8]{1,0:T(4,128)S(1)}, s32[4,8]{1,0:T(4,128)}, u32[]{:S(2)}) copy-start(s32[4,8]{1,0:T(4,128)} %requests.5) | copy-start | bytes 388
  1.9 7.9 %copy-start.6 = (s32[16]{0:T(128)S(1)}, s32[16]{0:T(128)}, u32[]{:S(2)}) copy-start(s32[16]{0:T(128)} %param.12) | copy-start | bytes 196
  1.9 8.0 %copy-start = (f32[4,3,16,4096]{3,2,1,0:T(8,128)S(1)}, f32[4,3,16,4096]{3,2,1,0:T(8,128)}, u32[]{:S(2)}) copy-start(f32[4,3,16,4096]{3,2,1,0:T(8,128)} %digits.5) | copy-start | bytes 9437188
  1.9 8.0 %copy-start.5 = (s32[8]{0:T(128)S(1)}, s32[8]{0:T(128)}, u32[]{:S(2)}) copy-start(s32[8]{0:T(128)} %rotations.3) | copy-start | bytes 100
  2.0 20.6 %collective-permute-start.29 = (f32[3,8,4096]{2,1,0:T(8,128)S(1)}, f32[3,8,4096]{2,1,0:T(8,128)S(1)}, u32[]{:S(2)}, u32[]{:S(2)}) collective-permute-start(f32[3,8,4096]{2,1,0:T(8,128)S(1)} %gather_digits.3), channel_id=1, source_target_pairs={{0,16},{16,0},{1,17},{17,1},{2,18},{18,2},{3,19},{19,3},{4,20},{20... | collective-permute-start | bytes 1179656 | tf_op jit(solution)/shard_map/ppermute | solution.py:370
  7.8 23.9 %collective-permute-start.28 = (f32[3,8,4096]{2,1,0:T(8,128)S(1)}, f32[3,8,4096]{2,1,0:T(8,128)S(1)}, u32[]{:S(2)}, u32[]{:S(2)}) collective-permute-start(f32[3,8,4096]{2,1,0:T(8,128)S(1)} %get-tuple-element.126), channel_id=1, source_target_pairs={{0,16},{16,0},{1,17},{17,1},{2,18},{18,2},{3,19},{19,3},{4,20},{20... | collective-permute-start | bytes 1179656 | tf_op jit(solution)/shard_map/ppermute | solution.py:370
  8.1 14.5 %collective-permute-start.27 = (s32[4,8]{1,0:T(4,128)S(1)}, s32[4,8]{1,0:T(4,128)S(1)}, u32[]{:S(2)}, u32[]{:S(2)}) collective-permute-start(s32[4,8]{1,0:T(4,128)S(1)} %copy-done.4), channel_id=1, source_target_pairs={{0,16},{16,0},{1,17},{17,1},{2,18},{18,2},{3,19},{19,3},{4,20},{20... | collective-permute-start | bytes 392 | tf_op jit(solution)/shard_map/ppermute | solution.py:22
  13.7 17.9 %collective-permute-start.31 = (f32[2,2,16,512]{3,2,1,0:T(8,128)S(1)}, f32[2,2,16,512]{3,2,1,0:T(8,128)S(1)}, u32[]{:S(2)}, u32[]{:S(2)}) collective-permute-start(f32[2,2,16,512]{3,2,1,0:T(8,128)S(1)} %get-tuple-element.129), channel_id=1, source_target_pairs={{0,15},{1,0},{2,1},{3,2},{4,3},{5,4},{6,5},{7,6},{8,7},{9,8},{10,9... | collective-permute-start | bytes 393224 | tf_op jit(solution)/shard_map/ppermute | solution.py:22
  25.4 6.3 %collective-permute-start.30 = (f32[1,2,8,512]{3,2,1,0:T(8,128)S(1)}, f32[1,2,8,512]{3,2,1,0:T(8,128)S(1)}, u32[]{:S(2)}, u32[]{:S(2)}) collective-permute-start(f32[1,2,8,512]{3,2,1,0:T(8,128)S(1)} %get-tuple-element.127), channel_id=1, source_target_pairs={{0,15},{1,0},{2,1},{3,2},{4,3},{5,4},{6,5},{7,6},{8,7},{9,8},{10,9... | collective-permute-start | bytes 98312 | tf_op jit(solution)/shard_map/ppermute | solution.py:22
  31.7 13.9 %collective-permute-start.21 = (f32[3,8,4096]{2,1,0:T(8,128)S(1)}, f32[3,8,4096]{2,1,0:T(8,128)S(1)}, u32[]{:S(2)}, u32[]{:S(2)}) collective-permute-start(f32[3,8,4096]{2,1,0:T(8,128)S(1)} %get-tuple-element.110), channel_id=1, source_target_pairs={{16,0},{17,1},{18,2},{19,3},{20,4},{21,5},{22,6},{23,7},{24,8},{25... | collective-permute-start | bytes 1179656 | tf_op jit(solution)/shard_map/cond/branch_2_fun/ppermute | solution.py:406
  33.0 17.3 %collective-permute-start.18 = (f32[3,8,4096]{2,1,0:T(8,128)}, f32[3,8,4096]{2,1,0:T(8,128)S(1)}, u32[]{:S(2)}, u32[]{:S(2)}) collective-permute-start(f32[3,8,4096]{2,1,0:T(8,128)} %get-tuple-element.106), channel_id=1, source_target_pairs={{16,0},{17,1},{18,2},{19,3},{20,4},{21,5},{22,6},{23,7},{24,8},{25... | collective-permute-start | bytes 1179656 | tf_op jit(solution)/shard_map/cond/branch_2_fun/ppermute | solution.py:406
  34.3 11.3 %copy-start.3 = (f32[4,3,2,16,4096]{4,3,2,1,0:T(8,128)S(1)}, f32[4,3,2,16,4096]{4,3,2,1,0:T(8,128)}, u32[]{:S(2)}) copy-start(f32[4,3,2,16,4096]{4,3,2,1,0:T(8,128)} %get-tuple-element.107.keys) | copy-start | bytes 18874372 | tf_op jit(solution)/shard_map/cond
  37.4 18.7 %collective-permute-start.24 = (f32[1,2,8,512]{3,2,1,0:T(8,128)S(1)}, f32[1,2,8,512]{3,2,1,0:T(8,128)S(1)}, u32[]{:S(2)}, u32[]{:S(2)}) collective-permute-start(f32[1,2,8,512]{3,2,1,0:T(8,128)S(1)} %get-tuple-element.114), channel_id=1, source_target_pairs={{0,15},{1,0},{2,1},{3,2},{4,3},{5,4},{6,5},{7,6},{8,7},{9,8},{10,9... | collective-permute-start | bytes 98312 | tf_op jit(solution)/shard_map/cond/branch_2_fun/ppermute | solution.py:22
  46.7 11.4 %collective-permute-start.22 = (f32[1,2,8,512]{3,2,1,0:T(8,128)S(1)}, f32[1,2,8,512]{3,2,1,0:T(8,128)S(1)}, u32[]{:S(2)}, u32[]{:S(2)}) collective-permute-start(f32[1,2,8,512]{3,2,1,0:T(8,128)S(1)} %get-tuple-element.111), channel_id=1, source_target_pairs={{0,15},{1,0},{2,1},{3,2},{4,3},{5,4},{6,5},{7,6},{8,7},{9,8},{10,9... | collective-permute-start | bytes 98312 | tf_op jit(solution)/shard_map/cond/branch_2_fun/ppermute | solution.py:22
  51.4 8.7 %collective-permute-start.19 = (f32[1,2,8,512]{3,2,1,0:T(8,128)S(1)}, f32[1,2,8,512]{3,2,1,0:T(8,128)S(1)}, u32[]{:S(2)}, u32[]{:S(2)}) collective-permute-start(f32[1,2,8,512]{3,2,1,0:T(8,128)S(1)} %get-tuple-element.108), channel_id=1, source_target_pairs={{0,15},{1,0},{2,1},{3,2},{4,3},{5,4},{6,5},{7,6},{8,7},{9,8},{10,9... | collective-permute-start | bytes 98312 | tf_op jit(solution)/shard_map/cond/branch_2_fun/ppermute | solution.py:22
  56.0 6.9 %collective-permute-start.26 = (f32[1,2,8,4096]{3,2,1,0:T(8,128)S(1)}, f32[1,2,8,4096]{3,2,1,0:T(8,128)S(1)}, u32[]{:S(2)}, u32[]{:S(2)}) collective-permute-start(f32[1,2,8,4096]{3,2,1,0:T(8,128)S(1)} %get-tuple-element.116), channel_id=1, source_target_pairs={{16,0},{0,16},{17,1},{1,17},{18,2},{2,18},{19,3},{3,19},{20,4},{4,... | collective-permute-start | bytes 786440 | tf_op jit(solution)/shard_map/cond/branch_2_fun/ppermute | solution.py:412
  56.1 12.3 %collective-permute-start.25 = (f32[1,2,8,4096]{3,2,1,0:T(8,128)S(1)}, f32[1,2,8,4096]{3,2,1,0:T(8,128)S(1)}, u32[]{:S(2)}, u32[]{:S(2)}) collective-permute-start(f32[1,2,8,4096]{3,2,1,0:T(8,128)S(1)} %add_tail.19), channel_id=1, source_target_pairs={{16,0},{0,16},{17,1},{1,17},{18,2},{2,18},{19,3},{3,19},{20,4},{4,... | collective-permute-start | bytes 786440 | tf_op jit(solution)/shard_map/cond/branch_2_fun/ppermute | solution.py:412
  58.2 13.8 %collective-permute-start.23 = (f32[1,2,8,4096]{3,2,1,0:T(8,128)S(1)}, f32[1,2,8,4096]{3,2,1,0:T(8,128)S(1)}, u32[]{:S(2)}, u32[]{:S(2)}) collective-permute-start(f32[1,2,8,4096]{3,2,1,0:T(8,128)S(1)} %add_tail.18), channel_id=1, source_target_pairs={{0,16},{1,17},{2,18},{3,19},{4,20},{5,21},{6,22},{7,23},{8,24},{9,... | collective-permute-start | bytes 786440 | tf_op jit(solution)/shard_map/cond/branch_2_fun/ppermute | solution.py:412
  60.1 14.7 %collective-permute-start.20 = (f32[1,2,8,4096]{3,2,1,0:T(8,128)S(1)}, f32[1,2,8,4096]{3,2,1,0:T(8,128)S(1)}, u32[]{:S(2)}, u32[]{:S(2)}) collective-permute-start(f32[1,2,8,4096]{3,2,1,0:T(8,128)S(1)} %add_tail.17), channel_id=1, source_target_pairs={{0,16},{1,17},{2,18},{3,19},{4,20},{5,21},{6,22},{7,23},{8,24},{9,... | collective-permute-start | bytes 786440 | tf_op jit(solution)/shard_map/cond/branch_2_fun/ppermute | solution.py:412

commit v6 on v5

--- a/solution.py
+++ b/solution.py
@@ -275,13 +275,10 @@
     return ranked(flags[:ciphers]), ranked(flags[ciphers:]), flags[:ciphers]
 
 
-def finish_kernel(ranks, blocks, groups, requests, modulus, local, *refs):
-    part = None
-    if len(refs) == 5:
-        part, _, out, done, sems = refs
-    else:
-        out, done, sems = refs
-    polys = out.shape[1]
+def finish_kernel(ranks, blocks, groups, pieces, tailed, requests, modulus, local, *refs):
+    parts, (out, done, sems) = refs[:pieces], refs[-3:]
+    tails = refs[pieces] if tailed else None
+    polys, _, columns = out.shape[1:]
     ours, theirs, _ = orders_of(requests, groups)
     stores = []
     for at, rank in enumerate(ranks):
@@ -295,9 +292,15 @@
                 total = local[0, poly, rows, :] * weights[0]
                 for slot in range(1, CAP):
                     total = total + local[slot, poly, rows, :] * weights[slot]
-                if part is not None:
-                    total = total + part[0, poly]
-                done[at, poly, here, :] = reduce_mod(total, wide) / wide
+                if pieces:
+                    total = total + parts[which][0, poly]
+                if tailed:
+                    last = columns - WIDEST
+                    wrapped = total[:, last:] + tails[0, poly, here, :]
+                    done[at, poly, here, pl.ds(0, last)] = reduce_mod(total[:, :last], wide) / wide
+                    done[at, poly, here, pl.ds(last, WIDEST)] = reduce_mod(wrapped, wide) / wide
+                else:
+                    done[at, poly, here, :] = reduce_mod(total, wide) / wide
                 stores.append(
                     pltpu.make_async_copy(done.at[at, poly, here], out.at[cipher, poly, rows], sems.at[len(stores)])
                 )
@@ -306,22 +309,25 @@
         store.wait()
 
 
-def finish(local, requests, modulus, ciphers, ranks, blocks, part=None, before=None):
+def finish(local, requests, modulus, ciphers, ranks, blocks, parts=(), before=None, tails=None):
     _, polys, _, columns = local.shape
     hbm = pl.BlockSpec(memory_space=pltpu.HBM)
     limbs = modulus.shape[0]
     work = len(ranks) * polys * len(blocks) * ROWS * columns
-    more = [] if part is None else [part, before]
+    more = [*parts] + ([] if tails is None else [tails])
+    specs = [VMEM] * (3 + len(more))
+    if before is not None:
+        more, specs = more + [before], specs + [hbm]
     return pl.pallas_call(
-        functools.partial(finish_kernel, ranks, blocks, lax.axis_size("grp")),
+        functools.partial(finish_kernel, ranks, blocks, lax.axis_size("grp"), len(parts), tails is not None),
         out_shape=jax.ShapeDtypeStruct((ciphers, polys, limbs, columns), jnp.float32),
-        in_specs=[VMEM, VMEM, VMEM] + ([] if part is None else [VMEM, hbm]),
+        in_specs=specs,
         out_specs=hbm,
         scratch_shapes=[
             pltpu.VMEM((len(ranks), polys, len(blocks) * ROWS, columns), jnp.float32),
             pltpu.SemaphoreType.DMA((len(ranks) * polys * len(blocks),)),
         ],
-        input_output_aliases={} if part is None else {4: 0},
+        input_output_aliases={} if before is None else {len(specs) - 1: 0},
         compiler_params=pltpu.CompilerParams(vmem_limit_bytes=8 << 20),
         cost_estimate=pl.CostEstimate(flops=20 * work, transcendentals=0, bytes_accessed=12 * work),
         name="finish",
@@ -363,22 +369,22 @@
     key_count = keys.shape[0]
     both = [(0, 1), (1, 0)]
     turns = [(slot, block) for slot in slots for block in blocks]
-    picked = {turns[0]: gather(digits, requests, 1, (turns[0],), 4)[0]}
+    picked = {turns[0]: gather(digits, requests, 1, (turns[0],))[0]}
     picked.update(zip(turns[1:], gather(digits, requests, 1, tuple(turns[1:]))))
     sent = {}
     for block in blocks:
         sent[0, block] = lax.ppermute(picked[0, block], "grp", both)
     asked = shifted(requests, "grp", 1)
     tail, resident = products(digits, keys, requests, rotations, modulus, slots, blocks, True, True)
-    arrived = shifted(tail, "limb", -1)
-    local = add_tail(resident, arrived)
     me = lax.axis_index("grp")
     rightward = jnp.where(me == 0, requests, asked)[:, key_count:]
     leftward = jnp.where(me == 0, asked, requests)[:, :key_count]
-    two_right = jnp.sum(jnp.max(rightward, axis=1)) > 1
-    two_left = jnp.sum(jnp.max(leftward, axis=1)) > 1
+    base = digits.shape[0] + 1
+    counts = jnp.sum(jnp.max(rightward, axis=1) + base * jnp.max(leftward, axis=1))
+    two_right = counts % base > 1
+    two_left = counts // base > 1
     case = jnp.where(two_right == two_left, 0, jnp.where(two_right, 1, 2))
-    ahead = remote(sent[0, 0], keys, asked, rotations, modulus, 0, 0)
+    ahead = joined(*remote(sent[0, 0], keys, asked, rotations, modulus, 0, 0))
 
     def branch(pairs):
         def run(*operands):
@@ -387,31 +393,53 @@
         return run
 
     branches = [branch(pairs) for pairs in (both, [(0, 1)], [(1, 0)])]
-    operands = (ahead, [picked[turn] for turn in turns[len(blocks) :]], [sent[0, block] for block in blocks[1:]], local)
+    operands = (ahead, [picked[turn] for turn in turns[len(blocks) :]], [sent[0, block] for block in blocks[1:]], tail, resident)
     return lax.switch(case, branches, *operands, keys, requests, asked, rotations, modulus)
 
 
 def remote(arrived, keys, asked, rotations, modulus, slot, block):
-    tail, resident = products(arrived[None], keys, asked, rotations, modulus, (slot,), (block,), False, slot == 0)
+    return products(arrived[None], keys, asked, rotations, modulus, (slot,), (block,), False, slot == 0)
+
+
+def joined(tail, resident):
     wrapped = shifted(tail, "limb", -1)
     return add_tail(resident, wrapped)
 
 
-def exchange(pairs, ahead, picked, arrived, local, keys, requests, asked, rotations, modulus):
+def exchange(pairs, ahead, picked, arrived, tail, resident, keys, requests, asked, rotations, modulus):
     ciphers = requests.shape[0]
-    blocks = local.shape[2] // ROWS
+    blocks = resident.shape[2] // ROWS
     turns = [(slot, block) for slot in range(CAP) for block in range(blocks)]
     sent = dict(zip(turns[1:blocks], arrived))
     for (slot, block), piece in zip(turns[blocks:], picked):
         sent[slot, block] = lax.ppermute(piece, "grp", pairs[slot])
+    local = joined(tail, resident)
     result = finish(local, requests, modulus, ciphers, tuple(range(CAP, ciphers)), tuple(range(blocks)))
     back = {}
+    late = []
     for turn in turns:
         slot, block = turn
-        whole = ahead if turn == turns[0] else remote(sent[turn], keys, asked, rotations, modulus, slot, block)
-        back[turn] = lax.ppermute(whole, "grp", [(target, source) for source, target in pairs[slot]])
+        ways = [(target, source) for source, target in pairs[slot]]
+        if turn == turns[0]:
+            whole = ahead
+        else:
+            tail, whole = remote(sent[turn], keys, asked, rotations, modulus, slot, block)
+            if len(ways) == 2:
+                whole = joined(tail, whole)
+            else:
+                late.append(tail)
+        if len(late) == blocks:
+            tails = lax.ppermute(jnp.concatenate(late, axis=2), "grp", ways)
+            tails = shifted(tails, "limb", -1)
+        back[turn] = lax.ppermute(whole, "grp", ways)
     for slot, block in turns:
-        result = finish(local, requests, modulus, ciphers, (slot,), (block,), back[slot, block], result)
+        if len(pairs[slot]) == 2:
+            result = finish(local, requests, modulus, ciphers, (slot,), (block,), (back[slot, block],), result)
+    if late:
+        pieces = tuple(back[turn] for turn in turns[blocks:])
+        result = finish(
+            local, requests, modulus, ciphers, (CAP - 1,), tuple(range(blocks)), pieces, result, tails
+        )
     return result
 
 

time: 76.2 us -> 68 us (0.89)
  starting transfers between devices: 29.9 us -> 23.5 us
  waiting for transfers between devices: 20.9 us -> 16.9 us
  Pallas kernels: 21.8 us -> 24 us
    ppermute x6 -> x5, starting transfers between devices: 18.7 us -> 8.37 us  [shifted(): return lax.ppermute(value, axis, pairs)]
    ppermute x6 -> x5, waiting for transfers between devices: 5.71 us -> 0.17 us  [shifted(): return lax.ppermute(value, axis, pairs)]
    ppermute x4 -> x5, starting transfers between devices: 5.34 us -> 7.47 us  [the longest x4 6.17 us: exchange(): back[turn] = lax.ppermute(whole, 'grp', ways)]
    pallas_call x5, Pallas kernels: 11.7 us -> 13.7 us  [products(): pl.pallas_call(functools.partial(products_kernel, slots, blocks, local, l...]
    ppermute x2, starting transfers between devices: 3.35 us -> 5.04 us  [key_switch_pair(): sent[0, block] = lax.ppermute(picked[0, block], 'grp', both)]
    ppermute x2, waiting for transfers between devices: 6.2 us -> 7.65 us  [exchange(): sent[slot, block] = lax.ppermute(piece, 'grp', pairs[slot])]
    pallas_call x2, Pallas kernels: 4.67 us -> 5.7 us  [gather(): pl.pallas_call(functools.partial(gather_kernel, wanted, cuts, steps, lax....]
    pallas_call x5 -> x4, Pallas kernels: 5.37 us -> 4.56 us  [finish(): pl.pallas_call(functools.partial(finish_kernel, ranks, blocks, lax.axis_s...]
  transfers between devices with their start and end apart: 14 -> 14, of which waited for: 7 -> 4; matrix products, arithmetic and copies ran while one was open for 2% -> 1% of each run, Pallas kernels for 25% -> 30%
where the time goes in v6:
time: 68 us; the launch traced here: 67.6 us
  Pallas kernels  24 us (35%)
  starting transfers between devices  23.5 us (35%)
  waiting for transfers between devices  16.9 us (25%)
  between operations  2.09 us (3%)
  other arithmetic  0.84 us (1%)
    pallas_call x5, Pallas kernels, products(): pl.pallas_call(functools.partial(products_kernel, slots, blocks, local, l...  13.7 us
    ppermute x1, waiting for transfers between devices, exchange(): tails = lax.ppermute(jnp.concatenate(late, axis=2), 'grp', ways)  9.07 us
    ppermute x5, starting transfers between devices, shifted(): return lax.ppermute(value, axis, pairs)  8.37 us
    ppermute x2, waiting for transfers between devices, exchange(): sent[slot, block] = lax.ppermute(piece, 'grp', pairs[slot])  7.65 us
    ppermute x4, starting transfers between devices, exchange(): back[turn] = lax.ppermute(whole, 'grp', ways)  6.17 us
    pallas_call x2, Pallas kernels, gather(): pl.pallas_call(functools.partial(gather_kernel, wanted, cuts, steps, lax....  5.7 us
    ppermute x2, starting transfers between devices, key_switch_pair(): sent[0, block] = lax.ppermute(picked[0, block], 'grp', both)  5.04 us
    pallas_call x4, Pallas kernels, finish(): pl.pallas_call(functools.partial(finish_kernel, ranks, blocks, lax.axis_s...  4.56 us
  transfers between devices with their start and end apart: 14, of which 4 were waited for; matrix products, arithmetic and copies ran while one was open for 1% of the time, Pallas kernels for 30%

profile of v6, /device:TPU:0, one launch (start us, length us, event | category | flops | bytes accessed | tf_op | source)
XLA Modules:
  0.0 67.6 jit_solution(2481238434663198451)
XLA Ops:
  0.0 0.0 copy-start.5
  0.0 2.7 %gather_digits.3 = f32[3,8,4096]{2,1,0:T(8,128)} custom-call(s32[4,8]{1,0:T(4,128)} %requests.5, f32[4,3,16,4096]{3,2,1,0:T(8,128)} %digits.5), custom_call_target="tpu_custom_call" | custom-call | bytes 786432 | tf_op jit(solution)/shard_map/gather_digits/pallas_call | solution.py:71
  2.7 0.0 copy-start.10
  2.7 0.0 copy-start
  2.7 3.0 %collective-permute-start.32 = (f32[3,8,4096]{2,1,0:T(8,128)}, f32[3,8,4096]{2,1,0:T(8,128)S(1)}, u32[]{:S(2)}, u32[]{:S(2)}) collective-permute-start(f32[3,8,4096]{2,1,0:T(8,128)} %gather_digits.3), channel_id=1, source_target_pairs={{0,16},{16,0},{1,17},{17,1},{2,18},{18,2},{3,19},{19,3},{4,20},{20... | collective-permute-start | bytes 1179656 | tf_op jit(solution)/shard_map/ppermute | solution.py:376
  5.7 0.0 copy-done.5
  5.7 0.1 collective-permute-start.30
  5.8 3.0 %gather_digits.2 = (f32[3,8,4096]{2,1,0:T(8,128)}, f32[3,8,4096]{2,1,0:T(8,128)}, f32[3,8,4096]{2,1,0:T(8,128)}) custom-call(s32[4,8]{1,0:T(4,128)S(1)} %copy-done.5, f32[4,3,16,4096]{3,2,1,0:T(8,128)} %digits.5), custom_call_target="tpu_custom_call" | custom-call | bytes 2359296 | tf_op jit(solution)/shard_map/gather_digits/pallas_call | solution.py:71
  8.9 2.0 %collective-permute-start.31 = (f32[3,8,4096]{2,1,0:T(8,128)}, f32[3,8,4096]{2,1,0:T(8,128)}, u32[]{:S(2)}, u32[]{:S(2)}) collective-permute-start(f32[3,8,4096]{2,1,0:T(8,128)} %get-tuple-element.137), channel_id=1, source_target_pairs={{0,16},{16,0},{1,17},{17,1},{2,18},{18,2},{3,19},{19,3},{4,20},{20... | collective-permute-start | bytes 1179656 | tf_op jit(solution)/shard_map/ppermute | solution.py:376
  10.9 0.0 copy-done.10
  10.9 0.1 broadcast_in_dim.36.modulus_ref
  11.0 0.0 copy-done
  11.0 4.8 %products.20 = (f32[2,2,16,512]{3,2,1,0:T(8,128)}, f32[2,2,16,4096]{3,2,1,0:T(8,128)}) custom-call(s32[4,8]{1,0:T(4,128)S(1)} %copy-done.5, s32[8]{0:T(128)} %rotations.3, f32[4,3,16,4096]{3,2,1,0:T(8,128)S(1)} %copy-done, f32[4,3,2,16,4096]{4,3,2,1,0:T(8,128)} %keys.3, f32[16,128]{1,0:T(8,128)S(1)} %broadcast_in_dim.36.modulus_ref), custom_call_target="tpu_custom_call" | custom-call | flops 20971520 | bytes 8912896 | tf_op jit(solution)/shard_map/products/pallas_call | solution.py:175
  15.8 0.2 collective-permute-done.30.requests
  16.0 0.2 slice_reduce_fusion
  16.1 0.0 collective-permute-done.32
  16.2 0.0 copy-start.4
  16.2 0.0 copy-start.6
  16.2 0.0 copy-start.7
  16.2 0.0 copy-start.8
  16.2 0.0 copy-start.9
  16.2 3.0 %products.21 = (f32[1,2,8,512]{3,2,1,0:T(8,128)S(1)}, f32[1,2,8,4096]{3,2,1,0:T(8,128)S(1)}) custom-call(s32[4,8]{1,0:T(4,128)S(1)} %collective-permute-done.30.requests, s32[8]{0:T(128)} %rotations.3, f32[1,3,8,4096]{3,2,1,0:T(8,128)S(1)} %bitcast.10, f32[4,3,2,16,4096]{4,3,2,1,0:T(8,128)} %keys.3, f32[16,128]{1,0:T(8,128)S(1)} %broadcast_in_dim.36.modulus_ref), custom_call_target="tpu_custom_call" | custom-call | flops 5242880 | bytes 3801088 | tf_op jit(solution)/shard_map/products/pallas_call | solution.py:175
  19.2 3.1 %collective-permute-start.33 = (f32[1,2,8,512]{3,2,1,0:T(8,128)S(1)}, f32[1,2,8,512]{3,2,1,0:T(8,128)S(1)}, u32[]{:S(2)}, u32[]{:S(2)}) collective-permute-start(f32[1,2,8,512]{3,2,1,0:T(8,128)S(1)} %get-tuple-element.138), channel_id=1, source_target_pairs={{0,15},{1,0},{2,1},{3,2},{4,3},{5,4},{6,5},{7,6},{8,7},{9,8},{10,9... | collective-permute-start | bytes 98312 | tf_op jit(solution)/shard_map/ppermute | solution.py:22
  22.3 0.6 add_reduce_fusion
  24.9 0.0 collective-permute-done.33.arrived
  24.9 0.0 collective-permute-done.31
  24.9 0.0 copy-done.4
  24.9 0.0 copy-done.6
  24.9 0.0 copy-done.7
  24.9 0.0 copy-done.8
  24.9 0.0 copy-done.9
  25.0 42.7 %conditional.1 = (f32[4,2,16,4096]{3,2,1,0:T(8,128)}) conditional(s32[]{:T(128)} %clamp.3, (f32[2,2,16,512]{3,2,1,0:T(8,128)S(1)}, f32[2,2,16,4096]{3,2,1,0:T(8,128)S(1)}, f32[3,8,4096]{2,1,0:T(8,128)S(1)}, s32[4,8]{1,0:T(4,128)S(1)}, s32[8]{0:T(128)S(1)}, /*index=5*/f32[4,3,2,16,4096]{4,3,2,1,0:T(8,128)}, f32[16,128]{1,0:T(8,128)S(1)}, ...), branch_computations={%region_3.4_spmd, %region_4.5_spmd, %region_5.6_spmd} | conditional | flops 26230784 | bytes 51511732 | solution.py:397
  25.0 1.3 %collective-permute-start.21 = (f32[3,8,4096]{2,1,0:T(8,128)S(1)}, f32[3,8,4096]{2,1,0:T(8,128)S(1)}, u32[]{:S(2)}, u32[]{:S(2)}) collective-permute-start(f32[3,8,4096]{2,1,0:T(8,128)S(1)} %get-tuple-element.115), channel_id=1, source_target_pairs={{16,0},{17,1},{18,2},{19,3},{20,4},{21,5},{22,6},{23,7},{24,8},{25... | collective-permute-start | bytes 1179656 | tf_op jit(solution)/shard_map/cond/branch_2_fun/ppermute | solution.py:415
  26.3 1.3 %collective-permute-start.23 = (f32[3,8,4096]{2,1,0:T(8,128)S(1)}, f32[3,8,4096]{2,1,0:T(8,128)S(1)}, u32[]{:S(2)}, u32[]{:S(2)}) collective-permute-start(f32[3,8,4096]{2,1,0:T(8,128)S(1)} %get-tuple-element.118), channel_id=1, source_target_pairs={{16,0},{17,1},{18,2},{19,3},{20,4},{21,5},{22,6},{23,7},{24,8},{25... | collective-permute-start | bytes 1179656 | tf_op jit(solution)/shard_map/cond/branch_2_fun/ppermute | solution.py:415
  27.6 0.0 copy-start.3
  27.6 3.7 %products.19 = (f32[1,2,8,512]{3,2,1,0:T(8,128)S(1)}, f32[1,2,8,4096]{3,2,1,0:T(8,128)S(1)}) custom-call(s32[4,8]{1,0:T(4,128)S(1)} %get-tuple-element.113.requests, s32[8]{0:T(128)S(1)} %get-tuple-element.114.rotations, f32[1,3,8,4096]{3,2,1,0:T(8,128)} %bitcast.8.digits, f32[4,3,2,16,4096]{4,3,2,1,0:T(8,128)} %get-tuple-element.116.keys, ...), custom_call_target="tpu_custom_call" | custom-call | flops 5242880 | bytes 3801088 | tf_op jit(solution)/shard_map/cond/branch_2_fun/products/pallas_call | solution.py:175
  31.3 3.5 %collective-permute-start.27 = (f32[1,2,8,512]{3,2,1,0:T(8,128)S(1)}, f32[1,2,8,512]{3,2,1,0:T(8,128)S(1)}, u32[]{:S(2)}, u32[]{:S(2)}) collective-permute-start(f32[1,2,8,512]{3,2,1,0:T(8,128)S(1)} %get-tuple-element.123), channel_id=1, source_target_pairs={{0,15},{1,0},{2,1},{3,2},{4,3},{5,4},{6,5},{7,6},{8,7},{9,8},{10,9... | collective-permute-start | bytes 98312 | tf_op jit(solution)/shard_map/cond/branch_2_fun/ppermute | solution.py:22
  34.8 0.2 collective-permute-start.20
  35.0 2.4 %collective-permute-start.29 = (f32[1,2,8,4096]{3,2,1,0:T(8,128)S(1)}, f32[1,2,8,4096]{3,2,1,0:T(8,128)S(1)}, u32[]{:S(2)}, u32[]{:S(2)}) collective-permute-start(f32[1,2,8,4096]{3,2,1,0:T(8,128)S(1)} %get-tuple-element.125), channel_id=1, source_target_pairs={{16,0},{0,16},{17,1},{1,17},{18,2},{2,18},{19,3},{3,19},{20,4},{4,... | collective-permute-start | bytes 786440 | tf_op jit(solution)/shard_map/cond/branch_2_fun/ppermute | solution.py:434
  37.4 0.0 collective-permute-done.27.arrived
  37.4 1.1 %collective-permute-start.28 = (f32[1,2,8,4096]{3,2,1,0:T(8,128)S(1)}, f32[1,2,8,4096]{3,2,1,0:T(8,128)S(1)}, u32[]{:S(2)}, u32[]{:S(2)}) collective-permute-start(f32[1,2,8,4096]{3,2,1,0:T(8,128)S(1)} %add_tail.16), channel_id=1, source_target_pairs={{16,0},{0,16},{17,1},{1,17},{18,2},{2,18},{19,3},{3,19},{20,4},{4,... | collective-permute-start | bytes 786440 | tf_op jit(solution)/shard_map/cond/branch_2_fun/ppermute | solution.py:434
  38.5 0.3 collective-permute-done.21
  38.9 0.0 copy-done.3
  38.9 1.1 %products.17 = (f32[1,2,8,512]{3,2,1,0:T(8,128)S(1)}, f32[1,2,8,4096]{3,2,1,0:T(8,128)S(1)}) custom-call(s32[4,8]{1,0:T(4,128)S(1)} %get-tuple-element.113.requests, s32[8]{0:T(128)S(1)} %get-tuple-element.114.rotations, f32[1,3,8,4096]{3,2,1,0:T(8,128)S(1)} %bitcast.14, f32[4,3,2,16,4096]{4,3,2,1,0:T(8,128)S(1)} %copy-done.3, ...), custom_call_target="tpu_custom_call" | custom-call | flops 5242880 | bytes 3801088 | tf_op jit(solution)/shard_map/cond/branch_2_fun/products/pallas_call | solution.py:175
  40.0 7.3 %collective-permute-done.23 = f32[3,8,4096]{2,1,0:T(8,128)S(1)} collective-permute-done((f32[3,8,4096]{2,1,0:T(8,128)S(1)}, f32[3,8,4096]{2,1,0:T(8,128)S(1)}, u32[]{:S(2)}, u32[]{:S(2)}) %collective-permute-start.23) | collective-permute-done | bytes 393248 | tf_op jit(solution)/shard_map/cond/branch_2_fun/ppermute | solution.py:415
  47.3 1.1 %products.18 = (f32[1,2,8,512]{3,2,1,0:T(8,128)S(1)}, f32[1,2,8,4096]{3,2,1,0:T(8,128)S(1)}) custom-call(s32[4,8]{1,0:T(4,128)S(1)} %get-tuple-element.113.requests, s32[8]{0:T(128)S(1)} %get-tuple-element.114.rotations, f32[1,3,8,4096]{3,2,1,0:T(8,128)S(1)} %bitcast.12, f32[4,3,2,16,4096]{4,3,2,1,0:T(8,128)S(1)} %copy-done.3, ...), custom_call_target="tpu_custom_call" | custom-call | flops 5242880 | bytes 3801088 | tf_op jit(solution)/shard_map/cond/branch_2_fun/products/pallas_call | solution.py:175
  48.4 1.3 %collective-permute-start.22 = (f32[1,2,8,4096]{3,2,1,0:T(8,128)S(1)}, f32[1,2,8,4096]{3,2,1,0:T(8,128)S(1)}, u32[]{:S(2)}, u32[]{:S(2)}) collective-permute-start(f32[1,2,8,4096]{3,2,1,0:T(8,128)S(1)} %get-tuple-element.117), channel_id=1, source_target_pairs={{0,16},{1,17},{2,18},{3,19},{4,20},{5,21},{6,22},{7,23},{8,24},{9,... | collective-permute-start | bytes 786440 | tf_op jit(solution)/shard_map/cond/branch_2_fun/ppermute | solution.py:434
  49.7 1.3 %collective-permute-start.24 = (f32[1,2,8,4096]{3,2,1,0:T(8,128)S(1)}, f32[1,2,8,4096]{3,2,1,0:T(8,128)S(1)}, u32[]{:S(2)}, u32[]{:S(2)}) collective-permute-start(f32[1,2,8,4096]{3,2,1,0:T(8,128)S(1)} %get-tuple-element.119), channel_id=1, source_target_pairs={{0,16},{1,17},{2,18},{3,19},{4,20},{5,21},{6,22},{7,23},{8,24},{9,... | collective-permute-start | bytes 786440 | tf_op jit(solution)/shard_map/cond/branch_2_fun/ppermute | solution.py:434
  51.1 0.0 collective-permute-done.20.arrived
  51.1 1.3 %collective-permute-start.25 = (f32[1,2,16,512]{3,2,1,0:T(8,128)S(1)}, f32[1,2,16,512]{3,2,1,0:T(8,128)S(1)}, u32[]{:S(2)}, u32[]{:S(2)}) collective-permute-start(f32[1,2,16,512]{3,2,1,0:T(8,128)S(1)} %pad_maximum_fusion.1), channel_id=1, source_target_pairs={{0,16},{1,17},{2,18},{3,19},{4,20},{5,21},{6,22},{7,23},{8,24},{9,... | collective-permute-start | bytes 196616 | tf_op jit(solution)/shard_map/cond/branch_2_fun/ppermute | solution.py:432
  52.4 9.1 %collective-permute-done.25 = f32[1,2,16,512]{3,2,1,0:T(8,128)S(1)} collective-permute-done((f32[1,2,16,512]{3,2,1,0:T(8,128)S(1)}, f32[1,2,16,512]{3,2,1,0:T(8,128)S(1)}, u32[]{:S(2)}, u32[]{:S(2)}) %collective-permute-start.25) | collective-permute-done | bytes 65568 | tf_op jit(solution)/shard_map/cond/branch_2_fun/ppermute | solution.py:432
  61.4 1.5 %collective-permute-start.26 = (f32[1,2,16,512]{3,2,1,0:T(8,128)S(1)}, f32[1,2,16,512]{3,2,1,0:T(8,128)S(1)}, u32[]{:S(2)}, u32[]{:S(2)}) collective-permute-start(f32[1,2,16,512]{3,2,1,0:T(8,128)S(1)} %collective-permute-done.25), channel_id=1, source_target_pairs={{0,15},{1,0},{2,1},{3,2},{4,3},{5,4},{6,5},{7,6},{8,7},{9,8},{10,9... | collective-permute-start | bytes 196616 | tf_op jit(solution)/shard_map/cond/branch_2_fun/ppermute | solution.py:22
  63.0 1.4 %finish.22.refs_1_ = f32[4,2,16,4096]{3,2,1,0:T(8,128)} custom-call(s32[4,8]{1,0:T(4,128)S(1)} %get-tuple-element.109.requests, f32[16,128]{1,0:T(8,128)S(1)} %get-tuple-element.110.modulus_ref.modulus, f32[2,2,16,4096]{3,2,1,0:T(8,128)S(1)} %add_tail.15.local), custom_call_target="tpu_custom_call" | custom-call | flops 5242880 | bytes 3145728 | tf_op jit(solution)/shard_map/cond/branch_2_fun/finish/pallas_call | solution.py:321
  64.4 0.0 collective-permute-done.29.refs_0_
  64.4 1.0 %finish.23.refs_1_ = f32[4,2,16,4096]{3,2,1,0:T(8,128)} custom-call(s32[4,8]{1,0:T(4,128)S(1)} %get-tuple-element.109.requests, f32[16,128]{1,0:T(8,128)S(1)} %get-tuple-element.110.modulus_ref.modulus, f32[2,2,16,4096]{3,2,1,0:T(8,128)S(1)} %add_tail.15.local, ...), custom_call_target="tpu_custom_call", output_to_operand_aliasing={{}: (4, {})} | custom-call | flops 1310720 | bytes 786432 | tf_op jit(solution)/shard_map/cond/branch_2_fun/finish/pallas_call | solution.py:321
  65.4 0.0 collective-permute-done.28.refs_0_
  65.5 1.0 %finish.24.refs_3_ = f32[4,2,16,4096]{3,2,1,0:T(8,128)} custom-call(s32[4,8]{1,0:T(4,128)S(1)} %get-tuple-element.109.requests, f32[16,128]{1,0:T(8,128)S(1)} %get-tuple-element.110.modulus_ref.modulus, f32[2,2,16,4096]{3,2,1,0:T(8,128)S(1)} %add_tail.15.local, ...), custom_call_target="tpu_custom_call", output_to_operand_aliasing={{}: (4, {})} | custom-call | flops 1310720 | bytes 786432 | tf_op jit(solution)/shard_map/cond/branch_2_fun/finish/pallas_call | solution.py:321
  66.5 0.0 collective-permute-done.26.refs_2_
  66.5 0.0 collective-permute-done.22.refs_0_
  66.5 0.0 collective-permute-done.24.refs_1_
  66.5 1.1 %finish.25 = f32[4,2,16,4096]{3,2,1,0:T(8,128)} custom-call(s32[4,8]{1,0:T(4,128)S(1)} %get-tuple-element.109.requests, f32[16,128]{1,0:T(8,128)S(1)} %get-tuple-element.110.modulus_ref.modulus, f32[2,2,16,4096]{3,2,1,0:T(8,128)S(1)} %add_tail.15.local, f32[1,2,8,4096]{3,2,1,0:T(8,128)S(1)} %collective-permute-done.22.refs_0_, ...), custom_call_target="tpu_custom_call", output_to_operand_aliasing={{}: (6, {})} | custom-call | flops 2621440 | bytes 1572864 | tf_op jit(solution)/shard_map/cond/branch_2_fun/finish/pallas_call | solution.py:321
  (6 shorter events, 0.1 us)
Async XLA Ops:
  0.0 5.7 %copy-start.5 = (s32[4,8]{1,0:T(4,128)S(1)}, s32[4,8]{1,0:T(4,128)}, u32[]{:S(2)}) copy-start(s32[4,8]{1,0:T(4,128)} %requests.5) | copy-start | bytes 388
  2.7 8.2 %copy-start.10 = (s32[16]{0:T(128)S(1)}, s32[16]{0:T(128)}, u32[]{:S(2)}) copy-start(s32[16]{0:T(128)} %param.12) | copy-start | bytes 196
  2.7 8.3 %copy-start = (f32[4,3,16,4096]{3,2,1,0:T(8,128)S(1)}, f32[4,3,16,4096]{3,2,1,0:T(8,128)}, u32[]{:S(2)}) copy-start(f32[4,3,16,4096]{3,2,1,0:T(8,128)} %digits.5) | copy-start | bytes 9437188
  2.7 13.4 %collective-permute-start.32 = (f32[3,8,4096]{2,1,0:T(8,128)}, f32[3,8,4096]{2,1,0:T(8,128)S(1)}, u32[]{:S(2)}, u32[]{:S(2)}) collective-permute-start(f32[3,8,4096]{2,1,0:T(8,128)} %gather_digits.3), channel_id=1, source_target_pairs={{0,16},{16,0},{1,17},{17,1},{2,18},{18,2},{3,19},{19,3},{4,20},{20... | collective-permute-start | bytes 1179656 | tf_op jit(solution)/shard_map/ppermute | solution.py:376
  5.7 10.2 %collective-permute-start.30 = (s32[4,8]{1,0:T(4,128)S(1)}, s32[4,8]{1,0:T(4,128)S(1)}, u32[]{:S(2)}, u32[]{:S(2)}) collective-permute-start(s32[4,8]{1,0:T(4,128)S(1)} %copy-done.5), channel_id=1, source_target_pairs={{0,16},{16,0},{1,17},{17,1},{2,18},{18,2},{3,19},{19,3},{4,20},{20... | collective-permute-start | bytes 392 | tf_op jit(solution)/shard_map/ppermute | solution.py:22
  8.9 16.0 %collective-permute-start.31 = (f32[3,8,4096]{2,1,0:T(8,128)}, f32[3,8,4096]{2,1,0:T(8,128)}, u32[]{:S(2)}, u32[]{:S(2)}) collective-permute-start(f32[3,8,4096]{2,1,0:T(8,128)} %get-tuple-element.137), channel_id=1, source_target_pairs={{0,16},{16,0},{1,17},{17,1},{2,18},{18,2},{3,19},{19,3},{4,20},{20... | collective-permute-start | bytes 1179656 | tf_op jit(solution)/shard_map/ppermute | solution.py:376
  16.2 8.8 %copy-start.4 = (f32[2,2,16,4096]{3,2,1,0:T(8,128)S(1)}, f32[2,2,16,4096]{3,2,1,0:T(8,128)}, u32[]{:S(2)}) copy-start(f32[2,2,16,4096]{3,2,1,0:T(8,128)} %get-tuple-element.134) | copy-start | bytes 3145732
  16.2 8.8 %copy-start.6 = (s32[8]{0:T(128)S(1)}, s32[8]{0:T(128)}, u32[]{:S(2)}) copy-start(s32[8]{0:T(128)} %rotations.3) | copy-start | bytes 100
  16.2 8.8 %copy-start.7 = (f32[3,8,4096]{2,1,0:T(8,128)S(1)}, f32[3,8,4096]{2,1,0:T(8,128)}, u32[]{:S(2)}) copy-start(f32[3,8,4096]{2,1,0:T(8,128)} %get-tuple-element.136) | copy-start | bytes 1179652
  16.2 8.8 %copy-start.8 = (f32[3,8,4096]{2,1,0:T(8,128)S(1)}, f32[3,8,4096]{2,1,0:T(8,128)}, u32[]{:S(2)}) copy-start(f32[3,8,4096]{2,1,0:T(8,128)} %get-tuple-element.135) | copy-start | bytes 1179652
  16.2 8.8 %copy-start.9 = (f32[2,2,16,512]{3,2,1,0:T(8,128)S(1)}, f32[2,2,16,512]{3,2,1,0:T(8,128)}, u32[]{:S(2)}) copy-start(f32[2,2,16,512]{3,2,1,0:T(8,128)} %get-tuple-element.133) | copy-start | bytes 393220
  19.2 5.6 %collective-permute-start.33 = (f32[1,2,8,512]{3,2,1,0:T(8,128)S(1)}, f32[1,2,8,512]{3,2,1,0:T(8,128)S(1)}, u32[]{:S(2)}, u32[]{:S(2)}) collective-permute-start(f32[1,2,8,512]{3,2,1,0:T(8,128)S(1)} %get-tuple-element.138), channel_id=1, source_target_pairs={{0,15},{1,0},{2,1},{3,2},{4,3},{5,4},{6,5},{7,6},{8,7},{9,8},{10,9... | collective-permute-start | bytes 98312 | tf_op jit(solution)/shard_map/ppermute | solution.py:22
  25.0 13.9 %collective-permute-start.21 = (f32[3,8,4096]{2,1,0:T(8,128)S(1)}, f32[3,8,4096]{2,1,0:T(8,128)S(1)}, u32[]{:S(2)}, u32[]{:S(2)}) collective-permute-start(f32[3,8,4096]{2,1,0:T(8,128)S(1)} %get-tuple-element.115), channel_id=1, source_target_pairs={{16,0},{17,1},{18,2},{19,3},{20,4},{21,5},{22,6},{23,7},{24,8},{25... | collective-permute-start | bytes 1179656 | tf_op jit(solution)/shard_map/cond/branch_2_fun/ppermute | solution.py:415
  26.3 21.0 %collective-permute-start.23 = (f32[3,8,4096]{2,1,0:T(8,128)S(1)}, f32[3,8,4096]{2,1,0:T(8,128)S(1)}, u32[]{:S(2)}, u32[]{:S(2)}) collective-permute-start(f32[3,8,4096]{2,1,0:T(8,128)S(1)} %get-tuple-element.118), channel_id=1, source_target_pairs={{16,0},{17,1},{18,2},{19,3},{20,4},{21,5},{22,6},{23,7},{24,8},{25... | collective-permute-start | bytes 1179656 | tf_op jit(solution)/shard_map/cond/branch_2_fun/ppermute | solution.py:415
  27.6 11.3 %copy-start.3 = (f32[4,3,2,16,4096]{4,3,2,1,0:T(8,128)S(1)}, f32[4,3,2,16,4096]{4,3,2,1,0:T(8,128)}, u32[]{:S(2)}) copy-start(f32[4,3,2,16,4096]{4,3,2,1,0:T(8,128)} %get-tuple-element.116.keys) | copy-start | bytes 18874372 | tf_op jit(solution)/shard_map/cond
  31.3 6.1 %collective-permute-start.27 = (f32[1,2,8,512]{3,2,1,0:T(8,128)S(1)}, f32[1,2,8,512]{3,2,1,0:T(8,128)S(1)}, u32[]{:S(2)}, u32[]{:S(2)}) collective-permute-start(f32[1,2,8,512]{3,2,1,0:T(8,128)S(1)} %get-tuple-element.123), channel_id=1, source_target_pairs={{0,15},{1,0},{2,1},{3,2},{4,3},{5,4},{6,5},{7,6},{8,7},{9,8},{10,9... | collective-permute-start | bytes 98312 | tf_op jit(solution)/shard_map/cond/branch_2_fun/ppermute | solution.py:22
  34.8 16.3 %collective-permute-start.20 = (f32[2,2,16,512]{3,2,1,0:T(8,128)S(1)}, f32[2,2,16,512]{3,2,1,0:T(8,128)S(1)}, u32[]{:S(2)}, u32[]{:S(2)}) collective-permute-start(f32[2,2,16,512]{3,2,1,0:T(8,128)S(1)} %get-tuple-element.111), channel_id=1, source_target_pairs={{0,15},{1,0},{2,1},{3,2},{4,3},{5,4},{6,5},{7,6},{8,7},{9,8},{10,9... | collective-permute-start | bytes 393224 | tf_op jit(solution)/shard_map/cond/branch_2_fun/ppermute | solution.py:22
  35.0 29.5 %collective-permute-start.29 = (f32[1,2,8,4096]{3,2,1,0:T(8,128)S(1)}, f32[1,2,8,4096]{3,2,1,0:T(8,128)S(1)}, u32[]{:S(2)}, u32[]{:S(2)}) collective-permute-start(f32[1,2,8,4096]{3,2,1,0:T(8,128)S(1)} %get-tuple-element.125), channel_id=1, source_target_pairs={{16,0},{0,16},{17,1},{1,17},{18,2},{2,18},{19,3},{3,19},{20,4},{4,... | collective-permute-start | bytes 786440 | tf_op jit(solution)/shard_map/cond/branch_2_fun/ppermute | solution.py:434
  37.4 28.0 %collective-permute-start.28 = (f32[1,2,8,4096]{3,2,1,0:T(8,128)S(1)}, f32[1,2,8,4096]{3,2,1,0:T(8,128)S(1)}, u32[]{:S(2)}, u32[]{:S(2)}) collective-permute-start(f32[1,2,8,4096]{3,2,1,0:T(8,128)S(1)} %add_tail.16), channel_id=1, source_target_pairs={{16,0},{0,16},{17,1},{1,17},{18,2},{2,18},{19,3},{3,19},{20,4},{4,... | collective-permute-start | bytes 786440 | tf_op jit(solution)/shard_map/cond/branch_2_fun/ppermute | solution.py:434
  48.4 18.1 %collective-permute-start.22 = (f32[1,2,8,4096]{3,2,1,0:T(8,128)S(1)}, f32[1,2,8,4096]{3,2,1,0:T(8,128)S(1)}, u32[]{:S(2)}, u32[]{:S(2)}) collective-permute-start(f32[1,2,8,4096]{3,2,1,0:T(8,128)S(1)} %get-tuple-element.117), channel_id=1, source_target_pairs={{0,16},{1,17},{2,18},{3,19},{4,20},{5,21},{6,22},{7,23},{8,24},{9,... | collective-permute-start | bytes 786440 | tf_op jit(solution)/shard_map/cond/branch_2_fun/ppermute | solution.py:434
  49.7 16.8 %collective-permute-start.24 = (f32[1,2,8,4096]{3,2,1,0:T(8,128)S(1)}, f32[1,2,8,4096]{3,2,1,0:T(8,128)S(1)}, u32[]{:S(2)}, u32[]{:S(2)}) collective-permute-start(f32[1,2,8,4096]{3,2,1,0:T(8,128)S(1)} %get-tuple-element.119), channel_id=1, source_target_pairs={{0,16},{1,17},{2,18},{3,19},{4,20},{5,21},{6,22},{7,23},{8,24},{9,... | collective-permute-start | bytes 786440 | tf_op jit(solution)/shard_map/cond/branch_2_fun/ppermute | solution.py:434
  51.1 10.4 %collective-permute-start.25 = (f32[1,2,16,512]{3,2,1,0:T(8,128)S(1)}, f32[1,2,16,512]{3,2,1,0:T(8,128)S(1)}, u32[]{:S(2)}, u32[]{:S(2)}) collective-permute-start(f32[1,2,16,512]{3,2,1,0:T(8,128)S(1)} %pad_maximum_fusion.1), channel_id=1, source_target_pairs={{0,16},{1,17},{2,18},{3,19},{4,20},{5,21},{6,22},{7,23},{8,24},{9,... | collective-permute-start | bytes 196616 | tf_op jit(solution)/shard_map/cond/branch_2_fun/ppermute | solution.py:432
  61.4 5.0 %collective-permute-start.26 = (f32[1,2,16,512]{3,2,1,0:T(8,128)S(1)}, f32[1,2,16,512]{3,2,1,0:T(8,128)S(1)}, u32[]{:S(2)}, u32[]{:S(2)}) collective-permute-start(f32[1,2,16,512]{3,2,1,0:T(8,128)S(1)} %collective-permute-done.25), channel_id=1, source_target_pairs={{0,15},{1,0},{2,1},{3,2},{4,3},{5,4},{6,5},{7,6},{8,7},{9,8},{10,9... | collective-permute-start | bytes 196616 | tf_op jit(solution)/shard_map/cond/branch_2_fun/ppermute | solution.py:22

commit v7 on v6

--- a/solution.py
+++ b/solution.py
@@ -78,7 +78,7 @@
         cost_estimate=pl.CostEstimate(
             flops=0, transcendentals=0, bytes_accessed=8 * len(wanted) * parts * ROWS * columns
         ),
-        name="gather_digits",
+        name="gather",
     )(requests, pltpu.with_memory_space_constraint(digits, pltpu.HBM))
 
 
@@ -369,7 +369,7 @@
     key_count = keys.shape[0]
     both = [(0, 1), (1, 0)]
     turns = [(slot, block) for slot in slots for block in blocks]
-    picked = {turns[0]: gather(digits, requests, 1, (turns[0],))[0]}
+    picked = {turns[0]: gather(digits, requests, 1, (turns[0],), 4)[0]}
     picked.update(zip(turns[1:], gather(digits, requests, 1, tuple(turns[1:]))))
     sent = {}
     for block in blocks:
@@ -379,10 +379,10 @@
     me = lax.axis_index("grp")
     rightward = jnp.where(me == 0, requests, asked)[:, key_count:]
     leftward = jnp.where(me == 0, asked, requests)[:, :key_count]
-    base = digits.shape[0] + 1
-    counts = jnp.sum(jnp.max(rightward, axis=1) + base * jnp.max(leftward, axis=1))
-    two_right = counts % base > 1
-    two_left = counts // base > 1
+    bits = digits.shape[0].bit_length()
+    counts = jnp.sum(jnp.max(rightward, axis=1) + (jnp.max(leftward, axis=1) << bits))
+    two_right = counts & ((1 << bits) - 1) > 1
+    two_left = counts >> bits > 1
     case = jnp.where(two_right == two_left, 0, jnp.where(two_right, 1, 2))
     ahead = joined(*remote(sent[0, 0], keys, asked, rotations, modulus, 0, 0))
 

time: 68 us -> 68 us (level)
  transfers between devices with their start and end apart: 14 -> 14, of which waited for: 4 -> 3; matrix products, arithmetic and copies ran while one was open for 1% -> 1% of each run, Pallas kernels for 30% -> 30%
where the time goes in v7:
time: 68 us; the launch traced here: 67.6 us
  starting transfers between devices  24.1 us (35%)
  Pallas kernels  24 us (35%)
  waiting for transfers between devices  16.9 us (25%)
  between operations  1.44 us (2%)
  other arithmetic  0.84 us (1%)
    pallas_call x5, Pallas kernels, products(): pl.pallas_call(functools.partial(products_kernel, slots, blocks, local, l...  13.7 us
    ppermute x1, waiting for transfers between devices, exchange(): tails = lax.ppermute(jnp.concatenate(late, axis=2), 'grp', ways)  9.71 us
    ppermute x5, starting transfers between devices, shifted(): return lax.ppermute(value, axis, pairs)  9.02 us
    ppermute x2, waiting for transfers between devices, exchange(): sent[slot, block] = lax.ppermute(piece, 'grp', pairs[slot])  7 us
    ppermute x4, starting transfers between devices, exchange(): back[turn] = lax.ppermute(whole, 'grp', ways)  6.17 us
    pallas_call x2, Pallas kernels, gather(): pl.pallas_call(functools.partial(gather_kernel, wanted, cuts, steps, lax....  5.69 us
    ppermute x2, starting transfers between devices, key_switch_pair(): sent[0, block] = lax.ppermute(picked[0, block], 'grp', both)  5.04 us
    pallas_call x4, Pallas kernels, finish(): pl.pallas_call(functools.partial(finish_kernel, ranks, blocks, lax.axis_s...  4.56 us
  transfers between devices with their start and end apart: 14, of which 3 were waited for; matrix products, arithmetic and copies ran while one was open for 1% of the time, Pallas kernels for 30%

profile of v7, /device:TPU:0, one launch (start us, length us, event | category | flops | bytes accessed | tf_op | source)
XLA Modules:
  0.0 67.6 jit_solution(15844446286651764799)
XLA Ops:
  0.0 0.0 copy-start.5
  0.0 2.7 %gather.3 = f32[3,8,4096]{2,1,0:T(8,128)} custom-call(s32[4,8]{1,0:T(4,128)} %requests.5, f32[4,3,16,4096]{3,2,1,0:T(8,128)} %digits.5), custom_call_target="tpu_custom_call" | custom-call | bytes 786432 | tf_op jit(solution)/shard_map/gather/pallas_call | solution.py:71
  2.7 0.0 copy-start.10
  2.7 0.0 copy-start
  2.7 3.0 %collective-permute-start.32 = (f32[3,8,4096]{2,1,0:T(8,128)}, f32[3,8,4096]{2,1,0:T(8,128)S(1)}, u32[]{:S(2)}, u32[]{:S(2)}) collective-permute-start(f32[3,8,4096]{2,1,0:T(8,128)} %gather.3), channel_id=1, source_target_pairs={{0,16},{16,0},{1,17},{17,1},{2,18},{18,2},{3,19},{19,3},{4,20},{20... | collective-permute-start | bytes 1179656 | tf_op jit(solution)/shard_map/ppermute | solution.py:376
  5.7 0.0 copy-done.5
  5.7 0.1 collective-permute-start.30
  5.8 3.0 %gather.2 = (f32[3,8,4096]{2,1,0:T(8,128)}, f32[3,8,4096]{2,1,0:T(8,128)}, f32[3,8,4096]{2,1,0:T(8,128)}) custom-call(s32[4,8]{1,0:T(4,128)S(1)} %copy-done.5, f32[4,3,16,4096]{3,2,1,0:T(8,128)} %digits.5), custom_call_target="tpu_custom_call" | custom-call | bytes 2359296 | tf_op jit(solution)/shard_map/gather/pallas_call | solution.py:71
  8.9 2.0 %collective-permute-start.31 = (f32[3,8,4096]{2,1,0:T(8,128)}, f32[3,8,4096]{2,1,0:T(8,128)}, u32[]{:S(2)}, u32[]{:S(2)}) collective-permute-start(f32[3,8,4096]{2,1,0:T(8,128)} %get-tuple-element.137), channel_id=1, source_target_pairs={{0,16},{16,0},{1,17},{17,1},{2,18},{18,2},{3,19},{19,3},{4,20},{20... | collective-permute-start | bytes 1179656 | tf_op jit(solution)/shard_map/ppermute | solution.py:376
  10.9 0.0 copy-done.10
  10.9 0.1 broadcast_in_dim.36.modulus_ref
  10.9 0.0 copy-done
  10.9 4.8 %products.20 = (f32[2,2,16,512]{3,2,1,0:T(8,128)}, f32[2,2,16,4096]{3,2,1,0:T(8,128)}) custom-call(s32[4,8]{1,0:T(4,128)S(1)} %copy-done.5, s32[8]{0:T(128)} %rotations.3, f32[4,3,16,4096]{3,2,1,0:T(8,128)S(1)} %copy-done, f32[4,3,2,16,4096]{4,3,2,1,0:T(8,128)} %keys.3, f32[16,128]{1,0:T(8,128)S(1)} %broadcast_in_dim.36.modulus_ref), custom_call_target="tpu_custom_call" | custom-call | flops 20971520 | bytes 8912896 | tf_op jit(solution)/shard_map/products/pallas_call | solution.py:175
  15.8 0.2 collective-permute-done.30.requests
  15.9 0.2 slice_reduce_fusion
  16.1 0.0 collective-permute-done.32
  16.1 0.0 copy-start.4
  16.2 0.0 copy-start.6
  16.2 0.0 copy-start.7
  16.2 0.0 copy-start.8
  16.2 0.0 copy-start.9
  16.2 3.0 %products.21 = (f32[1,2,8,512]{3,2,1,0:T(8,128)S(1)}, f32[1,2,8,4096]{3,2,1,0:T(8,128)S(1)}) custom-call(s32[4,8]{1,0:T(4,128)S(1)} %collective-permute-done.30.requests, s32[8]{0:T(128)} %rotations.3, f32[1,3,8,4096]{3,2,1,0:T(8,128)S(1)} %bitcast.10, f32[4,3,2,16,4096]{4,3,2,1,0:T(8,128)} %keys.3, f32[16,128]{1,0:T(8,128)S(1)} %broadcast_in_dim.36.modulus_ref), custom_call_target="tpu_custom_call" | custom-call | flops 5242880 | bytes 3801088 | tf_op jit(solution)/shard_map/products/pallas_call | solution.py:175
  19.2 3.1 %collective-permute-start.33 = (f32[1,2,8,512]{3,2,1,0:T(8,128)S(1)}, f32[1,2,8,512]{3,2,1,0:T(8,128)S(1)}, u32[]{:S(2)}, u32[]{:S(2)}) collective-permute-start(f32[1,2,8,512]{3,2,1,0:T(8,128)S(1)} %get-tuple-element.138), channel_id=1, source_target_pairs={{0,15},{1,0},{2,1},{3,2},{4,3},{5,4},{6,5},{7,6},{8,7},{9,8},{10,9... | collective-permute-start | bytes 98312 | tf_op jit(solution)/shard_map/ppermute | solution.py:22
  22.3 0.6 add_reduce_fusion
  24.2 0.0 collective-permute-done.33.arrived
  24.2 0.0 collective-permute-done.31
  24.2 0.0 copy-done.4
  24.3 0.0 copy-done.6
  24.3 0.0 copy-done.7
  24.3 0.0 copy-done.8
  24.3 0.0 copy-done.9
  24.3 43.3 %conditional.1 = (f32[4,2,16,4096]{3,2,1,0:T(8,128)}) conditional(s32[]{:T(128)} %clamp.3, (f32[2,2,16,512]{3,2,1,0:T(8,128)S(1)}, f32[2,2,16,4096]{3,2,1,0:T(8,128)S(1)}, f32[3,8,4096]{2,1,0:T(8,128)S(1)}, s32[4,8]{1,0:T(4,128)S(1)}, s32[8]{0:T(128)S(1)}, /*index=5*/f32[4,3,2,16,4096]{4,3,2,1,0:T(8,128)}, f32[16,128]{1,0:T(8,128)S(1)}, ...), branch_computations={%region_3.4_spmd, %region_4.5_spmd, %region_5.6_spmd} | conditional | flops 26230784 | bytes 51511732 | solution.py:397
  24.3 1.3 %collective-permute-start.21 = (f32[3,8,4096]{2,1,0:T(8,128)S(1)}, f32[3,8,4096]{2,1,0:T(8,128)S(1)}, u32[]{:S(2)}, u32[]{:S(2)}) collective-permute-start(f32[3,8,4096]{2,1,0:T(8,128)S(1)} %get-tuple-element.115), channel_id=1, source_target_pairs={{16,0},{17,1},{18,2},{19,3},{20,4},{21,5},{22,6},{23,7},{24,8},{25... | collective-permute-start | bytes 1179656 | tf_op jit(solution)/shard_map/cond/branch_2_fun/ppermute | solution.py:415
  25.6 1.3 %collective-permute-start.23 = (f32[3,8,4096]{2,1,0:T(8,128)S(1)}, f32[3,8,4096]{2,1,0:T(8,128)S(1)}, u32[]{:S(2)}, u32[]{:S(2)}) collective-permute-start(f32[3,8,4096]{2,1,0:T(8,128)S(1)} %get-tuple-element.118), channel_id=1, source_target_pairs={{16,0},{17,1},{18,2},{19,3},{20,4},{21,5},{22,6},{23,7},{24,8},{25... | collective-permute-start | bytes 1179656 | tf_op jit(solution)/shard_map/cond/branch_2_fun/ppermute | solution.py:415
  26.9 0.0 copy-start.3
  26.9 3.7 %products.19 = (f32[1,2,8,512]{3,2,1,0:T(8,128)S(1)}, f32[1,2,8,4096]{3,2,1,0:T(8,128)S(1)}) custom-call(s32[4,8]{1,0:T(4,128)S(1)} %get-tuple-element.113.requests, s32[8]{0:T(128)S(1)} %get-tuple-element.114.rotations, f32[1,3,8,4096]{3,2,1,0:T(8,128)} %bitcast.8.digits, f32[4,3,2,16,4096]{4,3,2,1,0:T(8,128)} %get-tuple-element.116.keys, ...), custom_call_target="tpu_custom_call" | custom-call | flops 5242880 | bytes 3801088 | tf_op jit(solution)/shard_map/cond/branch_2_fun/products/pallas_call | solution.py:175
  30.6 4.2 %collective-permute-start.27 = (f32[1,2,8,512]{3,2,1,0:T(8,128)S(1)}, f32[1,2,8,512]{3,2,1,0:T(8,128)S(1)}, u32[]{:S(2)}, u32[]{:S(2)}) collective-permute-start(f32[1,2,8,512]{3,2,1,0:T(8,128)S(1)} %get-tuple-element.123), channel_id=1, source_target_pairs={{0,15},{1,0},{2,1},{3,2},{4,3},{5,4},{6,5},{7,6},{8,7},{9,8},{10,9... | collective-permute-start | bytes 98312 | tf_op jit(solution)/shard_map/cond/branch_2_fun/ppermute | solution.py:22
  34.8 0.2 collective-permute-start.20
  34.9 2.4 %collective-permute-start.29 = (f32[1,2,8,4096]{3,2,1,0:T(8,128)S(1)}, f32[1,2,8,4096]{3,2,1,0:T(8,128)S(1)}, u32[]{:S(2)}, u32[]{:S(2)}) collective-permute-start(f32[1,2,8,4096]{3,2,1,0:T(8,128)S(1)} %get-tuple-element.125), channel_id=1, source_target_pairs={{16,0},{0,16},{17,1},{1,17},{18,2},{2,18},{19,3},{3,19},{20,4},{4,... | collective-permute-start | bytes 786440 | tf_op jit(solution)/shard_map/cond/branch_2_fun/ppermute | solution.py:434
  37.4 0.0 collective-permute-done.27.arrived
  37.4 1.1 %collective-permute-start.28 = (f32[1,2,8,4096]{3,2,1,0:T(8,128)S(1)}, f32[1,2,8,4096]{3,2,1,0:T(8,128)S(1)}, u32[]{:S(2)}, u32[]{:S(2)}) collective-permute-start(f32[1,2,8,4096]{3,2,1,0:T(8,128)S(1)} %add_tail.16), channel_id=1, source_target_pairs={{16,0},{0,16},{17,1},{1,17},{18,2},{2,18},{19,3},{3,19},{20,4},{4,... | collective-permute-start | bytes 786440 | tf_op jit(solution)/shard_map/cond/branch_2_fun/ppermute | solution.py:434
  38.5 0.0 collective-permute-done.21
  38.5 0.0 copy-done.3
  38.5 1.1 %products.17 = (f32[1,2,8,512]{3,2,1,0:T(8,128)S(1)}, f32[1,2,8,4096]{3,2,1,0:T(8,128)S(1)}) custom-call(s32[4,8]{1,0:T(4,128)S(1)} %get-tuple-element.113.requests, s32[8]{0:T(128)S(1)} %get-tuple-element.114.rotations, f32[1,3,8,4096]{3,2,1,0:T(8,128)S(1)} %bitcast.14, f32[4,3,2,16,4096]{4,3,2,1,0:T(8,128)S(1)} %copy-done.3, ...), custom_call_target="tpu_custom_call" | custom-call | flops 5242880 | bytes 3801088 | tf_op jit(solution)/shard_map/cond/branch_2_fun/products/pallas_call | solution.py:175
  39.6 7.0 %collective-permute-done.23 = f32[3,8,4096]{2,1,0:T(8,128)S(1)} collective-permute-done((f32[3,8,4096]{2,1,0:T(8,128)S(1)}, f32[3,8,4096]{2,1,0:T(8,128)S(1)}, u32[]{:S(2)}, u32[]{:S(2)}) %collective-permute-start.23) | collective-permute-done | bytes 393248 | tf_op jit(solution)/shard_map/cond/branch_2_fun/ppermute | solution.py:415
  46.6 1.1 %products.18 = (f32[1,2,8,512]{3,2,1,0:T(8,128)S(1)}, f32[1,2,8,4096]{3,2,1,0:T(8,128)S(1)}) custom-call(s32[4,8]{1,0:T(4,128)S(1)} %get-tuple-element.113.requests, s32[8]{0:T(128)S(1)} %get-tuple-element.114.rotations, f32[1,3,8,4096]{3,2,1,0:T(8,128)S(1)} %bitcast.12, f32[4,3,2,16,4096]{4,3,2,1,0:T(8,128)S(1)} %copy-done.3, ...), custom_call_target="tpu_custom_call" | custom-call | flops 5242880 | bytes 3801088 | tf_op jit(solution)/shard_map/cond/branch_2_fun/products/pallas_call | solution.py:175
  47.7 1.3 %collective-permute-start.22 = (f32[1,2,8,4096]{3,2,1,0:T(8,128)S(1)}, f32[1,2,8,4096]{3,2,1,0:T(8,128)S(1)}, u32[]{:S(2)}, u32[]{:S(2)}) collective-permute-start(f32[1,2,8,4096]{3,2,1,0:T(8,128)S(1)} %get-tuple-element.117), channel_id=1, source_target_pairs={{0,16},{1,17},{2,18},{3,19},{4,20},{5,21},{6,22},{7,23},{8,24},{9,... | collective-permute-start | bytes 786440 | tf_op jit(solution)/shard_map/cond/branch_2_fun/ppermute | solution.py:434
  49.1 1.3 %collective-permute-start.24 = (f32[1,2,8,4096]{3,2,1,0:T(8,128)S(1)}, f32[1,2,8,4096]{3,2,1,0:T(8,128)S(1)}, u32[]{:S(2)}, u32[]{:S(2)}) collective-permute-start(f32[1,2,8,4096]{3,2,1,0:T(8,128)S(1)} %get-tuple-element.119), channel_id=1, source_target_pairs={{0,16},{1,17},{2,18},{3,19},{4,20},{5,21},{6,22},{7,23},{8,24},{9,... | collective-permute-start | bytes 786440 | tf_op jit(solution)/shard_map/cond/branch_2_fun/ppermute | solution.py:434
  50.4 0.0 collective-permute-done.20.arrived
  50.4 1.3 %collective-permute-start.25 = (f32[1,2,16,512]{3,2,1,0:T(8,128)S(1)}, f32[1,2,16,512]{3,2,1,0:T(8,128)S(1)}, u32[]{:S(2)}, u32[]{:S(2)}) collective-permute-start(f32[1,2,16,512]{3,2,1,0:T(8,128)S(1)} %pad_maximum_fusion.1), channel_id=1, source_target_pairs={{0,16},{1,17},{2,18},{3,19},{4,20},{5,21},{6,22},{7,23},{8,24},{9,... | collective-permute-start | bytes 196616 | tf_op jit(solution)/shard_map/cond/branch_2_fun/ppermute | solution.py:432
  51.7 9.7 %collective-permute-done.25 = f32[1,2,16,512]{3,2,1,0:T(8,128)S(1)} collective-permute-done((f32[1,2,16,512]{3,2,1,0:T(8,128)S(1)}, f32[1,2,16,512]{3,2,1,0:T(8,128)S(1)}, u32[]{:S(2)}, u32[]{:S(2)}) %collective-permute-start.25) | collective-permute-done | bytes 65568 | tf_op jit(solution)/shard_map/cond/branch_2_fun/ppermute | solution.py:432
  61.4 1.5 %collective-permute-start.26 = (f32[1,2,16,512]{3,2,1,0:T(8,128)S(1)}, f32[1,2,16,512]{3,2,1,0:T(8,128)S(1)}, u32[]{:S(2)}, u32[]{:S(2)}) collective-permute-start(f32[1,2,16,512]{3,2,1,0:T(8,128)S(1)} %collective-permute-done.25), channel_id=1, source_target_pairs={{0,15},{1,0},{2,1},{3,2},{4,3},{5,4},{6,5},{7,6},{8,7},{9,8},{10,9... | collective-permute-start | bytes 196616 | tf_op jit(solution)/shard_map/cond/branch_2_fun/ppermute | solution.py:22
  63.0 1.4 %finish.22.refs_1_ = f32[4,2,16,4096]{3,2,1,0:T(8,128)} custom-call(s32[4,8]{1,0:T(4,128)S(1)} %get-tuple-element.109.requests, f32[16,128]{1,0:T(8,128)S(1)} %get-tuple-element.110.modulus_ref.modulus, f32[2,2,16,4096]{3,2,1,0:T(8,128)S(1)} %add_tail.15.local), custom_call_target="tpu_custom_call" | custom-call | flops 5242880 | bytes 3145728 | tf_op jit(solution)/shard_map/cond/branch_2_fun/finish/pallas_call | solution.py:321
  64.4 0.0 collective-permute-done.29.refs_0_
  64.4 1.0 %finish.23.refs_1_ = f32[4,2,16,4096]{3,2,1,0:T(8,128)} custom-call(s32[4,8]{1,0:T(4,128)S(1)} %get-tuple-element.109.requests, f32[16,128]{1,0:T(8,128)S(1)} %get-tuple-element.110.modulus_ref.modulus, f32[2,2,16,4096]{3,2,1,0:T(8,128)S(1)} %add_tail.15.local, ...), custom_call_target="tpu_custom_call", output_to_operand_aliasing={{}: (4, {})} | custom-call | flops 1310720 | bytes 786432 | tf_op jit(solution)/shard_map/cond/branch_2_fun/finish/pallas_call | solution.py:321
  65.4 0.0 collective-permute-done.28.refs_0_
  65.4 1.0 %finish.24.refs_3_ = f32[4,2,16,4096]{3,2,1,0:T(8,128)} custom-call(s32[4,8]{1,0:T(4,128)S(1)} %get-tuple-element.109.requests, f32[16,128]{1,0:T(8,128)S(1)} %get-tuple-element.110.modulus_ref.modulus, f32[2,2,16,4096]{3,2,1,0:T(8,128)S(1)} %add_tail.15.local, ...), custom_call_target="tpu_custom_call", output_to_operand_aliasing={{}: (4, {})} | custom-call | flops 1310720 | bytes 786432 | tf_op jit(solution)/shard_map/cond/branch_2_fun/finish/pallas_call | solution.py:321
  66.4 0.0 collective-permute-done.26.refs_2_
  66.4 0.0 collective-permute-done.22.refs_0_
  66.5 0.0 collective-permute-done.24.refs_1_
  66.5 1.1 %finish.25 = f32[4,2,16,4096]{3,2,1,0:T(8,128)} custom-call(s32[4,8]{1,0:T(4,128)S(1)} %get-tuple-element.109.requests, f32[16,128]{1,0:T(8,128)S(1)} %get-tuple-element.110.modulus_ref.modulus, f32[2,2,16,4096]{3,2,1,0:T(8,128)S(1)} %add_tail.15.local, f32[1,2,8,4096]{3,2,1,0:T(8,128)S(1)} %collective-permute-done.22.refs_0_, ...), custom_call_target="tpu_custom_call", output_to_operand_aliasing={{}: (6, {})} | custom-call | flops 2621440 | bytes 1572864 | tf_op jit(solution)/shard_map/cond/branch_2_fun/finish/pallas_call | solution.py:321
  (6 shorter events, 0.1 us)
Async XLA Ops:
  0.0 5.7 %copy-start.5 = (s32[4,8]{1,0:T(4,128)S(1)}, s32[4,8]{1,0:T(4,128)}, u32[]{:S(2)}) copy-start(s32[4,8]{1,0:T(4,128)} %requests.5) | copy-start | bytes 388
  2.7 8.2 %copy-start.10 = (s32[16]{0:T(128)S(1)}, s32[16]{0:T(128)}, u32[]{:S(2)}) copy-start(s32[16]{0:T(128)} %param.12) | copy-start | bytes 196
  2.7 8.3 %copy-start = (f32[4,3,16,4096]{3,2,1,0:T(8,128)S(1)}, f32[4,3,16,4096]{3,2,1,0:T(8,128)}, u32[]{:S(2)}) copy-start(f32[4,3,16,4096]{3,2,1,0:T(8,128)} %digits.5) | copy-start | bytes 9437188
  2.7 13.4 %collective-permute-start.32 = (f32[3,8,4096]{2,1,0:T(8,128)}, f32[3,8,4096]{2,1,0:T(8,128)S(1)}, u32[]{:S(2)}, u32[]{:S(2)}) collective-permute-start(f32[3,8,4096]{2,1,0:T(8,128)} %gather.3), channel_id=1, source_target_pairs={{0,16},{16,0},{1,17},{17,1},{2,18},{18,2},{3,19},{19,3},{4,20},{20... | collective-permute-start | bytes 1179656 | tf_op jit(solution)/shard_map/ppermute | solution.py:376
  5.7 10.2 %collective-permute-start.30 = (s32[4,8]{1,0:T(4,128)S(1)}, s32[4,8]{1,0:T(4,128)S(1)}, u32[]{:S(2)}, u32[]{:S(2)}) collective-permute-start(s32[4,8]{1,0:T(4,128)S(1)} %copy-done.5), channel_id=1, source_target_pairs={{0,16},{16,0},{1,17},{17,1},{2,18},{18,2},{3,19},{19,3},{4,20},{20... | collective-permute-start | bytes 392 | tf_op jit(solution)/shard_map/ppermute | solution.py:22
  8.9 15.4 %collective-permute-start.31 = (f32[3,8,4096]{2,1,0:T(8,128)}, f32[3,8,4096]{2,1,0:T(8,128)}, u32[]{:S(2)}, u32[]{:S(2)}) collective-permute-start(f32[3,8,4096]{2,1,0:T(8,128)} %get-tuple-element.137), channel_id=1, source_target_pairs={{0,16},{16,0},{1,17},{17,1},{2,18},{18,2},{3,19},{19,3},{4,20},{20... | collective-permute-start | bytes 1179656 | tf_op jit(solution)/shard_map/ppermute | solution.py:376
  16.1 8.1 %copy-start.4 = (f32[2,2,16,4096]{3,2,1,0:T(8,128)S(1)}, f32[2,2,16,4096]{3,2,1,0:T(8,128)}, u32[]{:S(2)}) copy-start(f32[2,2,16,4096]{3,2,1,0:T(8,128)} %get-tuple-element.134) | copy-start | bytes 3145732
  16.2 8.1 %copy-start.6 = (s32[8]{0:T(128)S(1)}, s32[8]{0:T(128)}, u32[]{:S(2)}) copy-start(s32[8]{0:T(128)} %rotations.3) | copy-start | bytes 100
  16.2 8.1 %copy-start.7 = (f32[3,8,4096]{2,1,0:T(8,128)S(1)}, f32[3,8,4096]{2,1,0:T(8,128)}, u32[]{:S(2)}) copy-start(f32[3,8,4096]{2,1,0:T(8,128)} %get-tuple-element.136) | copy-start | bytes 1179652
  16.2 8.1 %copy-start.8 = (f32[3,8,4096]{2,1,0:T(8,128)S(1)}, f32[3,8,4096]{2,1,0:T(8,128)}, u32[]{:S(2)}) copy-start(f32[3,8,4096]{2,1,0:T(8,128)} %get-tuple-element.135) | copy-start | bytes 1179652
  16.2 8.1 %copy-start.9 = (f32[2,2,16,512]{3,2,1,0:T(8,128)S(1)}, f32[2,2,16,512]{3,2,1,0:T(8,128)}, u32[]{:S(2)}) copy-start(f32[2,2,16,512]{3,2,1,0:T(8,128)} %get-tuple-element.133) | copy-start | bytes 393220
  19.2 5.0 %collective-permute-start.33 = (f32[1,2,8,512]{3,2,1,0:T(8,128)S(1)}, f32[1,2,8,512]{3,2,1,0:T(8,128)S(1)}, u32[]{:S(2)}, u32[]{:S(2)}) collective-permute-start(f32[1,2,8,512]{3,2,1,0:T(8,128)S(1)} %get-tuple-element.138), channel_id=1, source_target_pairs={{0,15},{1,0},{2,1},{3,2},{4,3},{5,4},{6,5},{7,6},{8,7},{9,8},{10,9... | collective-permute-start | bytes 98312 | tf_op jit(solution)/shard_map/ppermute | solution.py:22
  24.3 14.2 %collective-permute-start.21 = (f32[3,8,4096]{2,1,0:T(8,128)S(1)}, f32[3,8,4096]{2,1,0:T(8,128)S(1)}, u32[]{:S(2)}, u32[]{:S(2)}) collective-permute-start(f32[3,8,4096]{2,1,0:T(8,128)S(1)} %get-tuple-element.115), channel_id=1, source_target_pairs={{16,0},{17,1},{18,2},{19,3},{20,4},{21,5},{22,6},{23,7},{24,8},{25... | collective-permute-start | bytes 1179656 | tf_op jit(solution)/shard_map/cond/branch_2_fun/ppermute | solution.py:415
  25.6 21.0 %collective-permute-start.23 = (f32[3,8,4096]{2,1,0:T(8,128)S(1)}, f32[3,8,4096]{2,1,0:T(8,128)S(1)}, u32[]{:S(2)}, u32[]{:S(2)}) collective-permute-start(f32[3,8,4096]{2,1,0:T(8,128)S(1)} %get-tuple-element.118), channel_id=1, source_target_pairs={{16,0},{17,1},{18,2},{19,3},{20,4},{21,5},{22,6},{23,7},{24,8},{25... | collective-permute-start | bytes 1179656 | tf_op jit(solution)/shard_map/cond/branch_2_fun/ppermute | solution.py:415
  26.9 11.6 %copy-start.3 = (f32[4,3,2,16,4096]{4,3,2,1,0:T(8,128)S(1)}, f32[4,3,2,16,4096]{4,3,2,1,0:T(8,128)}, u32[]{:S(2)}) copy-start(f32[4,3,2,16,4096]{4,3,2,1,0:T(8,128)} %get-tuple-element.116.keys) | copy-start | bytes 18874372 | tf_op jit(solution)/shard_map/cond
  30.6 6.8 %collective-permute-start.27 = (f32[1,2,8,512]{3,2,1,0:T(8,128)S(1)}, f32[1,2,8,512]{3,2,1,0:T(8,128)S(1)}, u32[]{:S(2)}, u32[]{:S(2)}) collective-permute-start(f32[1,2,8,512]{3,2,1,0:T(8,128)S(1)} %get-tuple-element.123), channel_id=1, source_target_pairs={{0,15},{1,0},{2,1},{3,2},{4,3},{5,4},{6,5},{7,6},{8,7},{9,8},{10,9... | collective-permute-start | bytes 98312 | tf_op jit(solution)/shard_map/cond/branch_2_fun/ppermute | solution.py:22
  34.8 15.6 %collective-permute-start.20 = (f32[2,2,16,512]{3,2,1,0:T(8,128)S(1)}, f32[2,2,16,512]{3,2,1,0:T(8,128)S(1)}, u32[]{:S(2)}, u32[]{:S(2)}) collective-permute-start(f32[2,2,16,512]{3,2,1,0:T(8,128)S(1)} %get-tuple-element.111), channel_id=1, source_target_pairs={{0,15},{1,0},{2,1},{3,2},{4,3},{5,4},{6,5},{7,6},{8,7},{9,8},{10,9... | collective-permute-start | bytes 393224 | tf_op jit(solution)/shard_map/cond/branch_2_fun/ppermute | solution.py:22
  34.9 29.5 %collective-permute-start.29 = (f32[1,2,8,4096]{3,2,1,0:T(8,128)S(1)}, f32[1,2,8,4096]{3,2,1,0:T(8,128)S(1)}, u32[]{:S(2)}, u32[]{:S(2)}) collective-permute-start(f32[1,2,8,4096]{3,2,1,0:T(8,128)S(1)} %get-tuple-element.125), channel_id=1, source_target_pairs={{16,0},{0,16},{17,1},{1,17},{18,2},{2,18},{19,3},{3,19},{20,4},{4,... | collective-permute-start | bytes 786440 | tf_op jit(solution)/shard_map/cond/branch_2_fun/ppermute | solution.py:434
  37.4 28.0 %collective-permute-start.28 = (f32[1,2,8,4096]{3,2,1,0:T(8,128)S(1)}, f32[1,2,8,4096]{3,2,1,0:T(8,128)S(1)}, u32[]{:S(2)}, u32[]{:S(2)}) collective-permute-start(f32[1,2,8,4096]{3,2,1,0:T(8,128)S(1)} %add_tail.16), channel_id=1, source_target_pairs={{16,0},{0,16},{17,1},{1,17},{18,2},{2,18},{19,3},{3,19},{20,4},{4,... | collective-permute-start | bytes 786440 | tf_op jit(solution)/shard_map/cond/branch_2_fun/ppermute | solution.py:434
  47.7 18.7 %collective-permute-start.22 = (f32[1,2,8,4096]{3,2,1,0:T(8,128)S(1)}, f32[1,2,8,4096]{3,2,1,0:T(8,128)S(1)}, u32[]{:S(2)}, u32[]{:S(2)}) collective-permute-start(f32[1,2,8,4096]{3,2,1,0:T(8,128)S(1)} %get-tuple-element.117), channel_id=1, source_target_pairs={{0,16},{1,17},{2,18},{3,19},{4,20},{5,21},{6,22},{7,23},{8,24},{9,... | collective-permute-start | bytes 786440 | tf_op jit(solution)/shard_map/cond/branch_2_fun/ppermute | solution.py:434
  49.1 17.4 %collective-permute-start.24 = (f32[1,2,8,4096]{3,2,1,0:T(8,128)S(1)}, f32[1,2,8,4096]{3,2,1,0:T(8,128)S(1)}, u32[]{:S(2)}, u32[]{:S(2)}) collective-permute-start(f32[1,2,8,4096]{3,2,1,0:T(8,128)S(1)} %get-tuple-element.119), channel_id=1, source_target_pairs={{0,16},{1,17},{2,18},{3,19},{4,20},{5,21},{6,22},{7,23},{8,24},{9,... | collective-permute-start | bytes 786440 | tf_op jit(solution)/shard_map/cond/branch_2_fun/ppermute | solution.py:434
  50.4 11.0 %collective-permute-start.25 = (f32[1,2,16,512]{3,2,1,0:T(8,128)S(1)}, f32[1,2,16,512]{3,2,1,0:T(8,128)S(1)}, u32[]{:S(2)}, u32[]{:S(2)}) collective-permute-start(f32[1,2,16,512]{3,2,1,0:T(8,128)S(1)} %pad_maximum_fusion.1), channel_id=1, source_target_pairs={{0,16},{1,17},{2,18},{3,19},{4,20},{5,21},{6,22},{7,23},{8,24},{9,... | collective-permute-start | bytes 196616 | tf_op jit(solution)/shard_map/cond/branch_2_fun/ppermute | solution.py:432
  61.4 5.0 %collective-permute-start.26 = (f32[1,2,16,512]{3,2,1,0:T(8,128)S(1)}, f32[1,2,16,512]{3,2,1,0:T(8,128)S(1)}, u32[]{:S(2)}, u32[]{:S(2)}) collective-permute-start(f32[1,2,16,512]{3,2,1,0:T(8,128)S(1)} %collective-permute-done.25), channel_id=1, source_target_pairs={{0,15},{1,0},{2,1},{3,2},{4,3},{5,4},{6,5},{7,6},{8,7},{9,8},{10,9... | collective-permute-start | bytes 196616 | tf_op jit(solution)/shard_map/cond/branch_2_fun/ppermute | solution.py:22

commit v8 on v4

--- a/solution.py
+++ b/solution.py
@@ -314,61 +314,33 @@
 
 
 def key_switch_pair(digits, keys, requests, rotations, modulus):
+    ciphers = digits.shape[0]
     blocks = tuple(range(digits.shape[2] // ROWS))
     slots = tuple(range(CAP))
-    key_count = keys.shape[0]
-    both = [(0, 1), (1, 0)]
     turns = [(slot, block) for slot in slots for block in blocks]
     picked = {turns[0]: gather(digits, requests, 1, (turns[0],), 4)[0]}
     picked.update(zip(turns[1:], gather(digits, requests, 1, tuple(turns[1:]))))
     sent = {}
-    for block in blocks:
-        sent[0, block] = lax.ppermute(picked[0, block], "grp", both)
+    for slot, block in turns:
+        sent[slot, block] = shifted(picked[slot, block], "grp", 1)
     asked = shifted(requests, "grp", 1)
     tail, resident = products(digits, keys, requests, rotations, modulus, slots, blocks, True)
     arrived = shifted(tail, "limb", -1)
     local = add_tail(resident, arrived)
-    me = lax.axis_index("grp")
-    rightward = jnp.where(me == 0, requests, asked)[:, key_count:]
-    leftward = jnp.where(me == 0, asked, requests)[:, :key_count]
-    two_right = jnp.sum(jnp.max(rightward, axis=1)) > 1
-    two_left = jnp.sum(jnp.max(leftward, axis=1)) > 1
-    case = jnp.where(two_right == two_left, 0, jnp.where(two_right, 1, 2))
-    ahead = remote(sent[0, 0], keys, asked, rotations, modulus, 0, 0)
-
-    def branch(pairs):
-        def run(*operands):
-            return exchange((both, pairs), *operands)
-
-        return run
-
-    branches = [branch(pairs) for pairs in (both, [(0, 1)], [(1, 0)])]
-    operands = (ahead, [picked[turn] for turn in turns[len(blocks) :]], [sent[0, block] for block in blocks[1:]], local)
-    return lax.switch(case, branches, *operands, keys, requests, asked, rotations, modulus)
+    result, held = sums([local], ((0, slots),), requests, modulus, ciphers, True)
+    back = {}
+    for slot, block in turns:
+        whole = remote(sent[slot, block], keys, asked, rotations, modulus, slot, block)
+        back[slot, block] = shifted(whole, "grp", -1)
+    for slot, block in turns:
+        result = finish(back[slot, block], held, result, requests, modulus, slot, block)
+    return result
 
 
 def remote(arrived, keys, asked, rotations, modulus, slot, block):
     tail, resident = products(arrived[None], keys, asked, rotations, modulus, (slot,), (block,), False)
     wrapped = shifted(tail, "limb", -1)
     return add_tail(resident, wrapped)
-
-
-def exchange(pairs, ahead, picked, arrived, local, keys, requests, asked, rotations, modulus):
-    ciphers = requests.shape[0]
-    blocks = local.shape[2] // ROWS
-    turns = [(slot, block) for slot in range(CAP) for block in range(blocks)]
-    sent = dict(zip(turns[1:blocks], arrived))
-    for (slot, block), piece in zip(turns[blocks:], picked):
-        sent[slot, block] = lax.ppermute(piece, "grp", pairs[slot])
-    result, held = sums([local], ((0, tuple(range(CAP))),), requests, modulus, ciphers, True)
-    back = {}
-    for turn in turns:
-        slot, block = turn
-        whole = ahead if turn == turns[0] else remote(sent[turn], keys, asked, rotations, modulus, slot, block)
-        back[turn] = lax.ppermute(whole, "grp", [(target, source) for source, target in pairs[slot]])
-    for slot, block in turns:
-        result = finish(back[slot, block], held, result, requests, modulus, slot, block)
-    return result
 
 
 def solution(mesh):

time: 77.3 us -> 77.7 us (level)
  waiting for transfers between devices: 15.2 us -> 36.5 us
  starting transfers between devices: 30 us -> 19.1 us
  Pallas kernels: 28.5 us -> 20.9 us
  other arithmetic: 1.47 us -> 0.01 us
  between operations: 1.39 us -> 0.15 us
    ppermute x6 -> x14, waiting for transfers between devices: 4.93 us -> 36.5 us  [shifted(): return lax.ppermute(value, axis, pairs)]
    ppermute x8 -> x0, starting transfers between devices: 11.3 us -> none  [the longest x4 5.34 us: exchange(): lax.ppermute(whole, 'grp', [(target, source) for source, target in pairs[...]
    ppermute x8 -> x0, waiting for transfers between devices: 10.3 us -> none  [the longest x2 5.21 us: exchange(): sent[slot, block] = lax.ppermute(piece, 'grp', pairs[slot])]
    pallas_call x5, Pallas kernels: 14.5 us -> 7.65 us  [products(): pl.pallas_call(functools.partial(products_kernel, slots, blocks, local),...]
    reduce_sum x2 -> x0, other arithmetic: 1.29 us -> none  [the longest x1 0.65 us: key_switch_pair(): two_left = jnp.sum(jnp.max(leftward, axis=1)) > 1]
    ppermute x6 -> x14, starting transfers between devices: 18.7 us -> 19.1 us  [shifted(): return lax.ppermute(value, axis, pairs)]
  transfers between devices with their start and end apart: 14 -> 14, of which waited for: 6 -> 4; matrix products, arithmetic and copies ran while one was open for 2% -> 0% of each run, Pallas kernels for 33% -> 23%
where the time goes in v8:
time: 77.7 us; the launch traced here: 77.5 us
  waiting for transfers between devices  36.5 us (47%)
  Pallas kernels  20.9 us (27%)
  starting transfers between devices  19.1 us (25%)
  local copies, waits for them, and re-layouts  0.78 us (1%)
    ppermute x14, waiting for transfers between devices, shifted(): return lax.ppermute(value, axis, pairs)  36.5 us
    ppermute x14, starting transfers between devices, shifted(): return lax.ppermute(value, axis, pairs)  19.1 us
    pallas_call x5, Pallas kernels, products(): pl.pallas_call(functools.partial(products_kernel, slots, blocks, local),...  7.65 us
    pallas_call x1, Pallas kernels, sums(): pl.pallas_call(functools.partial(sums_kernel, owners, groups, ciphers, ke...  5.26 us
    pallas_call x4, Pallas kernels, finish(): pl.pallas_call(functools.partial(finish_kernel, slot, block, groups), out...  4.05 us
    pallas_call x2, Pallas kernels, gather(): pl.pallas_call(functools.partial(gather_kernel, wanted, cuts, steps, lax....  3.93 us
  transfers between devices with their start and end apart: 14, of which 4 were waited for; matrix products, arithmetic and copies ran while one was open for 0% of the time, Pallas kernels for 23%

profile of v8, /device:TPU:0, one launch (start us, length us, event | category | flops | bytes accessed | tf_op | source)
XLA Modules:
  0.0 77.5 jit_solution(8252923585592528675)
XLA Ops:
  0.0 0.0 copy-start.2
  0.0 0.7 copy-done.2
  0.7 0.0 copy-start
  0.7 1.9 %gather_digits.3 = f32[3,8,4096]{2,1,0:T(8,128)S(1)} custom-call(s32[4,8]{1,0:T(4,128)S(1)} %copy-done.2, f32[4,3,16,4096]{3,2,1,0:T(8,128)} %digits.5), custom_call_target="tpu_custom_call" | custom-call | bytes 786432 | tf_op jit(solution)/shard_map/gather_digits/pallas_call | solution.py:71
  2.6 0.0 copy-start.5
  2.6 0.0 copy-start.4
  2.6 3.0 %collective-permute-start.11 = (f32[3,8,4096]{2,1,0:T(8,128)S(1)}, f32[3,8,4096]{2,1,0:T(8,128)S(1)}, u32[]{:S(2)}, u32[]{:S(2)}) collective-permute-start(f32[3,8,4096]{2,1,0:T(8,128)S(1)} %gather_digits.3), channel_id=1, source_target_pairs={{0,16},{16,0},{1,17},{17,1},{2,18},{18,2},{3,19},{19,3},{4,20},{20... | collective-permute-start | bytes 1179656 | tf_op jit(solution)/shard_map/ppermute | solution.py:22
  5.7 2.0 %gather_digits.2 = (f32[3,8,4096]{2,1,0:T(8,128)S(1)}, f32[3,8,4096]{2,1,0:T(8,128)S(1)}, f32[3,8,4096]{2,1,0:T(8,128)S(1)}) custom-call(s32[4,8]{1,0:T(4,128)S(1)} %copy-done.2, f32[4,3,16,4096]{3,2,1,0:T(8,128)} %digits.5), custom_call_target="tpu_custom_call" | custom-call | bytes 2359296 | tf_op jit(solution)/shard_map/gather_digits/pallas_call | solution.py:71
  7.7 0.1 collective-permute-start.5
  7.8 2.0 %collective-permute-start.8 = (f32[3,8,4096]{2,1,0:T(8,128)S(1)}, f32[3,8,4096]{2,1,0:T(8,128)S(1)}, u32[]{:S(2)}, u32[]{:S(2)}) collective-permute-start(f32[3,8,4096]{2,1,0:T(8,128)S(1)} %get-tuple-element.29), channel_id=1, source_target_pairs={{0,16},{16,0},{1,17},{17,1},{2,18},{18,2},{3,19},{19,3},{4,20},{20... | collective-permute-start | bytes 1179656 | tf_op jit(solution)/shard_map/ppermute | solution.py:22
  9.8 0.1 collective-permute-start.1
  9.9 1.9 %collective-permute-start = (s32[4,8]{1,0:T(4,128)S(1)}, s32[4,8]{1,0:T(4,128)S(1)}, u32[]{:S(2)}, u32[]{:S(2)}) collective-permute-start(s32[4,8]{1,0:T(4,128)S(1)} %copy-done.2), channel_id=1, source_target_pairs={{0,16},{16,0},{1,17},{17,1},{2,18},{18,2},{3,19},{19,3},{4,20},{20... | collective-permute-start | bytes 392 | tf_op jit(solution)/shard_map/ppermute | solution.py:22
  11.8 0.0 copy-done.5
  11.8 28.3 %collective-permute-done.requests = s32[4,8]{1,0:T(4,128)S(1)} collective-permute-done((s32[4,8]{1,0:T(4,128)S(1)}, s32[4,8]{1,0:T(4,128)S(1)}, u32[]{:S(2)}, u32[]{:S(2)}) %collective-permute-start) | collective-permute-done | bytes 160 | tf_op jit(solution)/shard_map/ppermute | solution.py:22
  40.1 0.0 collective-permute-done.11
  40.1 0.1 broadcast_in_dim.18.modulus_ref.modulus
  40.2 0.0 copy-done
  40.2 0.0 copy-done.4
  40.2 1.6 %products.9 = (f32[1,2,8,512]{3,2,1,0:T(8,128)S(1)}, f32[1,2,8,4096]{3,2,1,0:T(8,128)S(1)}) custom-call(s32[4,8]{1,0:T(4,128)S(1)} %collective-permute-done.requests, s32[8]{0:T(128)S(1)} %copy-done.4, f32[1,3,8,4096]{3,2,1,0:T(8,128)S(1)} %bitcast.7, f32[4,3,2,16,4096]{4,3,2,1,0:T(8,128)S(1)} %copy-done, f32[16,128]{1,0:T(8,128)S(1)} %broadcast_in_dim.18.modulus_ref.modulus), custom_call_target="tpu_custom_call" | custom-call | flops 5242880 | bytes 3801088 | tf_op jit(solution)/shard_map/products/pallas_call | solution.py:144
  41.7 3.4 %collective-permute-start.12 = (f32[1,2,8,512]{3,2,1,0:T(8,128)S(1)}, f32[1,2,8,512]{3,2,1,0:T(8,128)S(1)}, u32[]{:S(2)}, u32[]{:S(2)}) collective-permute-start(f32[1,2,8,512]{3,2,1,0:T(8,128)S(1)} %get-tuple-element.32), channel_id=1, source_target_pairs={{0,15},{1,0},{2,1},{3,2},{4,3},{5,4},{6,5},{7,6},{8,7},{9,8},{10,9... | collective-permute-start | bytes 98312 | tf_op jit(solution)/shard_map/ppermute | solution.py:22
  45.2 0.0 collective-permute-done.5
  45.2 1.1 %products.7 = (f32[1,2,8,512]{3,2,1,0:T(8,128)S(1)}, f32[1,2,8,4096]{3,2,1,0:T(8,128)S(1)}) custom-call(s32[4,8]{1,0:T(4,128)S(1)} %collective-permute-done.requests, s32[8]{0:T(128)S(1)} %copy-done.4, f32[1,3,8,4096]{3,2,1,0:T(8,128)S(1)} %bitcast.6, f32[4,3,2,16,4096]{4,3,2,1,0:T(8,128)S(1)} %copy-done, f32[16,128]{1,0:T(8,128)S(1)} %broadcast_in_dim.18.modulus_ref.modulus), custom_call_target="tpu_custom_call" | custom-call | flops 5242880 | bytes 3801088 | tf_op jit(solution)/shard_map/products/pallas_call | solution.py:144
  46.3 1.6 %collective-permute-start.6 = (f32[1,2,8,512]{3,2,1,0:T(8,128)S(1)}, f32[1,2,8,512]{3,2,1,0:T(8,128)S(1)}, u32[]{:S(2)}, u32[]{:S(2)}) collective-permute-start(f32[1,2,8,512]{3,2,1,0:T(8,128)S(1)} %get-tuple-element.27), channel_id=1, source_target_pairs={{0,15},{1,0},{2,1},{3,2},{4,3},{5,4},{6,5},{7,6},{8,7},{9,8},{10,9... | collective-permute-start | bytes 98312 | tf_op jit(solution)/shard_map/ppermute | solution.py:22
  47.9 0.0 collective-permute-done.8
  47.9 1.6 %products.8 = (f32[1,2,8,512]{3,2,1,0:T(8,128)S(1)}, f32[1,2,8,4096]{3,2,1,0:T(8,128)S(1)}) custom-call(s32[4,8]{1,0:T(4,128)S(1)} %collective-permute-done.requests, s32[8]{0:T(128)S(1)} %copy-done.4, f32[1,3,8,4096]{3,2,1,0:T(8,128)S(1)} %bitcast.5, f32[4,3,2,16,4096]{4,3,2,1,0:T(8,128)S(1)} %copy-done, f32[16,128]{1,0:T(8,128)S(1)} %broadcast_in_dim.18.modulus_ref.modulus), custom_call_target="tpu_custom_call" | custom-call | flops 5242880 | bytes 3801088 | tf_op jit(solution)/shard_map/products/pallas_call | solution.py:144
  49.5 0.1 collective-permute-start.9
  49.6 0.0 collective-permute-done.1
  49.6 0.0 copy-start.1
  49.6 1.2 %products.5 = (f32[1,2,8,512]{3,2,1,0:T(8,128)S(1)}, f32[1,2,8,4096]{3,2,1,0:T(8,128)S(1)}) custom-call(s32[4,8]{1,0:T(4,128)S(1)} %collective-permute-done.requests, s32[8]{0:T(128)S(1)} %copy-done.4, f32[1,3,8,4096]{3,2,1,0:T(8,128)S(1)} %bitcast.4, f32[4,3,2,16,4096]{4,3,2,1,0:T(8,128)S(1)} %copy-done, f32[16,128]{1,0:T(8,128)S(1)} %broadcast_in_dim.18.modulus_ref.modulus), custom_call_target="tpu_custom_call" | custom-call | flops 5242880 | bytes 3801088 | tf_op jit(solution)/shard_map/products/pallas_call | solution.py:144
  50.8 0.0 copy-start.3
  50.8 0.6 collective-permute-start.2
  51.4 0.0 collective-permute-done.12.arrived
  51.4 0.3 collective-permute-start.13
  51.7 0.0 collective-permute-done.9.arrived
  51.7 1.8 %collective-permute-start.10 = (f32[1,2,8,4096]{3,2,1,0:T(8,128)S(1)}, f32[1,2,8,4096]{3,2,1,0:T(8,128)S(1)}, u32[]{:S(2)}, u32[]{:S(2)}) collective-permute-start(f32[1,2,8,4096]{3,2,1,0:T(8,128)S(1)} %add_tail.8), channel_id=1, source_target_pairs={{0,16},{16,0},{1,17},{17,1},{2,18},{18,2},{3,19},{19,3},{4,20},{20... | collective-permute-start | bytes 786440 | tf_op jit(solution)/shard_map/ppermute | solution.py:22
  53.6 0.0 collective-permute-done.6.arrived
  53.6 0.3 collective-permute-start.7
  53.9 0.0 collective-permute-done.2.arrived
  53.9 1.8 %collective-permute-start.3 = (f32[1,2,8,4096]{3,2,1,0:T(8,128)S(1)}, f32[1,2,8,4096]{3,2,1,0:T(8,128)S(1)}, u32[]{:S(2)}, u32[]{:S(2)}) collective-permute-start(f32[1,2,8,4096]{3,2,1,0:T(8,128)S(1)} %add_tail.5), channel_id=1, source_target_pairs={{0,16},{16,0},{1,17},{17,1},{2,18},{18,2},{3,19},{19,3},{4,20},{20... | collective-permute-start | bytes 786440 | tf_op jit(solution)/shard_map/ppermute | solution.py:22
  55.8 0.0 copy-done.1
  55.8 0.0 copy-done.3
  55.8 2.2 %products.6 = (f32[2,2,16,512]{3,2,1,0:T(8,128)S(1)}, f32[2,2,16,4096]{3,2,1,0:T(8,128)S(1)}) custom-call(s32[4,8]{1,0:T(4,128)S(1)} %copy-done.3, s32[8]{0:T(128)S(1)} %copy-done.4, f32[4,3,16,4096]{3,2,1,0:T(8,128)S(1)} %copy-done.1, f32[4,3,2,16,4096]{4,3,2,1,0:T(8,128)S(1)} %copy-done, f32[16,128]{1,0:T(8,128)S(1)} %broadcast_in_dim.18.modulus_ref.modulus), custom_call_target="tpu_custom_call" | custom-call | flops 20971520 | bytes 8912896 | tf_op jit(solution)/shard_map/products/pallas_call | solution.py:144
  58.0 1.9 %collective-permute-start.4 = (f32[2,2,16,512]{3,2,1,0:T(8,128)S(1)}, f32[2,2,16,512]{3,2,1,0:T(8,128)S(1)}, u32[]{:S(2)}, u32[]{:S(2)}) collective-permute-start(f32[2,2,16,512]{3,2,1,0:T(8,128)S(1)} %get-tuple-element.23), channel_id=1, source_target_pairs={{0,15},{1,0},{2,1},{3,2},{4,3},{5,4},{6,5},{7,6},{8,7},{9,8},{10,9... | collective-permute-start | bytes 393224 | tf_op jit(solution)/shard_map/ppermute | solution.py:22
  59.9 2.5 %collective-permute-done.4.arrived = f32[2,2,16,512]{3,2,1,0:T(8,128)S(1)} collective-permute-done((f32[2,2,16,512]{3,2,1,0:T(8,128)S(1)}, f32[2,2,16,512]{3,2,1,0:T(8,128)S(1)}, u32[]{:S(2)}, u32[]{:S(2)}) %collective-permute-start.4) | collective-permute-done | bytes 131104 | tf_op jit(solution)/shard_map/ppermute | solution.py:22
  62.5 5.3 %sums.1 = (f32[4,2,16,4096]{3,2,1,0:T(8,128)}, f32[2,2,16,4096]{3,2,1,0:T(8,128)S(1)}) custom-call(s32[4,8]{1,0:T(4,128)S(1)} %copy-done.3, f32[16,128]{1,0:T(8,128)S(1)} %broadcast_in_dim.18.modulus_ref.modulus, f32[2,2,16,4096]{3,2,1,0:T(8,128)S(1)} %add_tail.6.refs_0_), custom_call_target="tpu_custom_call" | custom-call | flops 10485760 | bytes 4194304 | tf_op jit(solution)/shard_map/sums/pallas_call | solution.py:221
  67.7 0.0 collective-permute-done.13.part
  67.8 1.0 %finish.4.before = f32[4,2,16,4096]{3,2,1,0:T(8,128)} custom-call(s32[4,8]{1,0:T(4,128)S(1)} %copy-done.3, f32[16,128]{1,0:T(8,128)S(1)} %broadcast_in_dim.18.modulus_ref.modulus, f32[1,2,8,4096]{3,2,1,0:T(8,128)S(1)} %collective-permute-done.13.part, f32[2,2,16,4096]{3,2,1,0:T(8,128)S(1)} %get-tuple-element.25.held, ...), custom_call_target="tpu_custom_call", output_to_operand_aliasing={{}: (4, {})} | custom-call | flops 1310720 | bytes 786432 | tf_op jit(solution)/shard_map/finish/pallas_call | solution.py:272
  68.8 0.0 collective-permute-done.10.part
  68.8 1.0 %finish.5.before = f32[4,2,16,4096]{3,2,1,0:T(8,128)} custom-call(s32[4,8]{1,0:T(4,128)S(1)} %copy-done.3, f32[16,128]{1,0:T(8,128)S(1)} %broadcast_in_dim.18.modulus_ref.modulus, f32[1,2,8,4096]{3,2,1,0:T(8,128)S(1)} %collective-permute-done.10.part, f32[2,2,16,4096]{3,2,1,0:T(8,128)S(1)} %get-tuple-element.25.held, ...), custom_call_target="tpu_custom_call", output_to_operand_aliasing={{}: (4, {})} | custom-call | flops 1310720 | bytes 786432 | tf_op jit(solution)/shard_map/finish/pallas_call | solution.py:272
  69.8 2.1 %collective-permute-done.7.part = f32[1,2,8,4096]{3,2,1,0:T(8,128)S(1)} collective-permute-done((f32[1,2,8,4096]{3,2,1,0:T(8,128)S(1)}, f32[1,2,8,4096]{3,2,1,0:T(8,128)S(1)}, u32[]{:S(2)}, u32[]{:S(2)}) %collective-permute-start.7) | collective-permute-done | bytes 262176 | tf_op jit(solution)/shard_map/ppermute | solution.py:22
  71.9 1.0 %finish.6.before = f32[4,2,16,4096]{3,2,1,0:T(8,128)} custom-call(s32[4,8]{1,0:T(4,128)S(1)} %copy-done.3, f32[16,128]{1,0:T(8,128)S(1)} %broadcast_in_dim.18.modulus_ref.modulus, f32[1,2,8,4096]{3,2,1,0:T(8,128)S(1)} %collective-permute-done.7.part, f32[2,2,16,4096]{3,2,1,0:T(8,128)S(1)} %get-tuple-element.25.held, ...), custom_call_target="tpu_custom_call", output_to_operand_aliasing={{}: (4, {})} | custom-call | flops 1310720 | bytes 786432 | tf_op jit(solution)/shard_map/finish/pallas_call | solution.py:272
  72.9 3.6 %collective-permute-done.3.part = f32[1,2,8,4096]{3,2,1,0:T(8,128)S(1)} collective-permute-done((f32[1,2,8,4096]{3,2,1,0:T(8,128)S(1)}, f32[1,2,8,4096]{3,2,1,0:T(8,128)S(1)}, u32[]{:S(2)}, u32[]{:S(2)}) %collective-permute-start.3) | collective-permute-done | bytes 262176 | tf_op jit(solution)/shard_map/ppermute | solution.py:22
  76.5 1.0 %finish.7 = f32[4,2,16,4096]{3,2,1,0:T(8,128)} custom-call(s32[4,8]{1,0:T(4,128)S(1)} %copy-done.3, f32[16,128]{1,0:T(8,128)S(1)} %broadcast_in_dim.18.modulus_ref.modulus, f32[1,2,8,4096]{3,2,1,0:T(8,128)S(1)} %collective-permute-done.3.part, f32[2,2,16,4096]{3,2,1,0:T(8,128)S(1)} %get-tuple-element.25.held, ...), custom_call_target="tpu_custom_call", output_to_operand_aliasing={{}: (4, {})} | custom-call | flops 1310720 | bytes 786432 | tf_op jit(solution)/shard_map/finish/pallas_call | solution.py:272
  (6 shorter events, 0.1 us)
Async XLA Ops:
  0.0 0.7 copy-start.2
  0.7 39.5 %copy-start = (f32[4,3,2,16,4096]{4,3,2,1,0:T(8,128)S(1)}, f32[4,3,2,16,4096]{4,3,2,1,0:T(8,128)}, u32[]{:S(2)}) copy-start(f32[4,3,2,16,4096]{4,3,2,1,0:T(8,128)} %keys.9) | copy-start | bytes 18874372
  2.6 9.2 %copy-start.5 = (s32[16]{0:T(128)S(1)}, s32[16]{0:T(128)}, u32[]{:S(2)}) copy-start(s32[16]{0:T(128)} %param.9) | copy-start | bytes 196
  2.6 37.6 %copy-start.4 = (s32[8]{0:T(128)S(1)}, s32[8]{0:T(128)}, u32[]{:S(2)}) copy-start(s32[8]{0:T(128)} %rotations.9) | copy-start | bytes 100
  2.6 37.5 %collective-permute-start.11 = (f32[3,8,4096]{2,1,0:T(8,128)S(1)}, f32[3,8,4096]{2,1,0:T(8,128)S(1)}, u32[]{:S(2)}, u32[]{:S(2)}) collective-permute-start(f32[3,8,4096]{2,1,0:T(8,128)S(1)} %gather_digits.3), channel_id=1, source_target_pairs={{0,16},{16,0},{1,17},{17,1},{2,18},{18,2},{3,19},{19,3},{4,20},{20... | collective-permute-start | bytes 1179656 | tf_op jit(solution)/shard_map/ppermute | solution.py:22
  7.7 37.5 %collective-permute-start.5 = (f32[3,8,4096]{2,1,0:T(8,128)S(1)}, f32[3,8,4096]{2,1,0:T(8,128)S(1)}, u32[]{:S(2)}, u32[]{:S(2)}) collective-permute-start(f32[3,8,4096]{2,1,0:T(8,128)S(1)} %get-tuple-element.26), channel_id=1, source_target_pairs={{0,16},{16,0},{1,17},{17,1},{2,18},{18,2},{3,19},{19,3},{4,20},{20... | collective-permute-start | bytes 1179656 | tf_op jit(solution)/shard_map/ppermute | solution.py:22
  7.8 40.2 %collective-permute-start.8 = (f32[3,8,4096]{2,1,0:T(8,128)S(1)}, f32[3,8,4096]{2,1,0:T(8,128)S(1)}, u32[]{:S(2)}, u32[]{:S(2)}) collective-permute-start(f32[3,8,4096]{2,1,0:T(8,128)S(1)} %get-tuple-element.29), channel_id=1, source_target_pairs={{0,16},{16,0},{1,17},{17,1},{2,18},{18,2},{3,19},{19,3},{4,20},{20... | collective-permute-start | bytes 1179656 | tf_op jit(solution)/shard_map/ppermute | solution.py:22
  9.8 39.8 %collective-permute-start.1 = (f32[3,8,4096]{2,1,0:T(8,128)S(1)}, f32[3,8,4096]{2,1,0:T(8,128)S(1)}, u32[]{:S(2)}, u32[]{:S(2)}) collective-permute-start(f32[3,8,4096]{2,1,0:T(8,128)S(1)} %get-tuple-element.20), channel_id=1, source_target_pairs={{0,16},{16,0},{1,17},{17,1},{2,18},{18,2},{3,19},{19,3},{4,20},{20... | collective-permute-start | bytes 1179656 | tf_op jit(solution)/shard_map/ppermute | solution.py:22
  9.9 30.2 %collective-permute-start = (s32[4,8]{1,0:T(4,128)S(1)}, s32[4,8]{1,0:T(4,128)S(1)}, u32[]{:S(2)}, u32[]{:S(2)}) collective-permute-start(s32[4,8]{1,0:T(4,128)S(1)} %copy-done.2), channel_id=1, source_target_pairs={{0,16},{16,0},{1,17},{17,1},{2,18},{18,2},{3,19},{19,3},{4,20},{20... | collective-permute-start | bytes 392 | tf_op jit(solution)/shard_map/ppermute | solution.py:22
  41.7 9.7 %collective-permute-start.12 = (f32[1,2,8,512]{3,2,1,0:T(8,128)S(1)}, f32[1,2,8,512]{3,2,1,0:T(8,128)S(1)}, u32[]{:S(2)}, u32[]{:S(2)}) collective-permute-start(f32[1,2,8,512]{3,2,1,0:T(8,128)S(1)} %get-tuple-element.32), channel_id=1, source_target_pairs={{0,15},{1,0},{2,1},{3,2},{4,3},{5,4},{6,5},{7,6},{8,7},{9,8},{10,9... | collective-permute-start | bytes 98312 | tf_op jit(solution)/shard_map/ppermute | solution.py:22
  46.3 7.2 %collective-permute-start.6 = (f32[1,2,8,512]{3,2,1,0:T(8,128)S(1)}, f32[1,2,8,512]{3,2,1,0:T(8,128)S(1)}, u32[]{:S(2)}, u32[]{:S(2)}) collective-permute-start(f32[1,2,8,512]{3,2,1,0:T(8,128)S(1)} %get-tuple-element.27), channel_id=1, source_target_pairs={{0,15},{1,0},{2,1},{3,2},{4,3},{5,4},{6,5},{7,6},{8,7},{9,8},{10,9... | collective-permute-start | bytes 98312 | tf_op jit(solution)/shard_map/ppermute | solution.py:22
  49.5 2.2 %collective-permute-start.9 = (f32[1,2,8,512]{3,2,1,0:T(8,128)S(1)}, f32[1,2,8,512]{3,2,1,0:T(8,128)S(1)}, u32[]{:S(2)}, u32[]{:S(2)}) collective-permute-start(f32[1,2,8,512]{3,2,1,0:T(8,128)S(1)} %get-tuple-element.30), channel_id=1, source_target_pairs={{0,15},{1,0},{2,1},{3,2},{4,3},{5,4},{6,5},{7,6},{8,7},{9,8},{10,9... | collective-permute-start | bytes 98312 | tf_op jit(solution)/shard_map/ppermute | solution.py:22
  49.6 6.2 %copy-start.1 = (f32[4,3,16,4096]{3,2,1,0:T(8,128)S(1)}, f32[4,3,16,4096]{3,2,1,0:T(8,128)}, u32[]{:S(2)}) copy-start(f32[4,3,16,4096]{3,2,1,0:T(8,128)} %digits.5) | copy-start | bytes 9437188
  50.8 5.0 %copy-start.3 = (s32[4,8]{1,0:T(4,128)S(1)}, s32[4,8]{1,0:T(4,128)}, u32[]{:S(2)}) copy-start(s32[4,8]{1,0:T(4,128)} %requests.15) | copy-start | bytes 388
  50.8 3.2 %collective-permute-start.2 = (f32[1,2,8,512]{3,2,1,0:T(8,128)S(1)}, f32[1,2,8,512]{3,2,1,0:T(8,128)S(1)}, u32[]{:S(2)}, u32[]{:S(2)}) collective-permute-start(f32[1,2,8,512]{3,2,1,0:T(8,128)S(1)} %get-tuple-element.21), channel_id=1, source_target_pairs={{0,15},{1,0},{2,1},{3,2},{4,3},{5,4},{6,5},{7,6},{8,7},{9,8},{10,9... | collective-permute-start | bytes 98312 | tf_op jit(solution)/shard_map/ppermute | solution.py:22
  51.4 16.3 %collective-permute-start.13 = (f32[1,2,8,4096]{3,2,1,0:T(8,128)S(1)}, f32[1,2,8,4096]{3,2,1,0:T(8,128)S(1)}, u32[]{:S(2)}, u32[]{:S(2)}) collective-permute-start(f32[1,2,8,4096]{3,2,1,0:T(8,128)S(1)} %add_tail.9), channel_id=1, source_target_pairs={{0,16},{16,0},{1,17},{17,1},{2,18},{18,2},{3,19},{19,3},{4,20},{20... | collective-permute-start | bytes 786440 | tf_op jit(solution)/shard_map/ppermute | solution.py:22
  51.7 17.0 %collective-permute-start.10 = (f32[1,2,8,4096]{3,2,1,0:T(8,128)S(1)}, f32[1,2,8,4096]{3,2,1,0:T(8,128)S(1)}, u32[]{:S(2)}, u32[]{:S(2)}) collective-permute-start(f32[1,2,8,4096]{3,2,1,0:T(8,128)S(1)} %add_tail.8), channel_id=1, source_target_pairs={{0,16},{16,0},{1,17},{17,1},{2,18},{18,2},{3,19},{19,3},{4,20},{20... | collective-permute-start | bytes 786440 | tf_op jit(solution)/shard_map/ppermute | solution.py:22
  53.6 18.3 %collective-permute-start.7 = (f32[1,2,8,4096]{3,2,1,0:T(8,128)S(1)}, f32[1,2,8,4096]{3,2,1,0:T(8,128)S(1)}, u32[]{:S(2)}, u32[]{:S(2)}) collective-permute-start(f32[1,2,8,4096]{3,2,1,0:T(8,128)S(1)} %add_tail.7), channel_id=1, source_target_pairs={{0,16},{16,0},{1,17},{17,1},{2,18},{18,2},{3,19},{19,3},{4,20},{20... | collective-permute-start | bytes 786440 | tf_op jit(solution)/shard_map/ppermute | solution.py:22
  53.9 22.5 %collective-permute-start.3 = (f32[1,2,8,4096]{3,2,1,0:T(8,128)S(1)}, f32[1,2,8,4096]{3,2,1,0:T(8,128)S(1)}, u32[]{:S(2)}, u32[]{:S(2)}) collective-permute-start(f32[1,2,8,4096]{3,2,1,0:T(8,128)S(1)} %add_tail.5), channel_id=1, source_target_pairs={{0,16},{16,0},{1,17},{17,1},{2,18},{18,2},{3,19},{19,3},{4,20},{20... | collective-permute-start | bytes 786440 | tf_op jit(solution)/shard_map/ppermute | solution.py:22
  58.0 4.4 %collective-permute-start.4 = (f32[2,2,16,512]{3,2,1,0:T(8,128)S(1)}, f32[2,2,16,512]{3,2,1,0:T(8,128)S(1)}, u32[]{:S(2)}, u32[]{:S(2)}) collective-permute-start(f32[2,2,16,512]{3,2,1,0:T(8,128)S(1)} %get-tuple-element.23), channel_id=1, source_target_pairs={{0,15},{1,0},{2,1},{3,2},{4,3},{5,4},{6,5},{7,6},{8,7},{9,8},{10,9... | collective-permute-start | bytes 393224 | tf_op jit(solution)/shard_map/ppermute | solution.py:22

commit v9 on v7

--- a/solution.py
+++ b/solution.py
@@ -194,7 +194,10 @@
 def add_tail_kernel(arrived, held, out):
     columns = held.shape[-1]
     at = pl.ds(columns - WIDEST, WIDEST)
-    out[:, :, :, at] = held[:, :, :, at] + arrived[...]
+    if columns > WIDEST:
+        body = pl.ds(0, columns - WIDEST)
+        out[:, :, :, body] = held[:, :, :, body]
+    out[:, :, :, at] = held[:, :, :, at] + arrived[: held.shape[0]]
 
 
 def add_tail(resident, arrived):
@@ -203,7 +206,6 @@
         out_shape=jax.ShapeDtypeStruct(resident.shape, jnp.float32),
         in_specs=[VMEM, VMEM],
         out_specs=VMEM,
-        input_output_aliases={1: 0},
         compiler_params=pltpu.CompilerParams(vmem_limit_bytes=8 << 20),
         name="add_tail",
     )(arrived, resident)
@@ -296,7 +298,7 @@
                     total = total + parts[which][0, poly]
                 if tailed:
                     last = columns - WIDEST
-                    wrapped = total[:, last:] + tails[0, poly, here, :]
+                    wrapped = total[:, last:] + tails[tails.shape[0] - 1, poly, here, :]
                     done[at, poly, here, pl.ds(0, last)] = reduce_mod(total[:, :last], wide) / wide
                     done[at, poly, here, pl.ds(last, WIDEST)] = reduce_mod(wrapped, wide) / wide
                 else:
@@ -375,7 +377,6 @@
     for block in blocks:
         sent[0, block] = lax.ppermute(picked[0, block], "grp", both)
     asked = shifted(requests, "grp", 1)
-    tail, resident = products(digits, keys, requests, rotations, modulus, slots, blocks, True, True)
     me = lax.axis_index("grp")
     rightward = jnp.where(me == 0, requests, asked)[:, key_count:]
     leftward = jnp.where(me == 0, asked, requests)[:, :key_count]
@@ -393,7 +394,7 @@
         return run
 
     branches = [branch(pairs) for pairs in (both, [(0, 1)], [(1, 0)])]
-    operands = (ahead, [picked[turn] for turn in turns[len(blocks) :]], [sent[0, block] for block in blocks[1:]], tail, resident)
+    operands = (ahead, [picked[turn] for turn in turns[len(blocks) :]], [sent[0, block] for block in blocks[1:]], digits)
     return lax.switch(case, branches, *operands, keys, requests, asked, rotations, modulus)
 
 
@@ -406,15 +407,16 @@
     return add_tail(resident, wrapped)
 
 
-def exchange(pairs, ahead, picked, arrived, tail, resident, keys, requests, asked, rotations, modulus):
+def exchange(pairs, ahead, picked, arrived, digits, keys, requests, asked, rotations, modulus):
     ciphers = requests.shape[0]
-    blocks = resident.shape[2] // ROWS
+    blocks = digits.shape[2] // ROWS
+    whole_blocks = tuple(range(blocks))
+    one_way = len(pairs[-1]) == 1
     turns = [(slot, block) for slot in range(CAP) for block in range(blocks)]
     sent = dict(zip(turns[1:blocks], arrived))
     for (slot, block), piece in zip(turns[blocks:], picked):
         sent[slot, block] = lax.ppermute(piece, "grp", pairs[slot])
-    local = joined(tail, resident)
-    result = finish(local, requests, modulus, ciphers, tuple(range(CAP, ciphers)), tuple(range(blocks)))
+    tail, resident = products(digits, keys, requests, rotations, modulus, tuple(range(CAP)), whole_blocks, True, True)
     back = {}
     late = []
     for turn in turns:
@@ -423,23 +425,29 @@
         if turn == turns[0]:
             whole = ahead
         else:
-            tail, whole = remote(sent[turn], keys, asked, rotations, modulus, slot, block)
+            wrapped, whole = remote(sent[turn], keys, asked, rotations, modulus, slot, block)
             if len(ways) == 2:
-                whole = joined(tail, whole)
+                whole = joined(wrapped, whole)
             else:
-                late.append(tail)
+                late.append(wrapped)
         if len(late) == blocks:
-            tails = lax.ppermute(jnp.concatenate(late, axis=2), "grp", ways)
-            tails = shifted(tails, "limb", -1)
+            returned = lax.ppermute(jnp.concatenate(late, axis=2), "grp", ways)
         back[turn] = lax.ppermute(whole, "grp", ways)
+    tails = None
+    if one_way:
+        tails = shifted(jnp.concatenate([tail, returned]), "limb", -1)
+        local = add_tail(resident, tails)
+    else:
+        local = joined(tail, resident)
+    result = finish(local, requests, modulus, ciphers, tuple(range(CAP, ciphers)), whole_blocks)
+    if one_way:
+        for slot in range(CAP):
+            pieces = tuple(back[slot, block] for block in range(blocks))
+            late = tails if slot == CAP - 1 else None
+            result = finish(local, requests, modulus, ciphers, (slot,), whole_blocks, pieces, result, late)
+        return result
     for slot, block in turns:
-        if len(pairs[slot]) == 2:
-            result = finish(local, requests, modulus, ciphers, (slot,), (block,), (back[slot, block],), result)
-    if late:
-        pieces = tuple(back[turn] for turn in turns[blocks:])
-        result = finish(
-            local, requests, modulus, ciphers, (CAP - 1,), tuple(range(blocks)), pieces, result, tails
-        )
+        result = finish(local, requests, modulus, ciphers, (slot,), (block,), (back[slot, block],), result)
     return result
 
 

time: 68 us -> 74.8 us (1.100)
  waiting for transfers between devices: 16.9 us -> 27.8 us
  Pallas kernels: 24 us -> 22 us
  starting transfers between devices: 24.1 us -> 22.2 us
    ppermute x1, waiting for transfers between devices: 9.71 us -> 0.01 us  [exchange(): returned = lax.ppermute(jnp.concatenate(late, axis=2), 'grp', ways)]
    ppermute x5 -> x4, waiting for transfers between devices: 0.17 us -> 9.08 us  [shifted(): return lax.ppermute(value, axis, pairs)]
    ppermute x2, waiting for transfers between devices: 7 us -> 14.8 us  [exchange(): sent[slot, block] = lax.ppermute(piece, 'grp', pairs[slot])]
    ppermute x4, waiting for transfers between devices: 0.01 us -> 3.96 us  [exchange(): back[turn] = lax.ppermute(whole, 'grp', ways)]
    pallas_call x2, Pallas kernels: 5.69 us -> 3.93 us  [gather(): pl.pallas_call(functools.partial(gather_kernel, wanted, cuts, steps, lax....]
    ppermute x5 -> x4, starting transfers between devices: 9.02 us -> 7.94 us  [shifted(): return lax.ppermute(value, axis, pairs)]
    ppermute x4, starting transfers between devices: 6.17 us -> 5.31 us  [exchange(): back[turn] = lax.ppermute(whole, 'grp', ways)]
    pallas_call x4 -> x3, Pallas kernels: 4.56 us -> 3.72 us  [finish(): pl.pallas_call(functools.partial(finish_kernel, ranks, blocks, lax.axis_s...]
  transfers between devices with their start and end apart: 14 -> 13, of which waited for: 3 -> 6; matrix products, arithmetic and copies ran while one was open for 1% -> 1% of each run, Pallas kernels for 30% -> 24%
where the time goes in v9:
time: 74.8 us; the launch traced here: 74.5 us
  waiting for transfers between devices  27.8 us (37%)
  starting transfers between devices  22.2 us (30%)
  Pallas kernels  22 us (29%)
  between operations  1.39 us (2%)
  other arithmetic  0.84 us (1%)
    ppermute x2, waiting for transfers between devices, exchange(): sent[slot, block] = lax.ppermute(piece, 'grp', pairs[slot])  14.8 us
    pallas_call x5, Pallas kernels, products(): pl.pallas_call(functools.partial(products_kernel, slots, blocks, local, l...  14.2 us
    ppermute x4, waiting for transfers between devices, shifted(): return lax.ppermute(value, axis, pairs)  9.08 us
    ppermute x4, starting transfers between devices, shifted(): return lax.ppermute(value, axis, pairs)  7.94 us
    ppermute x4, starting transfers between devices, exchange(): back[turn] = lax.ppermute(whole, 'grp', ways)  5.31 us
    ppermute x2, starting transfers between devices, key_switch_pair(): sent[0, block] = lax.ppermute(picked[0, block], 'grp', both)  5.04 us
    ppermute x4, waiting for transfers between devices, exchange(): back[turn] = lax.ppermute(whole, 'grp', ways)  3.96 us
    pallas_call x2, Pallas kernels, gather(): pl.pallas_call(functools.partial(gather_kernel, wanted, cuts, steps, lax....  3.93 us
  transfers between devices with their start and end apart: 13, of which 6 were waited for; matrix products, arithmetic and copies ran while one was open for 1% of the time, Pallas kernels for 24%

profile of v9, /device:TPU:0, one launch (start us, length us, event | category | flops | bytes accessed | tf_op | source)
XLA Modules:
  0.0 74.5 jit_solution(1959443811363070458)
XLA Ops:
  0.0 0.0 copy-start.6
  0.0 1.9 %gather.3 = f32[3,8,4096]{2,1,0:T(8,128)S(1)} custom-call(s32[4,8]{1,0:T(4,128)} %requests.3, f32[4,3,16,4096]{3,2,1,0:T(8,128)} %digits.3), custom_call_target="tpu_custom_call" | custom-call | bytes 786432 | tf_op jit(solution)/shard_map/gather/pallas_call | solution.py:71
  1.9 0.0 copy-start.8
  1.9 0.0 copy-start.7
  1.9 3.0 %collective-permute-start.30 = (f32[3,8,4096]{2,1,0:T(8,128)S(1)}, f32[3,8,4096]{2,1,0:T(8,128)S(1)}, u32[]{:S(2)}, u32[]{:S(2)}) collective-permute-start(f32[3,8,4096]{2,1,0:T(8,128)S(1)} %gather.3), channel_id=1, source_target_pairs={{0,16},{16,0},{1,17},{17,1},{2,18},{18,2},{3,19},{19,3},{4,20},{20... | collective-permute-start | bytes 1179656 | tf_op jit(solution)/shard_map/ppermute | solution.py:378
  5.0 0.0 copy-done.6
  5.0 0.1 collective-permute-start.28
  5.1 2.0 %gather.2 = (f32[3,8,4096]{2,1,0:T(8,128)S(1)}, f32[3,8,4096]{2,1,0:T(8,128)S(1)}, f32[3,8,4096]{2,1,0:T(8,128)S(1)}) custom-call(s32[4,8]{1,0:T(4,128)S(1)} %copy-done.6, f32[4,3,16,4096]{3,2,1,0:T(8,128)} %digits.3), custom_call_target="tpu_custom_call" | custom-call | bytes 2359296 | tf_op jit(solution)/shard_map/gather/pallas_call | solution.py:71
  7.1 2.0 %collective-permute-start.29 = (f32[3,8,4096]{2,1,0:T(8,128)S(1)}, f32[3,8,4096]{2,1,0:T(8,128)S(1)}, u32[]{:S(2)}, u32[]{:S(2)}) collective-permute-start(f32[3,8,4096]{2,1,0:T(8,128)S(1)} %get-tuple-element.130), channel_id=1, source_target_pairs={{0,16},{16,0},{1,17},{17,1},{2,18},{18,2},{3,19},{19,3},{4,20},{20... | collective-permute-start | bytes 1179656 | tf_op jit(solution)/shard_map/ppermute | solution.py:378
  9.1 0.0 copy-done.8
  9.1 5.9 %collective-permute-done.28.requests = s32[4,8]{1,0:T(4,128)S(1)} collective-permute-done((s32[4,8]{1,0:T(4,128)S(1)}, s32[4,8]{1,0:T(4,128)S(1)}, u32[]{:S(2)}, u32[]{:S(2)}) %collective-permute-start.28) | collective-permute-done | bytes 160 | tf_op jit(solution)/shard_map/ppermute | solution.py:22
  15.0 0.2 slice_reduce_fusion
  15.2 0.0 collective-permute-done.30
  15.2 0.1 broadcast_in_dim.36.modulus_ref
  15.3 0.0 copy-done.7
  15.3 2.8 %products.25 = (f32[1,2,8,512]{3,2,1,0:T(8,128)S(1)}, f32[1,2,8,4096]{3,2,1,0:T(8,128)S(1)}) custom-call(s32[4,8]{1,0:T(4,128)S(1)} %collective-permute-done.28.requests, s32[8]{0:T(128)S(1)} %copy-done.7, f32[1,3,8,4096]{3,2,1,0:T(8,128)S(1)} %bitcast.10, f32[4,3,2,16,4096]{4,3,2,1,0:T(8,128)} %keys.1, f32[16,128]{1,0:T(8,128)S(1)} %broadcast_in_dim.36.modulus_ref), custom_call_target="tpu_custom_call" | custom-call | flops 5242880 | bytes 3801088 | tf_op jit(solution)/shard_map/products/pallas_call | solution.py:175
  18.0 2.6 %collective-permute-start.31 = (f32[1,2,8,512]{3,2,1,0:T(8,128)S(1)}, f32[1,2,8,512]{3,2,1,0:T(8,128)S(1)}, u32[]{:S(2)}, u32[]{:S(2)}) collective-permute-start(f32[1,2,8,512]{3,2,1,0:T(8,128)S(1)} %get-tuple-element.131), channel_id=1, source_target_pairs={{0,15},{1,0},{2,1},{3,2},{4,3},{5,4},{6,5},{7,6},{8,7},{9,8},{10,9... | collective-permute-start | bytes 98312 | tf_op jit(solution)/shard_map/ppermute | solution.py:22
  20.6 0.6 add_reduce_fusion
  22.6 0.0 collective-permute-done.31.arrived
  22.6 0.0 collective-permute-done.29
  22.6 51.8 %conditional.1 = (f32[4,2,16,4096]{3,2,1,0:T(8,128)}) conditional(s32[]{:T(128)} %clamp.3, (s32[4,8]{1,0:T(4,128)S(1)}, s32[8]{0:T(128)S(1)}, f32[4,3,16,4096]{3,2,1,0:T(8,128)}, f32[4,3,2,16,4096]{4,3,2,1,0:T(8,128)}, f32[16,128]{1,0:T(8,128)S(1)}, /*index=5*/f32[3,8,4096]{2,1,0:T(8,128)S(1)}, s32[4,8]{1,0:T(4,128)S(1)}, ...), branch_computations={%region_3.4_spmd, %region_4.5_spmd, %region_5.6_spmd} | conditional | flops 47251456 | bytes 73400744 | solution.py:398
  22.7 1.3 %collective-permute-start.19 = (f32[3,8,4096]{2,1,0:T(8,128)S(1)}, f32[3,8,4096]{2,1,0:T(8,128)S(1)}, u32[]{:S(2)}, u32[]{:S(2)}) collective-permute-start(f32[3,8,4096]{2,1,0:T(8,128)S(1)} %get-tuple-element.112), channel_id=1, source_target_pairs={{16,0},{17,1},{18,2},{19,3},{20,4},{21,5},{22,6},{23,7},{24,8},{25... | collective-permute-start | bytes 1179656 | tf_op jit(solution)/shard_map/cond/branch_2_fun/ppermute | solution.py:418
  24.0 1.3 %collective-permute-start.20 = (f32[3,8,4096]{2,1,0:T(8,128)S(1)}, f32[3,8,4096]{2,1,0:T(8,128)S(1)}, u32[]{:S(2)}, u32[]{:S(2)}) collective-permute-start(f32[3,8,4096]{2,1,0:T(8,128)S(1)} %get-tuple-element.114), channel_id=1, source_target_pairs={{16,0},{17,1},{18,2},{19,3},{20,4},{21,5},{22,6},{23,7},{24,8},{25... | collective-permute-start | bytes 1179656 | tf_op jit(solution)/shard_map/cond/branch_2_fun/ppermute | solution.py:418
  25.3 11.3 %collective-permute-done.19 = f32[3,8,4096]{2,1,0:T(8,128)S(1)} collective-permute-done((f32[3,8,4096]{2,1,0:T(8,128)S(1)}, f32[3,8,4096]{2,1,0:T(8,128)S(1)}, u32[]{:S(2)}, u32[]{:S(2)}) %collective-permute-start.19) | collective-permute-done | bytes 393248 | tf_op jit(solution)/shard_map/cond/branch_2_fun/ppermute | solution.py:418
  36.5 0.0 copy-start.2
  36.5 3.5 %products.22 = (f32[1,2,8,512]{3,2,1,0:T(8,128)S(1)}, f32[1,2,8,4096]{3,2,1,0:T(8,128)S(1)}) custom-call(s32[4,8]{1,0:T(4,128)S(1)} %get-tuple-element.111.requests, s32[8]{0:T(128)S(1)} %get-tuple-element.107.rotations, f32[1,3,8,4096]{3,2,1,0:T(8,128)S(1)} %bitcast.16, f32[4,3,2,16,4096]{4,3,2,1,0:T(8,128)} %get-tuple-element.109.keys, ...), custom_call_target="tpu_custom_call" | custom-call | flops 5242880 | bytes 3801088 | tf_op jit(solution)/shard_map/cond/branch_2_fun/products/pallas_call | solution.py:175
  40.1 3.5 %collective-permute-done.20 = f32[3,8,4096]{2,1,0:T(8,128)S(1)} collective-permute-done((f32[3,8,4096]{2,1,0:T(8,128)S(1)}, f32[3,8,4096]{2,1,0:T(8,128)S(1)}, u32[]{:S(2)}, u32[]{:S(2)}) %collective-permute-start.20) | collective-permute-done | bytes 393248 | tf_op jit(solution)/shard_map/cond/branch_2_fun/ppermute | solution.py:418
  43.6 0.0 copy-done.2
  43.6 1.1 %products.23 = (f32[1,2,8,512]{3,2,1,0:T(8,128)S(1)}, f32[1,2,8,4096]{3,2,1,0:T(8,128)S(1)}) custom-call(s32[4,8]{1,0:T(4,128)S(1)} %get-tuple-element.111.requests, s32[8]{0:T(128)S(1)} %get-tuple-element.107.rotations, f32[1,3,8,4096]{3,2,1,0:T(8,128)S(1)} %bitcast.14, f32[4,3,2,16,4096]{4,3,2,1,0:T(8,128)S(1)} %copy-done.2, ...), custom_call_target="tpu_custom_call" | custom-call | flops 5242880 | bytes 3801088 | tf_op jit(solution)/shard_map/cond/branch_2_fun/products/pallas_call | solution.py:175
  44.7 1.3 %collective-permute-start.21 = (f32[1,2,16,512]{3,2,1,0:T(8,128)S(1)}, f32[1,2,16,512]{3,2,1,0:T(8,128)S(1)}, u32[]{:S(2)}, u32[]{:S(2)}) collective-permute-start(f32[1,2,16,512]{3,2,1,0:T(8,128)S(1)} %pad_maximum_fusion.3), channel_id=1, source_target_pairs={{0,16},{1,17},{2,18},{3,19},{4,20},{5,21},{6,22},{7,23},{8,24},{9,... | collective-permute-start | bytes 196616 | tf_op jit(solution)/shard_map/cond/branch_2_fun/ppermute | solution.py:434
  46.0 0.0 copy-start.5
  46.0 3.1 %products.24 = (f32[1,2,8,512]{3,2,1,0:T(8,128)S(1)}, f32[1,2,8,4096]{3,2,1,0:T(8,128)S(1)}) custom-call(s32[4,8]{1,0:T(4,128)S(1)} %get-tuple-element.111.requests, s32[8]{0:T(128)S(1)} %get-tuple-element.107.rotations, f32[1,3,8,4096]{3,2,1,0:T(8,128)S(1)} %bitcast.19, f32[4,3,2,16,4096]{4,3,2,1,0:T(8,128)} %get-tuple-element.109.keys, ...), custom_call_target="tpu_custom_call" | custom-call | flops 5242880 | bytes 3801088 | tf_op jit(solution)/shard_map/cond/branch_2_fun/products/pallas_call | solution.py:175
  49.1 3.5 %collective-permute-start.26 = (f32[1,2,8,512]{3,2,1,0:T(8,128)S(1)}, f32[1,2,8,512]{3,2,1,0:T(8,128)S(1)}, u32[]{:S(2)}, u32[]{:S(2)}) collective-permute-start(f32[1,2,8,512]{3,2,1,0:T(8,128)S(1)} %get-tuple-element.121), channel_id=1, source_target_pairs={{0,15},{1,0},{2,1},{3,2},{4,3},{5,4},{6,5},{7,6},{8,7},{9,8},{10,9... | collective-permute-start | bytes 98312 | tf_op jit(solution)/shard_map/cond/branch_2_fun/ppermute | solution.py:22
  52.6 0.0 collective-permute-start.25
  52.6 0.0 copy-done.5
  52.6 3.7 %products.21 = (f32[2,2,16,512]{3,2,1,0:T(8,128)S(1)}, f32[2,2,16,4096]{3,2,1,0:T(8,128)S(1)}) custom-call(s32[4,8]{1,0:T(4,128)S(1)} %get-tuple-element.105.requests, s32[8]{0:T(128)S(1)} %get-tuple-element.107.rotations, f32[4,3,16,4096]{3,2,1,0:T(8,128)S(1)} %copy-done.5, f32[4,3,2,16,4096]{4,3,2,1,0:T(8,128)} %get-tuple-element.109.keys, ...), custom_call_target="tpu_custom_call" | custom-call | flops 20971520 | bytes 8912896 | tf_op jit(solution)/shard_map/cond/branch_2_fun/products/pallas_call | solution.py:175
  56.3 0.0 collective-permute-done.26.arrived
  56.4 1.5 %collective-permute-start.27 = (f32[1,2,8,4096]{3,2,1,0:T(8,128)S(1)}, f32[1,2,8,4096]{3,2,1,0:T(8,128)S(1)}, u32[]{:S(2)}, u32[]{:S(2)}) collective-permute-start(f32[1,2,8,4096]{3,2,1,0:T(8,128)S(1)} %add_tail.16), channel_id=1, source_target_pairs={{16,0},{0,16},{17,1},{1,17},{18,2},{2,18},{19,3},{3,19},{20,4},{4,... | collective-permute-start | bytes 786440 | tf_op jit(solution)/shard_map/cond/branch_2_fun/ppermute | solution.py:435
  57.8 2.5 %collective-permute-start.23 = (f32[1,2,8,4096]{3,2,1,0:T(8,128)S(1)}, f32[1,2,8,4096]{3,2,1,0:T(8,128)S(1)}, u32[]{:S(2)}, u32[]{:S(2)}) collective-permute-start(f32[1,2,8,4096]{3,2,1,0:T(8,128)S(1)} %get-tuple-element.117), channel_id=1, source_target_pairs={{0,16},{1,17},{2,18},{3,19},{4,20},{5,21},{6,22},{7,23},{8,24},{9,... | collective-permute-start | bytes 786440 | tf_op jit(solution)/shard_map/cond/branch_2_fun/ppermute | solution.py:435
  60.4 1.3 %collective-permute-start.24 = (f32[1,2,8,4096]{3,2,1,0:T(8,128)S(1)}, f32[1,2,8,4096]{3,2,1,0:T(8,128)S(1)}, u32[]{:S(2)}, u32[]{:S(2)}) collective-permute-start(f32[1,2,8,4096]{3,2,1,0:T(8,128)S(1)} %get-tuple-element.118), channel_id=1, source_target_pairs={{0,16},{1,17},{2,18},{3,19},{4,20},{5,21},{6,22},{7,23},{8,24},{9,... | collective-permute-start | bytes 786440 | tf_op jit(solution)/shard_map/cond/branch_2_fun/ppermute | solution.py:435
  61.7 0.0 collective-permute-done.21
  61.7 1.8 %collective-permute-start.22 = (f32[3,2,16,512]{3,2,1,0:T(8,128)S(1)}, f32[3,2,16,512]{3,2,1,0:T(8,128)S(1)}, u32[]{:S(2)}, u32[]{:S(2)}) collective-permute-start(f32[3,2,16,512]{3,2,1,0:T(8,128)S(1)} %pad_maximum_fusion.2), channel_id=1, source_target_pairs={{0,15},{1,0},{2,1},{3,2},{4,3},{5,4},{6,5},{7,6},{8,7},{9,8},{10,9... | collective-permute-start | bytes 589832 | tf_op jit(solution)/shard_map/cond/branch_2_fun/ppermute | solution.py:22
  63.5 3.2 %collective-permute-done.22.arrived.refs_2_ = f32[3,2,16,512]{3,2,1,0:T(8,128)S(1)} collective-permute-done((f32[3,2,16,512]{3,2,1,0:T(8,128)S(1)}, f32[3,2,16,512]{3,2,1,0:T(8,128)S(1)}, u32[]{:S(2)}, u32[]{:S(2)}) %collective-permute-start.22) | collective-permute-done | bytes 196640 | tf_op jit(solution)/shard_map/cond/branch_2_fun/ppermute | solution.py:22
  66.7 0.1 add_tail.15.local
  66.7 1.4 %finish.19.refs_2_ = f32[4,2,16,4096]{3,2,1,0:T(8,128)} custom-call(s32[4,8]{1,0:T(4,128)S(1)} %get-tuple-element.105.requests, f32[16,128]{1,0:T(8,128)S(1)} %get-tuple-element.106.modulus_ref.modulus, f32[2,2,16,4096]{3,2,1,0:T(8,128)S(1)} %add_tail.15.local), custom_call_target="tpu_custom_call" | custom-call | flops 5242880 | bytes 3145728 | tf_op jit(solution)/shard_map/cond/branch_2_fun/finish/pallas_call | solution.py:323
  68.2 0.0 collective-permute-done.25.refs_0_
  68.2 0.0 collective-permute-done.27.refs_1_
  68.2 1.1 %finish.20.refs_3_ = f32[4,2,16,4096]{3,2,1,0:T(8,128)} custom-call(s32[4,8]{1,0:T(4,128)S(1)} %get-tuple-element.105.requests, f32[16,128]{1,0:T(8,128)S(1)} %get-tuple-element.106.modulus_ref.modulus, f32[2,2,16,4096]{3,2,1,0:T(8,128)S(1)} %add_tail.15.local, ...), custom_call_target="tpu_custom_call", output_to_operand_aliasing={{}: (5, {})} | custom-call | flops 2621440 | bytes 1572864 | tf_op jit(solution)/shard_map/cond/branch_2_fun/finish/pallas_call | solution.py:323
  69.4 0.8 %collective-permute-done.23.refs_0_ = f32[1,2,8,4096]{3,2,1,0:T(8,128)S(1)} collective-permute-done((f32[1,2,8,4096]{3,2,1,0:T(8,128)S(1)}, f32[1,2,8,4096]{3,2,1,0:T(8,128)S(1)}, u32[]{:S(2)}, u32[]{:S(2)}) %collective-permute-start.23) | collective-permute-done | bytes 262176 | tf_op jit(solution)/shard_map/cond/branch_2_fun/ppermute | solution.py:435
  70.2 3.2 %collective-permute-done.24.refs_1_ = f32[1,2,8,4096]{3,2,1,0:T(8,128)S(1)} collective-permute-done((f32[1,2,8,4096]{3,2,1,0:T(8,128)S(1)}, f32[1,2,8,4096]{3,2,1,0:T(8,128)S(1)}, u32[]{:S(2)}, u32[]{:S(2)}) %collective-permute-start.24) | collective-permute-done | bytes 262176 | tf_op jit(solution)/shard_map/cond/branch_2_fun/ppermute | solution.py:435
  73.3 1.1 %finish.21 = f32[4,2,16,4096]{3,2,1,0:T(8,128)} custom-call(s32[4,8]{1,0:T(4,128)S(1)} %get-tuple-element.105.requests, f32[16,128]{1,0:T(8,128)S(1)} %get-tuple-element.106.modulus_ref.modulus, f32[2,2,16,4096]{3,2,1,0:T(8,128)S(1)} %add_tail.15.local, f32[1,2,8,4096]{3,2,1,0:T(8,128)S(1)} %collective-permute-done.23.refs_0_, ...), custom_call_target="tpu_custom_call", output_to_operand_aliasing={{}: (6, {})} | custom-call | flops 2621440 | bytes 1572864 | tf_op jit(solution)/shard_map/cond/branch_2_fun/finish/pallas_call | solution.py:323
  (6 shorter events, 0.1 us)
Async XLA Ops:
  0.0 5.0 %copy-start.6 = (s32[4,8]{1,0:T(4,128)S(1)}, s32[4,8]{1,0:T(4,128)}, u32[]{:S(2)}) copy-start(s32[4,8]{1,0:T(4,128)} %requests.3) | copy-start | bytes 388
  1.9 7.2 %copy-start.8 = (s32[16]{0:T(128)S(1)}, s32[16]{0:T(128)}, u32[]{:S(2)}) copy-start(s32[16]{0:T(128)} %param.12) | copy-start | bytes 196
  1.9 13.3 %copy-start.7 = (s32[8]{0:T(128)S(1)}, s32[8]{0:T(128)}, u32[]{:S(2)}) copy-start(s32[8]{0:T(128)} %rotations.1) | copy-start | bytes 100
  1.9 13.2 %collective-permute-start.30 = (f32[3,8,4096]{2,1,0:T(8,128)S(1)}, f32[3,8,4096]{2,1,0:T(8,128)S(1)}, u32[]{:S(2)}, u32[]{:S(2)}) collective-permute-start(f32[3,8,4096]{2,1,0:T(8,128)S(1)} %gather.3), channel_id=1, source_target_pairs={{0,16},{16,0},{1,17},{17,1},{2,18},{18,2},{3,19},{19,3},{4,20},{20... | collective-permute-start | bytes 1179656 | tf_op jit(solution)/shard_map/ppermute | solution.py:378
  5.0 10.0 %collective-permute-start.28 = (s32[4,8]{1,0:T(4,128)S(1)}, s32[4,8]{1,0:T(4,128)S(1)}, u32[]{:S(2)}, u32[]{:S(2)}) collective-permute-start(s32[4,8]{1,0:T(4,128)S(1)} %copy-done.6), channel_id=1, source_target_pairs={{0,16},{16,0},{1,17},{17,1},{2,18},{18,2},{3,19},{19,3},{4,20},{20... | collective-permute-start | bytes 392 | tf_op jit(solution)/shard_map/ppermute | solution.py:22
  7.1 15.5 %collective-permute-start.29 = (f32[3,8,4096]{2,1,0:T(8,128)S(1)}, f32[3,8,4096]{2,1,0:T(8,128)S(1)}, u32[]{:S(2)}, u32[]{:S(2)}) collective-permute-start(f32[3,8,4096]{2,1,0:T(8,128)S(1)} %get-tuple-element.130), channel_id=1, source_target_pairs={{0,16},{16,0},{1,17},{17,1},{2,18},{18,2},{3,19},{19,3},{4,20},{20... | collective-permute-start | bytes 1179656 | tf_op jit(solution)/shard_map/ppermute | solution.py:378
  18.0 4.5 %collective-permute-start.31 = (f32[1,2,8,512]{3,2,1,0:T(8,128)S(1)}, f32[1,2,8,512]{3,2,1,0:T(8,128)S(1)}, u32[]{:S(2)}, u32[]{:S(2)}) collective-permute-start(f32[1,2,8,512]{3,2,1,0:T(8,128)S(1)} %get-tuple-element.131), channel_id=1, source_target_pairs={{0,15},{1,0},{2,1},{3,2},{4,3},{5,4},{6,5},{7,6},{8,7},{9,8},{10,9... | collective-permute-start | bytes 98312 | tf_op jit(solution)/shard_map/ppermute | solution.py:22
  22.7 13.9 %collective-permute-start.19 = (f32[3,8,4096]{2,1,0:T(8,128)S(1)}, f32[3,8,4096]{2,1,0:T(8,128)S(1)}, u32[]{:S(2)}, u32[]{:S(2)}) collective-permute-start(f32[3,8,4096]{2,1,0:T(8,128)S(1)} %get-tuple-element.112), channel_id=1, source_target_pairs={{16,0},{17,1},{18,2},{19,3},{20,4},{21,5},{22,6},{23,7},{24,8},{25... | collective-permute-start | bytes 1179656 | tf_op jit(solution)/shard_map/cond/branch_2_fun/ppermute | solution.py:418
  24.0 19.6 %collective-permute-start.20 = (f32[3,8,4096]{2,1,0:T(8,128)S(1)}, f32[3,8,4096]{2,1,0:T(8,128)S(1)}, u32[]{:S(2)}, u32[]{:S(2)}) collective-permute-start(f32[3,8,4096]{2,1,0:T(8,128)S(1)} %get-tuple-element.114), channel_id=1, source_target_pairs={{16,0},{17,1},{18,2},{19,3},{20,4},{21,5},{22,6},{23,7},{24,8},{25... | collective-permute-start | bytes 1179656 | tf_op jit(solution)/shard_map/cond/branch_2_fun/ppermute | solution.py:418
  36.5 7.0 %copy-start.2 = (f32[4,3,2,16,4096]{4,3,2,1,0:T(8,128)S(1)}, f32[4,3,2,16,4096]{4,3,2,1,0:T(8,128)}, u32[]{:S(2)}) copy-start(f32[4,3,2,16,4096]{4,3,2,1,0:T(8,128)} %get-tuple-element.109.keys) | copy-start | bytes 18874372 | tf_op jit(solution)/shard_map/cond
  44.7 17.0 %collective-permute-start.21 = (f32[1,2,16,512]{3,2,1,0:T(8,128)S(1)}, f32[1,2,16,512]{3,2,1,0:T(8,128)S(1)}, u32[]{:S(2)}, u32[]{:S(2)}) collective-permute-start(f32[1,2,16,512]{3,2,1,0:T(8,128)S(1)} %pad_maximum_fusion.3), channel_id=1, source_target_pairs={{0,16},{1,17},{2,18},{3,19},{4,20},{5,21},{6,22},{7,23},{8,24},{9,... | collective-permute-start | bytes 196616 | tf_op jit(solution)/shard_map/cond/branch_2_fun/ppermute | solution.py:434
  46.0 6.6 %copy-start.5 = (f32[4,3,16,4096]{3,2,1,0:T(8,128)S(1)}, f32[4,3,16,4096]{3,2,1,0:T(8,128)}, u32[]{:S(2)}) copy-start(f32[4,3,16,4096]{3,2,1,0:T(8,128)} %get-tuple-element.108.digits) | copy-start | bytes 9437188 | tf_op jit(solution)/shard_map/cond
  49.1 7.2 %collective-permute-start.26 = (f32[1,2,8,512]{3,2,1,0:T(8,128)S(1)}, f32[1,2,8,512]{3,2,1,0:T(8,128)S(1)}, u32[]{:S(2)}, u32[]{:S(2)}) collective-permute-start(f32[1,2,8,512]{3,2,1,0:T(8,128)S(1)} %get-tuple-element.121), channel_id=1, source_target_pairs={{0,15},{1,0},{2,1},{3,2},{4,3},{5,4},{6,5},{7,6},{8,7},{9,8},{10,9... | collective-permute-start | bytes 98312 | tf_op jit(solution)/shard_map/cond/branch_2_fun/ppermute | solution.py:22
  52.6 15.6 %collective-permute-start.25 = (f32[1,2,8,4096]{3,2,1,0:T(8,128)S(1)}, f32[1,2,8,4096]{3,2,1,0:T(8,128)S(1)}, u32[]{:S(2)}, u32[]{:S(2)}) collective-permute-start(f32[1,2,8,4096]{3,2,1,0:T(8,128)S(1)} %get-tuple-element.119), channel_id=1, source_target_pairs={{16,0},{0,16},{17,1},{1,17},{18,2},{2,18},{19,3},{3,19},{20,4},{4,... | collective-permute-start | bytes 786440 | tf_op jit(solution)/shard_map/cond/branch_2_fun/ppermute | solution.py:435
  56.4 11.8 %collective-permute-start.27 = (f32[1,2,8,4096]{3,2,1,0:T(8,128)S(1)}, f32[1,2,8,4096]{3,2,1,0:T(8,128)S(1)}, u32[]{:S(2)}, u32[]{:S(2)}) collective-permute-start(f32[1,2,8,4096]{3,2,1,0:T(8,128)S(1)} %add_tail.16), channel_id=1, source_target_pairs={{16,0},{0,16},{17,1},{1,17},{18,2},{2,18},{19,3},{3,19},{20,4},{4,... | collective-permute-start | bytes 786440 | tf_op jit(solution)/shard_map/cond/branch_2_fun/ppermute | solution.py:435
  57.8 12.3 %collective-permute-start.23 = (f32[1,2,8,4096]{3,2,1,0:T(8,128)S(1)}, f32[1,2,8,4096]{3,2,1,0:T(8,128)S(1)}, u32[]{:S(2)}, u32[]{:S(2)}) collective-permute-start(f32[1,2,8,4096]{3,2,1,0:T(8,128)S(1)} %get-tuple-element.117), channel_id=1, source_target_pairs={{0,16},{1,17},{2,18},{3,19},{4,20},{5,21},{6,22},{7,23},{8,24},{9,... | collective-permute-start | bytes 786440 | tf_op jit(solution)/shard_map/cond/branch_2_fun/ppermute | solution.py:435
  60.4 13.0 %collective-permute-start.24 = (f32[1,2,8,4096]{3,2,1,0:T(8,128)S(1)}, f32[1,2,8,4096]{3,2,1,0:T(8,128)S(1)}, u32[]{:S(2)}, u32[]{:S(2)}) collective-permute-start(f32[1,2,8,4096]{3,2,1,0:T(8,128)S(1)} %get-tuple-element.118), channel_id=1, source_target_pairs={{0,16},{1,17},{2,18},{3,19},{4,20},{5,21},{6,22},{7,23},{8,24},{9,... | collective-permute-start | bytes 786440 | tf_op jit(solution)/shard_map/cond/branch_2_fun/ppermute | solution.py:435
  61.7 5.0 %collective-permute-start.22 = (f32[3,2,16,512]{3,2,1,0:T(8,128)S(1)}, f32[3,2,16,512]{3,2,1,0:T(8,128)S(1)}, u32[]{:S(2)}, u32[]{:S(2)}) collective-permute-start(f32[3,2,16,512]{3,2,1,0:T(8,128)S(1)} %pad_maximum_fusion.2), channel_id=1, source_target_pairs={{0,15},{1,0},{2,1},{3,2},{4,3},{5,4},{6,5},{7,6},{8,7},{9,8},{10,9... | collective-permute-start | bytes 589832 | tf_op jit(solution)/shard_map/cond/branch_2_fun/ppermute | solution.py:22

commit v10 on v9

--- a/solution.py
+++ b/solution.py
@@ -197,7 +197,7 @@
     if columns > WIDEST:
         body = pl.ds(0, columns - WIDEST)
         out[:, :, :, body] = held[:, :, :, body]
-    out[:, :, :, at] = held[:, :, :, at] + arrived[: held.shape[0]]
+    out[:, :, :, at] = held[:, :, :, at] + arrived[...]
 
 
 def add_tail(resident, arrived):
@@ -298,7 +298,7 @@
                     total = total + parts[which][0, poly]
                 if tailed:
                     last = columns - WIDEST
-                    wrapped = total[:, last:] + tails[tails.shape[0] - 1, poly, here, :]
+                    wrapped = total[:, last:] + tails[0, poly, here, :]
                     done[at, poly, here, pl.ds(0, last)] = reduce_mod(total[:, :last], wide) / wide
                     done[at, poly, here, pl.ds(last, WIDEST)] = reduce_mod(wrapped, wide) / wide
                 else:
@@ -435,10 +435,8 @@
         back[turn] = lax.ppermute(whole, "grp", ways)
     tails = None
     if one_way:
-        tails = shifted(jnp.concatenate([tail, returned]), "limb", -1)
-        local = add_tail(resident, tails)
-    else:
-        local = joined(tail, resident)
+        tails = shifted(returned, "limb", -1)
+    local = joined(tail, resident)
     result = finish(local, requests, modulus, ciphers, tuple(range(CAP, ciphers)), whole_blocks)
     if one_way:
         for slot in range(CAP):

time: 74.8 us -> 66.8 us (0.89)
  waiting for transfers between devices: 27.8 us -> 22.9 us
  Pallas kernels: 22 us -> 19.5 us
  starting transfers between devices: 22.2 us -> 21.2 us
    ppermute x1, waiting for transfers between devices: 0.01 us -> 12.3 us  [exchange(): returned = lax.ppermute(jnp.concatenate(late, axis=2), 'grp', ways)]
    ppermute x2, waiting for transfers between devices: 14.8 us -> 4.68 us  [exchange(): sent[slot, block] = lax.ppermute(piece, 'grp', pairs[slot])]
    ppermute x4, waiting for transfers between devices: 3.96 us -> 0.01 us  [exchange(): back[turn] = lax.ppermute(whole, 'grp', ways)]
    ppermute x4 -> x5, waiting for transfers between devices: 9.08 us -> 5.89 us  [shifted(): return lax.ppermute(value, axis, pairs)]
    pallas_call x5, Pallas kernels: 14.2 us -> 11.8 us  [products(): pl.pallas_call(functools.partial(products_kernel, slots, blocks, local, l...]
    ppermute x4 -> x5, starting transfers between devices: 7.94 us -> 7.61 us  [shifted(): return lax.ppermute(value, axis, pairs)]
  transfers between devices with their start and end apart: 13 -> 14, of which waited for: 6 -> 3; matrix products, arithmetic and copies ran while one was open for 1% -> 1% of each run, Pallas kernels for 24% -> 25%
where the time goes in v10:
time: 66.8 us; the launch traced here: 66.2 us
  waiting for transfers between devices  22.9 us (34%)
  starting transfers between devices  21.2 us (32%)
  Pallas kernels  19.5 us (29%)
  between operations  1.39 us (2%)
  other arithmetic  0.83 us (1%)
    ppermute x1, waiting for transfers between devices, exchange(): returned = lax.ppermute(jnp.concatenate(late, axis=2), 'grp', ways)  12.3 us
    pallas_call x5, Pallas kernels, products(): pl.pallas_call(functools.partial(products_kernel, slots, blocks, local, l...  11.8 us
    ppermute x5, starting transfers between devices, shifted(): return lax.ppermute(value, axis, pairs)  7.61 us
    ppermute x5, waiting for transfers between devices, shifted(): return lax.ppermute(value, axis, pairs)  5.89 us
    ppermute x2, starting transfers between devices, key_switch_pair(): sent[0, block] = lax.ppermute(picked[0, block], 'grp', both)  5.04 us
    ppermute x4, starting transfers between devices, exchange(): back[turn] = lax.ppermute(whole, 'grp', ways)  4.7 us
    ppermute x2, waiting for transfers between devices, exchange(): sent[slot, block] = lax.ppermute(piece, 'grp', pairs[slot])  4.68 us
    pallas_call x2, Pallas kernels, gather(): pl.pallas_call(functools.partial(gather_kernel, wanted, cuts, steps, lax....  3.93 us
  transfers between devices with their start and end apart: 14, of which 3 were waited for; matrix products, arithmetic and copies ran while one was open for 1% of the time, Pallas kernels for 25%

profile of v10, /device:TPU:0, one launch (start us, length us, event | category | flops | bytes accessed | tf_op | source)
XLA Modules:
  0.0 66.2 jit_solution(7517939478120495678)
XLA Ops:
  0.0 0.0 copy-start.4
  0.0 1.9 %gather.3 = f32[3,8,4096]{2,1,0:T(8,128)S(1)} custom-call(s32[4,8]{1,0:T(4,128)} %requests.3, f32[4,3,16,4096]{3,2,1,0:T(8,128)} %digits.3), custom_call_target="tpu_custom_call" | custom-call | bytes 786432 | tf_op jit(solution)/shard_map/gather/pallas_call | solution.py:71
  1.9 0.0 copy-start.6
  1.9 0.0 copy-start.5
  1.9 3.0 %collective-permute-start.32 = (f32[3,8,4096]{2,1,0:T(8,128)S(1)}, f32[3,8,4096]{2,1,0:T(8,128)S(1)}, u32[]{:S(2)}, u32[]{:S(2)}) collective-permute-start(f32[3,8,4096]{2,1,0:T(8,128)S(1)} %gather.3), channel_id=1, source_target_pairs={{0,16},{16,0},{1,17},{17,1},{2,18},{18,2},{3,19},{19,3},{4,20},{20... | collective-permute-start | bytes 1179656 | tf_op jit(solution)/shard_map/ppermute | solution.py:378
  5.0 0.0 copy-done.4
  5.0 0.1 collective-permute-start.30
  5.1 2.0 %gather.2 = (f32[3,8,4096]{2,1,0:T(8,128)S(1)}, f32[3,8,4096]{2,1,0:T(8,128)S(1)}, f32[3,8,4096]{2,1,0:T(8,128)S(1)}) custom-call(s32[4,8]{1,0:T(4,128)S(1)} %copy-done.4, f32[4,3,16,4096]{3,2,1,0:T(8,128)} %digits.3), custom_call_target="tpu_custom_call" | custom-call | bytes 2359296 | tf_op jit(solution)/shard_map/gather/pallas_call | solution.py:71
  7.1 2.0 %collective-permute-start.31 = (f32[3,8,4096]{2,1,0:T(8,128)S(1)}, f32[3,8,4096]{2,1,0:T(8,128)S(1)}, u32[]{:S(2)}, u32[]{:S(2)}) collective-permute-start(f32[3,8,4096]{2,1,0:T(8,128)S(1)} %get-tuple-element.130), channel_id=1, source_target_pairs={{0,16},{16,0},{1,17},{17,1},{2,18},{18,2},{3,19},{19,3},{4,20},{20... | collective-permute-start | bytes 1179656 | tf_op jit(solution)/shard_map/ppermute | solution.py:378
  9.1 0.0 copy-done.6
  9.1 5.9 %collective-permute-done.30.requests = s32[4,8]{1,0:T(4,128)S(1)} collective-permute-done((s32[4,8]{1,0:T(4,128)S(1)}, s32[4,8]{1,0:T(4,128)S(1)}, u32[]{:S(2)}, u32[]{:S(2)}) %collective-permute-start.30) | collective-permute-done | bytes 160 | tf_op jit(solution)/shard_map/ppermute | solution.py:22
  15.0 0.2 slice_reduce_fusion
  15.2 0.0 collective-permute-done.32
  15.2 0.1 broadcast_in_dim.36.modulus_ref
  15.3 0.0 copy-done.5
  15.3 2.8 %products.25 = (f32[1,2,8,512]{3,2,1,0:T(8,128)S(1)}, f32[1,2,8,4096]{3,2,1,0:T(8,128)S(1)}) custom-call(s32[4,8]{1,0:T(4,128)S(1)} %collective-permute-done.30.requests, s32[8]{0:T(128)S(1)} %copy-done.5, f32[1,3,8,4096]{3,2,1,0:T(8,128)S(1)} %bitcast.10, f32[4,3,2,16,4096]{4,3,2,1,0:T(8,128)} %keys.1, f32[16,128]{1,0:T(8,128)S(1)} %broadcast_in_dim.36.modulus_ref), custom_call_target="tpu_custom_call" | custom-call | flops 5242880 | bytes 3801088 | tf_op jit(solution)/shard_map/products/pallas_call | solution.py:175
  18.0 2.6 %collective-permute-start.33 = (f32[1,2,8,512]{3,2,1,0:T(8,128)S(1)}, f32[1,2,8,512]{3,2,1,0:T(8,128)S(1)}, u32[]{:S(2)}, u32[]{:S(2)}) collective-permute-start(f32[1,2,8,512]{3,2,1,0:T(8,128)S(1)} %get-tuple-element.131), channel_id=1, source_target_pairs={{0,15},{1,0},{2,1},{3,2},{4,3},{5,4},{6,5},{7,6},{8,7},{9,8},{10,9... | collective-permute-start | bytes 98312 | tf_op jit(solution)/shard_map/ppermute | solution.py:22
  20.6 0.6 add_reduce_fusion
  22.6 0.0 collective-permute-done.33.arrived
  22.6 0.0 collective-permute-done.31
  22.6 43.6 %conditional.1 = (f32[4,2,16,4096]{3,2,1,0:T(8,128)}) conditional(s32[]{:T(128)} %clamp.3, (s32[4,8]{1,0:T(4,128)S(1)}, s32[8]{0:T(128)S(1)}, f32[4,3,16,4096]{3,2,1,0:T(8,128)}, f32[4,3,2,16,4096]{4,3,2,1,0:T(8,128)}, f32[16,128]{1,0:T(8,128)S(1)}, /*index=5*/f32[3,8,4096]{2,1,0:T(8,128)S(1)}, s32[4,8]{1,0:T(4,128)S(1)}, ...), branch_computations={%region_3.4_spmd, %region_4.5_spmd, %region_5.6_spmd} | conditional | flops 47202304 | bytes 72614352 | solution.py:398
  22.7 1.3 %collective-permute-start.21 = (f32[3,8,4096]{2,1,0:T(8,128)S(1)}, f32[3,8,4096]{2,1,0:T(8,128)S(1)}, u32[]{:S(2)}, u32[]{:S(2)}) collective-permute-start(f32[3,8,4096]{2,1,0:T(8,128)S(1)} %get-tuple-element.113), channel_id=1, source_target_pairs={{16,0},{17,1},{18,2},{19,3},{20,4},{21,5},{22,6},{23,7},{24,8},{25... | collective-permute-start | bytes 1179656 | tf_op jit(solution)/shard_map/cond/branch_2_fun/ppermute | solution.py:418
  24.0 1.3 %collective-permute-start.23 = (f32[3,8,4096]{2,1,0:T(8,128)S(1)}, f32[3,8,4096]{2,1,0:T(8,128)S(1)}, u32[]{:S(2)}, u32[]{:S(2)}) collective-permute-start(f32[3,8,4096]{2,1,0:T(8,128)S(1)} %get-tuple-element.115), channel_id=1, source_target_pairs={{16,0},{17,1},{18,2},{19,3},{20,4},{21,5},{22,6},{23,7},{24,8},{25... | collective-permute-start | bytes 1179656 | tf_op jit(solution)/shard_map/cond/branch_2_fun/ppermute | solution.py:418
  25.3 0.0 copy-start.3
  25.3 0.0 slice-start.2
  25.3 3.1 %products.24 = (f32[1,2,8,512]{3,2,1,0:T(8,128)S(1)}, f32[1,2,8,4096]{3,2,1,0:T(8,128)S(1)}) custom-call(s32[4,8]{1,0:T(4,128)S(1)} %get-tuple-element.112.requests, s32[8]{0:T(128)S(1)} %get-tuple-element.107.rotations, f32[1,3,8,4096]{3,2,1,0:T(8,128)S(1)} %bitcast.23, f32[4,3,2,16,4096]{4,3,2,1,0:T(8,128)} %get-tuple-element.109.keys, ...), custom_call_target="tpu_custom_call" | custom-call | flops 5242880 | bytes 3801088 | tf_op jit(solution)/shard_map/cond/branch_2_fun/products/pallas_call | solution.py:175
  28.4 4.1 %collective-permute-start.28 = (f32[1,2,8,512]{3,2,1,0:T(8,128)S(1)}, f32[1,2,8,512]{3,2,1,0:T(8,128)S(1)}, u32[]{:S(2)}, u32[]{:S(2)}) collective-permute-start(f32[1,2,8,512]{3,2,1,0:T(8,128)S(1)} %get-tuple-element.121), channel_id=1, source_target_pairs={{0,15},{1,0},{2,1},{3,2},{4,3},{5,4},{6,5},{7,6},{8,7},{9,8},{10,9... | collective-permute-start | bytes 98312 | tf_op jit(solution)/shard_map/cond/branch_2_fun/ppermute | solution.py:22
  32.5 0.0 copy-done.3
  32.5 0.0 slice-start.3
  32.5 3.7 %products.21 = (f32[2,2,16,512]{3,2,1,0:T(8,128)S(1)}, f32[2,2,16,4096]{3,2,1,0:T(8,128)S(1)}) custom-call(s32[4,8]{1,0:T(4,128)S(1)} %get-tuple-element.105.requests, s32[8]{0:T(128)S(1)} %get-tuple-element.107.rotations, f32[4,3,16,4096]{3,2,1,0:T(8,128)S(1)} %copy-done.3, f32[4,3,2,16,4096]{4,3,2,1,0:T(8,128)} %get-tuple-element.109.keys, ...), custom_call_target="tpu_custom_call" | custom-call | flops 20971520 | bytes 8912896 | tf_op jit(solution)/shard_map/cond/branch_2_fun/products/pallas_call | solution.py:175
  36.2 0.8 %collective-permute-start.20 = (f32[2,2,16,512]{3,2,1,0:T(8,128)S(1)}, f32[2,2,16,512]{3,2,1,0:T(8,128)S(1)}, u32[]{:S(2)}, u32[]{:S(2)}) collective-permute-start(f32[2,2,16,512]{3,2,1,0:T(8,128)S(1)} %get-tuple-element.110), channel_id=1, source_target_pairs={{0,15},{1,0},{2,1},{3,2},{4,3},{5,4},{6,5},{7,6},{8,7},{9,8},{10,9... | collective-permute-start | bytes 393224 | tf_op jit(solution)/shard_map/cond/branch_2_fun/ppermute | solution.py:22
  37.0 1.8 %collective-permute-start.27 = (f32[1,2,8,4096]{3,2,1,0:T(8,128)S(1)}, f32[1,2,8,4096]{3,2,1,0:T(8,128)S(1)}, u32[]{:S(2)}, u32[]{:S(2)}) collective-permute-start(f32[1,2,8,4096]{3,2,1,0:T(8,128)S(1)} %get-tuple-element.119), channel_id=1, source_target_pairs={{16,0},{0,16},{17,1},{1,17},{18,2},{2,18},{19,3},{3,19},{20,4},{4,... | collective-permute-start | bytes 786440 | tf_op jit(solution)/shard_map/cond/branch_2_fun/ppermute | solution.py:435
  38.9 0.0 collective-permute-done.28.arrived
  38.9 0.3 collective-permute-start.29
  39.2 0.0 collective-permute-done.21
  39.2 0.0 slice-done.2
  39.2 0.0 slice-done.3
  39.2 1.1 %products.22 = (f32[1,2,8,512]{3,2,1,0:T(8,128)S(1)}, f32[1,2,8,4096]{3,2,1,0:T(8,128)S(1)}) custom-call(s32[4,8]{1,0:T(4,128)S(1)} %get-tuple-element.112.requests, s32[8]{0:T(128)S(1)} %get-tuple-element.107.rotations, f32[1,3,8,4096]{3,2,1,0:T(8,128)S(1)} %bitcast.14, f32[4,3,2,16,4096]{4,3,2,1,0:T(8,128)S(1)} %bitcast.20, ...), custom_call_target="tpu_custom_call" | custom-call | flops 5242880 | bytes 3801088 | tf_op jit(solution)/shard_map/cond/branch_2_fun/products/pallas_call | solution.py:175
  40.3 4.7 %collective-permute-done.23 = f32[3,8,4096]{2,1,0:T(8,128)S(1)} collective-permute-done((f32[3,8,4096]{2,1,0:T(8,128)S(1)}, f32[3,8,4096]{2,1,0:T(8,128)S(1)}, u32[]{:S(2)}, u32[]{:S(2)}) %collective-permute-start.23) | collective-permute-done | bytes 393248 | tf_op jit(solution)/shard_map/cond/branch_2_fun/ppermute | solution.py:418
  45.0 1.1 %products.23 = (f32[1,2,8,512]{3,2,1,0:T(8,128)S(1)}, f32[1,2,8,4096]{3,2,1,0:T(8,128)S(1)}) custom-call(s32[4,8]{1,0:T(4,128)S(1)} %get-tuple-element.112.requests, s32[8]{0:T(128)S(1)} %get-tuple-element.107.rotations, f32[1,3,8,4096]{3,2,1,0:T(8,128)S(1)} %bitcast.12, f32[4,3,2,16,4096]{4,3,2,1,0:T(8,128)S(1)} %bitcast.20, ...), custom_call_target="tpu_custom_call" | custom-call | flops 5242880 | bytes 3801088 | tf_op jit(solution)/shard_map/cond/branch_2_fun/products/pallas_call | solution.py:175
  46.1 1.3 %collective-permute-start.22 = (f32[1,2,8,4096]{3,2,1,0:T(8,128)S(1)}, f32[1,2,8,4096]{3,2,1,0:T(8,128)S(1)}, u32[]{:S(2)}, u32[]{:S(2)}) collective-permute-start(f32[1,2,8,4096]{3,2,1,0:T(8,128)S(1)} %get-tuple-element.114), channel_id=1, source_target_pairs={{0,16},{1,17},{2,18},{3,19},{4,20},{5,21},{6,22},{7,23},{8,24},{9,... | collective-permute-start | bytes 786440 | tf_op jit(solution)/shard_map/cond/branch_2_fun/ppermute | solution.py:435
  47.4 1.3 %collective-permute-start.24 = (f32[1,2,8,4096]{3,2,1,0:T(8,128)S(1)}, f32[1,2,8,4096]{3,2,1,0:T(8,128)S(1)}, u32[]{:S(2)}, u32[]{:S(2)}) collective-permute-start(f32[1,2,8,4096]{3,2,1,0:T(8,128)S(1)} %get-tuple-element.116), channel_id=1, source_target_pairs={{0,16},{1,17},{2,18},{3,19},{4,20},{5,21},{6,22},{7,23},{8,24},{9,... | collective-permute-start | bytes 786440 | tf_op jit(solution)/shard_map/cond/branch_2_fun/ppermute | solution.py:435
  48.7 0.0 collective-permute-done.20.arrived
  48.7 1.3 %collective-permute-start.25 = (f32[1,2,16,512]{3,2,1,0:T(8,128)S(1)}, f32[1,2,16,512]{3,2,1,0:T(8,128)S(1)}, u32[]{:S(2)}, u32[]{:S(2)}) collective-permute-start(f32[1,2,16,512]{3,2,1,0:T(8,128)S(1)} %pad_maximum_fusion.1), channel_id=1, source_target_pairs={{0,16},{1,17},{2,18},{3,19},{4,20},{5,21},{6,22},{7,23},{8,24},{9,... | collective-permute-start | bytes 196616 | tf_op jit(solution)/shard_map/cond/branch_2_fun/ppermute | solution.py:434
  50.0 12.3 %collective-permute-done.25 = f32[1,2,16,512]{3,2,1,0:T(8,128)S(1)} collective-permute-done((f32[1,2,16,512]{3,2,1,0:T(8,128)S(1)}, f32[1,2,16,512]{3,2,1,0:T(8,128)S(1)}, u32[]{:S(2)}, u32[]{:S(2)}) %collective-permute-start.25) | collective-permute-done | bytes 65568 | tf_op jit(solution)/shard_map/cond/branch_2_fun/ppermute | solution.py:434
  62.3 0.0 collective-permute-start.26
  62.3 0.1 add_tail.15.local
  62.4 1.4 %finish.19.refs_2_ = f32[4,2,16,4096]{3,2,1,0:T(8,128)} custom-call(s32[4,8]{1,0:T(4,128)S(1)} %get-tuple-element.105.requests, f32[16,128]{1,0:T(8,128)S(1)} %get-tuple-element.106.modulus_ref.modulus, f32[2,2,16,4096]{3,2,1,0:T(8,128)S(1)} %add_tail.15.local), custom_call_target="tpu_custom_call" | custom-call | flops 5242880 | bytes 3145728 | tf_op jit(solution)/shard_map/cond/branch_2_fun/finish/pallas_call | solution.py:323
  63.9 0.0 collective-permute-done.27.refs_0_
  63.9 0.0 collective-permute-done.29.refs_1_
  63.9 1.1 %finish.20.refs_3_ = f32[4,2,16,4096]{3,2,1,0:T(8,128)} custom-call(s32[4,8]{1,0:T(4,128)S(1)} %get-tuple-element.105.requests, f32[16,128]{1,0:T(8,128)S(1)} %get-tuple-element.106.modulus_ref.modulus, f32[2,2,16,4096]{3,2,1,0:T(8,128)S(1)} %add_tail.15.local, ...), custom_call_target="tpu_custom_call", output_to_operand_aliasing={{}: (5, {})} | custom-call | flops 2621440 | bytes 1572864 | tf_op jit(solution)/shard_map/cond/branch_2_fun/finish/pallas_call | solution.py:323
  65.0 0.0 collective-permute-done.26.refs_2_
  65.0 0.0 collective-permute-done.22.refs_0_
  65.1 0.0 collective-permute-done.24.refs_1_
  65.1 1.1 %finish.21 = f32[4,2,16,4096]{3,2,1,0:T(8,128)} custom-call(s32[4,8]{1,0:T(4,128)S(1)} %get-tuple-element.105.requests, f32[16,128]{1,0:T(8,128)S(1)} %get-tuple-element.106.modulus_ref.modulus, f32[2,2,16,4096]{3,2,1,0:T(8,128)S(1)} %add_tail.15.local, f32[1,2,8,4096]{3,2,1,0:T(8,128)S(1)} %collective-permute-done.22.refs_0_, ...), custom_call_target="tpu_custom_call", output_to_operand_aliasing={{}: (6, {})} | custom-call | flops 2621440 | bytes 1572864 | tf_op jit(solution)/shard_map/cond/branch_2_fun/finish/pallas_call | solution.py:323
  (6 shorter events, 0.1 us)
Async XLA Ops:
  0.0 5.0 %copy-start.4 = (s32[4,8]{1,0:T(4,128)S(1)}, s32[4,8]{1,0:T(4,128)}, u32[]{:S(2)}) copy-start(s32[4,8]{1,0:T(4,128)} %requests.3) | copy-start | bytes 388
  1.9 7.2 %copy-start.6 = (s32[16]{0:T(128)S(1)}, s32[16]{0:T(128)}, u32[]{:S(2)}) copy-start(s32[16]{0:T(128)} %param.12) | copy-start | bytes 196
  1.9 13.3 %copy-start.5 = (s32[8]{0:T(128)S(1)}, s32[8]{0:T(128)}, u32[]{:S(2)}) copy-start(s32[8]{0:T(128)} %rotations.1) | copy-start | bytes 100
  1.9 13.2 %collective-permute-start.32 = (f32[3,8,4096]{2,1,0:T(8,128)S(1)}, f32[3,8,4096]{2,1,0:T(8,128)S(1)}, u32[]{:S(2)}, u32[]{:S(2)}) collective-permute-start(f32[3,8,4096]{2,1,0:T(8,128)S(1)} %gather.3), channel_id=1, source_target_pairs={{0,16},{16,0},{1,17},{17,1},{2,18},{18,2},{3,19},{19,3},{4,20},{20... | collective-permute-start | bytes 1179656 | tf_op jit(solution)/shard_map/ppermute | solution.py:378
  5.0 10.0 %collective-permute-start.30 = (s32[4,8]{1,0:T(4,128)S(1)}, s32[4,8]{1,0:T(4,128)S(1)}, u32[]{:S(2)}, u32[]{:S(2)}) collective-permute-start(s32[4,8]{1,0:T(4,128)S(1)} %copy-done.4), channel_id=1, source_target_pairs={{0,16},{16,0},{1,17},{17,1},{2,18},{18,2},{3,19},{19,3},{4,20},{20... | collective-permute-start | bytes 392 | tf_op jit(solution)/shard_map/ppermute | solution.py:22
  7.1 15.5 %collective-permute-start.31 = (f32[3,8,4096]{2,1,0:T(8,128)S(1)}, f32[3,8,4096]{2,1,0:T(8,128)S(1)}, u32[]{:S(2)}, u32[]{:S(2)}) collective-permute-start(f32[3,8,4096]{2,1,0:T(8,128)S(1)} %get-tuple-element.130), channel_id=1, source_target_pairs={{0,16},{16,0},{1,17},{17,1},{2,18},{18,2},{3,19},{19,3},{4,20},{20... | collective-permute-start | bytes 1179656 | tf_op jit(solution)/shard_map/ppermute | solution.py:378
  18.0 4.5 %collective-permute-start.33 = (f32[1,2,8,512]{3,2,1,0:T(8,128)S(1)}, f32[1,2,8,512]{3,2,1,0:T(8,128)S(1)}, u32[]{:S(2)}, u32[]{:S(2)}) collective-permute-start(f32[1,2,8,512]{3,2,1,0:T(8,128)S(1)} %get-tuple-element.131), channel_id=1, source_target_pairs={{0,15},{1,0},{2,1},{3,2},{4,3},{5,4},{6,5},{7,6},{8,7},{9,8},{10,9... | collective-permute-start | bytes 98312 | tf_op jit(solution)/shard_map/ppermute | solution.py:22
  22.7 16.5 %collective-permute-start.21 = (f32[3,8,4096]{2,1,0:T(8,128)S(1)}, f32[3,8,4096]{2,1,0:T(8,128)S(1)}, u32[]{:S(2)}, u32[]{:S(2)}) collective-permute-start(f32[3,8,4096]{2,1,0:T(8,128)S(1)} %get-tuple-element.113), channel_id=1, source_target_pairs={{16,0},{17,1},{18,2},{19,3},{20,4},{21,5},{22,6},{23,7},{24,8},{25... | collective-permute-start | bytes 1179656 | tf_op jit(solution)/shard_map/cond/branch_2_fun/ppermute | solution.py:418
  24.0 21.0 %collective-permute-start.23 = (f32[3,8,4096]{2,1,0:T(8,128)S(1)}, f32[3,8,4096]{2,1,0:T(8,128)S(1)}, u32[]{:S(2)}, u32[]{:S(2)}) collective-permute-start(f32[3,8,4096]{2,1,0:T(8,128)S(1)} %get-tuple-element.115), channel_id=1, source_target_pairs={{16,0},{17,1},{18,2},{19,3},{20,4},{21,5},{22,6},{23,7},{24,8},{25... | collective-permute-start | bytes 1179656 | tf_op jit(solution)/shard_map/cond/branch_2_fun/ppermute | solution.py:418
  25.3 7.2 %copy-start.3 = (f32[4,3,16,4096]{3,2,1,0:T(8,128)S(1)}, f32[4,3,16,4096]{3,2,1,0:T(8,128)}, u32[]{:S(2)}) copy-start(f32[4,3,16,4096]{3,2,1,0:T(8,128)} %get-tuple-element.108.digits) | copy-start | bytes 9437188 | tf_op jit(solution)/shard_map/cond
  25.3 13.9 %slice-start.2 = ((s8[6291456]{0:T(1024)(128)(4,1)}), s8[4194304]{0:T(1024)(128)(4,1)S(1)}, s32[]{:S(2)}) async-start(s8[6291456]{0:T(1024)(128)(4,1)} %bitcast.19), calls=%async_computation.2 | async-start | bytes 8388608 | tf_op jit(solution)/shard_map/cond
  28.4 10.5 %collective-permute-start.28 = (f32[1,2,8,512]{3,2,1,0:T(8,128)S(1)}, f32[1,2,8,512]{3,2,1,0:T(8,128)S(1)}, u32[]{:S(2)}, u32[]{:S(2)}) collective-permute-start(f32[1,2,8,512]{3,2,1,0:T(8,128)S(1)} %get-tuple-element.121), channel_id=1, source_target_pairs={{0,15},{1,0},{2,1},{3,2},{4,3},{5,4},{6,5},{7,6},{8,7},{9,8},{10,9... | collective-permute-start | bytes 98312 | tf_op jit(solution)/shard_map/cond/branch_2_fun/ppermute | solution.py:22
  32.5 6.7 %slice-start.3 = ((s8[6291456]{0:T(1024)(128)(4,1)}), s8[2097152]{0:T(1024)(128)(4,1)S(1)}, s32[]{:S(2)}) async-start(s8[6291456]{0:T(1024)(128)(4,1)} %bitcast.19), calls=%async_computation.3 | async-start | bytes 4194304 | tf_op jit(solution)/shard_map/cond
  36.2 12.5 %collective-permute-start.20 = (f32[2,2,16,512]{3,2,1,0:T(8,128)S(1)}, f32[2,2,16,512]{3,2,1,0:T(8,128)S(1)}, u32[]{:S(2)}, u32[]{:S(2)}) collective-permute-start(f32[2,2,16,512]{3,2,1,0:T(8,128)S(1)} %get-tuple-element.110), channel_id=1, source_target_pairs={{0,15},{1,0},{2,1},{3,2},{4,3},{5,4},{6,5},{7,6},{8,7},{9,8},{10,9... | collective-permute-start | bytes 393224 | tf_op jit(solution)/shard_map/cond/branch_2_fun/ppermute | solution.py:22
  37.0 26.8 %collective-permute-start.27 = (f32[1,2,8,4096]{3,2,1,0:T(8,128)S(1)}, f32[1,2,8,4096]{3,2,1,0:T(8,128)S(1)}, u32[]{:S(2)}, u32[]{:S(2)}) collective-permute-start(f32[1,2,8,4096]{3,2,1,0:T(8,128)S(1)} %get-tuple-element.119), channel_id=1, source_target_pairs={{16,0},{0,16},{17,1},{1,17},{18,2},{2,18},{19,3},{3,19},{20,4},{4,... | collective-permute-start | bytes 786440 | tf_op jit(solution)/shard_map/cond/branch_2_fun/ppermute | solution.py:435
  38.9 25.0 %collective-permute-start.29 = (f32[1,2,8,4096]{3,2,1,0:T(8,128)S(1)}, f32[1,2,8,4096]{3,2,1,0:T(8,128)S(1)}, u32[]{:S(2)}, u32[]{:S(2)}) collective-permute-start(f32[1,2,8,4096]{3,2,1,0:T(8,128)S(1)} %add_tail.16), channel_id=1, source_target_pairs={{16,0},{0,16},{17,1},{1,17},{18,2},{2,18},{19,3},{3,19},{20,4},{4,... | collective-permute-start | bytes 786440 | tf_op jit(solution)/shard_map/cond/branch_2_fun/ppermute | solution.py:435
  46.1 19.0 %collective-permute-start.22 = (f32[1,2,8,4096]{3,2,1,0:T(8,128)S(1)}, f32[1,2,8,4096]{3,2,1,0:T(8,128)S(1)}, u32[]{:S(2)}, u32[]{:S(2)}) collective-permute-start(f32[1,2,8,4096]{3,2,1,0:T(8,128)S(1)} %get-tuple-element.114), channel_id=1, source_target_pairs={{0,16},{1,17},{2,18},{3,19},{4,20},{5,21},{6,22},{7,23},{8,24},{9,... | collective-permute-start | bytes 786440 | tf_op jit(solution)/shard_map/cond/branch_2_fun/ppermute | solution.py:435
  47.4 17.7 %collective-permute-start.24 = (f32[1,2,8,4096]{3,2,1,0:T(8,128)S(1)}, f32[1,2,8,4096]{3,2,1,0:T(8,128)S(1)}, u32[]{:S(2)}, u32[]{:S(2)}) collective-permute-start(f32[1,2,8,4096]{3,2,1,0:T(8,128)S(1)} %get-tuple-element.116), channel_id=1, source_target_pairs={{0,16},{1,17},{2,18},{3,19},{4,20},{5,21},{6,22},{7,23},{8,24},{9,... | collective-permute-start | bytes 786440 | tf_op jit(solution)/shard_map/cond/branch_2_fun/ppermute | solution.py:435
  48.7 13.6 %collective-permute-start.25 = (f32[1,2,16,512]{3,2,1,0:T(8,128)S(1)}, f32[1,2,16,512]{3,2,1,0:T(8,128)S(1)}, u32[]{:S(2)}, u32[]{:S(2)}) collective-permute-start(f32[1,2,16,512]{3,2,1,0:T(8,128)S(1)} %pad_maximum_fusion.1), channel_id=1, source_target_pairs={{0,16},{1,17},{2,18},{3,19},{4,20},{5,21},{6,22},{7,23},{8,24},{9,... | collective-permute-start | bytes 196616 | tf_op jit(solution)/shard_map/cond/branch_2_fun/ppermute | solution.py:434
  62.3 2.7 %collective-permute-start.26 = (f32[1,2,16,512]{3,2,1,0:T(8,128)S(1)}, f32[1,2,16,512]{3,2,1,0:T(8,128)S(1)}, u32[]{:S(2)}, u32[]{:S(2)}) collective-permute-start(f32[1,2,16,512]{3,2,1,0:T(8,128)S(1)} %collective-permute-done.25), channel_id=1, source_target_pairs={{0,15},{1,0},{2,1},{3,2},{4,3},{5,4},{6,5},{7,6},{8,7},{9,8},{10,9... | collective-permute-start | bytes 196616 | tf_op jit(solution)/shard_map/cond/branch_2_fun/ppermute | solution.py:22

commit v11 on v8

--- a/solution.py
+++ b/solution.py
@@ -79,7 +79,7 @@
             flops=0, transcendentals=0, bytes_accessed=8 * len(wanted) * parts * ROWS * columns
         ),
         name="gather_digits",
-    )(requests, pltpu.with_memory_space_constraint(digits, pltpu.HBM))
+    )(*(pltpu.with_memory_space_constraint(array, pltpu.HBM) for array in (requests, digits)))
 
 
 def products_kernel(slots, blocks, local, requests, rotations, digits, keys, modulus_ref, tail, resident, rolled):
@@ -161,6 +161,9 @@
 def add_tail_kernel(arrived, held, out):
     columns = held.shape[-1]
     at = pl.ds(columns - WIDEST, WIDEST)
+    if columns > WIDEST:
+        body = pl.ds(0, columns - WIDEST)
+        out[:, :, :, body] = held[:, :, :, body]
     out[:, :, :, at] = held[:, :, :, at] + arrived[...]
 
 
@@ -170,7 +173,6 @@
         out_shape=jax.ShapeDtypeStruct(resident.shape, jnp.float32),
         in_specs=[VMEM, VMEM],
         out_specs=VMEM,
-        input_output_aliases={1: 0},
         compiler_params=pltpu.CompilerParams(vmem_limit_bytes=8 << 20),
         name="add_tail",
     )(arrived, resident)

time: 77.7 us -> 77.4 us (level)
  transfers between devices with their start and end apart: 14 -> 14, of which waited for: 4 -> 4; matrix products, arithmetic and copies ran while one was open for 0% -> 0% of each run, Pallas kernels for 23% -> 24%
where the time goes in v11:
time: 77.4 us; the launch traced here: 77.2 us
  waiting for transfers between devices  36.2 us (47%)
  Pallas kernels  21.5 us (28%)
  starting transfers between devices  19.2 us (25%)
    ppermute x14, waiting for transfers between devices, shifted(): return lax.ppermute(value, axis, pairs)  36.2 us
    ppermute x14, starting transfers between devices, shifted(): return lax.ppermute(value, axis, pairs)  19.2 us
    pallas_call x5, Pallas kernels, products(): pl.pallas_call(functools.partial(products_kernel, slots, blocks, local),...  7.64 us
    pallas_call x1, Pallas kernels, sums(): pl.pallas_call(functools.partial(sums_kernel, owners, groups, ciphers, ke...  5.26 us
    pallas_call x2, Pallas kernels, gather(): pl.pallas_call(functools.partial(gather_kernel, wanted, cuts, steps, lax....  4.42 us
    pallas_call x4, Pallas kernels, finish(): pl.pallas_call(functools.partial(finish_kernel, slot, block, groups), out...  4.05 us
  transfers between devices with their start and end apart: 14, of which 4 were waited for; matrix products, arithmetic and copies ran while one was open for 0% of the time, Pallas kernels for 24%

profile of v11, /device:TPU:0, one launch (start us, length us, event | category | flops | bytes accessed | tf_op | source)
XLA Modules:
  0.0 77.2 jit_solution(45055748107517156)
XLA Ops:
  0.0 0.0 copy-start
  0.0 2.3 %gather_digits.3 = f32[3,8,4096]{2,1,0:T(8,128)S(1)} custom-call(s32[4,8]{1,0:T(4,128)} %requests.15, f32[4,3,16,4096]{3,2,1,0:T(8,128)} %digits.5), custom_call_target="tpu_custom_call" | custom-call | bytes 786432 | tf_op jit(solution)/shard_map/gather_digits/pallas_call | solution.py:71
  2.3 0.0 copy-start.2
  2.3 0.0 copy-start.4
  2.3 0.0 copy-start.3
  2.3 3.0 %collective-permute-start.11 = (f32[3,8,4096]{2,1,0:T(8,128)S(1)}, f32[3,8,4096]{2,1,0:T(8,128)S(1)}, u32[]{:S(2)}, u32[]{:S(2)}) collective-permute-start(f32[3,8,4096]{2,1,0:T(8,128)S(1)} %gather_digits.3), channel_id=1, source_target_pairs={{0,16},{16,0},{1,17},{17,1},{2,18},{18,2},{3,19},{19,3},{4,20},{20... | collective-permute-start | bytes 1179656 | tf_op jit(solution)/shard_map/ppermute | solution.py:22
  5.4 2.1 %gather_digits.2 = (f32[3,8,4096]{2,1,0:T(8,128)S(1)}, f32[3,8,4096]{2,1,0:T(8,128)S(1)}, f32[3,8,4096]{2,1,0:T(8,128)S(1)}) custom-call(s32[4,8]{1,0:T(4,128)} %requests.15, f32[4,3,16,4096]{3,2,1,0:T(8,128)} %digits.5), custom_call_target="tpu_custom_call" | custom-call | bytes 2359296 | tf_op jit(solution)/shard_map/gather_digits/pallas_call | solution.py:71
  7.5 0.1 collective-permute-start.5
  7.6 2.0 %collective-permute-start.8 = (f32[3,8,4096]{2,1,0:T(8,128)S(1)}, f32[3,8,4096]{2,1,0:T(8,128)S(1)}, u32[]{:S(2)}, u32[]{:S(2)}) collective-permute-start(f32[3,8,4096]{2,1,0:T(8,128)S(1)} %get-tuple-element.29), channel_id=1, source_target_pairs={{0,16},{16,0},{1,17},{17,1},{2,18},{18,2},{3,19},{19,3},{4,20},{20... | collective-permute-start | bytes 1179656 | tf_op jit(solution)/shard_map/ppermute | solution.py:22
  9.6 0.1 collective-permute-start.1
  9.7 0.0 copy-done.2
  9.7 1.9 %collective-permute-start = (s32[4,8]{1,0:T(4,128)S(1)}, s32[4,8]{1,0:T(4,128)S(1)}, u32[]{:S(2)}, u32[]{:S(2)}) collective-permute-start(s32[4,8]{1,0:T(4,128)S(1)} %copy-done.2), channel_id=1, source_target_pairs={{0,16},{16,0},{1,17},{17,1},{2,18},{18,2},{3,19},{19,3},{4,20},{20... | collective-permute-start | bytes 392 | tf_op jit(solution)/shard_map/ppermute | solution.py:22
  11.6 0.0 copy-done.4
  11.6 28.2 %collective-permute-done.requests = s32[4,8]{1,0:T(4,128)S(1)} collective-permute-done((s32[4,8]{1,0:T(4,128)S(1)}, s32[4,8]{1,0:T(4,128)S(1)}, u32[]{:S(2)}, u32[]{:S(2)}) %collective-permute-start) | collective-permute-done | bytes 160 | tf_op jit(solution)/shard_map/ppermute | solution.py:22
  39.8 0.0 collective-permute-done.11
  39.8 0.1 broadcast_in_dim.18.modulus_ref.modulus
  39.9 0.0 copy-done
  39.9 0.0 copy-done.3
  39.9 1.6 %products.9 = (f32[1,2,8,512]{3,2,1,0:T(8,128)S(1)}, f32[1,2,8,4096]{3,2,1,0:T(8,128)S(1)}) custom-call(s32[4,8]{1,0:T(4,128)S(1)} %collective-permute-done.requests, s32[8]{0:T(128)S(1)} %copy-done.3, f32[1,3,8,4096]{3,2,1,0:T(8,128)S(1)} %bitcast.7, f32[4,3,2,16,4096]{4,3,2,1,0:T(8,128)S(1)} %copy-done, f32[16,128]{1,0:T(8,128)S(1)} %broadcast_in_dim.18.modulus_ref.modulus), custom_call_target="tpu_custom_call" | custom-call | flops 5242880 | bytes 3801088 | tf_op jit(solution)/shard_map/products/pallas_call | solution.py:144
  41.4 3.4 %collective-permute-start.12 = (f32[1,2,8,512]{3,2,1,0:T(8,128)S(1)}, f32[1,2,8,512]{3,2,1,0:T(8,128)S(1)}, u32[]{:S(2)}, u32[]{:S(2)}) collective-permute-start(f32[1,2,8,512]{3,2,1,0:T(8,128)S(1)} %get-tuple-element.32), channel_id=1, source_target_pairs={{0,15},{1,0},{2,1},{3,2},{4,3},{5,4},{6,5},{7,6},{8,7},{9,8},{10,9... | collective-permute-start | bytes 98312 | tf_op jit(solution)/shard_map/ppermute | solution.py:22
  44.9 0.0 collective-permute-done.5
  44.9 1.1 %products.7 = (f32[1,2,8,512]{3,2,1,0:T(8,128)S(1)}, f32[1,2,8,4096]{3,2,1,0:T(8,128)S(1)}) custom-call(s32[4,8]{1,0:T(4,128)S(1)} %collective-permute-done.requests, s32[8]{0:T(128)S(1)} %copy-done.3, f32[1,3,8,4096]{3,2,1,0:T(8,128)S(1)} %bitcast.6, f32[4,3,2,16,4096]{4,3,2,1,0:T(8,128)S(1)} %copy-done, f32[16,128]{1,0:T(8,128)S(1)} %broadcast_in_dim.18.modulus_ref.modulus), custom_call_target="tpu_custom_call" | custom-call | flops 5242880 | bytes 3801088 | tf_op jit(solution)/shard_map/products/pallas_call | solution.py:144
  46.0 1.6 %collective-permute-start.6 = (f32[1,2,8,512]{3,2,1,0:T(8,128)S(1)}, f32[1,2,8,512]{3,2,1,0:T(8,128)S(1)}, u32[]{:S(2)}, u32[]{:S(2)}) collective-permute-start(f32[1,2,8,512]{3,2,1,0:T(8,128)S(1)} %get-tuple-element.27), channel_id=1, source_target_pairs={{0,15},{1,0},{2,1},{3,2},{4,3},{5,4},{6,5},{7,6},{8,7},{9,8},{10,9... | collective-permute-start | bytes 98312 | tf_op jit(solution)/shard_map/ppermute | solution.py:22
  47.6 0.0 collective-permute-done.8
  47.6 1.6 %products.8 = (f32[1,2,8,512]{3,2,1,0:T(8,128)S(1)}, f32[1,2,8,4096]{3,2,1,0:T(8,128)S(1)}) custom-call(s32[4,8]{1,0:T(4,128)S(1)} %collective-permute-done.requests, s32[8]{0:T(128)S(1)} %copy-done.3, f32[1,3,8,4096]{3,2,1,0:T(8,128)S(1)} %bitcast.5, f32[4,3,2,16,4096]{4,3,2,1,0:T(8,128)S(1)} %copy-done, f32[16,128]{1,0:T(8,128)S(1)} %broadcast_in_dim.18.modulus_ref.modulus), custom_call_target="tpu_custom_call" | custom-call | flops 5242880 | bytes 3801088 | tf_op jit(solution)/shard_map/products/pallas_call | solution.py:144
  49.2 0.1 collective-permute-start.9
  49.3 0.0 collective-permute-done.1
  49.3 0.0 copy-start.1
  49.3 1.2 %products.5 = (f32[1,2,8,512]{3,2,1,0:T(8,128)S(1)}, f32[1,2,8,4096]{3,2,1,0:T(8,128)S(1)}) custom-call(s32[4,8]{1,0:T(4,128)S(1)} %collective-permute-done.requests, s32[8]{0:T(128)S(1)} %copy-done.3, f32[1,3,8,4096]{3,2,1,0:T(8,128)S(1)} %bitcast.4, f32[4,3,2,16,4096]{4,3,2,1,0:T(8,128)S(1)} %copy-done, f32[16,128]{1,0:T(8,128)S(1)} %broadcast_in_dim.18.modulus_ref.modulus), custom_call_target="tpu_custom_call" | custom-call | flops 5242880 | bytes 3801088 | tf_op jit(solution)/shard_map/products/pallas_call | solution.py:144
  50.5 0.6 collective-permute-start.2
  51.1 0.0 collective-permute-done.12.arrived
  51.1 0.3 collective-permute-start.13
  51.4 0.0 collective-permute-done.9.arrived
  51.5 1.8 %collective-permute-start.10 = (f32[1,2,8,4096]{3,2,1,0:T(8,128)S(1)}, f32[1,2,8,4096]{3,2,1,0:T(8,128)S(1)}, u32[]{:S(2)}, u32[]{:S(2)}) collective-permute-start(f32[1,2,8,4096]{3,2,1,0:T(8,128)S(1)} %add_tail.8), channel_id=1, source_target_pairs={{0,16},{16,0},{1,17},{17,1},{2,18},{18,2},{3,19},{19,3},{4,20},{20... | collective-permute-start | bytes 786440 | tf_op jit(solution)/shard_map/ppermute | solution.py:22
  53.3 0.0 collective-permute-done.6.arrived
  53.3 0.3 collective-permute-start.7
  53.6 0.0 collective-permute-done.2.arrived
  53.7 1.8 %collective-permute-start.3 = (f32[1,2,8,4096]{3,2,1,0:T(8,128)S(1)}, f32[1,2,8,4096]{3,2,1,0:T(8,128)S(1)}, u32[]{:S(2)}, u32[]{:S(2)}) collective-permute-start(f32[1,2,8,4096]{3,2,1,0:T(8,128)S(1)} %add_tail.5), channel_id=1, source_target_pairs={{0,16},{16,0},{1,17},{17,1},{2,18},{18,2},{3,19},{19,3},{4,20},{20... | collective-permute-start | bytes 786440 | tf_op jit(solution)/shard_map/ppermute | solution.py:22
  55.5 0.0 copy-done.1
  55.5 2.2 %products.6 = (f32[2,2,16,512]{3,2,1,0:T(8,128)S(1)}, f32[2,2,16,4096]{3,2,1,0:T(8,128)S(1)}) custom-call(s32[4,8]{1,0:T(4,128)S(1)} %copy-done.2, s32[8]{0:T(128)S(1)} %copy-done.3, f32[4,3,16,4096]{3,2,1,0:T(8,128)S(1)} %copy-done.1, f32[4,3,2,16,4096]{4,3,2,1,0:T(8,128)S(1)} %copy-done, f32[16,128]{1,0:T(8,128)S(1)} %broadcast_in_dim.18.modulus_ref.modulus), custom_call_target="tpu_custom_call" | custom-call | flops 20971520 | bytes 8912896 | tf_op jit(solution)/shard_map/products/pallas_call | solution.py:144
  57.8 2.0 %collective-permute-start.4 = (f32[2,2,16,512]{3,2,1,0:T(8,128)S(1)}, f32[2,2,16,512]{3,2,1,0:T(8,128)S(1)}, u32[]{:S(2)}, u32[]{:S(2)}) collective-permute-start(f32[2,2,16,512]{3,2,1,0:T(8,128)S(1)} %get-tuple-element.23), channel_id=1, source_target_pairs={{0,15},{1,0},{2,1},{3,2},{4,3},{5,4},{6,5},{7,6},{8,7},{9,8},{10,9... | collective-permute-start | bytes 393224 | tf_op jit(solution)/shard_map/ppermute | solution.py:22
  59.7 2.5 %collective-permute-done.4.arrived = f32[2,2,16,512]{3,2,1,0:T(8,128)S(1)} collective-permute-done((f32[2,2,16,512]{3,2,1,0:T(8,128)S(1)}, f32[2,2,16,512]{3,2,1,0:T(8,128)S(1)}, u32[]{:S(2)}, u32[]{:S(2)}) %collective-permute-start.4) | collective-permute-done | bytes 131104 | tf_op jit(solution)/shard_map/ppermute | solution.py:22
  62.3 0.1 add_tail.6.refs_0_
  62.3 5.3 %sums.1 = (f32[4,2,16,4096]{3,2,1,0:T(8,128)}, f32[2,2,16,4096]{3,2,1,0:T(8,128)S(1)}) custom-call(s32[4,8]{1,0:T(4,128)S(1)} %copy-done.2, f32[16,128]{1,0:T(8,128)S(1)} %broadcast_in_dim.18.modulus_ref.modulus, f32[2,2,16,4096]{3,2,1,0:T(8,128)S(1)} %add_tail.6.refs_0_), custom_call_target="tpu_custom_call" | custom-call | flops 10485760 | bytes 4194304 | tf_op jit(solution)/shard_map/sums/pallas_call | solution.py:223
  67.6 0.0 collective-permute-done.13.part
  67.6 1.0 %finish.4.before = f32[4,2,16,4096]{3,2,1,0:T(8,128)} custom-call(s32[4,8]{1,0:T(4,128)S(1)} %copy-done.2, f32[16,128]{1,0:T(8,128)S(1)} %broadcast_in_dim.18.modulus_ref.modulus, f32[1,2,8,4096]{3,2,1,0:T(8,128)S(1)} %collective-permute-done.13.part, f32[2,2,16,4096]{3,2,1,0:T(8,128)S(1)} %get-tuple-element.25.held, ...), custom_call_target="tpu_custom_call", output_to_operand_aliasing={{}: (4, {})} | custom-call | flops 1310720 | bytes 786432 | tf_op jit(solution)/shard_map/finish/pallas_call | solution.py:274
  68.6 0.0 collective-permute-done.10.part
  68.6 1.0 %finish.5.before = f32[4,2,16,4096]{3,2,1,0:T(8,128)} custom-call(s32[4,8]{1,0:T(4,128)S(1)} %copy-done.2, f32[16,128]{1,0:T(8,128)S(1)} %broadcast_in_dim.18.modulus_ref.modulus, f32[1,2,8,4096]{3,2,1,0:T(8,128)S(1)} %collective-permute-done.10.part, f32[2,2,16,4096]{3,2,1,0:T(8,128)S(1)} %get-tuple-element.25.held, ...), custom_call_target="tpu_custom_call", output_to_operand_aliasing={{}: (4, {})} | custom-call | flops 1310720 | bytes 786432 | tf_op jit(solution)/shard_map/finish/pallas_call | solution.py:274
  69.7 1.9 %collective-permute-done.7.part = f32[1,2,8,4096]{3,2,1,0:T(8,128)S(1)} collective-permute-done((f32[1,2,8,4096]{3,2,1,0:T(8,128)S(1)}, f32[1,2,8,4096]{3,2,1,0:T(8,128)S(1)}, u32[]{:S(2)}, u32[]{:S(2)}) %collective-permute-start.7) | collective-permute-done | bytes 262176 | tf_op jit(solution)/shard_map/ppermute | solution.py:22
  71.6 1.0 %finish.6.before = f32[4,2,16,4096]{3,2,1,0:T(8,128)} custom-call(s32[4,8]{1,0:T(4,128)S(1)} %copy-done.2, f32[16,128]{1,0:T(8,128)S(1)} %broadcast_in_dim.18.modulus_ref.modulus, f32[1,2,8,4096]{3,2,1,0:T(8,128)S(1)} %collective-permute-done.7.part, f32[2,2,16,4096]{3,2,1,0:T(8,128)S(1)} %get-tuple-element.25.held, ...), custom_call_target="tpu_custom_call", output_to_operand_aliasing={{}: (4, {})} | custom-call | flops 1310720 | bytes 786432 | tf_op jit(solution)/shard_map/finish/pallas_call | solution.py:274
  72.6 3.6 %collective-permute-done.3.part = f32[1,2,8,4096]{3,2,1,0:T(8,128)S(1)} collective-permute-done((f32[1,2,8,4096]{3,2,1,0:T(8,128)S(1)}, f32[1,2,8,4096]{3,2,1,0:T(8,128)S(1)}, u32[]{:S(2)}, u32[]{:S(2)}) %collective-permute-start.3) | collective-permute-done | bytes 262176 | tf_op jit(solution)/shard_map/ppermute | solution.py:22
  76.2 1.0 %finish.7 = f32[4,2,16,4096]{3,2,1,0:T(8,128)} custom-call(s32[4,8]{1,0:T(4,128)S(1)} %copy-done.2, f32[16,128]{1,0:T(8,128)S(1)} %broadcast_in_dim.18.modulus_ref.modulus, f32[1,2,8,4096]{3,2,1,0:T(8,128)S(1)} %collective-permute-done.3.part, f32[2,2,16,4096]{3,2,1,0:T(8,128)S(1)} %get-tuple-element.25.held, ...), custom_call_target="tpu_custom_call", output_to_operand_aliasing={{}: (4, {})} | custom-call | flops 1310720 | bytes 786432 | tf_op jit(solution)/shard_map/finish/pallas_call | solution.py:274
  (5 shorter events, 0.1 us)
Async XLA Ops:
  0.0 39.9 %copy-start = (f32[4,3,2,16,4096]{4,3,2,1,0:T(8,128)S(1)}, f32[4,3,2,16,4096]{4,3,2,1,0:T(8,128)}, u32[]{:S(2)}) copy-start(f32[4,3,2,16,4096]{4,3,2,1,0:T(8,128)} %keys.9) | copy-start | bytes 18874372
  2.3 7.4 %copy-start.2 = (s32[4,8]{1,0:T(4,128)S(1)}, s32[4,8]{1,0:T(4,128)}, u32[]{:S(2)}) copy-start(s32[4,8]{1,0:T(4,128)} %requests.15) | copy-start | bytes 388
  2.3 9.3 %copy-start.4 = (s32[16]{0:T(128)S(1)}, s32[16]{0:T(128)}, u32[]{:S(2)}) copy-start(s32[16]{0:T(128)} %param.9) | copy-start | bytes 196
  2.3 37.6 %copy-start.3 = (s32[8]{0:T(128)S(1)}, s32[8]{0:T(128)}, u32[]{:S(2)}) copy-start(s32[8]{0:T(128)} %rotations.9) | copy-start | bytes 100
  2.3 37.5 %collective-permute-start.11 = (f32[3,8,4096]{2,1,0:T(8,128)S(1)}, f32[3,8,4096]{2,1,0:T(8,128)S(1)}, u32[]{:S(2)}, u32[]{:S(2)}) collective-permute-start(f32[3,8,4096]{2,1,0:T(8,128)S(1)} %gather_digits.3), channel_id=1, source_target_pairs={{0,16},{16,0},{1,17},{17,1},{2,18},{18,2},{3,19},{19,3},{4,20},{20... | collective-permute-start | bytes 1179656 | tf_op jit(solution)/shard_map/ppermute | solution.py:22
  7.5 37.4 %collective-permute-start.5 = (f32[3,8,4096]{2,1,0:T(8,128)S(1)}, f32[3,8,4096]{2,1,0:T(8,128)S(1)}, u32[]{:S(2)}, u32[]{:S(2)}) collective-permute-start(f32[3,8,4096]{2,1,0:T(8,128)S(1)} %get-tuple-element.26), channel_id=1, source_target_pairs={{0,16},{16,0},{1,17},{17,1},{2,18},{18,2},{3,19},{19,3},{4,20},{20... | collective-permute-start | bytes 1179656 | tf_op jit(solution)/shard_map/ppermute | solution.py:22
  7.6 40.0 %collective-permute-start.8 = (f32[3,8,4096]{2,1,0:T(8,128)S(1)}, f32[3,8,4096]{2,1,0:T(8,128)S(1)}, u32[]{:S(2)}, u32[]{:S(2)}) collective-permute-start(f32[3,8,4096]{2,1,0:T(8,128)S(1)} %get-tuple-element.29), channel_id=1, source_target_pairs={{0,16},{16,0},{1,17},{17,1},{2,18},{18,2},{3,19},{19,3},{4,20},{20... | collective-permute-start | bytes 1179656 | tf_op jit(solution)/shard_map/ppermute | solution.py:22
  9.6 39.7 %collective-permute-start.1 = (f32[3,8,4096]{2,1,0:T(8,128)S(1)}, f32[3,8,4096]{2,1,0:T(8,128)S(1)}, u32[]{:S(2)}, u32[]{:S(2)}) collective-permute-start(f32[3,8,4096]{2,1,0:T(8,128)S(1)} %get-tuple-element.20), channel_id=1, source_target_pairs={{0,16},{16,0},{1,17},{17,1},{2,18},{18,2},{3,19},{19,3},{4,20},{20... | collective-permute-start | bytes 1179656 | tf_op jit(solution)/shard_map/ppermute | solution.py:22
  9.7 30.1 %collective-permute-start = (s32[4,8]{1,0:T(4,128)S(1)}, s32[4,8]{1,0:T(4,128)S(1)}, u32[]{:S(2)}, u32[]{:S(2)}) collective-permute-start(s32[4,8]{1,0:T(4,128)S(1)} %copy-done.2), channel_id=1, source_target_pairs={{0,16},{16,0},{1,17},{17,1},{2,18},{18,2},{3,19},{19,3},{4,20},{20... | collective-permute-start | bytes 392 | tf_op jit(solution)/shard_map/ppermute | solution.py:22
  41.4 9.6 %collective-permute-start.12 = (f32[1,2,8,512]{3,2,1,0:T(8,128)S(1)}, f32[1,2,8,512]{3,2,1,0:T(8,128)S(1)}, u32[]{:S(2)}, u32[]{:S(2)}) collective-permute-start(f32[1,2,8,512]{3,2,1,0:T(8,128)S(1)} %get-tuple-element.32), channel_id=1, source_target_pairs={{0,15},{1,0},{2,1},{3,2},{4,3},{5,4},{6,5},{7,6},{8,7},{9,8},{10,9... | collective-permute-start | bytes 98312 | tf_op jit(solution)/shard_map/ppermute | solution.py:22
  46.0 7.3 %collective-permute-start.6 = (f32[1,2,8,512]{3,2,1,0:T(8,128)S(1)}, f32[1,2,8,512]{3,2,1,0:T(8,128)S(1)}, u32[]{:S(2)}, u32[]{:S(2)}) collective-permute-start(f32[1,2,8,512]{3,2,1,0:T(8,128)S(1)} %get-tuple-element.27), channel_id=1, source_target_pairs={{0,15},{1,0},{2,1},{3,2},{4,3},{5,4},{6,5},{7,6},{8,7},{9,8},{10,9... | collective-permute-start | bytes 98312 | tf_op jit(solution)/shard_map/ppermute | solution.py:22
  49.2 2.2 %collective-permute-start.9 = (f32[1,2,8,512]{3,2,1,0:T(8,128)S(1)}, f32[1,2,8,512]{3,2,1,0:T(8,128)S(1)}, u32[]{:S(2)}, u32[]{:S(2)}) collective-permute-start(f32[1,2,8,512]{3,2,1,0:T(8,128)S(1)} %get-tuple-element.30), channel_id=1, source_target_pairs={{0,15},{1,0},{2,1},{3,2},{4,3},{5,4},{6,5},{7,6},{8,7},{9,8},{10,9... | collective-permute-start | bytes 98312 | tf_op jit(solution)/shard_map/ppermute | solution.py:22
  49.3 6.2 %copy-start.1 = (f32[4,3,16,4096]{3,2,1,0:T(8,128)S(1)}, f32[4,3,16,4096]{3,2,1,0:T(8,128)}, u32[]{:S(2)}) copy-start(f32[4,3,16,4096]{3,2,1,0:T(8,128)} %digits.5) | copy-start | bytes 9437188
  50.5 3.2 %collective-permute-start.2 = (f32[1,2,8,512]{3,2,1,0:T(8,128)S(1)}, f32[1,2,8,512]{3,2,1,0:T(8,128)S(1)}, u32[]{:S(2)}, u32[]{:S(2)}) collective-permute-start(f32[1,2,8,512]{3,2,1,0:T(8,128)S(1)} %get-tuple-element.21), channel_id=1, source_target_pairs={{0,15},{1,0},{2,1},{3,2},{4,3},{5,4},{6,5},{7,6},{8,7},{9,8},{10,9... | collective-permute-start | bytes 98312 | tf_op jit(solution)/shard_map/ppermute | solution.py:22
  51.1 16.5 %collective-permute-start.13 = (f32[1,2,8,4096]{3,2,1,0:T(8,128)S(1)}, f32[1,2,8,4096]{3,2,1,0:T(8,128)S(1)}, u32[]{:S(2)}, u32[]{:S(2)}) collective-permute-start(f32[1,2,8,4096]{3,2,1,0:T(8,128)S(1)} %add_tail.9), channel_id=1, source_target_pairs={{0,16},{16,0},{1,17},{17,1},{2,18},{18,2},{3,19},{19,3},{4,20},{20... | collective-permute-start | bytes 786440 | tf_op jit(solution)/shard_map/ppermute | solution.py:22
  51.5 17.2 %collective-permute-start.10 = (f32[1,2,8,4096]{3,2,1,0:T(8,128)S(1)}, f32[1,2,8,4096]{3,2,1,0:T(8,128)S(1)}, u32[]{:S(2)}, u32[]{:S(2)}) collective-permute-start(f32[1,2,8,4096]{3,2,1,0:T(8,128)S(1)} %add_tail.8), channel_id=1, source_target_pairs={{0,16},{16,0},{1,17},{17,1},{2,18},{18,2},{3,19},{19,3},{4,20},{20... | collective-permute-start | bytes 786440 | tf_op jit(solution)/shard_map/ppermute | solution.py:22
  53.3 18.3 %collective-permute-start.7 = (f32[1,2,8,4096]{3,2,1,0:T(8,128)S(1)}, f32[1,2,8,4096]{3,2,1,0:T(8,128)S(1)}, u32[]{:S(2)}, u32[]{:S(2)}) collective-permute-start(f32[1,2,8,4096]{3,2,1,0:T(8,128)S(1)} %add_tail.7), channel_id=1, source_target_pairs={{0,16},{16,0},{1,17},{17,1},{2,18},{18,2},{3,19},{19,3},{4,20},{20... | collective-permute-start | bytes 786440 | tf_op jit(solution)/shard_map/ppermute | solution.py:22
  53.7 22.5 %collective-permute-start.3 = (f32[1,2,8,4096]{3,2,1,0:T(8,128)S(1)}, f32[1,2,8,4096]{3,2,1,0:T(8,128)S(1)}, u32[]{:S(2)}, u32[]{:S(2)}) collective-permute-start(f32[1,2,8,4096]{3,2,1,0:T(8,128)S(1)} %add_tail.5), channel_id=1, source_target_pairs={{0,16},{16,0},{1,17},{17,1},{2,18},{18,2},{3,19},{19,3},{4,20},{20... | collective-permute-start | bytes 786440 | tf_op jit(solution)/shard_map/ppermute | solution.py:22
  57.8 4.5 %collective-permute-start.4 = (f32[2,2,16,512]{3,2,1,0:T(8,128)S(1)}, f32[2,2,16,512]{3,2,1,0:T(8,128)S(1)}, u32[]{:S(2)}, u32[]{:S(2)}) collective-permute-start(f32[2,2,16,512]{3,2,1,0:T(8,128)S(1)} %get-tuple-element.23), channel_id=1, source_target_pairs={{0,15},{1,0},{2,1},{3,2},{4,3},{5,4},{6,5},{7,6},{8,7},{9,8},{10,9... | collective-permute-start | bytes 393224 | tf_op jit(solution)/shard_map/ppermute | solution.py:22
